TPU v7x, 32 devices: a whole 2x2x4 slice. The times are simulated.
32 devices in a mesh: section: 2 (over core), chan: 4 (over z), tok: 4 (over y, x).
Axes of the slice: x: 2, y: 2, z: 4, core: 2. Of those that a mesh axis runs over, the one named last changes fastest.
Arguments:
- gate_streams: bfloat16 [2, 2, 8192, 2048], P('section', None, 'chan', 'tok'), may hold values from -6 to 6
- inputs: bfloat16 [8192, 2048], P('chan', 'tok'), may hold values from -6 to 6
- medium_taps: bfloat16 [8192, 128], P('chan'), may hold values from -0.5 to 0.5
- residues: float32 [8192, 16], P('chan'), may hold values from -3 to 3
- decay_rates: float32 [8192, 16], P('chan'), may hold values from 9.2773438e-05 to 0.034, as said below
Outputs:
- mixer_out: bfloat16 [2, 8192, 2048], P('section', 'chan', 'tok')
Inputs may be any that keep to these rules, and one draw needn't show every extreme that they name: `decay_rates`: every rate is positive.
All inputs are finite; a program needn't handle non-finite values.
Results may differ from a plain program's by a relative error of at most 0.0057.
Values may be sent and summed in bfloat16 or wider, within the bound.
No kernel may reach another device: no remote copies, remote signals or barrier semaphores. Data moves between devices by JAX's collectives and lax.ppermute only.
A program may use at most 128 MiB of HBM per device.

v0:
```python
import functools

import jax
import jax.numpy as jnp
import numpy as np
from jax import lax
from jax.experimental import pallas as pl
from jax.experimental.pallas import tpu as pltpu
from jax.sharding import PartitionSpec as P

SEGS = 8


def split_pair(matrix):
    high = jnp.asarray(matrix, jnp.float32).astype(jnp.bfloat16)
    low = (jnp.asarray(matrix, jnp.float32) - high.astype(jnp.float32)).astype(jnp.bfloat16)
    return high, low


def fourier_tables(window):
    size = 2 * window
    time = np.arange(size)[:, None]
    freq = np.arange(window)[None, :]
    angle = 2.0 * np.pi * ((time * freq) % size) / size
    nyquist = np.where(time % 2 == 0, 1.0, -1.0)
    real = np.cos(angle)
    imag = -np.sin(angle)
    imag_packed = imag.copy()
    imag_packed[:, :1] = nyquist
    forward = np.concatenate([real, imag_packed], axis=1)
    real_packed = real.copy()
    real_packed[:, :1] = nyquist
    taps_forward = np.concatenate([real, real_packed, imag], axis=1)[:window]
    weight = np.where(freq == 0, 1.0, 2.0) / size
    inverse_real = (np.cos(angle) * weight)[window:].T
    inverse_imag = -np.sin(angle) * weight
    inverse_imag[:, :1] = nyquist / size
    inverse = np.concatenate([inverse_real, inverse_imag[window:].T], axis=0)
    return forward, taps_forward, inverse


def dot_f32(left, right):
    return jnp.dot(left, right, preferred_element_type=jnp.float32)


def medium_kernel(
    place, gate_in, inputs, halo, gate_out, taps, fwd_h, fwd_l, tap_h, tap_l, inv_h, inv_l, out
):
    @pl.when(place[0] == 0)
    def _():
        channels, tokens = inputs.shape
        window = taps.shape[1]
        blocks = tokens // window
        product = (gate_in[0, 0].astype(jnp.float32) * inputs[...].astype(jnp.float32)).astype(
            jnp.bfloat16
        )
        started = jnp.where(place[1] > 0, 1.0, 0.0).astype(jnp.bfloat16)
        previous = halo[...] * started
        tap_rows = taps[...]
        tap_spec = dot_f32(tap_rows, tap_h[...]) + dot_f32(tap_rows, tap_l[...])
        real_a = tap_spec[:, :window]
        real_b = tap_spec[:, window : 2 * window]
        imag = tap_spec[:, 2 * window :]
        for block in range(blocks):
            current = product[:, block * window : (block + 1) * window]
            both = jnp.concatenate([previous, current], axis=1)
            spec = dot_f32(both, fwd_h[...]) + dot_f32(both, fwd_l[...])
            spec_a = spec[:, :window]
            spec_b = spec[:, window:]
            filtered = jnp.concatenate(
                [spec_a * real_a - spec_b * imag, spec_a * imag + spec_b * real_b], axis=1
            )
            high = filtered.astype(jnp.bfloat16)
            low = (filtered - high.astype(jnp.float32)).astype(jnp.bfloat16)
            medium = dot_f32(high, inv_h[...]) + (
                dot_f32(low, inv_h[...]) + dot_f32(high, inv_l[...])
            )
            gate = gate_out[0, 0, :, block * window : (block + 1) * window].astype(jnp.float32)
            out[:, block * window : (block + 1) * window] = (gate * medium).astype(jnp.bfloat16)
            previous = current


def medium_call(place, gate_streams, inputs, halo, taps, first, count):
    channels, tokens = count, inputs.shape[1]
    window = taps.shape[1]
    step = min(256, channels)
    base = first // step
    forward, taps_forward, inverse = fourier_tables(window)
    tables = split_pair(forward) + split_pair(taps_forward) + split_pair(inverse)

    def mine(i, place):
        return jnp.where(place[0] == 0, base + i, base)

    def whole(array):
        return pl.BlockSpec(array.shape, lambda i, place: (0, 0))

    return pl.pallas_call(
        medium_kernel,
        out_shape=jax.ShapeDtypeStruct((channels, tokens), jnp.bfloat16),
        grid_spec=pltpu.PrefetchScalarGridSpec(
            num_scalar_prefetch=1,
            grid=(channels // step,),
            in_specs=[
                pl.BlockSpec((1, 1, step, tokens), lambda i, place: (0, 1, mine(i, place), 0)),
                pl.BlockSpec((step, tokens), lambda i, place: (mine(i, place), 0)),
                pl.BlockSpec((step, window), lambda i, place: (mine(i, place), 0)),
                pl.BlockSpec((1, 1, step, tokens), lambda i, place: (0, 0, mine(i, place), 0)),
                pl.BlockSpec((step, window), lambda i, place: (mine(i, place), 0)),
            ]
            + [whole(t) for t in tables],
            out_specs=pl.BlockSpec(
                (step, tokens), lambda i, place: (jnp.where(place[0] == 0, i, 0), 0)
            ),
        ),
        name="medium",
    )(place, gate_streams, inputs, halo, gate_streams, taps, *tables)


def transposed_signal(signal, target):
    size = signal.shape[0]
    for block in range(signal.shape[1] // size):
        target[block * size : (block + 1) * size, :] = signal[
            :, block * size : (block + 1) * size
        ].T


def gated(gate_in, inputs, gated_medium):
    stream = inputs[...].astype(jnp.float32) + gated_medium[...].astype(jnp.float32)
    signal = (gate_in[0, 0].astype(jnp.float32) * stream).astype(jnp.bfloat16)
    return stream, signal.astype(jnp.float32)


def final_kernel(place, gate_in, inputs, gated_medium, rates, ends, total, turned):
    @pl.when(place[0] == 1)
    def _():
        _, signal = gated(gate_in, inputs, gated_medium)
        transposed_signal(signal, turned)
        width, tokens = signal.shape
        length = tokens // SEGS
        slow = rates[...].T
        modes = slow.shape[0]
        decay = jnp.exp(-slow)
        factors = [jnp.broadcast_to(decay[n : n + 1], (SEGS, width)) for n in range(modes)]

        def advance(i, states):
            fresh = turned[pl.ds(i, SEGS, stride=length), :]
            return tuple(s * f + fresh for s, f in zip(states, factors))

        states = lax.fori_loop(
            0,
            length,
            advance,
            tuple(jnp.zeros((SEGS, width), jnp.float32) for _ in range(modes)),
            unroll=4,
        )
        behind = (
            (SEGS - 1 - lax.broadcasted_iota(jnp.int32, (SEGS, width), 0)) * length
        ).astype(jnp.float32)
        rows = []
        for n in range(modes):
            ends[n] = states[n]
            weight = jnp.exp(-jnp.broadcast_to(slow[n : n + 1], (SEGS, width)) * behind)
            rows.append(jnp.sum(states[n] * weight, axis=0, keepdims=True))
        total[...] = jnp.concatenate(rows, axis=0)


def final_call(place, gate_streams, inputs, gated_medium, rates, first, count):
    tokens = inputs.shape[1]
    modes = rates.shape[1]
    step = 128
    base = first // step

    def here(i, place):
        return jnp.where(place[0] == 1, i, 0)

    def mine(i, place):
        return base + here(i, place)

    return pl.pallas_call(
        final_kernel,
        out_shape=(
            jax.ShapeDtypeStruct((modes, SEGS, count), jnp.float32),
            jax.ShapeDtypeStruct((modes, count), jnp.float32),
        ),
        grid_spec=pltpu.PrefetchScalarGridSpec(
            num_scalar_prefetch=1,
            grid=(count // step,),
            in_specs=[
                pl.BlockSpec((1, 1, step, tokens), lambda i, place: (0, 1, mine(i, place), 0)),
                pl.BlockSpec((step, tokens), lambda i, place: (mine(i, place), 0)),
                pl.BlockSpec((step, tokens), lambda i, place: (here(i, place), 0)),
                pl.BlockSpec((step, modes), lambda i, place: (mine(i, place), 0)),
            ],
            out_specs=(
                pl.BlockSpec((modes, SEGS, step), lambda i, place: (0, 0, here(i, place))),
                pl.BlockSpec((modes, step), lambda i, place: (0, here(i, place))),
            ),
            scratch_shapes=[pltpu.VMEM((tokens, step), jnp.float32)],
        ),
        name="final_states",
    )(place, gate_streams, inputs, gated_medium, rates)


def long_kernel(
    hops,
    place,
    gate_in,
    inputs,
    other_medium,
    own_medium,
    gate_out,
    rates,
    residues,
    ends,
    *rest,
):
    arrived = rest[:hops]
    out, turned, answer = rest[hops:]

    @pl.when(place[0] == 0)
    def _():
        out[0] = own_medium[...]

    @pl.when(place[0] == 1)
    def _():
        stream, signal = gated(gate_in, inputs, other_medium)
        transposed_signal(signal, turned)
        width, tokens = signal.shape
        length = tokens // SEGS
        slow = rates[...].T
        modes = slow.shape[0]
        scaled = residues[...].T * jnp.sqrt(1.0 - jnp.exp(-2.0 * slow))
        decay = jnp.exp(-slow)
        leap = jnp.exp(-slow * length)
        entering = jnp.zeros((modes, width), jnp.float32)
        for k in range(hops):
            keep = jnp.where(place[1] > k, 1.0, 0.0)
            entering = entering + arrived[k][...] * (jnp.exp(-slow * (tokens * k)) * keep)
        starts = []
        for n in range(modes):
            state = entering[n : n + 1]
            rows = [state]
            for seg in range(SEGS - 1):
                state = state * leap[n : n + 1] + ends[n, seg : seg + 1, :]
                rows.append(state)
            starts.append(jnp.concatenate(rows, axis=0))
        factors = [jnp.broadcast_to(decay[n : n + 1], (SEGS, width)) for n in range(modes)]
        weights = [jnp.broadcast_to(scaled[n : n + 1], (SEGS, width)) for n in range(modes)]

        def advance(i, states):
            fresh = turned[pl.ds(i, SEGS, stride=length), :]
            states = tuple(s * f + fresh for s, f in zip(states, factors))
            terms = [s * w for s, w in zip(states, weights)]
            while len(terms) > 1:
                terms = [a + b for a, b in zip(terms[::2], terms[1::2])]
            answer[pl.ds(i, SEGS, stride=length), :] = terms[0]
            return states

        lax.fori_loop(0, length, advance, tuple(starts), unroll=4)
        for block in range(tokens // width):
            part = slice(block * width, (block + 1) * width)
            gate = gate_out[0, 0, :, part].astype(jnp.float32)
            out[0, :, part] = (stream[:, part] + gate * answer[part, :].T).astype(jnp.bfloat16)


def long_call(place, gate_streams, inputs, other, own, rates, residues, ends, arrived, first):
    count, tokens = own.shape
    modes = rates.shape[1]
    step = 128
    base = first // step

    def here(i, place):
        return jnp.where(place[0] == 1, i, 0)

    def mine(i, place):
        return base + here(i, place)

    wide = (step, tokens)
    return pl.pallas_call(
        functools.partial(long_kernel, len(arrived)),
        out_shape=jax.ShapeDtypeStruct((1, count, tokens), jnp.bfloat16),
        grid_spec=pltpu.PrefetchScalarGridSpec(
            num_scalar_prefetch=1,
            grid=(count // step,),
            in_specs=[
                pl.BlockSpec((1, 1) + wide, lambda i, place: (0, 1, mine(i, place), 0)),
                pl.BlockSpec(wide, lambda i, place: (mine(i, place), 0)),
                pl.BlockSpec(wide, lambda i, place: (here(i, place), 0)),
                pl.BlockSpec(wide, lambda i, place: (jnp.where(place[0] == 0, i, 0), 0)),
                pl.BlockSpec((1, 1) + wide, lambda i, place: (0, 0, mine(i, place), 0)),
                pl.BlockSpec((step, modes), lambda i, place: (mine(i, place), 0)),
                pl.BlockSpec((step, modes), lambda i, place: (mine(i, place), 0)),
                pl.BlockSpec((modes, SEGS, step), lambda i, place: (0, 0, here(i, place))),
            ]
            + [pl.BlockSpec((modes, step), lambda i, place: (0, here(i, place)))] * len(arrived),
            out_specs=pl.BlockSpec((1,) + wide, lambda i, place: (0, i, 0)),
            scratch_shapes=[pltpu.VMEM((tokens, step), jnp.float32)] * 2,
        ),
        name="long",
    )(place, gate_streams, inputs, other, own, gate_streams, rates, residues, ends, *arrived)


def ring(value, axis, by):
    peers = lax.axis_size(axis)
    return lax.ppermute(value, axis, [(i, (i + by) % peers) for i in range(peers)])


def on_device(gate_streams, inputs, medium_taps, residues, decay_rates):
    channels, tokens = inputs.shape
    window = medium_taps.shape[1]
    place = jnp.stack([lax.axis_index("section"), lax.axis_index("tok")]).astype(jnp.int32)
    tail = slice(tokens - window, tokens)
    edge = (
        gate_streams[0, 1, :, tail].astype(jnp.float32) * inputs[:, tail].astype(jnp.float32)
    ).astype(jnp.bfloat16)
    halo = ring(edge, "tok", 1)
    medium = medium_call(place, gate_streams, inputs, halo, medium_taps, 0, channels)
    other = ring(medium, "section", 1)
    ends, total = final_call(place, gate_streams, inputs, other, decay_rates, 0, channels)
    arrived = [ring(total, "tok", by) for by in range(1, lax.axis_size("tok"))]
    return long_call(
        place, gate_streams, inputs, other, medium, decay_rates, residues, ends, arrived, 0
    )


def solution(mesh):
    placed = (
        P("section", None, "chan", "tok"),
        P("chan", "tok"),
        P("chan", None),
        P("chan", None),
        P("chan", None),
    )
    return jax.shard_map(
        on_device,
        mesh=mesh,
        in_specs=placed,
        out_specs=P("section", "chan", "tok"),
        check_vma=False,
    )
```

profile of v0, /device:TPU:1, one launch (start us, length us, event | category | flops | bytes accessed | tf_op | source)
XLA Modules:
  0.0 87.7 jit_solution(622947353323003899)
XLA Ops:
  0.0 1.4 %fusion = bf16[2048,128]{1,0:T(8,128)(2,1)S(1)} fusion(bf16[2048,512]{1,0:T(8,128)(2,1)} %inputs.5, bf16[1,2,2048,512]{3,2,1,0:T(8,128)(2,1)} %gate_out.3), kind=kLoop, calls=%fused_computation.1 | loop fusion | flops 1048576 | bytes 1572864 | tf_op jit(solution)/shard_map/convert_element_type | solution.py:315
  1.4 2.1 %collective-permute-start = (bf16[2048,128]{1,0:T(8,128)(2,1)S(1)}, bf16[2048,128]{1,0:T(8,128)(2,1)S(1)}, u32[]{:S(2)}, u32[]{:S(2)}) collective-permute-start(bf16[2048,128]{1,0:T(8,128)(2,1)S(1)} %fusion), channel_id=1, source_target_pairs={{0,1},{1,2},{2,3},{3,0},{4,5},{5,6},{6,7},{7,4},{8,9},{9,10},{10,1... | collective-permute-start | bytes 1572872 | tf_op jit(solution)/shard_map/ppermute | solution.py:305
  3.4 0.6 pad_add_fusion.place
  4.0 0.0 copy-start.5
  4.0 12.0 %collective-permute-done.halo = bf16[2048,128]{1,0:T(8,128)(2,1)S(1)} collective-permute-done((bf16[2048,128]{1,0:T(8,128)(2,1)S(1)}, bf16[2048,128]{1,0:T(8,128)(2,1)S(1)}, u32[]{:S(2)}, u32[]{:S(2)}) %collective-permute-start) | collective-permute-done | bytes 524320 | tf_op jit(solution)/shard_map/ppermute | solution.py:305
  16.0 0.0 copy-start.1
  16.0 0.8 copy-done.1
  16.8 3.3 %medium.1.own_medium = bf16[2048,512]{1,0:T(8,128)(2,1)} custom-call(s32[2]{0:T(128)} %pad_add_fusion.place, bf16[1,2,2048,512]{3,2,1,0:T(8,128)(2,1)} %gate_out.3, bf16[2048,512]{1,0:T(8,128)(2,1)} %inputs.5, bf16[2048,128]{1,0:T(8,128)(2,1)} %copy-done.1, bf16[1,2,2048,512]{3,2,1,0:T(8,128)(2,1)} %gate_out.3, bf16[2048,128]{1,0:T(8,128)(2,1)} %taps.1, ...), custom_call_target="tpu_custom_call" | custom-call | tf_op jit(solution)/shard_map/medium/pallas_call | solution.py:97
  20.1 14.7 %collective-permute-start.1 = (bf16[2048,512]{1,0:T(8,128)(2,1)}, bf16[2048,512]{1,0:T(8,128)(2,1)S(1)}, u32[]{:S(2)}, u32[]{:S(2)}) collective-permute-start(bf16[2048,512]{1,0:T(8,128)(2,1)} %medium.1.own_medium), channel_id=1, source_target_pairs={{0,16},{16,0},{1,17},{17,1},{2,18},{18,2},{3,19},{19,3},{4,20},{20... | collective-permute-start | bytes 6291464 | tf_op jit(solution)/shard_map/ppermute | solution.py:305
  34.8 0.0 copy-done.5
  34.8 1.3 %copy.13.rates = f32[2048,16]{1,0:T(8,128)} copy(f32[2048,16]{0,1:T(8,128)S(1)} %copy-done.5) | data formatting | bytes 262144 | tf_op args[4]
  36.1 0.0 copy-start.6
  36.1 2.7 %collective-permute-done.1.gated_medium.other_medium = bf16[2048,512]{1,0:T(8,128)(2,1)S(1)} collective-permute-done((bf16[2048,512]{1,0:T(8,128)(2,1)}, bf16[2048,512]{1,0:T(8,128)(2,1)S(1)}, u32[]{:S(2)}, u32[]{:S(2)}) %collective-permute-start.1) | collective-permute-done | bytes 2097184 | tf_op jit(solution)/shard_map/ppermute | solution.py:305
  38.8 0.0 copy-start
  38.8 1.3 %copy-done = bf16[2048,512]{1,0:T(8,128)(2,1)} copy-done((bf16[2048,512]{1,0:T(8,128)(2,1)}, bf16[2048,512]{1,0:T(8,128)(2,1)S(1)}, u32[]{:S(2)}) %copy-start) | copy-done | bytes 2097176
  40.1 16.0 %final_states.1 = (f32[16,8,2048]{2,1,0:T(8,128)}, f32[16,2048]{1,0:T(8,128)}) custom-call(s32[2]{0:T(128)} %pad_add_fusion.place, bf16[1,2,2048,512]{3,2,1,0:T(8,128)(2,1)} %gate_out.3, bf16[2048,512]{1,0:T(8,128)(2,1)} %inputs.5, bf16[2048,512]{1,0:T(8,128)(2,1)} %copy-done, f32[2048,16]{1,0:T(8,128)} %copy.13.rates), custom_call_target="tpu_custom_call" | custom-call | tf_op jit(solution)/shard_map/final_states/pallas_call | solution.py:179
  56.1 1.5 %collective-permute-start.4 = (f32[16,2048]{1,0:T(8,128)}, f32[16,2048]{1,0:T(8,128)S(1)}, u32[]{:S(2)}, u32[]{:S(2)}) collective-permute-start(f32[16,2048]{1,0:T(8,128)} %get-tuple-element.8), channel_id=1, source_target_pairs={{0,3},{1,0},{2,1},{3,2},{4,7},{5,4},{6,5},{7,6},{8,11},{9,8},{10,9... | collective-permute-start | bytes 393224 | tf_op jit(solution)/shard_map/ppermute | solution.py:305
  57.5 0.2 collective-permute-start.3
  57.8 1.2 %collective-permute-start.2 = (f32[16,2048]{1,0:T(8,128)}, f32[16,2048]{1,0:T(8,128)S(1)}, u32[]{:S(2)}, u32[]{:S(2)}) collective-permute-start(f32[16,2048]{1,0:T(8,128)} %get-tuple-element.8), channel_id=1, source_target_pairs={{0,1},{1,2},{2,3},{3,0},{4,5},{5,6},{6,7},{7,4},{8,9},{9,10},{10,1... | collective-permute-start | bytes 393224 | tf_op jit(solution)/shard_map/ppermute | solution.py:305
  59.0 0.0 copy-done.6
  59.0 1.3 %copy.14.residues = f32[2048,16]{1,0:T(8,128)} copy(f32[2048,16]{0,1:T(8,128)S(1)} %copy-done.6) | data formatting | bytes 262144 | tf_op args[3]
  60.3 0.0 collective-permute-done.4.rest_2_
  60.3 0.0 copy-start.2
  60.3 2.7 %collective-permute-done.3.rest_1_ = f32[16,2048]{1,0:T(8,128)S(1)} collective-permute-done((f32[16,2048]{1,0:T(8,128)}, f32[16,2048]{1,0:T(8,128)S(1)}, u32[]{:S(2)}, u32[]{:S(2)}) %collective-permute-start.3) | collective-permute-done | bytes 131104 | tf_op jit(solution)/shard_map/ppermute | solution.py:305
  63.0 0.0 copy-start.3
  63.0 0.0 collective-permute-done.2.rest_0_
  63.0 0.0 copy-start.4
  63.0 0.0 copy-done.2
  63.0 0.6 copy-done.3
  63.6 0.1 copy-done.4
  63.7 24.1 %long.1 = bf16[1,2048,512]{2,1,0:T(8,128)(2,1)} custom-call(s32[2]{0:T(128)} %pad_add_fusion.place, bf16[1,2,2048,512]{3,2,1,0:T(8,128)(2,1)} %gate_out.3, bf16[2048,512]{1,0:T(8,128)(2,1)} %inputs.5, bf16[2048,512]{1,0:T(8,128)(2,1)} %copy-done, bf16[2048,512]{1,0:T(8,128)(2,1)} %medium.1.own_medium, bf16[1,2,2048,512]{3,2,1,0:T(8,128)(2,1)} %gate_out.3, ...), custom_call_target="tpu_custom_call" | custom-call | tf_op jit(solution)/shard_map/long/pallas_call | solution.py:279
Async XLA Ops:
  1.4 14.7 %collective-permute-start = (bf16[2048,128]{1,0:T(8,128)(2,1)S(1)}, bf16[2048,128]{1,0:T(8,128)(2,1)S(1)}, u32[]{:S(2)}, u32[]{:S(2)}) collective-permute-start(bf16[2048,128]{1,0:T(8,128)(2,1)S(1)} %fusion), channel_id=1, source_target_pairs={{0,1},{1,2},{2,3},{3,0},{4,5},{5,6},{6,7},{7,4},{8,9},{9,10},{10,1... | collective-permute-start | bytes 1572872 | tf_op jit(solution)/shard_map/ppermute | solution.py:305
  4.0 30.7 %copy-start.5 = (f32[2048,16]{0,1:T(8,128)S(1)}, f32[2048,16]{0,1:T(8,128)}, u32[]{:S(2)}) copy-start(f32[2048,16]{0,1:T(8,128)} %param.15) | copy-start | bytes 393220
  16.0 0.8 copy-start.1
  20.1 18.7 %collective-permute-start.1 = (bf16[2048,512]{1,0:T(8,128)(2,1)}, bf16[2048,512]{1,0:T(8,128)(2,1)S(1)}, u32[]{:S(2)}, u32[]{:S(2)}) collective-permute-start(bf16[2048,512]{1,0:T(8,128)(2,1)} %medium.1.own_medium), channel_id=1, source_target_pairs={{0,16},{16,0},{1,17},{17,1},{2,18},{18,2},{3,19},{19,3},{4,20},{20... | collective-permute-start | bytes 6291464 | tf_op jit(solution)/shard_map/ppermute | solution.py:305
  36.1 22.9 %copy-start.6 = (f32[2048,16]{0,1:T(8,128)S(1)}, f32[2048,16]{0,1:T(8,128)}, u32[]{:S(2)}) copy-start(f32[2048,16]{0,1:T(8,128)} %param.14) | copy-start | bytes 393220
  38.8 1.3 %copy-start = (bf16[2048,512]{1,0:T(8,128)(2,1)}, bf16[2048,512]{1,0:T(8,128)(2,1)S(1)}, u32[]{:S(2)}) copy-start(bf16[2048,512]{1,0:T(8,128)(2,1)S(1)} %collective-permute-done.1.gated_medium.other_medium) | copy-start | bytes 6291460
  56.1 4.2 %collective-permute-start.4 = (f32[16,2048]{1,0:T(8,128)}, f32[16,2048]{1,0:T(8,128)S(1)}, u32[]{:S(2)}, u32[]{:S(2)}) collective-permute-start(f32[16,2048]{1,0:T(8,128)} %get-tuple-element.8), channel_id=1, source_target_pairs={{0,3},{1,0},{2,1},{3,2},{4,7},{5,4},{6,5},{7,6},{8,11},{9,8},{10,9... | collective-permute-start | bytes 393224 | tf_op jit(solution)/shard_map/ppermute | solution.py:305
  57.5 5.4 %collective-permute-start.3 = (f32[16,2048]{1,0:T(8,128)}, f32[16,2048]{1,0:T(8,128)S(1)}, u32[]{:S(2)}, u32[]{:S(2)}) collective-permute-start(f32[16,2048]{1,0:T(8,128)} %get-tuple-element.8), channel_id=1, source_target_pairs={{0,2},{1,3},{2,0},{3,1},{4,6},{5,7},{6,4},{7,5},{8,10},{9,11},{10,... | collective-permute-start | bytes 393224 | tf_op jit(solution)/shard_map/ppermute | solution.py:305
  57.8 5.2 %collective-permute-start.2 = (f32[16,2048]{1,0:T(8,128)}, f32[16,2048]{1,0:T(8,128)S(1)}, u32[]{:S(2)}, u32[]{:S(2)}) collective-permute-start(f32[16,2048]{1,0:T(8,128)} %get-tuple-element.8), channel_id=1, source_target_pairs={{0,1},{1,2},{2,3},{3,0},{4,5},{5,6},{6,7},{7,4},{8,9},{9,10},{10,1... | collective-permute-start | bytes 393224 | tf_op jit(solution)/shard_map/ppermute | solution.py:305
  60.3 2.7 %copy-start.2 = (f32[16,2048]{1,0:T(8,128)}, f32[16,2048]{1,0:T(8,128)S(1)}, u32[]{:S(2)}) copy-start(f32[16,2048]{1,0:T(8,128)S(1)} %collective-permute-done.4.rest_2_) | copy-start | bytes 393220
  63.0 0.6 copy-start.3
  63.0 0.7 copy-start.4
where the time goes:
time: 88.2 us; the launch traced here: 87.7 us
  Pallas kernels  43.3 us (49%)
  starting transfers between devices  19.7 us (22%)
  waiting for transfers between devices  17.3 us (20%)
  local copies, waits for them, and re-layouts  5.44 us (6%)
  other arithmetic  1.96 us (2%)
    pallas_call x1, Pallas kernels, long_call(): pl.pallas_call(functools.partial(long_kernel, len(arrived)), out_shape=ja...  24.1 us
    ppermute x5, starting transfers between devices, ring(): lax.ppermute(value, axis, [(i, (i + by) % peers) for i in range(peers)])  19.7 us
    ppermute x5, waiting for transfers between devices, ring(): lax.ppermute(value, axis, [(i, (i + by) % peers) for i in range(peers)])  17.3 us
    pallas_call x1, Pallas kernels, final_call(): pl.pallas_call(final_kernel, out_shape=(jax.ShapeDtypeStruct((modes, SEGS...  16 us
    unnamed x16, local copies, waits for them, and re-layouts  5.44 us
    pallas_call x1, Pallas kernels, medium_call(): pl.pallas_call(medium_kernel, out_shape=jax.ShapeDtypeStruct((channels, t...  3.27 us
  transfers between devices with their start and end apart: 5, of which 3 were waited for; matrix products, arithmetic and copies ran while one was open for 4% of the time, Pallas kernels for 0%

commit v1 on v0

v1 whole, which is shorter than its diff:
```python
import functools

import jax
import jax.numpy as jnp
import numpy as np
from jax import lax
from jax.experimental import pallas as pl
from jax.experimental.pallas import tpu as pltpu
from jax.sharding import PartitionSpec as P

ROWS = 8


def split_pair(matrix):
    high = jnp.asarray(matrix, jnp.float32).astype(jnp.bfloat16)
    low = (jnp.asarray(matrix, jnp.float32) - high.astype(jnp.float32)).astype(jnp.bfloat16)
    return high, low


def stacked(matrix, axis):
    return jnp.concatenate(split_pair(matrix), axis=axis)


def fourier_tables(window):
    size = 2 * window
    time = np.arange(window)[:, None]
    freq = np.arange(window)[None, :]
    angle = 2.0 * np.pi * ((time * freq) % size) / size
    sign = np.where(freq % 2 == 0, 1.0, -1.0)
    nyquist = np.where(time % 2 == 0, 1.0, -1.0)
    weight = np.where(freq == 0, 1.0, 2.0) / size
    forward, inverse = [], []
    for odd in range(2):
        flip = sign if odd else np.ones_like(sign)
        real = np.cos(angle) * flip
        imag = -np.sin(angle) * flip
        imag[:, :1] = nyquist
        forward.append(stacked(np.concatenate([real, imag], axis=1), 0))
        back_real = np.cos(angle) * weight * flip
        back_imag = -np.sin(angle) * weight * flip
        back_imag[:, :1] = nyquist / size
        inverse.append(stacked(np.concatenate([back_real.T, back_imag.T], axis=0), 1))
    return forward, inverse


def turned_tables(window):
    half = window // 2
    time = np.arange(window)[:, None]
    freq = 2 * np.arange(half)[None, :] + 1
    angle = np.pi * ((time * freq) % (2 * window)) / window
    real, imag = np.cos(angle), -np.sin(angle)
    zero = np.zeros_like(real)
    forward = np.concatenate(
        [
            np.concatenate([real, zero, imag, zero], axis=1),
            np.concatenate([zero, real, zero, imag], axis=1),
        ],
        axis=0,
    )
    inverse = forward.T * (2.0 / window)
    doubled = np.concatenate([real, real, imag, imag], axis=1)
    return forward, inverse, doubled


def dot_f32(left, right):
    return jnp.dot(left, right, preferred_element_type=jnp.float32)


def dot_turned(left, right):
    return lax.dot_general(
        left, right, (((1,), (1,)), ((), ())), preferred_element_type=jnp.float32
    )


def medium_kernel(
    place, gate_in, inputs, halo, gate_out, taps, fwd_even, fwd_odd, inv_even, inv_odd, out
):
    @pl.when(place[0] == 0)
    def _():
        channels, tokens = inputs.shape
        window = taps.shape[1]
        blocks = tokens // window
        forward = (fwd_even, fwd_odd)
        inverse = (inv_even, inv_odd)
        tap_rows = taps[...]
        spec = dot_f32(jnp.concatenate([tap_rows, tap_rows], axis=1), fwd_even[...])
        lane = lax.broadcasted_iota(jnp.int32, (channels, window), 1)
        real, packed = spec[:, :window], spec[:, window:]
        real_b = jnp.where(lane == 0, packed, real)
        imag = jnp.where(lane == 0, 0.0, packed)
        started = jnp.where(place[1] > 0, 1.0, 0.0).astype(jnp.bfloat16)

        def spectrum(block, rows):
            return dot_f32(jnp.concatenate([rows, rows], axis=1), forward[block % 2][...])

        before = spectrum(-1, halo[...] * started)
        for block in range(blocks):
            part = slice(block * window, (block + 1) * window)
            product = gate_in[0, 0, :, part].astype(jnp.float32) * inputs[:, part].astype(
                jnp.float32
            )
            current = spectrum(block, product.astype(jnp.bfloat16))
            total = before + current
            before = current
            a, b = total[:, :window], total[:, window:]
            filtered = jnp.concatenate([a * real - b * imag, a * imag + b * real_b], axis=1)
            pair = dot_f32(filtered.astype(jnp.bfloat16), inverse[block % 2][...])
            medium = pair[:, :window] + pair[:, window:]
            gate = gate_out[0, 0, :, part].astype(jnp.float32)
            out[:, part] = (gate * medium).astype(jnp.bfloat16)


def whole(array):
    return pl.BlockSpec(array.shape, lambda i, place: (0,) * array.ndim)


def only(section, base=0):
    return lambda i, place: jnp.where(place[0] == section, base + i, base)


def medium_call(place, gate_streams, inputs, halo, taps, first, count):
    tokens = inputs.shape[1]
    window = taps.shape[1]
    step = min(256, count)
    forward, inverse = fourier_tables(window)
    tables = forward + inverse
    row = only(0, first // step)
    own = only(0)
    return pl.pallas_call(
        medium_kernel,
        out_shape=jax.ShapeDtypeStruct((count, tokens), jnp.bfloat16),
        grid_spec=pltpu.PrefetchScalarGridSpec(
            num_scalar_prefetch=1,
            grid=(count // step,),
            in_specs=[
                pl.BlockSpec((1, 1, step, tokens), lambda i, p: (0, 1, row(i, p), 0)),
                pl.BlockSpec((step, tokens), lambda i, p: (row(i, p), 0)),
                pl.BlockSpec((step, window), lambda i, p: (own(i, p), 0)),
                pl.BlockSpec((1, 1, step, tokens), lambda i, p: (0, 0, row(i, p), 0)),
                pl.BlockSpec((step, window), lambda i, p: (row(i, p), 0)),
            ]
            + [whole(t) for t in tables],
            out_specs=pl.BlockSpec((step, tokens), lambda i, p: (own(i, p), 0)),
        ),
        name="medium",
    )(place, gate_streams, inputs, halo, gate_streams, taps, *tables)


def lane_mask(modes):
    shape = (ROWS, ROWS * modes)
    lane = lax.broadcasted_iota(jnp.int32, shape, 1)
    return lane // modes == lax.broadcasted_iota(jnp.int32, shape, 0)


def wide_row(ref, group, modes):
    return jnp.broadcast_to(ref[group : group + 1, :], (ROWS, ROWS * modes))


def powers(slow, window, first, falling):
    row = lax.broadcasted_iota(jnp.int32, slow.shape, 0).astype(jnp.float32)
    hop = jnp.exp(-slow * ROWS)
    tile = jnp.exp(-slow * (first + (ROWS - 1 - row if falling else row)))
    tiles = [tile]
    for _ in range(window // ROWS - 1):
        tile = tile * hop
        tiles.append(tile)
    if falling:
        tiles = tiles[::-1]
    return jnp.concatenate(tiles, axis=0).astype(jnp.bfloat16)


def scale_of(residues, slow):
    return residues * jnp.sqrt(1.0 - jnp.exp(-2.0 * slow))


def response_kernel(modes, place, rates, residues, table_h, table_l, out):
    @pl.when(place[0] == 1)
    def _():
        window = table_h.shape[0]
        mask = lane_mask(modes)
        parts = []
        for group in range(rates.shape[0]):
            slow = wide_row(rates, group, modes)
            scale = scale_of(wide_row(residues, group, modes), slow)
            scale = jnp.where(mask, scale / (1.0 + jnp.exp(-slow * window)), 0.0)
            high = scale.astype(jnp.bfloat16).astype(jnp.float32)
            both = jnp.concatenate([high, scale - high], axis=0).astype(jnp.bfloat16)
            pair = dot_turned(both, powers(slow, window, 0.0, False))
            parts.append(pair[:ROWS] + pair[ROWS:])
        taps = jnp.concatenate(parts, axis=0)
        high = taps.astype(jnp.bfloat16)
        low = (taps - high.astype(jnp.float32)).astype(jnp.bfloat16)
        out[...] = dot_f32(high, table_h[...]) + (
            dot_f32(low, table_h[...]) + dot_f32(high, table_l[...])
        )


def response_call(place, rates, residues, modes, window, first, count):
    step = 128
    tables = split_pair(turned_tables(window)[2])
    rows = step // ROWS
    row = only(1, first // step)
    own = only(1)
    return pl.pallas_call(
        functools.partial(response_kernel, modes),
        out_shape=jax.ShapeDtypeStruct((count, 2 * window), jnp.float32),
        grid_spec=pltpu.PrefetchScalarGridSpec(
            num_scalar_prefetch=1,
            grid=(count // step,),
            in_specs=[
                pl.BlockSpec((rows, ROWS * modes), lambda i, p: (row(i, p), 0)),
                pl.BlockSpec((rows, ROWS * modes), lambda i, p: (row(i, p), 0)),
            ]
            + [whole(t) for t in tables],
            out_specs=pl.BlockSpec((step, 2 * window), lambda i, p: (own(i, p), 0)),
        ),
        name="response",
    )(place, rates, residues, *tables)


def stream_part(inputs, gated_medium, part):
    return inputs[:, part].astype(jnp.float32) + gated_medium[:, part].astype(jnp.float32)


def states_kernel(modes, window, place, gate_in, inputs, gated_medium, rates, ends, total):
    @pl.when(place[0] == 1)
    def _():
        blocks = inputs.shape[1] // window
        mask = lane_mask(modes)
        signal = (
            gate_in[0, 0].astype(jnp.float32) * stream_part(inputs, gated_medium, slice(None))
        ).astype(jnp.bfloat16)
        sums = []
        for group in range(rates.shape[0]):
            rows = slice(group * ROWS, (group + 1) * ROWS)
            slow = wide_row(rates, group, modes)
            left = jnp.concatenate(
                [signal[rows, b * window : (b + 1) * window] for b in range(blocks)], axis=0
            )
            found = dot_f32(left, powers(slow, window, 0.0, True))
            leap = jnp.exp(-slow * window)
            state = None
            for b in range(blocks):
                end = jnp.where(mask, found[b * ROWS : (b + 1) * ROWS], 0.0)
                ends[b, rows, :] = end
                state = end if state is None else state * leap + end
            sums.append(jnp.sum(state, axis=0, keepdims=True))
        total[...] = jnp.concatenate(sums, axis=0)


def states_call(place, gate_streams, inputs, gated_medium, rates, modes, window, first, count):
    tokens = inputs.shape[1]
    step = 128
    row = only(1, first // step)
    own = only(1)
    lanes = ROWS * modes
    return pl.pallas_call(
        functools.partial(states_kernel, modes, window),
        out_shape=(
            jax.ShapeDtypeStruct((tokens // window, count, lanes), jnp.float32),
            jax.ShapeDtypeStruct((count // ROWS, lanes), jnp.float32),
        ),
        grid_spec=pltpu.PrefetchScalarGridSpec(
            num_scalar_prefetch=1,
            grid=(count // step,),
            in_specs=[
                pl.BlockSpec((1, 1, step, tokens), lambda i, p: (0, 1, row(i, p), 0)),
                pl.BlockSpec((step, tokens), lambda i, p: (row(i, p), 0)),
                pl.BlockSpec((step, tokens), lambda i, p: (own(i, p), 0)),
                pl.BlockSpec((step // ROWS, lanes), lambda i, p: (row(i, p), 0)),
            ],
            out_specs=(
                pl.BlockSpec((tokens // window, step, lanes), lambda i, p: (0, own(i, p), 0)),
                pl.BlockSpec((step // ROWS, lanes), lambda i, p: (own(i, p), 0)),
            ),
        ),
        name="states",
    )(place, gate_streams, inputs, gated_medium, rates)


def within_kernel(place, gate_in, inputs, gated_medium, response, fwd_h, fwd_l, inverse, out):
    @pl.when(place[0] == 1)
    def _():
        size = fwd_h.shape[0]
        half = size // 2
        real, imag = response[:, :half], response[:, half:]
        for pair in range(inputs.shape[1] // size):
            part = slice(pair * size, (pair + 1) * size)
            signal = (
                gate_in[0, 0, :, part].astype(jnp.float32)
                * stream_part(inputs, gated_medium, part)
            ).astype(jnp.bfloat16)
            spec = dot_f32(signal, fwd_h[...]) + dot_f32(signal, fwd_l[...])
            a, b = spec[:, :half], spec[:, half:]
            filtered = jnp.concatenate([a * real - b * imag, a * imag + b * real], axis=1)
            out[:, part] = dot_f32(filtered.astype(jnp.bfloat16), inverse[...])


def within_call(place, gate_streams, inputs, gated_medium, response, first, count):
    tokens = inputs.shape[1]
    window = response.shape[1] // 2
    step = min(256, count)
    forward, inverse, _ = turned_tables(window)
    tables = split_pair(forward) + split_pair(inverse)[:1]
    row = only(1, first // step)
    own = only(1)
    return pl.pallas_call(
        within_kernel,
        out_shape=jax.ShapeDtypeStruct((count, tokens), jnp.float32),
        grid_spec=pltpu.PrefetchScalarGridSpec(
            num_scalar_prefetch=1,
            grid=(count // step,),
            in_specs=[
                pl.BlockSpec((1, 1, step, tokens), lambda i, p: (0, 1, row(i, p), 0)),
                pl.BlockSpec((step, tokens), lambda i, p: (row(i, p), 0)),
                pl.BlockSpec((step, tokens), lambda i, p: (own(i, p), 0)),
                pl.BlockSpec((step, 2 * window), lambda i, p: (own(i, p), 0)),
            ]
            + [whole(t) for t in tables],
            out_specs=pl.BlockSpec((step, tokens), lambda i, p: (own(i, p), 0)),
        ),
        name="within",
    )(place, gate_streams, inputs, gated_medium, response, *tables)


def output_kernel(
    hops,
    modes,
    window,
    place,
    within,
    inputs,
    other_medium,
    own_medium,
    gate_out,
    rates,
    residues,
    ends,
    *rest,
):
    arrived, out = rest[:hops], rest[hops]

    @pl.when(place[0] == 0)
    def _():
        out[0] = own_medium[...]

    @pl.when(place[0] == 1)
    def _():
        tokens = inputs.shape[1]
        blocks = tokens // window
        mask = lane_mask(modes)
        rows_all = rates[...]
        entering = jnp.zeros_like(rows_all)
        for k in range(hops):
            keep = jnp.where(place[1] > k, 1.0, 0.0)
            entering = entering + arrived[k][...] * (jnp.exp(-rows_all * (tokens * k)) * keep)
        for group in range(rates.shape[0]):
            rows = slice(group * ROWS, (group + 1) * ROWS)
            slow = wide_row(rates, group, modes)
            scale = scale_of(wide_row(residues, group, modes), slow)
            leap = jnp.exp(-slow * window)
            share = scale / (1.0 + leap)
            start = jnp.broadcast_to(entering[group : group + 1], slow.shape)
            state = jnp.where(mask, start, 0.0)
            lefts = []
            for b in range(blocks):
                end = ends[b, rows, :]
                lefts.append(state * scale + end * share)
                state = state * leap + end
            left = jnp.concatenate(lefts, axis=0).astype(jnp.bfloat16)
            across = dot_turned(left, powers(slow, window, 1.0, False))
            for b in range(blocks):
                part = slice(b * window, (b + 1) * window)
                stream = inputs[rows, part].astype(jnp.float32) + other_medium[
                    rows, part
                ].astype(jnp.float32)
                long_out = within[rows, part] + across[b * ROWS : (b + 1) * ROWS]
                gate = gate_out[0, 0, rows, part].astype(jnp.float32)
                out[0, rows, part] = (stream + gate * long_out).astype(jnp.bfloat16)


def output_call(
    place, gate_streams, within, inputs, other, own, rates, residues, ends, arrived, window, first
):
    count, tokens = own.shape
    lanes = rates.shape[1]
    step = 128
    row = only(1, first // step)
    here = only(1)
    there = only(0)
    wide = (step, tokens)
    small = (step // ROWS, lanes)
    return pl.pallas_call(
        functools.partial(output_kernel, len(arrived), lanes // ROWS, window),
        out_shape=jax.ShapeDtypeStruct((1, count, tokens), jnp.bfloat16),
        grid_spec=pltpu.PrefetchScalarGridSpec(
            num_scalar_prefetch=1,
            grid=(count // step,),
            in_specs=[
                pl.BlockSpec(wide, lambda i, p: (here(i, p), 0)),
                pl.BlockSpec(wide, lambda i, p: (row(i, p), 0)),
                pl.BlockSpec(wide, lambda i, p: (here(i, p), 0)),
                pl.BlockSpec(wide, lambda i, p: (there(i, p), 0)),
                pl.BlockSpec((1, 1) + wide, lambda i, p: (0, 0, row(i, p), 0)),
                pl.BlockSpec(small, lambda i, p: (row(i, p), 0)),
                pl.BlockSpec(small, lambda i, p: (row(i, p), 0)),
                pl.BlockSpec(
                    (tokens // window, step, lanes), lambda i, p: (0, here(i, p), 0)
                ),
            ]
            + [pl.BlockSpec(small, lambda i, p: (here(i, p), 0))] * len(arrived),
            out_specs=pl.BlockSpec((1,) + wide, lambda i, p: (0, i, 0)),
        ),
        name="output",
    )(place, within, inputs, other, own, gate_streams, rates, residues, ends, *arrived)


def ring(value, axis, by):
    peers = lax.axis_size(axis)
    return lax.ppermute(value, axis, [(i, (i + by) % peers) for i in range(peers)])


def on_device(gate_streams, inputs, medium_taps, residues, decay_rates):
    channels, tokens = inputs.shape
    window = medium_taps.shape[1]
    modes = decay_rates.shape[1]
    place = jnp.stack([lax.axis_index("section"), lax.axis_index("tok")]).astype(jnp.int32)
    tail = slice(tokens - window, tokens)
    edge = (
        gate_streams[0, 1, :, tail].astype(jnp.float32) * inputs[:, tail].astype(jnp.float32)
    ).astype(jnp.bfloat16)
    halo = ring(edge, "tok", 1)
    rates = decay_rates.reshape(channels // ROWS, ROWS * modes)
    weights = residues.reshape(channels // ROWS, ROWS * modes)
    response = response_call(place, rates, weights, modes, window, 0, channels)
    medium = medium_call(place, gate_streams, inputs, halo, medium_taps, 0, channels)
    other = ring(medium, "section", 1)
    ends, total = states_call(
        place, gate_streams, inputs, other, rates, modes, window, 0, channels
    )
    arrived = [ring(total, "tok", by) for by in range(1, lax.axis_size("tok"))]
    within = within_call(place, gate_streams, inputs, other, response, 0, channels)
    return output_call(
        place, gate_streams, within, inputs, other, medium, rates, weights, ends, arrived, window, 0
    )


def solution(mesh):
    placed = (
        P("section", None, "chan", "tok"),
        P("chan", "tok"),
        P("chan", None),
        P("chan", None),
        P("chan", None),
    )
    return jax.shard_map(
        on_device,
        mesh=mesh,
        in_specs=placed,
        out_specs=P("section", "chan", "tok"),
        check_vma=False,
    )
```

time: 88.2 us -> 93.4 us (1.059); the launches traced: 87.7 us -> 91.6 us
  Pallas kernels: 43.3 us -> 55.9 us
  starting transfers between devices: 19.7 us -> 13.6 us
  waiting for transfers between devices: 17.3 us -> 14.6 us
    pallas_call x3 -> x5, Pallas kernels: 43.3 us -> 55.9 us  [the longest x1 15.9 us: output_call(): pl.pallas_call(functools.partial(output_kernel, len(arrived), lanes // RO...]
    ppermute x5, starting transfers between devices: 19.7 us -> 13.6 us  [ring(): lax.ppermute(value, axis, [(i, (i + by) % peers) for i in range(peers)])]
    ppermute x5, waiting for transfers between devices: 17.3 us -> 14.6 us  [ring(): lax.ppermute(value, axis, [(i, (i + by) % peers) for i in range(peers)])]
    reshape x0 -> x2, local copies, waits for them, and re-layouts: none -> 1.93 us  [the longest x1 0.97 us: on_device(): rates = decay_rates.reshape(channels // ROWS, ROWS * modes)]
    unnamed x16, local copies, waits for them, and re-layouts: 5.44 us -> 3.51 us
  transfers between devices with their start and end apart: 5 -> 5, of which waited for: 3 -> 2; matrix products, arithmetic and copies ran while one was open for 4% -> 4% of each run, Pallas kernels for 0% -> 26%
where the time goes in v1:
time: 93.4 us; the launch traced here: 91.6 us
  Pallas kernels  55.9 us (60%)
  waiting for transfers between devices  14.6 us (16%)
  starting transfers between devices  13.6 us (15%)
  local copies, waits for them, and re-layouts  5.44 us (6%)
  other arithmetic  2 us (2%)
    pallas_call x1, Pallas kernels, output_call(): pl.pallas_call(functools.partial(output_kernel, len(arrived), lanes // RO...  15.9 us
    ppermute x5, waiting for transfers between devices, ring(): lax.ppermute(value, axis, [(i, (i + by) % peers) for i in range(peers)])  14.6 us
    pallas_call x1, Pallas kernels, states_call(): pl.pallas_call(functools.partial(states_kernel, modes, window), out_shape...  13.6 us
    ppermute x5, starting transfers between devices, ring(): lax.ppermute(value, axis, [(i, (i + by) % peers) for i in range(peers)])  13.6 us
    pallas_call x1, Pallas kernels, response_call(): pl.pallas_call(functools.partial(response_kernel, modes), out_shape=jax.S...  13.1 us
    pallas_call x1, Pallas kernels, within_call(): pl.pallas_call(within_kernel, out_shape=jax.ShapeDtypeStruct((count, toke...  10.7 us
    unnamed x16, local copies, waits for them, and re-layouts  3.51 us
    pallas_call x1, Pallas kernels, medium_call(): pl.pallas_call(medium_kernel, out_shape=jax.ShapeDtypeStruct((count, toke...  2.74 us
  transfers between devices with their start and end apart: 5, of which 2 were waited for; matrix products, arithmetic and copies ran while one was open for 4% of the time, Pallas kernels for 26%

profile of v1, /device:TPU:1, one launch (start us, length us, event | category | flops | bytes accessed | tf_op | source)
XLA Modules:
  0.0 91.6 jit_solution(18281116943897110024)
XLA Ops:
  0.0 1.4 %fusion = bf16[2048,128]{1,0:T(8,128)(2,1)S(1)} fusion(bf16[2048,512]{1,0:T(8,128)(2,1)} %inputs.7, bf16[1,2,2048,512]{3,2,1,0:T(8,128)(2,1)} %gate_out.3), kind=kLoop, calls=%fused_computation.1 | loop fusion | flops 1048576 | bytes 1572864 | tf_op jit(solution)/shard_map/convert_element_type | solution.py:431
  1.4 2.1 %collective-permute-start = (bf16[2048,128]{1,0:T(8,128)(2,1)S(1)}, bf16[2048,128]{1,0:T(8,128)(2,1)S(1)}, u32[]{:S(2)}, u32[]{:S(2)}) collective-permute-start(bf16[2048,128]{1,0:T(8,128)(2,1)S(1)} %fusion), channel_id=1, source_target_pairs={{0,1},{1,2},{2,3},{3,0},{4,5},{5,6},{6,7},{7,4},{8,9},{9,10},{10,1... | collective-permute-start | bytes 1572872 | tf_op jit(solution)/shard_map/ppermute | solution.py:420
  3.4 0.7 pad_add_fusion.place
  4.1 0.0 copy-start.5
  4.1 11.9 %collective-permute-done.halo = bf16[2048,128]{1,0:T(8,128)(2,1)S(1)} collective-permute-done((bf16[2048,128]{1,0:T(8,128)(2,1)S(1)}, bf16[2048,128]{1,0:T(8,128)(2,1)S(1)}, u32[]{:S(2)}, u32[]{:S(2)}) %collective-permute-start) | collective-permute-done | bytes 524320 | tf_op jit(solution)/shard_map/ppermute | solution.py:420
  16.0 0.0 copy-start.1
  16.0 0.8 copy-done.1
  16.8 2.7 %medium.1.own_medium = bf16[2048,512]{1,0:T(8,128)(2,1)} custom-call(s32[2]{0:T(128)} %pad_add_fusion.place, bf16[1,2,2048,512]{3,2,1,0:T(8,128)(2,1)} %gate_out.3, bf16[2048,512]{1,0:T(8,128)(2,1)} %inputs.7, bf16[2048,128]{1,0:T(8,128)(2,1)} %copy-done.1, bf16[1,2,2048,512]{3,2,1,0:T(8,128)(2,1)} %gate_out.3, bf16[2048,128]{1,0:T(8,128)(2,1)} %taps.1, ...), custom_call_target="tpu_custom_call" | custom-call | tf_op jit(solution)/shard_map/medium/pallas_call | solution.py:129
  19.6 8.6 %collective-permute-start.1 = (bf16[2048,512]{1,0:T(8,128)(2,1)}, bf16[2048,512]{1,0:T(8,128)(2,1)S(1)}, u32[]{:S(2)}, u32[]{:S(2)}) collective-permute-start(bf16[2048,512]{1,0:T(8,128)(2,1)} %medium.1.own_medium), channel_id=1, source_target_pairs={{0,16},{16,0},{1,17},{17,1},{2,18},{18,2},{3,19},{19,3},{4,20},{20... | collective-permute-start | bytes 6291464 | tf_op jit(solution)/shard_map/ppermute | solution.py:420
  28.1 0.0 copy-done.5
  28.2 0.3 copy.21
  28.5 1.0 %reshape.8.rates = f32[256,128]{1,0:T(8,128)} reshape(f32[2048,16]{1,0:T(8,128)S(1)} %copy.21) | data formatting | bytes 262144 | tf_op jit(solution)/shard_map/reshape | solution.py:433
  29.5 0.0 copy-start.6
  29.5 2.7 %collective-permute-done.1.gated_medium.other_medium = bf16[2048,512]{1,0:T(8,128)(2,1)S(1)} collective-permute-done((bf16[2048,512]{1,0:T(8,128)(2,1)}, bf16[2048,512]{1,0:T(8,128)(2,1)S(1)}, u32[]{:S(2)}, u32[]{:S(2)}) %collective-permute-start.1) | collective-permute-done | bytes 2097184 | tf_op jit(solution)/shard_map/ppermute | solution.py:420
  32.1 0.0 copy-start
  32.1 1.3 %copy-done = bf16[2048,512]{1,0:T(8,128)(2,1)} copy-done((bf16[2048,512]{1,0:T(8,128)(2,1)}, bf16[2048,512]{1,0:T(8,128)(2,1)S(1)}, u32[]{:S(2)}) %copy-start) | copy-done | bytes 2097176
  33.5 13.6 %states.1 = (f32[4,2048,128]{2,1,0:T(8,128)}, f32[256,128]{1,0:T(8,128)}) custom-call(s32[2]{0:T(128)} %pad_add_fusion.place, bf16[1,2,2048,512]{3,2,1,0:T(8,128)(2,1)} %gate_out.3, bf16[2048,512]{1,0:T(8,128)(2,1)} %inputs.7, bf16[2048,512]{1,0:T(8,128)(2,1)} %copy-done, f32[256,128]{1,0:T(8,128)} %reshape.8.rates), custom_call_target="tpu_custom_call" | custom-call | tf_op jit(solution)/shard_map/states/pallas_call | solution.py:257
  47.0 1.5 %collective-permute-start.4 = (f32[256,128]{1,0:T(8,128)}, f32[256,128]{1,0:T(8,128)S(1)}, u32[]{:S(2)}, u32[]{:S(2)}) collective-permute-start(f32[256,128]{1,0:T(8,128)} %get-tuple-element.8), channel_id=1, source_target_pairs={{0,3},{1,0},{2,1},{3,2},{4,7},{5,4},{6,5},{7,6},{8,11},{9,8},{10,9... | collective-permute-start | bytes 393224 | tf_op jit(solution)/shard_map/ppermute | solution.py:420
  48.5 0.2 collective-permute-start.3
  48.7 1.2 %collective-permute-start.2 = (f32[256,128]{1,0:T(8,128)}, f32[256,128]{1,0:T(8,128)S(1)}, u32[]{:S(2)}, u32[]{:S(2)}) collective-permute-start(f32[256,128]{1,0:T(8,128)} %get-tuple-element.8), channel_id=1, source_target_pairs={{0,1},{1,2},{2,3},{3,0},{4,5},{5,6},{6,7},{7,4},{8,9},{9,10},{10,1... | collective-permute-start | bytes 393224 | tf_op jit(solution)/shard_map/ppermute | solution.py:420
  49.9 0.0 copy-done.6
  49.9 0.3 copy.22
  50.3 1.0 %reshape.9.residues = f32[256,128]{1,0:T(8,128)} reshape(f32[2048,16]{1,0:T(8,128)S(1)} %copy.22) | data formatting | bytes 262144 | tf_op jit(solution)/shard_map/reshape | solution.py:434
  51.2 13.1 %response.1 = f32[2048,256]{1,0:T(8,128)} custom-call(s32[2]{0:T(128)} %pad_add_fusion.place, f32[256,128]{1,0:T(8,128)} %reshape.8.rates, f32[256,128]{1,0:T(8,128)} %reshape.9.residues, bf16[128,256]{1,0:T(8,128)(2,1)} %constant.52.table_h, bf16[128,256]{1,0:T(8,128)(2,1)} %constant.55.table_l), custom_call_target="tpu_custom_call" | custom-call | tf_op jit(solution)/shard_map/response/pallas_call | solution.py:204
  64.3 10.7 %within.1 = f32[2048,512]{1,0:T(8,128)} custom-call(s32[2]{0:T(128)} %pad_add_fusion.place, bf16[1,2,2048,512]{3,2,1,0:T(8,128)(2,1)} %gate_out.3, bf16[2048,512]{1,0:T(8,128)(2,1)} %inputs.7, bf16[2048,512]{1,0:T(8,128)(2,1)} %copy-done, f32[2048,256]{1,0:T(8,128)} %response.1, bf16[256,256]{1,0:T(8,128)(2,1)} %constant.56.fwd_h, ...), custom_call_target="tpu_custom_call" | custom-call | tf_op jit(solution)/shard_map/within/pallas_call | solution.py:307
  75.0 0.0 collective-permute-done.4.rest_2_
  75.0 0.0 copy-start.2
  75.0 0.0 collective-permute-done.3.rest_1_
  75.0 0.0 copy-start.3
  75.0 0.0 collective-permute-done.2.rest_0_
  75.0 0.0 copy-start.4
  75.0 0.6 copy-done.2
  75.6 0.1 copy-done.3
  75.7 0.1 copy-done.4
  75.8 15.9 %output.1 = bf16[1,2048,512]{2,1,0:T(8,128)(2,1)} custom-call(s32[2]{0:T(128)} %pad_add_fusion.place, f32[2048,512]{1,0:T(8,128)} %within.1, bf16[2048,512]{1,0:T(8,128)(2,1)} %inputs.7, bf16[2048,512]{1,0:T(8,128)(2,1)} %copy-done, bf16[2048,512]{1,0:T(8,128)(2,1)} %medium.1.own_medium, bf16[1,2,2048,512]{3,2,1,0:T(8,128)(2,1)} %gate_out.3, ...), custom_call_target="tpu_custom_call" | custom-call | tf_op jit(solution)/shard_map/output/pallas_call | solution.py:393
Async XLA Ops:
  1.4 14.7 %collective-permute-start = (bf16[2048,128]{1,0:T(8,128)(2,1)S(1)}, bf16[2048,128]{1,0:T(8,128)(2,1)S(1)}, u32[]{:S(2)}, u32[]{:S(2)}) collective-permute-start(bf16[2048,128]{1,0:T(8,128)(2,1)S(1)} %fusion), channel_id=1, source_target_pairs={{0,1},{1,2},{2,3},{3,0},{4,5},{5,6},{6,7},{7,4},{8,9},{9,10},{10,1... | collective-permute-start | bytes 1572872 | tf_op jit(solution)/shard_map/ppermute | solution.py:420
  4.1 24.1 %copy-start.5 = (f32[2048,16]{0,1:T(8,128)S(1)}, f32[2048,16]{0,1:T(8,128)}, u32[]{:S(2)}) copy-start(f32[2048,16]{0,1:T(8,128)} %param.22) | copy-start | bytes 393220
  16.0 0.8 copy-start.1
  19.6 12.6 %collective-permute-start.1 = (bf16[2048,512]{1,0:T(8,128)(2,1)}, bf16[2048,512]{1,0:T(8,128)(2,1)S(1)}, u32[]{:S(2)}, u32[]{:S(2)}) collective-permute-start(bf16[2048,512]{1,0:T(8,128)(2,1)} %medium.1.own_medium), channel_id=1, source_target_pairs={{0,16},{16,0},{1,17},{17,1},{2,18},{18,2},{3,19},{19,3},{4,20},{20... | collective-permute-start | bytes 6291464 | tf_op jit(solution)/shard_map/ppermute | solution.py:420
  29.5 20.5 %copy-start.6 = (f32[2048,16]{0,1:T(8,128)S(1)}, f32[2048,16]{0,1:T(8,128)}, u32[]{:S(2)}) copy-start(f32[2048,16]{0,1:T(8,128)} %param.21) | copy-start | bytes 393220
  32.1 1.3 %copy-start = (bf16[2048,512]{1,0:T(8,128)(2,1)}, bf16[2048,512]{1,0:T(8,128)(2,1)S(1)}, u32[]{:S(2)}) copy-start(bf16[2048,512]{1,0:T(8,128)(2,1)S(1)} %collective-permute-done.1.gated_medium.other_medium) | copy-start | bytes 6291460
  47.0 27.9 %collective-permute-start.4 = (f32[256,128]{1,0:T(8,128)}, f32[256,128]{1,0:T(8,128)S(1)}, u32[]{:S(2)}, u32[]{:S(2)}) collective-permute-start(f32[256,128]{1,0:T(8,128)} %get-tuple-element.8), channel_id=1, source_target_pairs={{0,3},{1,0},{2,1},{3,2},{4,7},{5,4},{6,5},{7,6},{8,11},{9,8},{10,9... | collective-permute-start | bytes 393224 | tf_op jit(solution)/shard_map/ppermute | solution.py:420
  48.5 26.5 %collective-permute-start.3 = (f32[256,128]{1,0:T(8,128)}, f32[256,128]{1,0:T(8,128)S(1)}, u32[]{:S(2)}, u32[]{:S(2)}) collective-permute-start(f32[256,128]{1,0:T(8,128)} %get-tuple-element.8), channel_id=1, source_target_pairs={{0,2},{1,3},{2,0},{3,1},{4,6},{5,7},{6,4},{7,5},{8,10},{9,11},{10,... | collective-permute-start | bytes 393224 | tf_op jit(solution)/shard_map/ppermute | solution.py:420
  48.7 26.3 %collective-permute-start.2 = (f32[256,128]{1,0:T(8,128)}, f32[256,128]{1,0:T(8,128)S(1)}, u32[]{:S(2)}, u32[]{:S(2)}) collective-permute-start(f32[256,128]{1,0:T(8,128)} %get-tuple-element.8), channel_id=1, source_target_pairs={{0,1},{1,2},{2,3},{3,0},{4,5},{5,6},{6,7},{7,4},{8,9},{9,10},{10,1... | collective-permute-start | bytes 393224 | tf_op jit(solution)/shard_map/ppermute | solution.py:420
  75.0 0.7 copy-start.2
  75.0 0.7 copy-start.3
  75.0 0.7 copy-start.4

commit v2 on v1

v2 whole, which is shorter than its diff:
```python
import functools

import jax
import jax.numpy as jnp
import numpy as np
from jax import lax
from jax.experimental import pallas as pl
from jax.experimental.pallas import tpu as pltpu
from jax.sharding import PartitionSpec as P

ROWS = 8


def split_pair(matrix):
    high = jnp.asarray(matrix, jnp.float32).astype(jnp.bfloat16)
    low = (jnp.asarray(matrix, jnp.float32) - high.astype(jnp.float32)).astype(jnp.bfloat16)
    return high, low


def stacked(matrix, axis):
    return jnp.concatenate(split_pair(matrix), axis=axis)


def fourier_tables(window):
    size = 2 * window
    time = np.arange(window)[:, None]
    freq = np.arange(window)[None, :]
    angle = 2.0 * np.pi * ((time * freq) % size) / size
    sign = np.where(freq % 2 == 0, 1.0, -1.0)
    nyquist = np.where(time % 2 == 0, 1.0, -1.0)
    weight = np.where(freq == 0, 1.0, 2.0) / size
    forward, inverse = [], []
    for odd in range(2):
        flip = sign if odd else np.ones_like(sign)
        real = np.cos(angle) * flip
        imag = -np.sin(angle) * flip
        imag[:, :1] = nyquist
        forward.append(stacked(np.concatenate([real, imag], axis=1), 0))
        back_real = np.cos(angle) * weight * flip
        back_imag = -np.sin(angle) * weight * flip
        back_imag[:, :1] = nyquist / size
        inverse.append(stacked(np.concatenate([back_real.T, back_imag.T], axis=0), 1))
    return forward, inverse


def turned_tables(window):
    half = window // 2
    time = np.arange(window)[:, None]
    freq = 2 * np.arange(half)[None, :] + 1
    angle = np.pi * ((time * freq) % (2 * window)) / window
    real, imag = np.cos(angle), -np.sin(angle)
    zero = np.zeros_like(real)
    forward = np.concatenate(
        [
            np.concatenate([real, zero, imag, zero], axis=1),
            np.concatenate([zero, real, zero, imag], axis=1),
        ],
        axis=0,
    )
    inverse = forward.T * (2.0 / window)
    doubled = np.concatenate([real, real, imag, imag], axis=1)
    return forward, inverse, doubled


PAIR = 16


def dot_f32(left, right):
    return jnp.dot(left, right, preferred_element_type=jnp.float32)


def dot_turned(left, right):
    return lax.dot_general(
        left, right, (((1,), (1,)), ((), ())), preferred_element_type=jnp.float32
    )


def whole(array):
    return pl.BlockSpec(array.shape, lambda i, place: (0,) * array.ndim)


def mine(share, step):
    return lambda i, place: place[0] * (share // step) + i


def by_section(place, body):
    for section in range(2):
        pl.when(place[0] == section)(functools.partial(body, section))


def lane_mask(modes):
    shape = (ROWS, ROWS * modes)
    lane = lax.broadcasted_iota(jnp.int32, shape, 1)
    return lane // modes == lax.broadcasted_iota(jnp.int32, shape, 0)


def spread(ref, group):
    return jnp.broadcast_to(ref[group : group + 1, :], (ROWS, ref.shape[1]))


def powers(slow, hop, window, first, falling):
    row = lax.broadcasted_iota(jnp.int32, slow.shape, 0).astype(jnp.float32)
    tiles = [jnp.exp(-slow * (first + (ROWS - 1 - row if falling else row)))]
    while len(tiles) < window // ROWS:
        tiles = tiles + [tile * hop for tile in tiles]
        hop = hop * hop
    if falling:
        tiles = tiles[::-1]
    return jnp.concatenate(tiles, axis=0).astype(jnp.bfloat16)


def both_powers(rates, hops, pair, window, first, falling):
    sides = [
        powers(spread(rates, g), spread(hops, g), window, first, falling)
        for g in (2 * pair, 2 * pair + 1)
    ]
    return jnp.concatenate(sides, axis=1)


def two_sided(upper, lower):
    zero = jnp.zeros_like(upper)
    return jnp.concatenate(
        [
            jnp.concatenate([upper, zero], axis=1),
            jnp.concatenate([zero, lower], axis=1),
        ],
        axis=0,
    )


def scale_of(residues, slow):
    return residues * jnp.sqrt(1.0 - jnp.exp(-2.0 * slow))


def response_kernel(modes, place, rates, residues, table_h, table_l, out, hops, scales):
    window = table_h.shape[0]
    mask = lane_mask(modes)
    slow = rates[...]
    hops[...] = jnp.exp(-slow * ROWS)
    scales[...] = scale_of(residues[...], slow) / (1.0 + jnp.exp(-slow * window))
    parts = []
    for pair in range(rates.shape[0] // 2):
        scale = two_sided(
            jnp.where(mask, spread(scales, 2 * pair), 0.0),
            jnp.where(mask, spread(scales, 2 * pair + 1), 0.0),
        )
        high = scale.astype(jnp.bfloat16).astype(jnp.float32)
        both = jnp.concatenate([high, scale - high], axis=0).astype(jnp.bfloat16)
        found = dot_turned(both, both_powers(rates, hops, pair, window, 0.0, False))
        parts.append(found[:PAIR] + found[PAIR:])
    taps = jnp.concatenate(parts, axis=0)
    high = taps.astype(jnp.bfloat16)
    low = (taps - high.astype(jnp.float32)).astype(jnp.bfloat16)
    out[...] = dot_f32(high, table_h[...]) + (
        dot_f32(low, table_h[...]) + dot_f32(high, table_l[...])
    )


def response_call(place, rates, residues, modes, window, share):
    step = min(256, share)
    tables = split_pair(turned_tables(window)[2])
    small = (step // ROWS, ROWS * modes)
    row = mine(share, step)
    return pl.pallas_call(
        functools.partial(response_kernel, modes),
        out_shape=jax.ShapeDtypeStruct((share, 2 * window), jnp.float32),
        grid_spec=pltpu.PrefetchScalarGridSpec(
            num_scalar_prefetch=1,
            grid=(share // step,),
            in_specs=[pl.BlockSpec(small, lambda i, p: (row(i, p), 0))] * 2
            + [whole(t) for t in tables],
            out_specs=pl.BlockSpec((step, 2 * window), lambda i, p: (i, 0)),
            scratch_shapes=[pltpu.VMEM(small, jnp.float32)] * 2,
        ),
        name="response",
    )(place, rates, residues, *tables)


def front_kernel(
    modes,
    place,
    local,
    remote,
    inputs,
    halo_low,
    halo_high,
    taps,
    rates,
    fwd_even,
    fwd_odd,
    inv_even,
    inv_odd,
    medium_out,
    ends,
    total,
    hops,
    leaps,
):
    channels, tokens = inputs.shape
    window = taps.shape[1]
    blocks = tokens // window
    forward = (fwd_even, fwd_odd)
    inverse = (inv_even, inv_odd)
    slow = rates[...]
    hops[...] = jnp.exp(-slow * ROWS)
    leaps[...] = jnp.exp(-slow * window)

    def body(section):
        first = local.at[0] if section == 0 else remote
        second = remote if section == 0 else local.at[0]
        halo = halo_low if section == 0 else halo_high
        tap_rows = taps[...]
        started = jnp.where(place[1] > 0, 1.0, 0.0).astype(jnp.bfloat16)
        parts = [slice(b * window, (b + 1) * window) for b in range(blocks)]
        sources = [
            (first[1, :, part].astype(jnp.float32) * inputs[:, part].astype(jnp.float32)).astype(
                jnp.bfloat16
            )
            for part in parts
        ]
        sources = [halo[...] * started] + sources
        even = [tap_rows] + sources[1::2]
        odd = sources[0::2]
        spectra = []
        for table, members in zip(forward, (even, odd)):
            rows = jnp.concatenate(members, axis=0)
            found = dot_f32(jnp.concatenate([rows, rows], axis=1), table[...])
            spectra.append(
                [found[k * channels : (k + 1) * channels] for k in range(len(members))]
            )
        lane = lax.broadcasted_iota(jnp.int32, (channels, window), 1)
        real, packed = spectra[0][0][:, :window], spectra[0][0][:, window:]
        real_b = jnp.where(lane == 0, packed, real)
        imag = jnp.where(lane == 0, 0.0, packed)
        in_order = [None] * (blocks + 1)
        in_order[1::2] = spectra[0][1:]
        in_order[0::2] = spectra[1]
        products = []
        for block in range(blocks):
            mixed = in_order[block] + in_order[block + 1]
            a, b = mixed[:, :window], mixed[:, window:]
            products.append(
                jnp.concatenate([a * real - b * imag, a * imag + b * real_b], axis=1).astype(
                    jnp.bfloat16
                )
            )
        signals = [None] * blocks
        for parity in range(2):
            members = products[parity::2]
            found = dot_f32(jnp.concatenate(members, axis=0), inverse[parity][...])
            for k in range(len(members)):
                block = 2 * k + parity
                rows = slice(k * channels, (k + 1) * channels)
                medium = found[rows, :window] + found[rows, window:]
                gate = first[0, :, parts[block]].astype(jnp.float32)
                gated = (gate * medium).astype(jnp.bfloat16)
                medium_out[:, parts[block]] = gated
                stream = inputs[:, parts[block]].astype(jnp.float32) + gated.astype(jnp.float32)
                signals[block] = (
                    second[1, :, parts[block]].astype(jnp.float32) * stream
                ).astype(jnp.bfloat16)
        mask = lane_mask(modes)
        lanes = ROWS * modes
        sums = []
        for pair in range(channels // PAIR):
            rows = slice(pair * PAIR, (pair + 1) * PAIR)
            left = jnp.concatenate([signal[rows] for signal in signals], axis=0)
            found = dot_f32(left, both_powers(rates, hops, pair, window, 0.0, True))
            for side in range(2):
                leap = spread(leaps, 2 * pair + side)
                state = None
                for b in range(blocks):
                    top = b * PAIR + side * ROWS
                    end = jnp.where(
                        mask, found[top : top + ROWS, side * lanes : (side + 1) * lanes], 0.0
                    )
                    at = pair * PAIR + side * ROWS
                    ends[b, at : at + ROWS, :] = end
                    state = end if state is None else state * leap + end
                sums.append(jnp.sum(state, axis=0, keepdims=True))
        total[...] = jnp.concatenate(sums, axis=0)

    by_section(place, body)


def front_call(place, gate_streams, swapped, inputs, halos, taps, rates, modes, share):
    tokens = inputs.shape[1]
    window = taps.shape[1]
    step = min(256, share)
    forward, inverse = fourier_tables(window)
    tables = forward + inverse
    row = mine(share, step)
    lanes = ROWS * modes
    small = (step // ROWS, lanes)
    blocks = tokens // window
    return pl.pallas_call(
        functools.partial(front_kernel, modes),
        out_shape=(
            jax.ShapeDtypeStruct((share, tokens), jnp.bfloat16),
            jax.ShapeDtypeStruct((blocks, share, lanes), jnp.float32),
            jax.ShapeDtypeStruct((share // ROWS, lanes), jnp.float32),
        ),
        grid_spec=pltpu.PrefetchScalarGridSpec(
            num_scalar_prefetch=1,
            grid=(share // step,),
            in_specs=[
                pl.BlockSpec((1, 2, step, tokens), lambda i, p: (0, 0, row(i, p), 0)),
                pl.BlockSpec((2, step, tokens), lambda i, p: (0, i, 0)),
                pl.BlockSpec((step, tokens), lambda i, p: (row(i, p), 0)),
                pl.BlockSpec((step, window), lambda i, p: (i, 0)),
                pl.BlockSpec((step, window), lambda i, p: (i, 0)),
                pl.BlockSpec((step, window), lambda i, p: (row(i, p), 0)),
                pl.BlockSpec(small, lambda i, p: (row(i, p), 0)),
            ]
            + [whole(t) for t in tables],
            out_specs=(
                pl.BlockSpec((step, tokens), lambda i, p: (i, 0)),
                pl.BlockSpec((blocks, step, lanes), lambda i, p: (0, i, 0)),
                pl.BlockSpec(small, lambda i, p: (i, 0)),
            ),
            scratch_shapes=[pltpu.VMEM(small, jnp.float32)] * 2,
        ),
        name="front",
    )(place, gate_streams, swapped, inputs, *halos, taps, rates, *tables)


def within_kernel(place, local, remote, inputs, gated_medium, response, fwd_h, fwd_l, inverse, out):
    size = fwd_h.shape[0]
    half = size // 2

    def body(section):
        gate_in = remote.at[0] if section == 0 else local.at[0, 0]
        real, imag = response[:, :half], response[:, half:]
        for pair in range(inputs.shape[1] // size):
            part = slice(pair * size, (pair + 1) * size)
            stream = inputs[:, part].astype(jnp.float32) + gated_medium[:, part].astype(
                jnp.float32
            )
            signal = (gate_in[:, part].astype(jnp.float32) * stream).astype(jnp.bfloat16)
            spec = dot_f32(signal, fwd_h[...]) + dot_f32(signal, fwd_l[...])
            a, b = spec[:, :half], spec[:, half:]
            filtered = jnp.concatenate([a * real - b * imag, a * imag + b * real], axis=1)
            out[:, part] = dot_f32(filtered.astype(jnp.bfloat16), inverse[...])

    by_section(place, body)


def within_call(place, gate_streams, swapped, inputs, gated_medium, response, share):
    tokens = inputs.shape[1]
    window = response.shape[1] // 2
    step = min(256, share)
    forward, inverse, _ = turned_tables(window)
    tables = split_pair(forward) + split_pair(inverse)[:1]
    row = mine(share, step)
    return pl.pallas_call(
        within_kernel,
        out_shape=jax.ShapeDtypeStruct((share, tokens), jnp.float32),
        grid_spec=pltpu.PrefetchScalarGridSpec(
            num_scalar_prefetch=1,
            grid=(share // step,),
            in_specs=[
                pl.BlockSpec((1, 1, step, tokens), lambda i, p: (0, 1, row(i, p), 0)),
                pl.BlockSpec((1, step, tokens), lambda i, p: (1, i, 0)),
                pl.BlockSpec((step, tokens), lambda i, p: (row(i, p), 0)),
                pl.BlockSpec((step, tokens), lambda i, p: (i, 0)),
                pl.BlockSpec((step, 2 * window), lambda i, p: (i, 0)),
            ]
            + [whole(t) for t in tables],
            out_specs=pl.BlockSpec((step, tokens), lambda i, p: (i, 0)),
        ),
        name="within",
    )(place, gate_streams, swapped, inputs, gated_medium, response, *tables)


def output_kernel(
    count,
    modes,
    window,
    place,
    local,
    remote,
    within,
    inputs,
    gated_medium,
    rates,
    residues,
    ends,
    *rest,
):
    arrived, (out, hops, leaps, scales, shares, starts) = rest[:count], rest[count:]
    channels, tokens = inputs.shape
    blocks = tokens // window
    mask = lane_mask(modes)
    slow = rates[...]
    leap_all = jnp.exp(-slow * window)
    scale_all = scale_of(residues[...], slow)
    hops[...] = jnp.exp(-slow * ROWS)
    leaps[...] = leap_all
    scales[...] = scale_all
    shares[...] = scale_all / (1.0 + leap_all)
    entering = jnp.zeros_like(slow)
    for k in range(count):
        keep = jnp.where(place[1] > k, 1.0, 0.0)
        entering = entering + arrived[k][...] * (jnp.exp(-slow * (tokens * k)) * keep)
    starts[...] = entering

    def body(section):
        gate_out = remote.at[0] if section == 0 else local.at[0, 0]
        for pair in range(channels // PAIR):
            rows = slice(pair * PAIR, (pair + 1) * PAIR)
            sides = []
            for side in range(2):
                group = 2 * pair + side
                leap, scale = spread(leaps, group), spread(scales, group)
                share = spread(shares, group)
                state = jnp.where(mask, spread(starts, group), 0.0)
                at = pair * PAIR + side * ROWS
                lefts = []
                for b in range(blocks):
                    end = ends[b, at : at + ROWS, :]
                    lefts.append(state * scale + end * share)
                    state = state * leap + end
                sides.append(lefts)
            left = jnp.concatenate(
                [two_sided(upper, lower) for upper, lower in zip(*sides)], axis=0
            ).astype(jnp.bfloat16)
            across = dot_turned(left, both_powers(rates, hops, pair, window, 1.0, False))
            for b in range(blocks):
                part = slice(b * window, (b + 1) * window)
                stream = inputs[rows, part].astype(jnp.float32) + gated_medium[
                    rows, part
                ].astype(jnp.float32)
                long_out = within[rows, part] + across[b * PAIR : (b + 1) * PAIR]
                gate = gate_out[rows, part].astype(jnp.float32)
                out[rows, part] = (stream + gate * long_out).astype(jnp.bfloat16)

    by_section(place, body)


def output_call(
    place, gate_streams, swapped, within, inputs, medium, rates, residues, ends, arrived, window
):
    share, tokens = medium.shape
    lanes = rates.shape[1]
    step = min(256, share)
    row = mine(share, step)
    wide = (step, tokens)
    small = (step // ROWS, lanes)
    return pl.pallas_call(
        functools.partial(output_kernel, len(arrived), lanes // ROWS, window),
        out_shape=jax.ShapeDtypeStruct((share, tokens), jnp.bfloat16),
        grid_spec=pltpu.PrefetchScalarGridSpec(
            num_scalar_prefetch=1,
            grid=(share // step,),
            in_specs=[
                pl.BlockSpec((1, 1) + wide, lambda i, p: (0, 0, row(i, p), 0)),
                pl.BlockSpec((1,) + wide, lambda i, p: (0, i, 0)),
                pl.BlockSpec(wide, lambda i, p: (i, 0)),
                pl.BlockSpec(wide, lambda i, p: (row(i, p), 0)),
                pl.BlockSpec(wide, lambda i, p: (i, 0)),
                pl.BlockSpec(small, lambda i, p: (row(i, p), 0)),
                pl.BlockSpec(small, lambda i, p: (row(i, p), 0)),
                pl.BlockSpec((tokens // window, step, lanes), lambda i, p: (0, i, 0)),
            ]
            + [pl.BlockSpec(small, lambda i, p: (i, 0))] * len(arrived),
            out_specs=pl.BlockSpec(wide, lambda i, p: (i, 0)),
            scratch_shapes=[pltpu.VMEM(small, jnp.float32)] * 5,
        ),
        name="output",
    )(
        place, gate_streams, swapped, within, inputs, medium, rates, residues, ends, *arrived
    )


def ring(value, axis, by):
    peers = lax.axis_size(axis)
    return lax.ppermute(value, axis, [(i, (i + by) % peers) for i in range(peers)])


def edge_to(value, section):
    peers = lax.axis_size("tok")
    pairs = [(i, section * peers + (i + 1) % peers) for i in range(peers)]
    pairs += [(peers + i, (1 - section) * peers + i) for i in range(peers)]
    return lax.ppermute(value, ("section", "tok"), pairs)


def on_device(gate_streams, inputs, medium_taps, residues, decay_rates):
    channels, tokens = inputs.shape
    share = channels // 2
    window = medium_taps.shape[1]
    modes = decay_rates.shape[1]
    section = lax.axis_index("section")
    place = jnp.stack([section, lax.axis_index("tok")]).astype(jnp.int32)
    tail = slice(tokens - window, tokens)
    edge = (
        gate_streams[0, 1, :, tail].astype(jnp.float32) * inputs[:, tail].astype(jnp.float32)
    ).astype(jnp.bfloat16)
    halos = [edge_to(edge[s * share : (s + 1) * share], s) for s in range(2)]
    lent = lax.dynamic_slice_in_dim(gate_streams[0], (1 - section) * share, share, 1)
    swapped = ring(lent, "section", 1)
    rates = decay_rates.reshape(channels // ROWS, ROWS * modes)
    weights = residues.reshape(channels // ROWS, ROWS * modes)
    response = response_call(place, rates, weights, modes, window, share)
    medium, ends, total = front_call(
        place, gate_streams, swapped, inputs, halos, medium_taps, rates, modes, share
    )
    arrived = [ring(total, "tok", by) for by in range(1, lax.axis_size("tok"))]
    medium_other = ring(medium, "section", 1)
    within = within_call(place, gate_streams, swapped, inputs, medium, response, share)
    mixed = output_call(
        place, gate_streams, swapped, within, inputs, medium, rates, weights, ends, arrived, window
    )
    mixed_other = ring(mixed, "section", 1)
    leading = section == 0
    upper = jnp.where(leading, medium, mixed_other)
    lower = jnp.where(leading, medium_other, mixed)
    return jnp.concatenate([upper, lower], axis=0)[None]


def solution(mesh):
    placed = (
        P("section", None, "chan", "tok"),
        P("chan", "tok"),
        P("chan", None),
        P("chan", None),
        P("chan", None),
    )
    return jax.shard_map(
        on_device,
        mesh=mesh,
        in_specs=placed,
        out_specs=P("section", "chan", "tok"),
        check_vma=False,
    )
```

time: 93.4 us -> 56.5 us (0.60)
  Pallas kernels: 55.9 us -> 26.4 us
  waiting for transfers between devices: 14.6 us -> 2.96 us
  local copies, waits for them, and re-layouts: 5.44 us -> 9.12 us
  other arithmetic: 2 us -> 4.95 us
  starting transfers between devices: 13.6 us -> 11.9 us
    ppermute x5 -> x6, waiting for transfers between devices: 14.6 us -> 1.17 us  [ring(): lax.ppermute(value, axis, [(i, (i + by) % peers) for i in range(peers)])]
    pallas_call x3 -> x2, Pallas kernels: 27 us -> 14.5 us  [the longest x1 7.81 us: front_call(): pl.pallas_call(functools.partial(front_kernel, modes), out_shape=(jax.Sha...]
    pallas_call x1, Pallas kernels: 15.9 us -> 6.66 us  [output_call(): pl.pallas_call(functools.partial(output_kernel, len(arrived), lanes // RO...]
    pallas_call x1, Pallas kernels: 13.1 us -> 5.32 us  [response_call(): pl.pallas_call(functools.partial(response_kernel, modes), out_shape=jax.S...]
    ppermute x5 -> x6, starting transfers between devices: 13.6 us -> 7.81 us  [ring(): lax.ppermute(value, axis, [(i, (i + by) % peers) for i in range(peers)])]
    ppermute x0 -> x2, starting transfers between devices: none -> 4.05 us  [edge_to(): return lax.ppermute(value, ('section', 'tok'), pairs)]
    dynamic_slice x0 -> x1, local copies, waits for them, and re-layouts: none -> 3.04 us  [on_device(): lax.dynamic_slice_in_dim(gate_streams[0], (1 - section) * share, share, 1)]
    ppermute x0 -> x2, waiting for transfers between devices: none -> 1.79 us  [edge_to(): return lax.ppermute(value, ('section', 'tok'), pairs)]
  transfers between devices with their start and end apart: 5 -> 8, of which waited for: 2 -> 2; matrix products, arithmetic and copies ran while one was open for 4% -> 12% of each run, Pallas kernels for 26% -> 34%
where the time goes in v2:
time: 56.5 us; the launch traced here: 55.4 us
  Pallas kernels  26.4 us (47%)
  starting transfers between devices  11.9 us (21%)
  local copies, waits for them, and re-layouts  9.12 us (16%)
  other arithmetic  4.95 us (9%)
  waiting for transfers between devices  2.96 us (5%)
    ppermute x6, starting transfers between devices, ring(): lax.ppermute(value, axis, [(i, (i + by) % peers) for i in range(peers)])  7.81 us
    pallas_call x1, Pallas kernels, front_call(): pl.pallas_call(functools.partial(front_kernel, modes), out_shape=(jax.Sha...  7.81 us
    pallas_call x1, Pallas kernels, within_call(): pl.pallas_call(within_kernel, out_shape=jax.ShapeDtypeStruct((share, toke...  6.66 us
    pallas_call x1, Pallas kernels, output_call(): pl.pallas_call(functools.partial(output_kernel, len(arrived), lanes // RO...  6.66 us
    pallas_call x1, Pallas kernels, response_call(): pl.pallas_call(functools.partial(response_kernel, modes), out_shape=jax.S...  5.32 us
    ppermute x2, starting transfers between devices, edge_to(): return lax.ppermute(value, ('section', 'tok'), pairs)  4.05 us
    unnamed x18, local copies, waits for them, and re-layouts  3.33 us
    dynamic_slice x1, local copies, waits for them, and re-layouts, on_device(): lax.dynamic_slice_in_dim(gate_streams[0], (1 - section) * share, share, 1)  3.04 us
  transfers between devices with their start and end apart: 8, of which 2 were waited for; matrix products, arithmetic and copies ran while one was open for 12% of the time, Pallas kernels for 34%

profile of v2, /device:TPU:1, one launch (start us, length us, event | category | flops | bytes accessed | tf_op | source)
XLA Modules:
  0.0 55.4 jit_solution(16240318817538613361)
XLA Ops:
  0.0 3.0 %dynamic-slice_bitcast_fusion = bf16[2,1024,512]{2,1,0:T(8,128)(2,1)} fusion(bf16[1,2,2048,512]{3,2,1,0:T(8,128)(2,1)} %local.5, s32[]{:T(128)S(6)} %select_n.16), kind=kLoop, calls=%fused_computation.1 | loop fusion | bytes 4194308 | tf_op jit(solution)/shard_map/dynamic_slice | solution.py:499
  3.0 0.0 copy-start.3
  3.0 0.0 collective-permute-start
  3.1 1.4 %fusion = bf16[2048,128]{1,0:T(8,128)(2,1)S(1)} fusion(bf16[2048,512]{1,0:T(8,128)(2,1)} %inputs.5, bf16[1,2,2048,512]{3,2,1,0:T(8,128)(2,1)} %local.5), kind=kLoop, calls=%fused_computation.3 | loop fusion | flops 1048576 | bytes 1572864 | tf_op jit(solution)/shard_map/convert_element_type | solution.py:497
  4.5 0.8 %fusion.1 = (bf16[1024,128]{1,0:T(8,128)(2,1)}, bf16[1024,128]{1,0:T(8,128)(2,1)}) fusion(bf16[2048,128]{1,0:T(8,128)(2,1)S(1)} %fusion), kind=kLoop, calls=%fused_computation.7 | loop fusion | bytes 1048576 | tf_op jit(solution)/shard_map/slice | solution.py:498
  5.3 0.5 collective-permute-start.2
  5.7 3.6 %collective-permute-start.1 = (bf16[1024,128]{1,0:T(8,128)(2,1)}, bf16[1024,128]{1,0:T(8,128)(2,1)}, u32[]{:S(2)}, u32[]{:S(2)}) collective-permute-start(bf16[1024,128]{1,0:T(8,128)(2,1)} %get-tuple-element.12), channel_id=1, source_target_pairs={{0,1},{1,2},{2,3},{3,0},{16,16},{17,17},{18,18},{19,19},{4,5},{5,6... | collective-permute-start | bytes 786440 | tf_op jit(solution)/shard_map/ppermute | solution.py:484
  9.3 0.0 copy-done.3
  9.3 0.3 copy.21
  9.7 1.0 %reshape.9.rates = f32[256,128]{1,0:T(8,128)} reshape(f32[2048,16]{1,0:T(8,128)S(1)} %copy.21) | data formatting | bytes 262144 | tf_op jit(solution)/shard_map/reshape | solution.py:501
  10.6 0.7 %pad_add_fusion.place = s32[2]{0:T(128)} fusion(s32[1]{0:T(128)} %bitcast.1, s32[1]{0:T(128)} %bitcast), kind=kLoop, calls=%fused_computation.6 | loop fusion | flops 2 | bytes 16 | tf_op jit(solution)/shard_map/stack | solution.py:493
  11.3 0.0 copy-start.4
  11.3 1.8 %collective-permute-done.2.halo_high = bf16[1024,128]{1,0:T(8,128)(2,1)S(1)} collective-permute-done((bf16[1024,128]{1,0:T(8,128)(2,1)}, bf16[1024,128]{1,0:T(8,128)(2,1)S(1)}, u32[]{:S(2)}, u32[]{:S(2)}) %collective-permute-start.2) | collective-permute-done | bytes 262176 | tf_op jit(solution)/shard_map/ppermute | solution.py:484
  13.1 0.0 copy-start.2
  13.1 0.0 collective-permute-done.1.halo_low
  13.1 0.0 collective-permute-done.remote
  13.1 0.7 %copy-done.2 = bf16[1024,128]{1,0:T(8,128)(2,1)} copy-done((bf16[1024,128]{1,0:T(8,128)(2,1)}, bf16[1024,128]{1,0:T(8,128)(2,1)S(1)}, u32[]{:S(2)}) %copy-start.2) | copy-done | bytes 262168
  13.8 0.0 copy-start
  13.8 1.3 %copy-done = bf16[2,1024,512]{2,1,0:T(8,128)(2,1)} copy-done((bf16[2,1024,512]{2,1,0:T(8,128)(2,1)}, bf16[2,1024,512]{2,1,0:T(8,128)(2,1)S(1)}, u32[]{:S(2)}) %copy-start) | copy-done | bytes 2097176
  15.1 7.8 %front.1 = (bf16[1024,512]{1,0:T(8,128)(2,1)}, f32[4,1024,128]{2,1,0:T(8,128)}, f32[128,128]{1,0:T(8,128)}) custom-call(s32[2]{0:T(128)} %pad_add_fusion.place, bf16[1,2,2048,512]{3,2,1,0:T(8,128)(2,1)} %local.5, bf16[2,1024,512]{2,1,0:T(8,128)(2,1)} %copy-done, bf16[2048,512]{1,0:T(8,128)(2,1)} %inputs.5, ...), custom_call_target="tpu_custom_call" | custom-call | tf_op jit(solution)/shard_map/front/pallas_call | solution.py:296
  22.9 4.1 %collective-permute-start.7 = (bf16[1024,512]{1,0:T(8,128)(2,1)}, bf16[1024,512]{1,0:T(8,128)(2,1)S(1)}, u32[]{:S(2)}, u32[]{:S(2)}) collective-permute-start(bf16[1024,512]{1,0:T(8,128)(2,1)} %get-tuple-element.8.gated_medium), channel_id=1, source_target_pairs={{0,16},{16,0},{1,17},{17,1},{2,18},{18,2},{3,19},{19,3},{4,20},{20... | collective-permute-start | bytes 3145736 | tf_op jit(solution)/shard_map/ppermute | solution.py:477
  27.0 0.7 %collective-permute-start.5 = (f32[128,128]{1,0:T(8,128)}, f32[128,128]{1,0:T(8,128)S(1)}, u32[]{:S(2)}, u32[]{:S(2)}) collective-permute-start(f32[128,128]{1,0:T(8,128)} %get-tuple-element.10), channel_id=1, source_target_pairs={{0,3},{1,0},{2,1},{3,2},{4,7},{5,4},{6,5},{7,6},{8,11},{9,8},{10,9... | collective-permute-start | bytes 196616 | tf_op jit(solution)/shard_map/ppermute | solution.py:477
  27.7 0.8 %collective-permute-start.4 = (f32[128,128]{1,0:T(8,128)}, f32[128,128]{1,0:T(8,128)S(1)}, u32[]{:S(2)}, u32[]{:S(2)}) collective-permute-start(f32[128,128]{1,0:T(8,128)} %get-tuple-element.10), channel_id=1, source_target_pairs={{0,2},{1,3},{2,0},{3,1},{4,6},{5,7},{6,4},{7,5},{8,10},{9,11},{10,... | collective-permute-start | bytes 196616 | tf_op jit(solution)/shard_map/ppermute | solution.py:477
  28.5 1.2 %collective-permute-start.3 = (f32[128,128]{1,0:T(8,128)}, f32[128,128]{1,0:T(8,128)S(1)}, u32[]{:S(2)}, u32[]{:S(2)}) collective-permute-start(f32[128,128]{1,0:T(8,128)} %get-tuple-element.10), channel_id=1, source_target_pairs={{0,1},{1,2},{2,3},{3,0},{4,5},{5,6},{6,7},{7,4},{8,9},{9,10},{10,1... | collective-permute-start | bytes 196616 | tf_op jit(solution)/shard_map/ppermute | solution.py:477
  29.7 0.0 copy-done.4
  29.7 0.3 copy.22
  30.1 1.0 %reshape.10.residues = f32[256,128]{1,0:T(8,128)} reshape(f32[2048,16]{1,0:T(8,128)S(1)} %copy.22) | data formatting | bytes 262144 | tf_op jit(solution)/shard_map/reshape | solution.py:502
  31.0 5.3 %response.1 = f32[1024,256]{1,0:T(8,128)} custom-call(s32[2]{0:T(128)} %pad_add_fusion.place, f32[256,128]{1,0:T(8,128)} %reshape.9.rates, f32[256,128]{1,0:T(8,128)} %reshape.10.residues, bf16[128,256]{1,0:T(8,128)(2,1)} %constant.61.table_h, bf16[128,256]{1,0:T(8,128)(2,1)} %constant.64.table_l), custom_call_target="tpu_custom_call" | custom-call | tf_op jit(solution)/shard_map/response/pallas_call | solution.py:164
  36.3 6.7 %within.1 = f32[1024,512]{1,0:T(8,128)} custom-call(s32[2]{0:T(128)} %pad_add_fusion.place, bf16[1,2,2048,512]{3,2,1,0:T(8,128)(2,1)} %local.5, bf16[2,1024,512]{2,1,0:T(8,128)(2,1)} %copy-done, bf16[2048,512]{1,0:T(8,128)(2,1)} %inputs.5, bf16[1024,512]{1,0:T(8,128)(2,1)} %get-tuple-element.8.gated_medium, f32[1024,256]{1,0:T(8,128)} %response.1, ...), custom_call_target="tpu_custom_call" | custom-call | tf_op jit(solution)/shard_map/within/pallas_call | solution.py:355
  43.0 0.0 collective-permute-done.5.rest_2_
  43.0 0.0 copy-start.5
  43.0 0.0 collective-permute-done.4.rest_1_
  43.0 0.0 copy-start.6
  43.0 0.0 collective-permute-done.3.rest_0_
  43.0 0.0 copy-start.7
  43.1 0.6 %copy-done.5 = f32[128,128]{1,0:T(8,128)} copy-done((f32[128,128]{1,0:T(8,128)}, f32[128,128]{1,0:T(8,128)S(1)}, u32[]{:S(2)}) %copy-start.5) | copy-done | bytes 65560
  43.6 0.0 copy-done.6
  43.7 0.0 copy-done.7
  43.7 6.7 %output.1 = bf16[1024,512]{1,0:T(8,128)(2,1)} custom-call(s32[2]{0:T(128)} %pad_add_fusion.place, bf16[1,2,2048,512]{3,2,1,0:T(8,128)(2,1)} %local.5, bf16[2,1024,512]{2,1,0:T(8,128)(2,1)} %copy-done, f32[1024,512]{1,0:T(8,128)} %within.1, bf16[2048,512]{1,0:T(8,128)(2,1)} %inputs.5, bf16[1024,512]{1,0:T(8,128)(2,1)} %get-tuple-element.8.gated_medium, ...), custom_call_target="tpu_custom_call" | custom-call | tf_op jit(solution)/shard_map/output/pallas_call | solution.py:449
  50.4 0.0 copy-start.1
  50.4 1.0 %collective-permute-start.6 = (bf16[1024,512]{1,0:T(8,128)(2,1)}, bf16[1024,512]{1,0:T(8,128)(2,1)S(1)}, u32[]{:S(2)}, u32[]{:S(2)}) collective-permute-start(bf16[1024,512]{1,0:T(8,128)(2,1)} %output.1), channel_id=1, source_target_pairs={{0,16},{16,0},{1,17},{17,1},{2,18},{18,2},{3,19},{19,3},{4,20},{20... | collective-permute-start | bytes 3145736 | tf_op jit(solution)/shard_map/ppermute | solution.py:477
  51.4 0.0 collective-permute-done.7
  51.4 1.3 %broadcast_select_fusion = bf16[1024,512]{1,0:T(8,128)(2,1)S(1)} fusion(bf16[1024,512]{1,0:T(8,128)(2,1)S(1)} %collective-permute-done.7, bf16[1024,512]{1,0:T(8,128)(2,1)} %output.1, pred[]{:T(512)S(6)} %eq.3), kind=kLoop, calls=%fused_computation.4 | loop fusion | flops 524288 | bytes 3145729 | tf_op jit(solution)/shard_map/jit(_where)/select_n | solution.py:516
  52.7 1.2 %collective-permute-done.6 = bf16[1024,512]{1,0:T(8,128)(2,1)S(1)} collective-permute-done((bf16[1024,512]{1,0:T(8,128)(2,1)}, bf16[1024,512]{1,0:T(8,128)(2,1)S(1)}, u32[]{:S(2)}, u32[]{:S(2)}) %collective-permute-start.6) | collective-permute-done | bytes 1048608 | tf_op jit(solution)/shard_map/ppermute | solution.py:477
  53.8 0.0 copy-done.1
  53.9 0.1 broadcast_select_fusion.1
  54.0 1.5 %maximum_bitcast_fusion = bf16[1,2048,512]{2,1,0:T(8,128)(2,1)} fusion(bf16[1024,512]{1,0:T(8,128)(2,1)S(1)} %broadcast_select_fusion, bf16[1024,512]{1,0:T(8,128)(2,1)S(1)} %broadcast_select_fusion.1), kind=kLoop, calls=%fused_computation | loop fusion | flops 4194304 | bytes 4194304 | tf_op jit(solution)/shard_map/broadcast_in_dim | solution.py:517
Async XLA Ops:
  3.0 6.3 %copy-start.3 = (f32[2048,16]{0,1:T(8,128)S(1)}, f32[2048,16]{0,1:T(8,128)}, u32[]{:S(2)}) copy-start(f32[2048,16]{0,1:T(8,128)} %param.22) | copy-start | bytes 393220
  3.0 10.0 %collective-permute-start = (bf16[2,1024,512]{2,1,0:T(8,128)(2,1)}, bf16[2,1024,512]{2,1,0:T(8,128)(2,1)S(1)}, u32[]{:S(2)}, u32[]{:S(2)}) collective-permute-start(bf16[2,1024,512]{2,1,0:T(8,128)(2,1)} %dynamic-slice_bitcast_fusion), channel_id=1, source_target_pairs={{0,16},{16,0},{1,17},{17,1},{2,18},{18,2},{3,19},{19,3},{4,20},{20... | collective-permute-start | bytes 6291464 | tf_op jit(solution)/shard_map/ppermute | solution.py:477
  5.3 7.8 %collective-permute-start.2 = (bf16[1024,128]{1,0:T(8,128)(2,1)}, bf16[1024,128]{1,0:T(8,128)(2,1)S(1)}, u32[]{:S(2)}, u32[]{:S(2)}) collective-permute-start(bf16[1024,128]{1,0:T(8,128)(2,1)} %get-tuple-element.11), channel_id=1, source_target_pairs={{0,17},{1,18},{2,19},{3,16},{16,0},{17,1},{18,2},{19,3},{4,21},{5,... | collective-permute-start | bytes 786440 | tf_op jit(solution)/shard_map/ppermute | solution.py:484
  5.7 7.3 %collective-permute-start.1 = (bf16[1024,128]{1,0:T(8,128)(2,1)}, bf16[1024,128]{1,0:T(8,128)(2,1)}, u32[]{:S(2)}, u32[]{:S(2)}) collective-permute-start(bf16[1024,128]{1,0:T(8,128)(2,1)} %get-tuple-element.12), channel_id=1, source_target_pairs={{0,1},{1,2},{2,3},{3,0},{16,16},{17,17},{18,18},{19,19},{4,5},{5,6... | collective-permute-start | bytes 786440 | tf_op jit(solution)/shard_map/ppermute | solution.py:484
  11.3 18.4 %copy-start.4 = (f32[2048,16]{0,1:T(8,128)S(1)}, f32[2048,16]{0,1:T(8,128)}, u32[]{:S(2)}) copy-start(f32[2048,16]{0,1:T(8,128)} %param.21) | copy-start | bytes 393220
  13.1 0.7 %copy-start.2 = (bf16[1024,128]{1,0:T(8,128)(2,1)}, bf16[1024,128]{1,0:T(8,128)(2,1)S(1)}, u32[]{:S(2)}) copy-start(bf16[1024,128]{1,0:T(8,128)(2,1)S(1)} %collective-permute-done.2.halo_high) | copy-start | bytes 786436
  13.8 1.3 %copy-start = (bf16[2,1024,512]{2,1,0:T(8,128)(2,1)}, bf16[2,1024,512]{2,1,0:T(8,128)(2,1)S(1)}, u32[]{:S(2)}) copy-start(bf16[2,1024,512]{2,1,0:T(8,128)(2,1)S(1)} %collective-permute-done.remote) | copy-start | bytes 6291460
  22.9 28.4 %collective-permute-start.7 = (bf16[1024,512]{1,0:T(8,128)(2,1)}, bf16[1024,512]{1,0:T(8,128)(2,1)S(1)}, u32[]{:S(2)}, u32[]{:S(2)}) collective-permute-start(bf16[1024,512]{1,0:T(8,128)(2,1)} %get-tuple-element.8.gated_medium), channel_id=1, source_target_pairs={{0,16},{16,0},{1,17},{17,1},{2,18},{18,2},{3,19},{19,3},{4,20},{20... | collective-permute-start | bytes 3145736 | tf_op jit(solution)/shard_map/ppermute | solution.py:477
  27.0 16.0 %collective-permute-start.5 = (f32[128,128]{1,0:T(8,128)}, f32[128,128]{1,0:T(8,128)S(1)}, u32[]{:S(2)}, u32[]{:S(2)}) collective-permute-start(f32[128,128]{1,0:T(8,128)} %get-tuple-element.10), channel_id=1, source_target_pairs={{0,3},{1,0},{2,1},{3,2},{4,7},{5,4},{6,5},{7,6},{8,11},{9,8},{10,9... | collective-permute-start | bytes 196616 | tf_op jit(solution)/shard_map/ppermute | solution.py:477
  27.7 15.3 %collective-permute-start.4 = (f32[128,128]{1,0:T(8,128)}, f32[128,128]{1,0:T(8,128)S(1)}, u32[]{:S(2)}, u32[]{:S(2)}) collective-permute-start(f32[128,128]{1,0:T(8,128)} %get-tuple-element.10), channel_id=1, source_target_pairs={{0,2},{1,3},{2,0},{3,1},{4,6},{5,7},{6,4},{7,5},{8,10},{9,11},{10,... | collective-permute-start | bytes 196616 | tf_op jit(solution)/shard_map/ppermute | solution.py:477
  28.5 14.5 %collective-permute-start.3 = (f32[128,128]{1,0:T(8,128)}, f32[128,128]{1,0:T(8,128)S(1)}, u32[]{:S(2)}, u32[]{:S(2)}) collective-permute-start(f32[128,128]{1,0:T(8,128)} %get-tuple-element.10), channel_id=1, source_target_pairs={{0,1},{1,2},{2,3},{3,0},{4,5},{5,6},{6,7},{7,4},{8,9},{9,10},{10,1... | collective-permute-start | bytes 196616 | tf_op jit(solution)/shard_map/ppermute | solution.py:477
  43.0 0.6 %copy-start.5 = (f32[128,128]{1,0:T(8,128)}, f32[128,128]{1,0:T(8,128)S(1)}, u32[]{:S(2)}) copy-start(f32[128,128]{1,0:T(8,128)S(1)} %collective-permute-done.5.rest_2_) | copy-start | bytes 196612
  43.0 0.7 %copy-start.6 = (f32[128,128]{1,0:T(8,128)}, f32[128,128]{1,0:T(8,128)S(1)}, u32[]{:S(2)}) copy-start(f32[128,128]{1,0:T(8,128)S(1)} %collective-permute-done.4.rest_1_) | copy-start | bytes 196612
  43.0 0.7 %copy-start.7 = (f32[128,128]{1,0:T(8,128)}, f32[128,128]{1,0:T(8,128)S(1)}, u32[]{:S(2)}) copy-start(f32[128,128]{1,0:T(8,128)S(1)} %collective-permute-done.3.rest_0_) | copy-start | bytes 196612
  50.4 3.5 %copy-start.1 = (bf16[1024,512]{1,0:T(8,128)(2,1)S(1)}, bf16[1024,512]{1,0:T(8,128)(2,1)}, u32[]{:S(2)}) copy-start(bf16[1024,512]{1,0:T(8,128)(2,1)} %get-tuple-element.8.gated_medium) | copy-start | bytes 3145732
  50.4 3.5 %collective-permute-start.6 = (bf16[1024,512]{1,0:T(8,128)(2,1)}, bf16[1024,512]{1,0:T(8,128)(2,1)S(1)}, u32[]{:S(2)}, u32[]{:S(2)}) collective-permute-start(bf16[1024,512]{1,0:T(8,128)(2,1)} %output.1), channel_id=1, source_target_pairs={{0,16},{16,0},{1,17},{17,1},{2,18},{18,2},{3,19},{19,3},{4,20},{20... | collective-permute-start | bytes 3145736 | tf_op jit(solution)/shard_map/ppermute | solution.py:477

commit v3 on v2

--- a/solution.py
+++ b/solution.py
@@ -63,6 +63,18 @@
 
 
 PAIR = 16
+COMPILER = pltpu.CompilerParams(vmem_limit_bytes=16 << 20)
+
+
+def parked(*arrays):
+    return [pltpu.with_memory_space_constraint(a, pltpu.HBM) for a in arrays]
+
+
+def cost(share, tokens, work):
+    size = share * tokens
+    return pl.CostEstimate(
+        flops=size * work, bytes_accessed=size * 12, transcendentals=size // 64
+    )
 
 
 def dot_f32(left, right):
@@ -76,16 +88,16 @@
 
 
 def whole(array):
-    return pl.BlockSpec(array.shape, lambda i, place: (0,) * array.ndim)
+    return pl.BlockSpec(array.shape, lambda i, p, t: (0,) * array.ndim)
 
 
 def mine(share, step):
-    return lambda i, place: place[0] * (share // step) + i
-
-
-def by_section(place, body):
+    return lambda i, p, t: p[0] * (share // step) + i
+
+
+def by_section(sec, body):
     for section in range(2):
-        pl.when(place[0] == section)(functools.partial(body, section))
+        pl.when(sec[0] == section)(functools.partial(body, section))
 
 
 def lane_mask(modes):
@@ -132,7 +144,7 @@
     return residues * jnp.sqrt(1.0 - jnp.exp(-2.0 * slow))
 
 
-def response_kernel(modes, place, rates, residues, table_h, table_l, out, hops, scales):
+def response_kernel(modes, sec, tok, rates, residues, table_h, table_l, out, hops, scales):
     window = table_h.shape[0]
     mask = lane_mask(modes)
     slow = rates[...]
@@ -165,20 +177,23 @@
         functools.partial(response_kernel, modes),
         out_shape=jax.ShapeDtypeStruct((share, 2 * window), jnp.float32),
         grid_spec=pltpu.PrefetchScalarGridSpec(
-            num_scalar_prefetch=1,
+            num_scalar_prefetch=2,
             grid=(share // step,),
-            in_specs=[pl.BlockSpec(small, lambda i, p: (row(i, p), 0))] * 2
+            in_specs=[pl.BlockSpec(small, lambda i, p, t: (row(i, p, t), 0))] * 2
             + [whole(t) for t in tables],
-            out_specs=pl.BlockSpec((step, 2 * window), lambda i, p: (i, 0)),
+            out_specs=pl.BlockSpec((step, 2 * window), lambda i, p, t: (i, 0)),
             scratch_shapes=[pltpu.VMEM(small, jnp.float32)] * 2,
         ),
         name="response",
-    )(place, rates, residues, *tables)
+        cost_estimate=cost(share, 4 * window, 600),
+        compiler_params=COMPILER,
+    )(*place, rates, residues, *parked(*tables))
 
 
 def front_kernel(
     modes,
-    place,
+    sec,
+    tok,
     local,
     remote,
     inputs,
@@ -186,6 +201,7 @@
     halo_high,
     taps,
     rates,
+    after,
     fwd_even,
     fwd_odd,
     inv_even,
@@ -210,7 +226,7 @@
         second = remote if section == 0 else local.at[0]
         halo = halo_low if section == 0 else halo_high
         tap_rows = taps[...]
-        started = jnp.where(place[1] > 0, 1.0, 0.0).astype(jnp.bfloat16)
+        started = jnp.where(tok[0] > 0, 1.0, 0.0).astype(jnp.bfloat16)
         parts = [slice(b * window, (b + 1) * window) for b in range(blocks)]
         sources = [
             (first[1, :, part].astype(jnp.float32) * inputs[:, part].astype(jnp.float32)).astype(
@@ -280,10 +296,12 @@
                 sums.append(jnp.sum(state, axis=0, keepdims=True))
         total[...] = jnp.concatenate(sums, axis=0)
 
-    by_section(place, body)
-
-
-def front_call(place, gate_streams, swapped, inputs, halos, taps, rates, modes, share):
+    by_section(sec, body)
+
+
+def front_call(
+    place, gate_streams, swapped, inputs, halos, taps, rates, after, modes, share
+):
     tokens = inputs.shape[1]
     window = taps.shape[1]
     step = min(256, share)
@@ -301,30 +319,33 @@
             jax.ShapeDtypeStruct((share // ROWS, lanes), jnp.float32),
         ),
         grid_spec=pltpu.PrefetchScalarGridSpec(
-            num_scalar_prefetch=1,
+            num_scalar_prefetch=2,
             grid=(share // step,),
             in_specs=[
-                pl.BlockSpec((1, 2, step, tokens), lambda i, p: (0, 0, row(i, p), 0)),
-                pl.BlockSpec((2, step, tokens), lambda i, p: (0, i, 0)),
-                pl.BlockSpec((step, tokens), lambda i, p: (row(i, p), 0)),
-                pl.BlockSpec((step, window), lambda i, p: (i, 0)),
-                pl.BlockSpec((step, window), lambda i, p: (i, 0)),
-                pl.BlockSpec((step, window), lambda i, p: (row(i, p), 0)),
-                pl.BlockSpec(small, lambda i, p: (row(i, p), 0)),
+                pl.BlockSpec((1, 2, step, tokens), lambda i, p, t: (0, 0, row(i, p, t), 0)),
+                pl.BlockSpec((2, step, tokens), lambda i, p, t: (0, i, 0)),
+                pl.BlockSpec((step, tokens), lambda i, p, t: (row(i, p, t), 0)),
+                pl.BlockSpec((step, window), lambda i, p, t: (i, 0)),
+                pl.BlockSpec((step, window), lambda i, p, t: (i, 0)),
+                pl.BlockSpec((step, window), lambda i, p, t: (row(i, p, t), 0)),
+                pl.BlockSpec(small, lambda i, p, t: (row(i, p, t), 0)),
+                pl.BlockSpec(memory_space=pl.ANY),
             ]
             + [whole(t) for t in tables],
             out_specs=(
-                pl.BlockSpec((step, tokens), lambda i, p: (i, 0)),
-                pl.BlockSpec((blocks, step, lanes), lambda i, p: (0, i, 0)),
-                pl.BlockSpec(small, lambda i, p: (i, 0)),
+                pl.BlockSpec((step, tokens), lambda i, p, t: (i, 0)),
+                pl.BlockSpec((blocks, step, lanes), lambda i, p, t: (0, i, 0)),
+                pl.BlockSpec(small, lambda i, p, t: (i, 0)),
             ),
             scratch_shapes=[pltpu.VMEM(small, jnp.float32)] * 2,
         ),
         name="front",
-    )(place, gate_streams, swapped, inputs, *halos, taps, rates, *tables)
-
-
-def within_kernel(place, local, remote, inputs, gated_medium, response, fwd_h, fwd_l, inverse, out):
+        cost_estimate=cost(share, tokens, 2000),
+        compiler_params=COMPILER,
+    )(*place, gate_streams, swapped, inputs, *halos, taps, rates, after, *parked(*tables))
+
+
+def within_kernel(sec, tok, local, remote, inputs, gated_medium, response, fwd_h, fwd_l, inverse, out):
     size = fwd_h.shape[0]
     half = size // 2
 
@@ -342,7 +363,7 @@
             filtered = jnp.concatenate([a * real - b * imag, a * imag + b * real], axis=1)
             out[:, part] = dot_f32(filtered.astype(jnp.bfloat16), inverse[...])
 
-    by_section(place, body)
+    by_section(sec, body)
 
 
 def within_call(place, gate_streams, swapped, inputs, gated_medium, response, share):
@@ -356,27 +377,30 @@
         within_kernel,
         out_shape=jax.ShapeDtypeStruct((share, tokens), jnp.float32),
         grid_spec=pltpu.PrefetchScalarGridSpec(
-            num_scalar_prefetch=1,
+            num_scalar_prefetch=2,
             grid=(share // step,),
             in_specs=[
-                pl.BlockSpec((1, 1, step, tokens), lambda i, p: (0, 1, row(i, p), 0)),
-                pl.BlockSpec((1, step, tokens), lambda i, p: (1, i, 0)),
-                pl.BlockSpec((step, tokens), lambda i, p: (row(i, p), 0)),
-                pl.BlockSpec((step, tokens), lambda i, p: (i, 0)),
-                pl.BlockSpec((step, 2 * window), lambda i, p: (i, 0)),
+                pl.BlockSpec((1, 1, step, tokens), lambda i, p, t: (0, 1, row(i, p, t), 0)),
+                pl.BlockSpec((1, step, tokens), lambda i, p, t: (1, i, 0)),
+                pl.BlockSpec((step, tokens), lambda i, p, t: (row(i, p, t), 0)),
+                pl.BlockSpec((step, tokens), lambda i, p, t: (i, 0)),
+                pl.BlockSpec((step, 2 * window), lambda i, p, t: (i, 0)),
             ]
             + [whole(t) for t in tables],
-            out_specs=pl.BlockSpec((step, tokens), lambda i, p: (i, 0)),
+            out_specs=pl.BlockSpec((step, tokens), lambda i, p, t: (i, 0)),
         ),
         name="within",
-    )(place, gate_streams, swapped, inputs, gated_medium, response, *tables)
+        cost_estimate=cost(share, tokens, 1500),
+        compiler_params=COMPILER,
+    )(*place, gate_streams, swapped, inputs, gated_medium, response, *parked(*tables))
 
 
 def output_kernel(
     count,
     modes,
     window,
-    place,
+    sec,
+    tok,
     local,
     remote,
     within,
@@ -400,7 +424,7 @@
     shares[...] = scale_all / (1.0 + leap_all)
     entering = jnp.zeros_like(slow)
     for k in range(count):
-        keep = jnp.where(place[1] > k, 1.0, 0.0)
+        keep = jnp.where(tok[0] > k, 1.0, 0.0)
         entering = entering + arrived[k][...] * (jnp.exp(-slow * (tokens * k)) * keep)
     starts[...] = entering
 
@@ -434,7 +458,7 @@
                 gate = gate_out[rows, part].astype(jnp.float32)
                 out[rows, part] = (stream + gate * long_out).astype(jnp.bfloat16)
 
-    by_section(place, body)
+    by_section(sec, body)
 
 
 def output_call(
@@ -450,26 +474,73 @@
         functools.partial(output_kernel, len(arrived), lanes // ROWS, window),
         out_shape=jax.ShapeDtypeStruct((share, tokens), jnp.bfloat16),
         grid_spec=pltpu.PrefetchScalarGridSpec(
-            num_scalar_prefetch=1,
+            num_scalar_prefetch=2,
             grid=(share // step,),
             in_specs=[
-                pl.BlockSpec((1, 1) + wide, lambda i, p: (0, 0, row(i, p), 0)),
-                pl.BlockSpec((1,) + wide, lambda i, p: (0, i, 0)),
-                pl.BlockSpec(wide, lambda i, p: (i, 0)),
-                pl.BlockSpec(wide, lambda i, p: (row(i, p), 0)),
-                pl.BlockSpec(wide, lambda i, p: (i, 0)),
-                pl.BlockSpec(small, lambda i, p: (row(i, p), 0)),
-                pl.BlockSpec(small, lambda i, p: (row(i, p), 0)),
-                pl.BlockSpec((tokens // window, step, lanes), lambda i, p: (0, i, 0)),
+                pl.BlockSpec((1, 1) + wide, lambda i, p, t: (0, 0, row(i, p, t), 0)),
+                pl.BlockSpec((1,) + wide, lambda i, p, t: (0, i, 0)),
+                pl.BlockSpec(wide, lambda i, p, t: (i, 0)),
+                pl.BlockSpec(wide, lambda i, p, t: (row(i, p, t), 0)),
+                pl.BlockSpec(wide, lambda i, p, t: (i, 0)),
+                pl.BlockSpec(small, lambda i, p, t: (row(i, p, t), 0)),
+                pl.BlockSpec(small, lambda i, p, t: (row(i, p, t), 0)),
+                pl.BlockSpec((tokens // window, step, lanes), lambda i, p, t: (0, i, 0)),
             ]
-            + [pl.BlockSpec(small, lambda i, p: (i, 0))] * len(arrived),
-            out_specs=pl.BlockSpec(wide, lambda i, p: (i, 0)),
+            + [pl.BlockSpec(small, lambda i, p, t: (i, 0))] * len(arrived),
+            out_specs=pl.BlockSpec(wide, lambda i, p, t: (i, 0)),
             scratch_shapes=[pltpu.VMEM(small, jnp.float32)] * 5,
         ),
         name="output",
+        cost_estimate=cost(share, tokens, 1500),
+        compiler_params=COMPILER,
     )(
-        place, gate_streams, swapped, within, inputs, medium, rates, residues, ends, *arrived
-    )
+        *place, gate_streams, swapped, within, inputs, medium, rates, residues, ends, *arrived
+    )
+
+
+def lend_kernel(sec, tok, gates, gate_tail, input_tail, out, low, high):
+    out[...] = gates[0]
+    share = low.shape[0]
+
+    @pl.when(pl.program_id(0) == 0)
+    def _():
+        for half, target in enumerate((low, high)):
+            rows = slice(half * share, (half + 1) * share)
+            target[...] = (
+                gate_tail[0, 0, rows, :].astype(jnp.float32)
+                * input_tail[rows, :].astype(jnp.float32)
+            ).astype(jnp.bfloat16)
+
+
+def lend_call(place, gate_streams, inputs, window, share):
+    channels, tokens = inputs.shape
+    step = min(512, share)
+    count = share // step
+    last = tokens // window - 1
+    edge = jax.ShapeDtypeStruct((share, window), jnp.bfloat16)
+    return pl.pallas_call(
+        lend_kernel,
+        out_shape=(jax.ShapeDtypeStruct((2, share, tokens), jnp.bfloat16), edge, edge),
+        grid_spec=pltpu.PrefetchScalarGridSpec(
+            num_scalar_prefetch=2,
+            grid=(count,),
+            in_specs=[
+                pl.BlockSpec(
+                    (1, 2, step, tokens), lambda i, p, t: (0, 0, (1 - p[0]) * count + i, 0)
+                ),
+                pl.BlockSpec((1, 1, channels, window), lambda i, p, t: (0, 1, 0, last)),
+                pl.BlockSpec((channels, window), lambda i, p, t: (0, last)),
+            ],
+            out_specs=(
+                pl.BlockSpec((2, step, tokens), lambda i, p, t: (0, i, 0)),
+                pl.BlockSpec((share, window), lambda i, p, t: (0, 0)),
+                pl.BlockSpec((share, window), lambda i, p, t: (0, 0)),
+            ),
+        ),
+        name="lend",
+        cost_estimate=cost(share, tokens, 2),
+        compiler_params=COMPILER,
+    )(*place, gate_streams, gate_streams, inputs)
 
 
 def ring(value, axis, by):
@@ -487,22 +558,21 @@
 def on_device(gate_streams, inputs, medium_taps, residues, decay_rates):
     channels, tokens = inputs.shape
     share = channels // 2
+    gate_streams, inputs, medium_taps = parked(gate_streams, inputs, medium_taps)
     window = medium_taps.shape[1]
     modes = decay_rates.shape[1]
     section = lax.axis_index("section")
-    place = jnp.stack([section, lax.axis_index("tok")]).astype(jnp.int32)
-    tail = slice(tokens - window, tokens)
-    edge = (
-        gate_streams[0, 1, :, tail].astype(jnp.float32) * inputs[:, tail].astype(jnp.float32)
-    ).astype(jnp.bfloat16)
-    halos = [edge_to(edge[s * share : (s + 1) * share], s) for s in range(2)]
-    lent = lax.dynamic_slice_in_dim(gate_streams[0], (1 - section) * share, share, 1)
+    place = tuple(
+        lax.axis_index(axis).astype(jnp.int32).reshape(1) for axis in ("section", "tok")
+    )
+    lent, *edges = lend_call(place, gate_streams, inputs, window, share)
+    halos = parked(*(edge_to(edges[s], s) for s in range(2)))
     swapped = ring(lent, "section", 1)
     rates = decay_rates.reshape(channels // ROWS, ROWS * modes)
     weights = residues.reshape(channels // ROWS, ROWS * modes)
     response = response_call(place, rates, weights, modes, window, share)
     medium, ends, total = front_call(
-        place, gate_streams, swapped, inputs, halos, medium_taps, rates, modes, share
+        place, gate_streams, swapped, inputs, halos, medium_taps, rates, response, modes, share
     )
     arrived = [ring(total, "tok", by) for by in range(1, lax.axis_size("tok"))]
     medium_other = ring(medium, "section", 1)

time: 56.5 us -> 43.1 us (0.76)
  Pallas kernels: 26.4 us -> 21.6 us
  local copies, waits for them, and re-layouts: 9.12 us -> 6.38 us
  other arithmetic: 4.95 us -> 2.9 us
  starting transfers between devices: 11.9 us -> 10.1 us
  waiting for transfers between devices: 2.96 us -> 1.17 us
    pallas_call x0 -> x1, Pallas kernels: none -> 3.09 us  [lend_call(): pl.pallas_call(lend_kernel, out_shape=(jax.ShapeDtypeStruct((2, share, to...]
    dynamic_slice x1 -> x0, local copies, waits for them, and re-layouts: 3.04 us -> none  [on_device(): lax.dynamic_slice_in_dim(gate_streams[0], (1 - section) * share, share, 1)]
    ppermute x6, starting transfers between devices: 7.81 us -> 5.05 us  [ring(): lax.ppermute(value, axis, [(i, (i + by) % peers) for i in range(peers)])]
    pallas_call x1, Pallas kernels: 6.66 us -> 4.27 us  [within_call(): pl.pallas_call(within_kernel, out_shape=jax.ShapeDtypeStruct((share, toke...]
    pallas_call x1, Pallas kernels: 7.81 us -> 5.68 us  [front_call(): pl.pallas_call(functools.partial(front_kernel, modes), out_shape=(jax.Sha...]
    pallas_call x1, Pallas kernels: 6.66 us -> 4.75 us  [output_call(): pl.pallas_call(functools.partial(output_kernel, len(arrived), lanes // RO...]
    ppermute x2, waiting for transfers between devices: 1.79 us -> 0.01 us  [edge_to(): return lax.ppermute(value, ('section', 'tok'), pairs)]
    pallas_call x1, Pallas kernels: 5.32 us -> 3.79 us  [response_call(): pl.pallas_call(functools.partial(response_kernel, modes), out_shape=jax.S...]
  transfers between devices with their start and end apart: 8 -> 8, of which waited for: 2 -> 1; matrix products, arithmetic and copies ran while one was open for 12% -> 17% of each run, Pallas kernels for 34% -> 30%
where the time goes in v3:
time: 43.1 us; the launch traced here: 42.3 us
  Pallas kernels  21.6 us (50%)
  starting transfers between devices  10.1 us (23%)
  local copies, waits for them, and re-layouts  6.38 us (15%)
  other arithmetic  2.9 us (7%)
  waiting for transfers between devices  1.17 us (3%)
    pallas_call x1, Pallas kernels, front_call(): pl.pallas_call(functools.partial(front_kernel, modes), out_shape=(jax.Sha...  5.68 us
    ppermute x2, starting transfers between devices, edge_to(): return lax.ppermute(value, ('section', 'tok'), pairs)  5.07 us
    ppermute x6, starting transfers between devices, ring(): lax.ppermute(value, axis, [(i, (i + by) % peers) for i in range(peers)])  5.05 us
    pallas_call x1, Pallas kernels, output_call(): pl.pallas_call(functools.partial(output_kernel, len(arrived), lanes // RO...  4.75 us
    pallas_call x1, Pallas kernels, within_call(): pl.pallas_call(within_kernel, out_shape=jax.ShapeDtypeStruct((share, toke...  4.27 us
    pallas_call x1, Pallas kernels, response_call(): pl.pallas_call(functools.partial(response_kernel, modes), out_shape=jax.S...  3.79 us
    unnamed x8, local copies, waits for them, and re-layouts  3.32 us
    pallas_call x1, Pallas kernels, lend_call(): pl.pallas_call(lend_kernel, out_shape=(jax.ShapeDtypeStruct((2, share, to...  3.09 us
  transfers between devices with their start and end apart: 8, of which 1 were waited for; matrix products, arithmetic and copies ran while one was open for 17% of the time, Pallas kernels for 30%

profile of v3, /device:TPU:1, one launch (start us, length us, event | category | flops | bytes accessed | tf_op | source)
XLA Modules:
  0.0 42.3 jit_solution(7576465987167940145)
XLA Ops:
  0.0 0.0 copy-start.1
  0.0 3.1 %lend.1 = (bf16[2,1024,512]{2,1,0:T(8,128)(2,1)}, bf16[1024,128]{1,0:T(8,128)(2,1)S(1)}, bf16[1024,128]{1,0:T(8,128)(2,1)S(1)}) custom-call(s32[1]{0:T(128)} %bitcast.sec, s32[1]{0:T(128)} %bitcast.1.tok, bf16[1,2,2048,512]{3,2,1,0:T(8,128)(2,1)} %local.5, bf16[1,2,2048,512]{3,2,1,0:T(8,128)(2,1)} %local.5, bf16[2048,512]{1,0:T(8,128)(2,1)} %inputs.5), custom_call_target="tpu_custom_call" | custom-call | flops 1048576 | bytes 6291456 | tf_op jit(solution)/shard_map/lend/pallas_call | solution.py:521
  3.1 0.0 copy-start.2
  3.1 0.0 collective-permute-start
  3.1 0.8 %collective-permute-start.1 = (bf16[1024,128]{1,0:T(8,128)(2,1)S(1)}, bf16[1024,128]{1,0:T(8,128)(2,1)S(1)}, u32[]{:S(2)}, u32[]{:S(2)}) collective-permute-start(bf16[1024,128]{1,0:T(8,128)(2,1)S(1)} %get-tuple-element.12), channel_id=1, source_target_pairs={{0,1},{1,2},{2,3},{3,0},{16,16},{17,17},{18,18},{19,19},{4,5},{5,6... | collective-permute-start | bytes 786440 | tf_op jit(solution)/shard_map/ppermute | solution.py:555
  3.9 4.3 %collective-permute-start.2 = (bf16[1024,128]{1,0:T(8,128)(2,1)S(1)}, bf16[1024,128]{1,0:T(8,128)(2,1)}, u32[]{:S(2)}, u32[]{:S(2)}) collective-permute-start(bf16[1024,128]{1,0:T(8,128)(2,1)S(1)} %get-tuple-element.13), channel_id=1, source_target_pairs={{0,17},{1,18},{2,19},{3,16},{16,0},{17,1},{18,2},{19,3},{4,21},{5,... | collective-permute-start | bytes 786440 | tf_op jit(solution)/shard_map/ppermute | solution.py:555
  8.2 0.0 copy-done.1
  8.2 1.3 %copy.21 = f32[2048,16]{1,0:T(8,128)} copy(f32[2048,16]{0,1:T(8,128)S(1)} %copy-done.1) | data formatting | bytes 262144 | tf_op args[4]
  9.5 1.5 %reshape.14.rates = f32[256,128]{1,0:T(8,128)S(1)} reshape(f32[2048,16]{1,0:T(8,128)} %copy.21) | data formatting | bytes 262144 | tf_op jit(solution)/shard_map/reshape | solution.py:571
  11.0 0.0 copy-done.2
  11.0 1.3 %copy.22 = f32[2048,16]{1,0:T(8,128)} copy(f32[2048,16]{0,1:T(8,128)S(1)} %copy-done.2) | data formatting | bytes 262144 | tf_op args[3]
  12.4 1.5 %reshape.15.residues = f32[256,128]{1,0:T(8,128)S(1)} reshape(f32[2048,16]{1,0:T(8,128)} %copy.22) | data formatting | bytes 262144 | tf_op jit(solution)/shard_map/reshape | solution.py:572
  13.9 3.8 %response.1.after = f32[1024,256]{1,0:T(8,128)S(1)} custom-call(s32[1]{0:T(128)} %bitcast.sec, s32[1]{0:T(128)} %bitcast.1.tok, f32[256,128]{1,0:T(8,128)S(1)} %reshape.14.rates, f32[256,128]{1,0:T(8,128)S(1)} %reshape.15.residues, bf16[128,256]{1,0:T(8,128)(2,1)} %constant.34.table_h, bf16[128,256]{1,0:T(8,128)(2,1)} %constant.37.table_l), custom_call_target="tpu_custom_call" | custom-call | flops 314572800 | bytes 6291456 | tf_op jit(solution)/shard_map/response/pallas_call | solution.py:176
  17.7 0.0 collective-permute-done.1.halo_low
  17.7 0.0 copy-start
  17.7 0.0 collective-permute-done.2.halo_high
  17.7 0.7 %copy-done = bf16[1024,128]{1,0:T(8,128)(2,1)} copy-done((bf16[1024,128]{1,0:T(8,128)(2,1)}, bf16[1024,128]{1,0:T(8,128)(2,1)S(1)}, u32[]{:S(2)}) %copy-start) | copy-done | bytes 262168
  18.4 0.0 collective-permute-done.remote
  18.4 5.7 %front.1 = (bf16[1024,512]{1,0:T(8,128)(2,1)S(1)}, f32[4,1024,128]{2,1,0:T(8,128)S(1)}, f32[128,128]{1,0:T(8,128)S(1)}) custom-call(s32[1]{0:T(128)} %bitcast.sec, s32[1]{0:T(128)} %bitcast.1.tok, bf16[1,2,2048,512]{3,2,1,0:T(8,128)(2,1)} %local.5, bf16[2,1024,512]{2,1,0:T(8,128)(2,1)S(1)} %collective-permute-done.remote, bf16[2048,512]{1,0:T(8,128)(2,1)} %inputs.5, ...), custom_call_target="tpu_custom_call" | custom-call | flops 1048576000 | bytes 6291456 | tf_op jit(solution)/shard_map/front/pallas_call | solution.py:314
  24.1 0.1 collective-permute-start.7
  24.2 1.2 %collective-permute-start.3 = (f32[128,128]{1,0:T(8,128)S(1)}, f32[128,128]{1,0:T(8,128)S(1)}, u32[]{:S(2)}, u32[]{:S(2)}) collective-permute-start(f32[128,128]{1,0:T(8,128)S(1)} %get-tuple-element.16), channel_id=1, source_target_pairs={{0,1},{1,2},{2,3},{3,0},{4,5},{5,6},{6,7},{7,4},{8,9},{9,10},{10,1... | collective-permute-start | bytes 196616 | tf_op jit(solution)/shard_map/ppermute | solution.py:548
  25.4 0.1 collective-permute-start.4
  25.5 2.3 %collective-permute-start.5 = (f32[128,128]{1,0:T(8,128)S(1)}, f32[128,128]{1,0:T(8,128)S(1)}, u32[]{:S(2)}, u32[]{:S(2)}) collective-permute-start(f32[128,128]{1,0:T(8,128)S(1)} %get-tuple-element.16), channel_id=1, source_target_pairs={{0,3},{1,0},{2,1},{3,2},{4,7},{5,4},{6,5},{7,6},{8,11},{9,8},{10,9... | collective-permute-start | bytes 196616 | tf_op jit(solution)/shard_map/ppermute | solution.py:548
  27.8 4.3 %within.1 = f32[1024,512]{1,0:T(8,128)S(1)} custom-call(s32[1]{0:T(128)} %bitcast.sec, s32[1]{0:T(128)} %bitcast.1.tok, bf16[1,2,2048,512]{3,2,1,0:T(8,128)(2,1)} %local.5, bf16[2,1024,512]{2,1,0:T(8,128)(2,1)S(1)} %collective-permute-done.remote, bf16[2048,512]{1,0:T(8,128)(2,1)} %inputs.5, bf16[1024,512]{1,0:T(8,128)(2,1)S(1)} %get-tuple-element.14.gated_medium, ...), custom_call_target="tpu_custom_call" | custom-call | flops 786432000 | bytes 6291456 | tf_op jit(solution)/shard_map/within/pallas_call | solution.py:376
  32.1 0.0 collective-permute-done.3.rest_0_
  32.1 0.0 collective-permute-done.4.rest_1_
  32.1 0.0 collective-permute-done.5.rest_2_
  32.1 4.7 %output.1 = bf16[1024,512]{1,0:T(8,128)(2,1)} custom-call(s32[1]{0:T(128)} %bitcast.sec, s32[1]{0:T(128)} %bitcast.1.tok, bf16[1,2,2048,512]{3,2,1,0:T(8,128)(2,1)} %local.5, bf16[2,1024,512]{2,1,0:T(8,128)(2,1)S(1)} %collective-permute-done.remote, f32[1024,512]{1,0:T(8,128)S(1)} %within.1, bf16[2048,512]{1,0:T(8,128)(2,1)} %inputs.5, ...), custom_call_target="tpu_custom_call" | custom-call | flops 786432000 | bytes 6291456 | tf_op jit(solution)/shard_map/output/pallas_call | solution.py:473
  36.9 1.3 %collective-permute-start.6 = (bf16[1024,512]{1,0:T(8,128)(2,1)}, bf16[1024,512]{1,0:T(8,128)(2,1)S(1)}, u32[]{:S(2)}, u32[]{:S(2)}) collective-permute-start(bf16[1024,512]{1,0:T(8,128)(2,1)} %output.1), channel_id=1, source_target_pairs={{0,16},{16,0},{1,17},{17,1},{2,18},{18,2},{3,19},{19,3},{4,20},{20... | collective-permute-start | bytes 3145736 | tf_op jit(solution)/shard_map/ppermute | solution.py:548
  38.2 0.0 collective-permute-done.7
  38.2 1.3 %broadcast_select_fusion = bf16[1024,512]{1,0:T(8,128)(2,1)S(1)} fusion(bf16[1024,512]{1,0:T(8,128)(2,1)} %collective-permute-done.7, bf16[1024,512]{1,0:T(8,128)(2,1)} %output.1, pred[]{:T(512)S(6)} %eq.3), kind=kLoop, calls=%fused_computation.1 | loop fusion | flops 524288 | bytes 3145729 | tf_op jit(solution)/shard_map/jit(_where)/select_n | solution.py:586
  39.5 1.2 %collective-permute-done.6 = bf16[1024,512]{1,0:T(8,128)(2,1)S(1)} collective-permute-done((bf16[1024,512]{1,0:T(8,128)(2,1)}, bf16[1024,512]{1,0:T(8,128)(2,1)S(1)}, u32[]{:S(2)}, u32[]{:S(2)}) %collective-permute-start.6) | collective-permute-done | bytes 1048608 | tf_op jit(solution)/shard_map/ppermute | solution.py:548
  40.7 0.1 broadcast_select_fusion.1
  40.8 1.5 %maximum_bitcast_fusion = bf16[1,2048,512]{2,1,0:T(8,128)(2,1)} fusion(bf16[1024,512]{1,0:T(8,128)(2,1)S(1)} %broadcast_select_fusion, bf16[1024,512]{1,0:T(8,128)(2,1)S(1)} %broadcast_select_fusion.1), kind=kLoop, calls=%fused_computation | loop fusion | flops 4194304 | bytes 4194304 | tf_op jit(solution)/shard_map/broadcast_in_dim | solution.py:587
Async XLA Ops:
  0.0 8.2 %copy-start.1 = (f32[2048,16]{0,1:T(8,128)S(1)}, f32[2048,16]{0,1:T(8,128)}, u32[]{:S(2)}) copy-start(f32[2048,16]{0,1:T(8,128)} %param.22) | copy-start | bytes 393220
  3.1 7.9 %copy-start.2 = (f32[2048,16]{0,1:T(8,128)S(1)}, f32[2048,16]{0,1:T(8,128)}, u32[]{:S(2)}) copy-start(f32[2048,16]{0,1:T(8,128)} %param.21) | copy-start | bytes 393220
  3.1 15.3 %collective-permute-start = (bf16[2,1024,512]{2,1,0:T(8,128)(2,1)}, bf16[2,1024,512]{2,1,0:T(8,128)(2,1)S(1)}, u32[]{:S(2)}, u32[]{:S(2)}) collective-permute-start(bf16[2,1024,512]{2,1,0:T(8,128)(2,1)} %get-tuple-element.11), channel_id=1, source_target_pairs={{0,16},{16,0},{1,17},{17,1},{2,18},{18,2},{3,19},{19,3},{4,20},{20... | collective-permute-start | bytes 6291464 | tf_op jit(solution)/shard_map/ppermute | solution.py:548
  3.1 14.6 %collective-permute-start.1 = (bf16[1024,128]{1,0:T(8,128)(2,1)S(1)}, bf16[1024,128]{1,0:T(8,128)(2,1)S(1)}, u32[]{:S(2)}, u32[]{:S(2)}) collective-permute-start(bf16[1024,128]{1,0:T(8,128)(2,1)S(1)} %get-tuple-element.12), channel_id=1, source_target_pairs={{0,1},{1,2},{2,3},{3,0},{16,16},{17,17},{18,18},{19,19},{4,5},{5,6... | collective-permute-start | bytes 786440 | tf_op jit(solution)/shard_map/ppermute | solution.py:555
  3.9 13.8 %collective-permute-start.2 = (bf16[1024,128]{1,0:T(8,128)(2,1)S(1)}, bf16[1024,128]{1,0:T(8,128)(2,1)}, u32[]{:S(2)}, u32[]{:S(2)}) collective-permute-start(bf16[1024,128]{1,0:T(8,128)(2,1)S(1)} %get-tuple-element.13), channel_id=1, source_target_pairs={{0,17},{1,18},{2,19},{3,16},{16,0},{17,1},{18,2},{19,3},{4,21},{5,... | collective-permute-start | bytes 786440 | tf_op jit(solution)/shard_map/ppermute | solution.py:555
  17.7 0.7 %copy-start = (bf16[1024,128]{1,0:T(8,128)(2,1)}, bf16[1024,128]{1,0:T(8,128)(2,1)S(1)}, u32[]{:S(2)}) copy-start(bf16[1024,128]{1,0:T(8,128)(2,1)S(1)} %collective-permute-done.1.halo_low) | copy-start | bytes 786436
  24.1 14.1 %collective-permute-start.7 = (bf16[1024,512]{1,0:T(8,128)(2,1)S(1)}, bf16[1024,512]{1,0:T(8,128)(2,1)}, u32[]{:S(2)}, u32[]{:S(2)}) collective-permute-start(bf16[1024,512]{1,0:T(8,128)(2,1)S(1)} %get-tuple-element.14.gated_medium), channel_id=1, source_target_pairs={{0,16},{16,0},{1,17},{17,1},{2,18},{18,2},{3,19},{19,3},{4,20},{20... | collective-permute-start | bytes 3145736 | tf_op jit(solution)/shard_map/ppermute | solution.py:548
  24.2 7.9 %collective-permute-start.3 = (f32[128,128]{1,0:T(8,128)S(1)}, f32[128,128]{1,0:T(8,128)S(1)}, u32[]{:S(2)}, u32[]{:S(2)}) collective-permute-start(f32[128,128]{1,0:T(8,128)S(1)} %get-tuple-element.16), channel_id=1, source_target_pairs={{0,1},{1,2},{2,3},{3,0},{4,5},{5,6},{6,7},{7,4},{8,9},{9,10},{10,1... | collective-permute-start | bytes 196616 | tf_op jit(solution)/shard_map/ppermute | solution.py:548
  25.4 6.7 %collective-permute-start.4 = (f32[128,128]{1,0:T(8,128)S(1)}, f32[128,128]{1,0:T(8,128)S(1)}, u32[]{:S(2)}, u32[]{:S(2)}) collective-permute-start(f32[128,128]{1,0:T(8,128)S(1)} %get-tuple-element.16), channel_id=1, source_target_pairs={{0,2},{1,3},{2,0},{3,1},{4,6},{5,7},{6,4},{7,5},{8,10},{9,11},{10,... | collective-permute-start | bytes 196616 | tf_op jit(solution)/shard_map/ppermute | solution.py:548
  25.5 6.6 %collective-permute-start.5 = (f32[128,128]{1,0:T(8,128)S(1)}, f32[128,128]{1,0:T(8,128)S(1)}, u32[]{:S(2)}, u32[]{:S(2)}) collective-permute-start(f32[128,128]{1,0:T(8,128)S(1)} %get-tuple-element.16), channel_id=1, source_target_pairs={{0,3},{1,0},{2,1},{3,2},{4,7},{5,4},{6,5},{7,6},{8,11},{9,8},{10,9... | collective-permute-start | bytes 196616 | tf_op jit(solution)/shard_map/ppermute | solution.py:548
  36.9 3.8 %collective-permute-start.6 = (bf16[1024,512]{1,0:T(8,128)(2,1)}, bf16[1024,512]{1,0:T(8,128)(2,1)S(1)}, u32[]{:S(2)}, u32[]{:S(2)}) collective-permute-start(bf16[1024,512]{1,0:T(8,128)(2,1)} %output.1), channel_id=1, source_target_pairs={{0,16},{16,0},{1,17},{17,1},{2,18},{18,2},{3,19},{19,3},{4,20},{20... | collective-permute-start | bytes 3145736 | tf_op jit(solution)/shard_map/ppermute | solution.py:548

commit v4 on v3

--- a/solution.py
+++ b/solution.py
@@ -63,6 +63,7 @@
 
 
 PAIR = 16
+WITHIN_STEP = 512
 COMPILER = pltpu.CompilerParams(vmem_limit_bytes=16 << 20)
 
 
@@ -121,9 +122,9 @@
     return jnp.concatenate(tiles, axis=0).astype(jnp.bfloat16)
 
 
-def both_powers(rates, hops, pair, window, first, falling):
+def both_powers(rates, hops, pair, window, falling):
     sides = [
-        powers(spread(rates, g), spread(hops, g), window, first, falling)
+        powers(spread(rates, g), spread(hops, g), window, 0.0, falling)
         for g in (2 * pair, 2 * pair + 1)
     ]
     return jnp.concatenate(sides, axis=1)
@@ -144,21 +145,52 @@
     return residues * jnp.sqrt(1.0 - jnp.exp(-2.0 * slow))
 
 
-def response_kernel(modes, sec, tok, rates, residues, table_h, table_l, out, hops, scales):
+def in_rows(ref, tall):
+    modes, channels = ref.shape
+    tall[...] = ref[...].T
+    count = channels // ROWS
+    return jnp.concatenate(
+        [tall[pl.ds(c, count, stride=ROWS), :] for c in range(ROWS)], axis=1
+    )
+
+
+def response_kernel(
+    sec,
+    tok,
+    rates,
+    residues,
+    table_h,
+    table_l,
+    out,
+    rate_rows,
+    scale_rows,
+    rising,
+    falling,
+    tall,
+    hops,
+    scales,
+):
     window = table_h.shape[0]
+    modes = rates.shape[0]
     mask = lane_mask(modes)
-    slow = rates[...]
+    slow = in_rows(rates, tall)
+    rate_rows[...] = slow
+    scale = scale_of(in_rows(residues, tall), slow)
+    scale_rows[...] = scale
     hops[...] = jnp.exp(-slow * ROWS)
-    scales[...] = scale_of(residues[...], slow) / (1.0 + jnp.exp(-slow * window))
+    scales[...] = scale / (1.0 + jnp.exp(-slow * window))
     parts = []
-    for pair in range(rates.shape[0] // 2):
-        scale = two_sided(
+    for pair in range(rate_rows.shape[0] // 2):
+        both = two_sided(
             jnp.where(mask, spread(scales, 2 * pair), 0.0),
             jnp.where(mask, spread(scales, 2 * pair + 1), 0.0),
         )
-        high = scale.astype(jnp.bfloat16).astype(jnp.float32)
-        both = jnp.concatenate([high, scale - high], axis=0).astype(jnp.bfloat16)
-        found = dot_turned(both, both_powers(rates, hops, pair, window, 0.0, False))
+        high = both.astype(jnp.bfloat16).astype(jnp.float32)
+        both = jnp.concatenate([high, both - high], axis=0).astype(jnp.bfloat16)
+        table = both_powers(rate_rows, hops, pair, window, False)
+        rising[pair] = table
+        falling[pair] = both_powers(rate_rows, hops, pair, window, True)
+        found = dot_turned(both, table)
         parts.append(found[:PAIR] + found[PAIR:])
     taps = jnp.concatenate(parts, axis=0)
     high = taps.astype(jnp.bfloat16)
@@ -168,21 +200,42 @@
     )
 
 
-def response_call(place, rates, residues, modes, window, share):
+def response_call(place, rates, residues, window, share):
     step = min(256, share)
+    modes = rates.shape[0]
+    lanes = ROWS * modes
     tables = split_pair(turned_tables(window)[2])
-    small = (step // ROWS, ROWS * modes)
+    small = (step // ROWS, lanes)
+    large = (step // PAIR, window, 2 * lanes)
     row = mine(share, step)
+    rows_shape = jax.ShapeDtypeStruct((share // ROWS, lanes), jnp.float32)
+    table_shape = jax.ShapeDtypeStruct((share // PAIR, window, 2 * lanes), jnp.bfloat16)
     return pl.pallas_call(
-        functools.partial(response_kernel, modes),
-        out_shape=jax.ShapeDtypeStruct((share, 2 * window), jnp.float32),
+        response_kernel,
+        out_shape=(
+            jax.ShapeDtypeStruct((share, 2 * window), jnp.float32),
+            rows_shape,
+            rows_shape,
+            table_shape,
+            table_shape,
+        ),
         grid_spec=pltpu.PrefetchScalarGridSpec(
             num_scalar_prefetch=2,
             grid=(share // step,),
-            in_specs=[pl.BlockSpec(small, lambda i, p, t: (row(i, p, t), 0))] * 2
+            in_specs=[pl.BlockSpec((modes, step), lambda i, p, t: (0, row(i, p, t)))] * 2
             + [whole(t) for t in tables],
-            out_specs=pl.BlockSpec((step, 2 * window), lambda i, p, t: (i, 0)),
-            scratch_shapes=[pltpu.VMEM(small, jnp.float32)] * 2,
+            out_specs=(
+                pl.BlockSpec((step, 2 * window), lambda i, p, t: (i, 0)),
+                pl.BlockSpec(small, lambda i, p, t: (i, 0)),
+                pl.BlockSpec(small, lambda i, p, t: (i, 0)),
+                pl.BlockSpec(large, lambda i, p, t: (i, 0, 0)),
+                pl.BlockSpec(large, lambda i, p, t: (i, 0, 0)),
+            ),
+            scratch_shapes=[
+                pltpu.VMEM((step, modes), jnp.float32),
+                pltpu.VMEM(small, jnp.float32),
+                pltpu.VMEM(small, jnp.float32),
+            ],
         ),
         name="response",
         cost_estimate=cost(share, 4 * window, 600),
@@ -201,7 +254,7 @@
     halo_high,
     taps,
     rates,
-    after,
+    falling,
     fwd_even,
     fwd_odd,
     inv_even,
@@ -209,7 +262,6 @@
     medium_out,
     ends,
     total,
-    hops,
     leaps,
 ):
     channels, tokens = inputs.shape
@@ -217,9 +269,7 @@
     blocks = tokens // window
     forward = (fwd_even, fwd_odd)
     inverse = (inv_even, inv_odd)
-    slow = rates[...]
-    hops[...] = jnp.exp(-slow * ROWS)
-    leaps[...] = jnp.exp(-slow * window)
+    leaps[...] = jnp.exp(-rates[...] * window)
 
     def body(section):
         first = local.at[0] if section == 0 else remote
@@ -228,12 +278,7 @@
         tap_rows = taps[...]
         started = jnp.where(tok[0] > 0, 1.0, 0.0).astype(jnp.bfloat16)
         parts = [slice(b * window, (b + 1) * window) for b in range(blocks)]
-        sources = [
-            (first[1, :, part].astype(jnp.float32) * inputs[:, part].astype(jnp.float32)).astype(
-                jnp.bfloat16
-            )
-            for part in parts
-        ]
+        sources = [first[1, :, part] * inputs[:, part] for part in parts]
         sources = [halo[...] * started] + sources
         even = [tap_rows] + sources[1::2]
         odd = sources[0::2]
@@ -281,7 +326,7 @@
         for pair in range(channels // PAIR):
             rows = slice(pair * PAIR, (pair + 1) * PAIR)
             left = jnp.concatenate([signal[rows] for signal in signals], axis=0)
-            found = dot_f32(left, both_powers(rates, hops, pair, window, 0.0, True))
+            found = dot_f32(left, falling[pair])
             for side in range(2):
                 leap = spread(leaps, 2 * pair + side)
                 state = None
@@ -300,7 +345,7 @@
 
 
 def front_call(
-    place, gate_streams, swapped, inputs, halos, taps, rates, after, modes, share
+    place, gate_streams, swapped, inputs, halos, taps, rates, falling, modes, share
 ):
     tokens = inputs.shape[1]
     window = taps.shape[1]
@@ -328,8 +373,8 @@
                 pl.BlockSpec((step, window), lambda i, p, t: (i, 0)),
                 pl.BlockSpec((step, window), lambda i, p, t: (i, 0)),
                 pl.BlockSpec((step, window), lambda i, p, t: (row(i, p, t), 0)),
-                pl.BlockSpec(small, lambda i, p, t: (row(i, p, t), 0)),
-                pl.BlockSpec(memory_space=pl.ANY),
+                pl.BlockSpec(small, lambda i, p, t: (i, 0)),
+                pl.BlockSpec((step // PAIR, window, 2 * lanes), lambda i, p, t: (i, 0, 0)),
             ]
             + [whole(t) for t in tables],
             out_specs=(
@@ -337,12 +382,12 @@
                 pl.BlockSpec((blocks, step, lanes), lambda i, p, t: (0, i, 0)),
                 pl.BlockSpec(small, lambda i, p, t: (i, 0)),
             ),
-            scratch_shapes=[pltpu.VMEM(small, jnp.float32)] * 2,
+            scratch_shapes=[pltpu.VMEM(small, jnp.float32)],
         ),
         name="front",
         cost_estimate=cost(share, tokens, 2000),
         compiler_params=COMPILER,
-    )(*place, gate_streams, swapped, inputs, *halos, taps, rates, after, *parked(*tables))
+    )(*place, gate_streams, swapped, inputs, *halos, taps, rates, falling, *parked(*tables))
 
 
 def within_kernel(sec, tok, local, remote, inputs, gated_medium, response, fwd_h, fwd_l, inverse, out):
@@ -351,17 +396,29 @@
 
     def body(section):
         gate_in = remote.at[0] if section == 0 else local.at[0, 0]
+        channels, tokens = inputs.shape
         real, imag = response[:, :half], response[:, half:]
-        for pair in range(inputs.shape[1] // size):
-            part = slice(pair * size, (pair + 1) * size)
+        parts = [slice(k * size, (k + 1) * size) for k in range(tokens // size)]
+        signals = []
+        for part in parts:
             stream = inputs[:, part].astype(jnp.float32) + gated_medium[:, part].astype(
                 jnp.float32
             )
-            signal = (gate_in[:, part].astype(jnp.float32) * stream).astype(jnp.bfloat16)
-            spec = dot_f32(signal, fwd_h[...]) + dot_f32(signal, fwd_l[...])
-            a, b = spec[:, :half], spec[:, half:]
-            filtered = jnp.concatenate([a * real - b * imag, a * imag + b * real], axis=1)
-            out[:, part] = dot_f32(filtered.astype(jnp.bfloat16), inverse[...])
+            signals.append((gate_in[:, part].astype(jnp.float32) * stream).astype(jnp.bfloat16))
+        signal = jnp.concatenate(signals, axis=0)
+        spec = dot_f32(signal, fwd_h[...]) + dot_f32(signal, fwd_l[...])
+        filtered = []
+        for k in range(len(parts)):
+            rows = slice(k * channels, (k + 1) * channels)
+            a, b = spec[rows, :half], spec[rows, half:]
+            filtered.append(
+                jnp.concatenate([a * real - b * imag, a * imag + b * real], axis=1).astype(
+                    jnp.bfloat16
+                )
+            )
+        found = dot_f32(jnp.concatenate(filtered, axis=0), inverse[...])
+        for k, part in enumerate(parts):
+            out[:, part] = found[k * channels : (k + 1) * channels]
 
     by_section(sec, body)
 
@@ -369,7 +426,7 @@
 def within_call(place, gate_streams, swapped, inputs, gated_medium, response, share):
     tokens = inputs.shape[1]
     window = response.shape[1] // 2
-    step = min(256, share)
+    step = min(WITHIN_STEP, share)
     forward, inverse, _ = turned_tables(window)
     tables = split_pair(forward) + split_pair(inverse)[:1]
     row = mine(share, step)
@@ -407,29 +464,31 @@
     inputs,
     gated_medium,
     rates,
-    residues,
+    scale_rows,
+    rising,
     ends,
     *rest,
 ):
-    arrived, (out, hops, leaps, scales, shares, starts) = rest[:count], rest[count:]
+    arrived, (keep, send, leaps, scales, shares, starts) = rest[:count], rest[count:]
     channels, tokens = inputs.shape
     blocks = tokens // window
     mask = lane_mask(modes)
     slow = rates[...]
     leap_all = jnp.exp(-slow * window)
-    scale_all = scale_of(residues[...], slow)
-    hops[...] = jnp.exp(-slow * ROWS)
+    scale_all = scale_rows[...] * jnp.exp(-slow)
     leaps[...] = leap_all
     scales[...] = scale_all
     shares[...] = scale_all / (1.0 + leap_all)
     entering = jnp.zeros_like(slow)
     for k in range(count):
-        keep = jnp.where(tok[0] > k, 1.0, 0.0)
-        entering = entering + arrived[k][...] * (jnp.exp(-slow * (tokens * k)) * keep)
+        known = jnp.where(tok[0] > k, 1.0, 0.0)
+        entering = entering + arrived[k][...] * (jnp.exp(-slow * (tokens * k)) * known)
     starts[...] = entering
 
     def body(section):
         gate_out = remote.at[0] if section == 0 else local.at[0, 0]
+        out = send if section == 0 else keep.at[0]
+        (keep.at[0] if section == 0 else send)[...] = gated_medium[...]
         for pair in range(channels // PAIR):
             rows = slice(pair * PAIR, (pair + 1) * PAIR)
             sides = []
@@ -448,7 +507,7 @@
             left = jnp.concatenate(
                 [two_sided(upper, lower) for upper, lower in zip(*sides)], axis=0
             ).astype(jnp.bfloat16)
-            across = dot_turned(left, both_powers(rates, hops, pair, window, 1.0, False))
+            across = dot_turned(left, rising[pair])
             for b in range(blocks):
                 part = slice(b * window, (b + 1) * window)
                 stream = inputs[rows, part].astype(jnp.float32) + gated_medium[
@@ -462,7 +521,7 @@
 
 
 def output_call(
-    place, gate_streams, swapped, within, inputs, medium, rates, residues, ends, arrived, window
+    place, gate_streams, swapped, within, inputs, medium, rates, scales, rising, ends, arrived, window
 ):
     share, tokens = medium.shape
     lanes = rates.shape[1]
@@ -472,7 +531,10 @@
     small = (step // ROWS, lanes)
     return pl.pallas_call(
         functools.partial(output_kernel, len(arrived), lanes // ROWS, window),
-        out_shape=jax.ShapeDtypeStruct((share, tokens), jnp.bfloat16),
+        out_shape=(
+            jax.ShapeDtypeStruct((1,) + inputs.shape, jnp.bfloat16),
+            jax.ShapeDtypeStruct((share, tokens), jnp.bfloat16),
+        ),
         grid_spec=pltpu.PrefetchScalarGridSpec(
             num_scalar_prefetch=2,
             grid=(share // step,),
@@ -482,20 +544,53 @@
                 pl.BlockSpec(wide, lambda i, p, t: (i, 0)),
                 pl.BlockSpec(wide, lambda i, p, t: (row(i, p, t), 0)),
                 pl.BlockSpec(wide, lambda i, p, t: (i, 0)),
-                pl.BlockSpec(small, lambda i, p, t: (row(i, p, t), 0)),
-                pl.BlockSpec(small, lambda i, p, t: (row(i, p, t), 0)),
+                pl.BlockSpec(small, lambda i, p, t: (i, 0)),
+                pl.BlockSpec(small, lambda i, p, t: (i, 0)),
+                pl.BlockSpec((step // PAIR, window, 2 * lanes), lambda i, p, t: (i, 0, 0)),
                 pl.BlockSpec((tokens // window, step, lanes), lambda i, p, t: (0, i, 0)),
             ]
             + [pl.BlockSpec(small, lambda i, p, t: (i, 0))] * len(arrived),
-            out_specs=pl.BlockSpec(wide, lambda i, p, t: (i, 0)),
-            scratch_shapes=[pltpu.VMEM(small, jnp.float32)] * 5,
+            out_specs=(
+                pl.BlockSpec((1,) + wide, lambda i, p, t: (0, row(i, p, t), 0)),
+                pl.BlockSpec(wide, lambda i, p, t: (i, 0)),
+            ),
+            scratch_shapes=[pltpu.VMEM(small, jnp.float32)] * 4,
         ),
         name="output",
         cost_estimate=cost(share, tokens, 1500),
         compiler_params=COMPILER,
     )(
-        *place, gate_streams, swapped, within, inputs, medium, rates, residues, ends, *arrived
-    )
+        *place, gate_streams, swapped, within, inputs, medium, rates, scales, rising, ends, *arrived
+    )
+
+
+def place_kernel(sec, tok, own, received, out):
+    out[0] = received[...]
+
+
+def place_call(place, own, received):
+    share, tokens = received.shape
+    step = min(512, share)
+    count = share // step
+    return pl.pallas_call(
+        place_kernel,
+        out_shape=jax.ShapeDtypeStruct(own.shape, own.dtype),
+        grid_spec=pltpu.PrefetchScalarGridSpec(
+            num_scalar_prefetch=2,
+            grid=(count,),
+            in_specs=[
+                pl.BlockSpec(memory_space=pl.ANY),
+                pl.BlockSpec((step, tokens), lambda i, p, t: (i, 0)),
+            ],
+            out_specs=pl.BlockSpec(
+                (1, step, tokens), lambda i, p, t: (0, (1 - p[0]) * count + i, 0)
+            ),
+        ),
+        input_output_aliases={2: 0},
+        name="placing",
+        cost_estimate=cost(share, tokens, 2),
+        compiler_params=COMPILER,
+    )(*place, own, received)
 
 
 def lend_kernel(sec, tok, gates, gate_tail, input_tail, out, low, high):
@@ -566,25 +661,20 @@
         lax.axis_index(axis).astype(jnp.int32).reshape(1) for axis in ("section", "tok")
     )
     lent, *edges = lend_call(place, gate_streams, inputs, window, share)
-    halos = parked(*(edge_to(edges[s], s) for s in range(2)))
+    halos = [edge_to(edges[s], s) for s in range(2)]
     swapped = ring(lent, "section", 1)
-    rates = decay_rates.reshape(channels // ROWS, ROWS * modes)
-    weights = residues.reshape(channels // ROWS, ROWS * modes)
-    response = response_call(place, rates, weights, modes, window, share)
+    response, rates, scales, rising, falling = response_call(
+        place, decay_rates.T, residues.T, window, share
+    )
     medium, ends, total = front_call(
-        place, gate_streams, swapped, inputs, halos, medium_taps, rates, response, modes, share
+        place, gate_streams, swapped, inputs, halos, medium_taps, rates, falling, modes, share
     )
     arrived = [ring(total, "tok", by) for by in range(1, lax.axis_size("tok"))]
-    medium_other = ring(medium, "section", 1)
     within = within_call(place, gate_streams, swapped, inputs, medium, response, share)
-    mixed = output_call(
-        place, gate_streams, swapped, within, inputs, medium, rates, weights, ends, arrived, window
-    )
-    mixed_other = ring(mixed, "section", 1)
-    leading = section == 0
-    upper = jnp.where(leading, medium, mixed_other)
-    lower = jnp.where(leading, medium_other, mixed)
-    return jnp.concatenate([upper, lower], axis=0)[None]
+    keep, send = output_call(
+        place, gate_streams, swapped, within, inputs, medium, rates, scales, rising, ends, arrived, window
+    )
+    return place_call(place, keep, ring(send, "section", 1))
 
 
 def solution(mesh):

time: 43.1 us -> 35.9 us (0.83)
  local copies, waits for them, and re-layouts: 6.38 us -> 0.01 us
  waiting for transfers between devices: 1.17 us -> 4.19 us
  other arithmetic: 2.9 us -> 0 us
  starting transfers between devices: 10.1 us -> 9.62 us
    unnamed x8 -> x4, local copies, waits for them, and re-layouts: 3.32 us -> 0.01 us
    reshape x2 -> x0, local copies, waits for them, and re-layouts: 3.06 us -> none  [the longest x1 1.53 us: on_device(): rates = decay_rates.reshape(channels // ROWS, ROWS * modes)]
    pallas_call x1 -> x2, Pallas kernels: 3.79 us -> 6.45 us  [the longest x1 5.45 us: response_call(): pl.pallas_call(response_kernel, out_shape=(jax.ShapeDtypeStruct((share, 2...]
    ppermute x2, waiting for transfers between devices: 0.01 us -> 1.89 us  [edge_to(): return lax.ppermute(value, ('section', 'tok'), pairs)]
    pallas_call x1, Pallas kernels: 4.27 us -> 2.77 us  [within_call(): pl.pallas_call(within_kernel, out_shape=jax.ShapeDtypeStruct((share, toke...]
    broadcast_in_dim x1 -> x0, other arithmetic: 1.46 us -> none  [on_device(): return jnp.concatenate([upper, lower], axis=0)[None]]
    select_n x2 -> x0, other arithmetic: 1.45 us -> none  [the longest x1 1.34 us: on_device(): lower = jnp.where(leading, medium_other, mixed)]
    ppermute x6 -> x5, waiting for transfers between devices: 1.17 us -> 2.3 us  [ring(): lax.ppermute(value, axis, [(i, (i + by) % peers) for i in range(peers)])]
  transfers between devices with their start and end apart: 8 -> 7, of which waited for: 1 -> 2; matrix products, arithmetic and copies ran while one was open for 17% -> 0% of each run, Pallas kernels for 30% -> 23%
where the time goes in v4:
time: 35.9 us; the launch traced here: 35.2 us
  Pallas kernels  21.3 us (59%)
  starting transfers between devices  9.62 us (27%)
  waiting for transfers between devices  4.19 us (12%)
    pallas_call x1, Pallas kernels, response_call(): pl.pallas_call(response_kernel, out_shape=(jax.ShapeDtypeStruct((share, 2...  5.45 us
    pallas_call x1, Pallas kernels, front_call(): pl.pallas_call(functools.partial(front_kernel, modes), out_shape=(jax.Sha...  5.24 us
    ppermute x2, starting transfers between devices, edge_to(): return lax.ppermute(value, ('section', 'tok'), pairs)  4.94 us
    pallas_call x1, Pallas kernels, output_call(): pl.pallas_call(functools.partial(output_kernel, len(arrived), lanes // RO...  4.7 us
    ppermute x5, starting transfers between devices, ring(): lax.ppermute(value, axis, [(i, (i + by) % peers) for i in range(peers)])  4.67 us
    pallas_call x1, Pallas kernels, within_call(): pl.pallas_call(within_kernel, out_shape=jax.ShapeDtypeStruct((share, toke...  2.77 us
    ppermute x5, waiting for transfers between devices, ring(): lax.ppermute(value, axis, [(i, (i + by) % peers) for i in range(peers)])  2.3 us
    pallas_call x1, Pallas kernels, lend_call(): pl.pallas_call(lend_kernel, out_shape=(jax.ShapeDtypeStruct((2, share, to...  2.12 us
  transfers between devices with their start and end apart: 7, of which 2 were waited for; matrix products, arithmetic and copies ran while one was open for 0% of the time, Pallas kernels for 23%

profile of v4, /device:TPU:1, one launch (start us, length us, event | category | flops | bytes accessed | tf_op | source)
XLA Modules:
  0.0 35.2 jit_solution(3851849739687116977)
XLA Ops:
  0.0 0.0 copy-start
  0.0 0.0 copy-start.1
  0.0 2.1 %lend.1 = (bf16[2,1024,512]{2,1,0:T(8,128)(2,1)S(1)}, bf16[1024,128]{1,0:T(8,128)(2,1)S(1)}, bf16[1024,128]{1,0:T(8,128)(2,1)S(1)}) custom-call(s32[1]{0:T(128)} %bitcast.sec, s32[1]{0:T(128)} %bitcast.1.tok, bf16[1,2,2048,512]{3,2,1,0:T(8,128)(2,1)} %local.5, bf16[1,2,2048,512]{3,2,1,0:T(8,128)(2,1)} %local.5, bf16[2048,512]{1,0:T(8,128)(2,1)} %inputs.5), custom_call_target="tpu_custom_call" | custom-call | flops 1048576 | bytes 6291456 | tf_op jit(solution)/shard_map/lend/pallas_call | solution.py:616
  2.1 0.1 collective-permute-start
  2.2 0.7 %collective-permute-start.1 = (bf16[1024,128]{1,0:T(8,128)(2,1)S(1)}, bf16[1024,128]{1,0:T(8,128)(2,1)S(1)}, u32[]{:S(2)}, u32[]{:S(2)}) collective-permute-start(bf16[1024,128]{1,0:T(8,128)(2,1)S(1)} %get-tuple-element.19), channel_id=1, source_target_pairs={{0,1},{1,2},{2,3},{3,0},{16,16},{17,17},{18,18},{19,19},{4,5},{5,6... | collective-permute-start | bytes 786440 | tf_op jit(solution)/shard_map/ppermute | solution.py:650
  2.9 4.3 %collective-permute-start.2 = (bf16[1024,128]{1,0:T(8,128)(2,1)S(1)}, bf16[1024,128]{1,0:T(8,128)(2,1)S(1)}, u32[]{:S(2)}, u32[]{:S(2)}) collective-permute-start(bf16[1024,128]{1,0:T(8,128)(2,1)S(1)} %get-tuple-element.20), channel_id=1, source_target_pairs={{0,17},{1,18},{2,19},{3,16},{16,0},{17,1},{18,2},{19,3},{4,21},{5,... | collective-permute-start | bytes 786440 | tf_op jit(solution)/shard_map/ppermute | solution.py:650
  7.2 0.0 copy-done
  7.2 0.0 copy-done.1
  7.2 5.5 %response.1 = (f32[1024,256]{1,0:T(8,128)S(1)}, f32[128,128]{1,0:T(8,128)S(1)}, f32[128,128]{1,0:T(8,128)S(1)}, bf16[64,128,256]{2,1,0:T(8,128)(2,1)S(1)}, bf16[64,128,256]{2,1,0:T(8,128)(2,1)S(1)}) custom-call(s32[1]{0:T(128)} %bitcast.sec, s32[1]{0:T(128)} %bitcast.1.tok, f32[16,2048]{1,0:T(8,128)S(1)} %bitcast.4, f32[16,2048]{1,0:T(8,128)S(1)} %bitcast.5, ...), custom_call_target="tpu_custom_call" | custom-call | flops 314572800 | bytes 6291456 | tf_op jit(solution)/shard_map/response/pallas_call | solution.py:213
  12.6 0.0 collective-permute-done.1.halo_low
  12.6 1.9 %collective-permute-done.2.halo_high = bf16[1024,128]{1,0:T(8,128)(2,1)S(1)} collective-permute-done((bf16[1024,128]{1,0:T(8,128)(2,1)S(1)}, bf16[1024,128]{1,0:T(8,128)(2,1)S(1)}, u32[]{:S(2)}, u32[]{:S(2)}) %collective-permute-start.2) | collective-permute-done | bytes 262176 | tf_op jit(solution)/shard_map/ppermute | solution.py:650
  14.5 0.0 collective-permute-done.remote
  14.5 5.2 %front.1 = (bf16[1024,512]{1,0:T(8,128)(2,1)S(1)}, f32[4,1024,128]{2,1,0:T(8,128)S(1)}, f32[128,128]{1,0:T(8,128)S(1)}) custom-call(s32[1]{0:T(128)} %bitcast.sec, s32[1]{0:T(128)} %bitcast.1.tok, bf16[1,2,2048,512]{3,2,1,0:T(8,128)(2,1)} %local.5, bf16[2,1024,512]{2,1,0:T(8,128)(2,1)S(1)} %collective-permute-done.remote, bf16[2048,512]{1,0:T(8,128)(2,1)} %inputs.5, ...), custom_call_target="tpu_custom_call" | custom-call | flops 1048576000 | bytes 6291456 | tf_op jit(solution)/shard_map/front/pallas_call | solution.py:359
  19.8 1.8 %collective-permute-start.5 = (f32[128,128]{1,0:T(8,128)S(1)}, f32[128,128]{1,0:T(8,128)S(1)}, u32[]{:S(2)}, u32[]{:S(2)}) collective-permute-start(f32[128,128]{1,0:T(8,128)S(1)} %get-tuple-element.28), channel_id=1, source_target_pairs={{0,3},{1,0},{2,1},{3,2},{4,7},{5,4},{6,5},{7,6},{8,11},{9,8},{10,9... | collective-permute-start | bytes 196616 | tf_op jit(solution)/shard_map/ppermute | solution.py:643
  21.6 0.2 collective-permute-start.4
  21.8 1.2 %collective-permute-start.3 = (f32[128,128]{1,0:T(8,128)S(1)}, f32[128,128]{1,0:T(8,128)S(1)}, u32[]{:S(2)}, u32[]{:S(2)}) collective-permute-start(f32[128,128]{1,0:T(8,128)S(1)} %get-tuple-element.28), channel_id=1, source_target_pairs={{0,1},{1,2},{2,3},{3,0},{4,5},{5,6},{6,7},{7,4},{8,9},{9,10},{10,1... | collective-permute-start | bytes 196616 | tf_op jit(solution)/shard_map/ppermute | solution.py:643
  23.0 2.8 %within.1 = f32[1024,512]{1,0:T(8,128)S(1)} custom-call(s32[1]{0:T(128)} %bitcast.sec, s32[1]{0:T(128)} %bitcast.1.tok, bf16[1,2,2048,512]{3,2,1,0:T(8,128)(2,1)} %local.5, bf16[2,1024,512]{2,1,0:T(8,128)(2,1)S(1)} %collective-permute-done.remote, bf16[2048,512]{1,0:T(8,128)(2,1)} %inputs.5, bf16[1024,512]{1,0:T(8,128)(2,1)S(1)} %get-tuple-element.23.gated_medium, ...), custom_call_target="tpu_custom_call" | custom-call | flops 786432000 | bytes 6291456 | tf_op jit(solution)/shard_map/within/pallas_call | solution.py:433
  25.8 0.0 collective-permute-done.5.rest_2_
  25.8 0.0 collective-permute-done.4.rest_1_
  25.8 0.0 collective-permute-done.3.rest_0_
  25.8 4.7 %output.1 = (bf16[1,2048,512]{2,1,0:T(8,128)(2,1)}, bf16[1024,512]{1,0:T(8,128)(2,1)S(1)}) custom-call(s32[1]{0:T(128)} %bitcast.sec, s32[1]{0:T(128)} %bitcast.1.tok, bf16[1,2,2048,512]{3,2,1,0:T(8,128)(2,1)} %local.5, bf16[2,1024,512]{2,1,0:T(8,128)(2,1)S(1)} %collective-permute-done.remote, f32[1024,512]{1,0:T(8,128)S(1)} %within.1, ...), custom_call_target="tpu_custom_call" | custom-call | flops 786432000 | bytes 6291456 | tf_op jit(solution)/shard_map/output/pallas_call | solution.py:532
  30.5 1.4 %collective-permute-start.6 = (bf16[1024,512]{1,0:T(8,128)(2,1)S(1)}, bf16[1024,512]{1,0:T(8,128)(2,1)S(1)}, u32[]{:S(2)}, u32[]{:S(2)}) collective-permute-start(bf16[1024,512]{1,0:T(8,128)(2,1)S(1)} %get-tuple-element.30), channel_id=1, source_target_pairs={{0,16},{16,0},{1,17},{17,1},{2,18},{18,2},{3,19},{19,3},{4,20},{20... | collective-permute-start | bytes 3145736 | tf_op jit(solution)/shard_map/ppermute | solution.py:643
  31.9 2.3 %collective-permute-done.6.received = bf16[1024,512]{1,0:T(8,128)(2,1)S(1)} collective-permute-done((bf16[1024,512]{1,0:T(8,128)(2,1)S(1)}, bf16[1024,512]{1,0:T(8,128)(2,1)S(1)}, u32[]{:S(2)}, u32[]{:S(2)}) %collective-permute-start.6) | collective-permute-done | bytes 1048608 | tf_op jit(solution)/shard_map/ppermute | solution.py:643
  34.2 1.0 %placing.1 = bf16[1,2048,512]{2,1,0:T(8,128)(2,1)} custom-call(s32[1]{0:T(128)} %bitcast.sec, s32[1]{0:T(128)} %bitcast.1.tok, bf16[1,2048,512]{2,1,0:T(8,128)(2,1)} %get-tuple-element.29.own, bf16[1024,512]{1,0:T(8,128)(2,1)S(1)} %collective-permute-done.6.received), custom_call_target="tpu_custom_call", output_to_operand_aliasing={{}: (2, {})} | custom-call | flops 1048576 | bytes 6291456 | tf_op jit(solution)/shard_map/placing/pallas_call | solution.py:575
Async XLA Ops:
  0.0 7.2 %copy-start = (f32[2048,16]{0,1:T(8,128)S(1)}, f32[2048,16]{0,1:T(8,128)}, u32[]{:S(2)}) copy-start(f32[2048,16]{0,1:T(8,128)} %param.22) | copy-start | bytes 393220
  0.0 7.2 %copy-start.1 = (f32[2048,16]{0,1:T(8,128)S(1)}, f32[2048,16]{0,1:T(8,128)}, u32[]{:S(2)}) copy-start(f32[2048,16]{0,1:T(8,128)} %param.21) | copy-start | bytes 393220
  2.1 12.4 %collective-permute-start = (bf16[2,1024,512]{2,1,0:T(8,128)(2,1)S(1)}, bf16[2,1024,512]{2,1,0:T(8,128)(2,1)S(1)}, u32[]{:S(2)}, u32[]{:S(2)}) collective-permute-start(bf16[2,1024,512]{2,1,0:T(8,128)(2,1)S(1)} %get-tuple-element.18), channel_id=1, source_target_pairs={{0,16},{16,0},{1,17},{17,1},{2,18},{18,2},{3,19},{19,3},{4,20},{20... | collective-permute-start | bytes 6291464 | tf_op jit(solution)/shard_map/ppermute | solution.py:643
  2.2 10.4 %collective-permute-start.1 = (bf16[1024,128]{1,0:T(8,128)(2,1)S(1)}, bf16[1024,128]{1,0:T(8,128)(2,1)S(1)}, u32[]{:S(2)}, u32[]{:S(2)}) collective-permute-start(bf16[1024,128]{1,0:T(8,128)(2,1)S(1)} %get-tuple-element.19), channel_id=1, source_target_pairs={{0,1},{1,2},{2,3},{3,0},{16,16},{17,17},{18,18},{19,19},{4,5},{5,6... | collective-permute-start | bytes 786440 | tf_op jit(solution)/shard_map/ppermute | solution.py:650
  2.9 11.6 %collective-permute-start.2 = (bf16[1024,128]{1,0:T(8,128)(2,1)S(1)}, bf16[1024,128]{1,0:T(8,128)(2,1)S(1)}, u32[]{:S(2)}, u32[]{:S(2)}) collective-permute-start(bf16[1024,128]{1,0:T(8,128)(2,1)S(1)} %get-tuple-element.20), channel_id=1, source_target_pairs={{0,17},{1,18},{2,19},{3,16},{16,0},{17,1},{18,2},{19,3},{4,21},{5,... | collective-permute-start | bytes 786440 | tf_op jit(solution)/shard_map/ppermute | solution.py:650
  19.8 6.0 %collective-permute-start.5 = (f32[128,128]{1,0:T(8,128)S(1)}, f32[128,128]{1,0:T(8,128)S(1)}, u32[]{:S(2)}, u32[]{:S(2)}) collective-permute-start(f32[128,128]{1,0:T(8,128)S(1)} %get-tuple-element.28), channel_id=1, source_target_pairs={{0,3},{1,0},{2,1},{3,2},{4,7},{5,4},{6,5},{7,6},{8,11},{9,8},{10,9... | collective-permute-start | bytes 196616 | tf_op jit(solution)/shard_map/ppermute | solution.py:643
  21.6 4.2 %collective-permute-start.4 = (f32[128,128]{1,0:T(8,128)S(1)}, f32[128,128]{1,0:T(8,128)S(1)}, u32[]{:S(2)}, u32[]{:S(2)}) collective-permute-start(f32[128,128]{1,0:T(8,128)S(1)} %get-tuple-element.28), channel_id=1, source_target_pairs={{0,2},{1,3},{2,0},{3,1},{4,6},{5,7},{6,4},{7,5},{8,10},{9,11},{10,... | collective-permute-start | bytes 196616 | tf_op jit(solution)/shard_map/ppermute | solution.py:643
  21.8 4.0 %collective-permute-start.3 = (f32[128,128]{1,0:T(8,128)S(1)}, f32[128,128]{1,0:T(8,128)S(1)}, u32[]{:S(2)}, u32[]{:S(2)}) collective-permute-start(f32[128,128]{1,0:T(8,128)S(1)} %get-tuple-element.28), channel_id=1, source_target_pairs={{0,1},{1,2},{2,3},{3,0},{4,5},{5,6},{6,7},{7,4},{8,9},{9,10},{10,1... | collective-permute-start | bytes 196616 | tf_op jit(solution)/shard_map/ppermute | solution.py:643
  30.5 3.7 %collective-permute-start.6 = (bf16[1024,512]{1,0:T(8,128)(2,1)S(1)}, bf16[1024,512]{1,0:T(8,128)(2,1)S(1)}, u32[]{:S(2)}, u32[]{:S(2)}) collective-permute-start(bf16[1024,512]{1,0:T(8,128)(2,1)S(1)} %get-tuple-element.30), channel_id=1, source_target_pairs={{0,16},{16,0},{1,17},{17,1},{2,18},{18,2},{3,19},{19,3},{4,20},{20... | collective-permute-start | bytes 3145736 | tf_op jit(solution)/shard_map/ppermute | solution.py:643

commit v5 on v4

--- a/solution.py
+++ b/solution.py
@@ -88,12 +88,16 @@
     )
 
 
-def whole(array):
-    return pl.BlockSpec(array.shape, lambda i, p, t: (0,) * array.ndim)
-
-
-def mine(share, step):
-    return lambda i, p, t: p[0] * (share // step) + i
+VMEM_SPEC = pl.BlockSpec(memory_space=pltpu.VMEM)
+SMEM_SPEC = pl.BlockSpec(memory_space=pltpu.SMEM)
+ANY_SPEC = pl.BlockSpec(memory_space=pl.ANY)
+
+
+def rows_at(ref, step, i, axis=0):
+    start = i * step
+    if not isinstance(i, int):
+        start = pl.multiple_of(start, step)
+    return ref.at[(slice(None),) * axis + (pl.ds(start, step),)]
 
 
 def by_section(sec, body):
@@ -154,127 +158,141 @@
     )
 
 
-def response_kernel(
-    sec,
-    tok,
-    rates,
-    residues,
-    table_h,
-    table_l,
-    out,
-    rate_rows,
-    scale_rows,
-    rising,
-    falling,
-    tall,
-    hops,
-    scales,
-):
+def response_kernel(count, sec, tok, rates, residues, table_h, table_l, *rest):
+    gates, inputs, taps = rest[:3]
+    tables = rest[3 : 3 + count]
+    out, rate_rows, scale_rows, rising, falling = rest[3 + count : 8 + count]
+    own_gates, own_inputs, own_taps = rest[8 + count : 11 + count]
+    own_tables = rest[11 + count : 11 + 2 * count]
+    tall, hops, scales, arrival = rest[11 + 2 * count :]
+    share = out.shape[0]
+    modes = rates.shape[0]
     window = table_h.shape[0]
-    modes = rates.shape[0]
+    step = tall.shape[0]
+    first = pl.multiple_of(sec[0] * share, share)
+    mine = pl.ds(first, share)
+    pairs = [(gates.at[0, :, mine, :], own_gates)]
+    pairs += [(inputs.at[mine, :], own_inputs), (taps.at[mine, :], own_taps)]
+    pairs += list(zip(tables, own_tables))
+    copies = [
+        pltpu.make_async_copy(source, target, arrival.at[k])
+        for k, (source, target) in enumerate(pairs)
+    ]
+    for copy in copies:
+        copy.start()
     mask = lane_mask(modes)
-    slow = in_rows(rates, tall)
-    rate_rows[...] = slow
-    scale = scale_of(in_rows(residues, tall), slow)
-    scale_rows[...] = scale
-    hops[...] = jnp.exp(-slow * ROWS)
-    scales[...] = scale / (1.0 + jnp.exp(-slow * window))
-    parts = []
-    for pair in range(rate_rows.shape[0] // 2):
-        both = two_sided(
-            jnp.where(mask, spread(scales, 2 * pair), 0.0),
-            jnp.where(mask, spread(scales, 2 * pair + 1), 0.0),
+
+    @pl.loop(0, share // step)
+    def _(i):
+        lanes = pl.ds(pl.multiple_of(first + i * step, step), step)
+        slow = in_rows(rates.at[:, lanes], tall)
+        scale = scale_of(in_rows(residues.at[:, lanes], tall), slow)
+        small = step // ROWS
+        own_rates = rows_at(rate_rows, small, i)
+        own_rates[...] = slow
+        rows_at(scale_rows, small, i)[...] = scale
+        hops[...] = jnp.exp(-slow * ROWS)
+        scales[...] = scale / (1.0 + jnp.exp(-slow * window))
+        up, down = rows_at(rising, step // PAIR, i), rows_at(falling, step // PAIR, i)
+        parts = []
+        for pair in range(step // PAIR):
+            both = two_sided(
+                jnp.where(mask, spread(scales, 2 * pair), 0.0),
+                jnp.where(mask, spread(scales, 2 * pair + 1), 0.0),
+            )
+            high = both.astype(jnp.bfloat16).astype(jnp.float32)
+            both = jnp.concatenate([high, both - high], axis=0).astype(jnp.bfloat16)
+            table = both_powers(own_rates, hops, pair, window, False)
+            up[pair] = table
+            down[pair] = both_powers(own_rates, hops, pair, window, True)
+            found = dot_turned(both, table)
+            parts.append(found[:PAIR] + found[PAIR:])
+        response = jnp.concatenate(parts, axis=0)
+        high = response.astype(jnp.bfloat16)
+        low = (response - high.astype(jnp.float32)).astype(jnp.bfloat16)
+        rows_at(out, step, i)[...] = dot_f32(high, table_h[...]) + (
+            dot_f32(low, table_h[...]) + dot_f32(high, table_l[...])
         )
-        high = both.astype(jnp.bfloat16).astype(jnp.float32)
-        both = jnp.concatenate([high, both - high], axis=0).astype(jnp.bfloat16)
-        table = both_powers(rate_rows, hops, pair, window, False)
-        rising[pair] = table
-        falling[pair] = both_powers(rate_rows, hops, pair, window, True)
-        found = dot_turned(both, table)
-        parts.append(found[:PAIR] + found[PAIR:])
-    taps = jnp.concatenate(parts, axis=0)
-    high = taps.astype(jnp.bfloat16)
-    low = (taps - high.astype(jnp.float32)).astype(jnp.bfloat16)
-    out[...] = dot_f32(high, table_h[...]) + (
-        dot_f32(low, table_h[...]) + dot_f32(high, table_l[...])
-    )
-
-
-def response_call(place, rates, residues, window, share):
+
+    for copy in copies:
+        copy.wait()
+
+
+def response_call(place, rates, residues, gates, inputs, taps, tables, window, share):
+    tokens = inputs.shape[1]
     step = min(256, share)
     modes = rates.shape[0]
     lanes = ROWS * modes
-    tables = split_pair(turned_tables(window)[2])
+    spectra = split_pair(turned_tables(window)[2])
     small = (step // ROWS, lanes)
-    large = (step // PAIR, window, 2 * lanes)
-    row = mine(share, step)
-    rows_shape = jax.ShapeDtypeStruct((share // ROWS, lanes), jnp.float32)
-    table_shape = jax.ShapeDtypeStruct((share // PAIR, window, 2 * lanes), jnp.bfloat16)
-    return pl.pallas_call(
-        response_kernel,
-        out_shape=(
-            jax.ShapeDtypeStruct((share, 2 * window), jnp.float32),
-            rows_shape,
-            rows_shape,
-            table_shape,
-            table_shape,
-        ),
-        grid_spec=pltpu.PrefetchScalarGridSpec(
-            num_scalar_prefetch=2,
-            grid=(share // step,),
-            in_specs=[pl.BlockSpec((modes, step), lambda i, p, t: (0, row(i, p, t)))] * 2
-            + [whole(t) for t in tables],
-            out_specs=(
-                pl.BlockSpec((step, 2 * window), lambda i, p, t: (i, 0)),
-                pl.BlockSpec(small, lambda i, p, t: (i, 0)),
-                pl.BlockSpec(small, lambda i, p, t: (i, 0)),
-                pl.BlockSpec(large, lambda i, p, t: (i, 0, 0)),
-                pl.BlockSpec(large, lambda i, p, t: (i, 0, 0)),
-            ),
-            scratch_shapes=[
-                pltpu.VMEM((step, modes), jnp.float32),
-                pltpu.VMEM(small, jnp.float32),
-                pltpu.VMEM(small, jnp.float32),
-            ],
-        ),
+    shape = lambda dims, kind=jnp.float32: jax.ShapeDtypeStruct(dims, kind)
+    power_shape = shape((share // PAIR, window, 2 * lanes), jnp.bfloat16)
+    outs = [shape((share, 2 * window))] + [shape((share // ROWS, lanes))] * 2
+    outs += [power_shape] * 2
+    outs += [
+        shape((2, share, tokens), gates.dtype),
+        shape((share, tokens), inputs.dtype),
+        shape((share, window), taps.dtype),
+    ]
+    outs += [shape(t.shape, t.dtype) for t in tables]
+    staged = 3 + len(tables)
+    found = pl.pallas_call(
+        functools.partial(response_kernel, len(tables)),
+        out_shape=tuple(outs),
+        in_specs=[SMEM_SPEC] * 2 + [VMEM_SPEC] * 4 + [ANY_SPEC] * staged,
+        out_specs=(VMEM_SPEC,) * len(outs),
+        scratch_shapes=[
+            pltpu.VMEM((step, modes), jnp.float32),
+            pltpu.VMEM(small, jnp.float32),
+            pltpu.VMEM(small, jnp.float32),
+            pltpu.SemaphoreType.DMA((staged,)),
+        ],
         name="response",
         cost_estimate=cost(share, 4 * window, 600),
         compiler_params=COMPILER,
-    )(*place, rates, residues, *parked(*tables))
+    )(*place, rates, residues, *spectra, *parked(gates, inputs, taps, *tables))
+    return found[:5], found[5:8], found[8:]
 
 
 def front_kernel(
     modes,
+    step,
     sec,
     tok,
-    local,
-    remote,
-    inputs,
+    local_all,
+    remote_all,
+    inputs_all,
     halo_low,
     halo_high,
-    taps,
+    taps_all,
     rates,
-    falling,
+    falling_all,
     fwd_even,
     fwd_odd,
     inv_even,
     inv_odd,
-    medium_out,
-    ends,
-    total,
-    leaps,
+    medium_all,
+    ends_all,
+    total_all,
+    leaps_all,
 ):
-    channels, tokens = inputs.shape
-    window = taps.shape[1]
+    share, tokens = inputs_all.shape
+    window = taps_all.shape[1]
     blocks = tokens // window
     forward = (fwd_even, fwd_odd)
     inverse = (inv_even, inv_odd)
-    leaps[...] = jnp.exp(-rates[...] * window)
-
-    def body(section):
-        first = local.at[0] if section == 0 else remote
-        second = remote if section == 0 else local.at[0]
-        halo = halo_low if section == 0 else halo_high
+    leaps_all[...] = jnp.exp(-rates[...] * window)
+
+    def chunk(section, i):
+        first, second = (local_all, remote_all) if section == 0 else (remote_all, local_all)
+        first, second = rows_at(first, step, i, 1), rows_at(second, step, i, 1)
+        halo = rows_at(halo_low if section == 0 else halo_high, step, i)
+        inputs, taps = rows_at(inputs_all, step, i), rows_at(taps_all, step, i)
+        medium_out, ends = rows_at(medium_all, step, i), rows_at(ends_all, step, i, 1)
+        leaps = rows_at(leaps_all, step // ROWS, i)
+        falling = rows_at(falling_all, step // PAIR, i)
+        total = rows_at(total_all, step // ROWS, i)
+        channels = step
         tap_rows = taps[...]
         started = jnp.where(tok[0] > 0, 1.0, 0.0).astype(jnp.bfloat16)
         parts = [slice(b * window, (b + 1) * window) for b in range(blocks)]
@@ -341,62 +359,57 @@
                 sums.append(jnp.sum(state, axis=0, keepdims=True))
         total[...] = jnp.concatenate(sums, axis=0)
 
+    def body(section):
+        pl.loop(0, share // step)(functools.partial(chunk, section))
+
     by_section(sec, body)
 
 
-def front_call(
-    place, gate_streams, swapped, inputs, halos, taps, rates, falling, modes, share
-):
-    tokens = inputs.shape[1]
+def front_call(place, gates, swapped, inputs, halos, taps, rates, falling, tables, modes):
+    share, tokens = inputs.shape
     window = taps.shape[1]
-    step = min(256, share)
-    forward, inverse = fourier_tables(window)
-    tables = forward + inverse
-    row = mine(share, step)
     lanes = ROWS * modes
-    small = (step // ROWS, lanes)
-    blocks = tokens // window
+    small = (share // ROWS, lanes)
+    operands = [gates, swapped, inputs, *halos, taps, rates, falling, *tables]
     return pl.pallas_call(
-        functools.partial(front_kernel, modes),
+        functools.partial(front_kernel, modes, min(256, share)),
         out_shape=(
             jax.ShapeDtypeStruct((share, tokens), jnp.bfloat16),
-            jax.ShapeDtypeStruct((blocks, share, lanes), jnp.float32),
-            jax.ShapeDtypeStruct((share // ROWS, lanes), jnp.float32),
+            jax.ShapeDtypeStruct((tokens // window, share, lanes), jnp.float32),
+            jax.ShapeDtypeStruct(small, jnp.float32),
         ),
-        grid_spec=pltpu.PrefetchScalarGridSpec(
-            num_scalar_prefetch=2,
-            grid=(share // step,),
-            in_specs=[
-                pl.BlockSpec((1, 2, step, tokens), lambda i, p, t: (0, 0, row(i, p, t), 0)),
-                pl.BlockSpec((2, step, tokens), lambda i, p, t: (0, i, 0)),
-                pl.BlockSpec((step, tokens), lambda i, p, t: (row(i, p, t), 0)),
-                pl.BlockSpec((step, window), lambda i, p, t: (i, 0)),
-                pl.BlockSpec((step, window), lambda i, p, t: (i, 0)),
-                pl.BlockSpec((step, window), lambda i, p, t: (row(i, p, t), 0)),
-                pl.BlockSpec(small, lambda i, p, t: (i, 0)),
-                pl.BlockSpec((step // PAIR, window, 2 * lanes), lambda i, p, t: (i, 0, 0)),
-            ]
-            + [whole(t) for t in tables],
-            out_specs=(
-                pl.BlockSpec((step, tokens), lambda i, p, t: (i, 0)),
-                pl.BlockSpec((blocks, step, lanes), lambda i, p, t: (0, i, 0)),
-                pl.BlockSpec(small, lambda i, p, t: (i, 0)),
-            ),
-            scratch_shapes=[pltpu.VMEM(small, jnp.float32)],
-        ),
+        in_specs=[SMEM_SPEC] * 2 + [VMEM_SPEC] * len(operands),
+        out_specs=(VMEM_SPEC,) * 3,
+        scratch_shapes=[pltpu.VMEM(small, jnp.float32)],
         name="front",
         cost_estimate=cost(share, tokens, 2000),
         compiler_params=COMPILER,
-    )(*place, gate_streams, swapped, inputs, *halos, taps, rates, falling, *parked(*tables))
-
-
-def within_kernel(sec, tok, local, remote, inputs, gated_medium, response, fwd_h, fwd_l, inverse, out):
+    )(*place, *operands)
+
+
+def within_kernel(
+    step,
+    sec,
+    tok,
+    local_all,
+    remote_all,
+    inputs_all,
+    medium_all,
+    response_all,
+    fwd_h,
+    fwd_l,
+    inverse,
+    out_all,
+):
+    share, tokens = inputs_all.shape
     size = fwd_h.shape[0]
     half = size // 2
 
-    def body(section):
-        gate_in = remote.at[0] if section == 0 else local.at[0, 0]
-        channels, tokens = inputs.shape
+    def chunk(section, i):
+        gate_in = rows_at((remote_all if section == 0 else local_all).at[1], step, i)
+        inputs, gated_medium = rows_at(inputs_all, step, i), rows_at(medium_all, step, i)
+        response, out = rows_at(response_all, step, i), rows_at(out_all, step, i)
+        channels = step
         real, imag = response[:, :half], response[:, half:]
         parts = [slice(k * size, (k + 1) * size) for k in range(tokens // size)]
         signals = []
@@ -420,75 +433,71 @@
         for k, part in enumerate(parts):
             out[:, part] = found[k * channels : (k + 1) * channels]
 
+    def body(section):
+        pl.loop(0, share // step)(functools.partial(chunk, section))
+
     by_section(sec, body)
 
 
-def within_call(place, gate_streams, swapped, inputs, gated_medium, response, share):
-    tokens = inputs.shape[1]
-    window = response.shape[1] // 2
-    step = min(WITHIN_STEP, share)
-    forward, inverse, _ = turned_tables(window)
-    tables = split_pair(forward) + split_pair(inverse)[:1]
-    row = mine(share, step)
+def within_call(place, gates, swapped, inputs, medium, response, tables):
+    share, tokens = inputs.shape
+    operands = [gates, swapped, inputs, medium, response, *tables]
     return pl.pallas_call(
-        within_kernel,
+        functools.partial(within_kernel, min(WITHIN_STEP, share)),
         out_shape=jax.ShapeDtypeStruct((share, tokens), jnp.float32),
-        grid_spec=pltpu.PrefetchScalarGridSpec(
-            num_scalar_prefetch=2,
-            grid=(share // step,),
-            in_specs=[
-                pl.BlockSpec((1, 1, step, tokens), lambda i, p, t: (0, 1, row(i, p, t), 0)),
-                pl.BlockSpec((1, step, tokens), lambda i, p, t: (1, i, 0)),
-                pl.BlockSpec((step, tokens), lambda i, p, t: (row(i, p, t), 0)),
-                pl.BlockSpec((step, tokens), lambda i, p, t: (i, 0)),
-                pl.BlockSpec((step, 2 * window), lambda i, p, t: (i, 0)),
-            ]
-            + [whole(t) for t in tables],
-            out_specs=pl.BlockSpec((step, tokens), lambda i, p, t: (i, 0)),
-        ),
+        in_specs=[SMEM_SPEC] * 2 + [VMEM_SPEC] * len(operands),
+        out_specs=VMEM_SPEC,
         name="within",
         cost_estimate=cost(share, tokens, 1500),
         compiler_params=COMPILER,
-    )(*place, gate_streams, swapped, inputs, gated_medium, response, *parked(*tables))
+    )(*place, *operands)
 
 
 def output_kernel(
     count,
     modes,
     window,
+    step,
     sec,
     tok,
-    local,
-    remote,
-    within,
-    inputs,
-    gated_medium,
+    local_all,
+    remote_all,
+    within_all,
+    inputs_all,
+    medium_all,
     rates,
     scale_rows,
-    rising,
-    ends,
+    rising_all,
+    ends_all,
     *rest,
 ):
-    arrived, (keep, send, leaps, scales, shares, starts) = rest[:count], rest[count:]
-    channels, tokens = inputs.shape
+    arrived = rest[:count]
+    result, send, leaps_all, scales_all, shares_all, starts_all, mixed, done = rest[count:]
+    share, tokens = inputs_all.shape
     blocks = tokens // window
     mask = lane_mask(modes)
     slow = rates[...]
     leap_all = jnp.exp(-slow * window)
     scale_all = scale_rows[...] * jnp.exp(-slow)
-    leaps[...] = leap_all
-    scales[...] = scale_all
-    shares[...] = scale_all / (1.0 + leap_all)
+    leaps_all[...] = leap_all
+    scales_all[...] = scale_all
+    shares_all[...] = scale_all / (1.0 + leap_all)
     entering = jnp.zeros_like(slow)
     for k in range(count):
         known = jnp.where(tok[0] > k, 1.0, 0.0)
         entering = entering + arrived[k][...] * (jnp.exp(-slow * (tokens * k)) * known)
-    starts[...] = entering
-
-    def body(section):
-        gate_out = remote.at[0] if section == 0 else local.at[0, 0]
-        out = send if section == 0 else keep.at[0]
-        (keep.at[0] if section == 0 else send)[...] = gated_medium[...]
+    starts_all[...] = entering
+
+    def chunk(section, out_all, i):
+        gate_out = rows_at((remote_all if section == 0 else local_all).at[0], step, i)
+        inputs, gated_medium = rows_at(inputs_all, step, i), rows_at(medium_all, step, i)
+        within, out = rows_at(within_all, step, i), rows_at(out_all, step, i)
+        ends = rows_at(ends_all, step, i, 1)
+        rising = rows_at(rising_all, step // PAIR, i)
+        small = step // ROWS
+        leaps, scales = rows_at(leaps_all, small, i), rows_at(scales_all, small, i)
+        shares, starts = rows_at(shares_all, small, i), rows_at(starts_all, small, i)
+        channels = step
         for pair in range(channels // PAIR):
             rows = slice(pair * PAIR, (pair + 1) * PAIR)
             sides = []
@@ -517,75 +526,60 @@
                 gate = gate_out[rows, part].astype(jnp.float32)
                 out[rows, part] = (stream + gate * long_out).astype(jnp.bfloat16)
 
+    def body(section):
+        target = result.at[0, pl.ds(section * share, share), :]
+        early = pltpu.make_async_copy(medium_all, target if section == 0 else send, done.at[0])
+        early.start()
+        pl.loop(0, share // step)(functools.partial(chunk, section, mixed if section else send))
+        if section == 1:
+            late = pltpu.make_async_copy(mixed, target, done.at[1])
+            late.start()
+            late.wait()
+        early.wait()
+
     by_section(sec, body)
 
 
 def output_call(
-    place, gate_streams, swapped, within, inputs, medium, rates, scales, rising, ends, arrived, window
+    place, gates, swapped, within, inputs, medium, rates, scales, rising, ends, arrived, window
 ):
     share, tokens = medium.shape
     lanes = rates.shape[1]
     step = min(256, share)
-    row = mine(share, step)
-    wide = (step, tokens)
-    small = (step // ROWS, lanes)
+    small = (share // ROWS, lanes)
+    operands = [gates, swapped, within, inputs, medium, rates, scales, rising, ends, *arrived]
     return pl.pallas_call(
-        functools.partial(output_kernel, len(arrived), lanes // ROWS, window),
+        functools.partial(output_kernel, len(arrived), lanes // ROWS, window, step),
         out_shape=(
-            jax.ShapeDtypeStruct((1,) + inputs.shape, jnp.bfloat16),
+            jax.ShapeDtypeStruct((1, 2 * share, tokens), jnp.bfloat16),
             jax.ShapeDtypeStruct((share, tokens), jnp.bfloat16),
         ),
-        grid_spec=pltpu.PrefetchScalarGridSpec(
-            num_scalar_prefetch=2,
-            grid=(share // step,),
-            in_specs=[
-                pl.BlockSpec((1, 1) + wide, lambda i, p, t: (0, 0, row(i, p, t), 0)),
-                pl.BlockSpec((1,) + wide, lambda i, p, t: (0, i, 0)),
-                pl.BlockSpec(wide, lambda i, p, t: (i, 0)),
-                pl.BlockSpec(wide, lambda i, p, t: (row(i, p, t), 0)),
-                pl.BlockSpec(wide, lambda i, p, t: (i, 0)),
-                pl.BlockSpec(small, lambda i, p, t: (i, 0)),
-                pl.BlockSpec(small, lambda i, p, t: (i, 0)),
-                pl.BlockSpec((step // PAIR, window, 2 * lanes), lambda i, p, t: (i, 0, 0)),
-                pl.BlockSpec((tokens // window, step, lanes), lambda i, p, t: (0, i, 0)),
-            ]
-            + [pl.BlockSpec(small, lambda i, p, t: (i, 0))] * len(arrived),
-            out_specs=(
-                pl.BlockSpec((1,) + wide, lambda i, p, t: (0, row(i, p, t), 0)),
-                pl.BlockSpec(wide, lambda i, p, t: (i, 0)),
-            ),
-            scratch_shapes=[pltpu.VMEM(small, jnp.float32)] * 4,
-        ),
+        in_specs=[SMEM_SPEC] * 2 + [VMEM_SPEC] * len(operands),
+        out_specs=(ANY_SPEC, VMEM_SPEC),
+        scratch_shapes=[pltpu.VMEM(small, jnp.float32)] * 4
+        + [pltpu.VMEM((share, tokens), jnp.bfloat16), pltpu.SemaphoreType.DMA((2,))],
         name="output",
         cost_estimate=cost(share, tokens, 1500),
         compiler_params=COMPILER,
-    )(
-        *place, gate_streams, swapped, within, inputs, medium, rates, scales, rising, ends, *arrived
-    )
-
-
-def place_kernel(sec, tok, own, received, out):
-    out[0] = received[...]
+    )(*place, *operands)
+
+
+def place_kernel(sec, tok, own, received, out, done):
+    share = received.shape[0]
+    other = pl.ds(pl.multiple_of((1 - sec[0]) * share, share), share)
+    copy = pltpu.make_async_copy(received, out.at[0, other, :], done)
+    copy.start()
+    copy.wait()
 
 
 def place_call(place, own, received):
     share, tokens = received.shape
-    step = min(512, share)
-    count = share // step
     return pl.pallas_call(
         place_kernel,
         out_shape=jax.ShapeDtypeStruct(own.shape, own.dtype),
-        grid_spec=pltpu.PrefetchScalarGridSpec(
-            num_scalar_prefetch=2,
-            grid=(count,),
-            in_specs=[
-                pl.BlockSpec(memory_space=pl.ANY),
-                pl.BlockSpec((step, tokens), lambda i, p, t: (i, 0)),
-            ],
-            out_specs=pl.BlockSpec(
-                (1, step, tokens), lambda i, p, t: (0, (1 - p[0]) * count + i, 0)
-            ),
-        ),
+        in_specs=[SMEM_SPEC] * 2 + [ANY_SPEC, VMEM_SPEC],
+        out_specs=ANY_SPEC,
+        scratch_shapes=[pltpu.SemaphoreType.DMA],
         input_output_aliases={2: 0},
         name="placing",
         cost_estimate=cost(share, tokens, 2),
@@ -635,7 +629,7 @@
         name="lend",
         cost_estimate=cost(share, tokens, 2),
         compiler_params=COMPILER,
-    )(*place, gate_streams, gate_streams, inputs)
+    )(*place, *parked(gate_streams, gate_streams, inputs))
 
 
 def ring(value, axis, by):
@@ -653,7 +647,6 @@
 def on_device(gate_streams, inputs, medium_taps, residues, decay_rates):
     channels, tokens = inputs.shape
     share = channels // 2
-    gate_streams, inputs, medium_taps = parked(gate_streams, inputs, medium_taps)
     window = medium_taps.shape[1]
     modes = decay_rates.shape[1]
     section = lax.axis_index("section")
@@ -663,16 +656,29 @@
     lent, *edges = lend_call(place, gate_streams, inputs, window, share)
     halos = [edge_to(edges[s], s) for s in range(2)]
     swapped = ring(lent, "section", 1)
-    response, rates, scales, rising, falling = response_call(
-        place, decay_rates.T, residues.T, window, share
-    )
+    forward, inverse = fourier_tables(window)
+    turned, back, _ = turned_tables(window)
+    tables = [*forward, *inverse, *split_pair(turned), split_pair(back)[0]]
+    built, own, tables = response_call(
+        place,
+        decay_rates.T,
+        residues.T,
+        gate_streams,
+        inputs,
+        medium_taps,
+        tables,
+        window,
+        share,
+    )
+    response, rates, scales, rising, falling = built
+    gates, inputs, taps = own
     medium, ends, total = front_call(
-        place, gate_streams, swapped, inputs, halos, medium_taps, rates, falling, modes, share
+        place, gates, swapped, inputs, halos, taps, rates, falling, tables[:4], modes
     )
     arrived = [ring(total, "tok", by) for by in range(1, lax.axis_size("tok"))]
-    within = within_call(place, gate_streams, swapped, inputs, medium, response, share)
+    within = within_call(place, gates, swapped, inputs, medium, response, tables[4:])
     keep, send = output_call(
-        place, gate_streams, swapped, within, inputs, medium, rates, scales, rising, ends, arrived, window
+        place, gates, swapped, within, inputs, medium, rates, scales, rising, ends, arrived, window
     )
     return place_call(place, keep, ring(send, "section", 1))
 

time: 35.9 us -> 31.2 us (0.87)
  Pallas kernels: 21.3 us -> 15.5 us
  waiting for transfers between devices: 4.19 us -> 6.41 us
  starting transfers between devices: 9.62 us -> 8.68 us
    pallas_call x3, Pallas kernels: 13.5 us -> 9.29 us  [the longest x1 4.63 us: response_call(): pl.pallas_call(functools.partial(response_kernel, len(tables)), out_shape...]
    pallas_call x1, Pallas kernels: 4.7 us -> 3.08 us  [output_call(): pl.pallas_call(functools.partial(output_kernel, len(arrived), lanes // RO...]
    ppermute x5, waiting for transfers between devices: 2.3 us -> 3.71 us  [ring(): lax.ppermute(value, axis, [(i, (i + by) % peers) for i in range(peers)])]
    ppermute x5, starting transfers between devices: 4.67 us -> 3.74 us  [ring(): lax.ppermute(value, axis, [(i, (i + by) % peers) for i in range(peers)])]
    ppermute x2, waiting for transfers between devices: 1.89 us -> 2.7 us  [edge_to(): return lax.ppermute(value, ('section', 'tok'), pairs)]
  transfers between devices with their start and end apart: 7 -> 7, of which waited for: 2 -> 4; matrix products, arithmetic and copies ran while one was open for 0% -> 0% of each run, Pallas kernels for 23% -> 20%
where the time goes in v5:
time: 31.2 us; the launch traced here: 30.7 us
  Pallas kernels  15.5 us (50%)
  starting transfers between devices  8.68 us (28%)
  waiting for transfers between devices  6.41 us (21%)
    ppermute x2, starting transfers between devices, edge_to(): return lax.ppermute(value, ('section', 'tok'), pairs)  4.94 us
    pallas_call x1, Pallas kernels, response_call(): pl.pallas_call(functools.partial(response_kernel, len(tables)), out_shape...  4.63 us
    ppermute x5, starting transfers between devices, ring(): lax.ppermute(value, axis, [(i, (i + by) % peers) for i in range(peers)])  3.74 us
    ppermute x5, waiting for transfers between devices, ring(): lax.ppermute(value, axis, [(i, (i + by) % peers) for i in range(peers)])  3.71 us
    pallas_call x1, Pallas kernels, front_call(): pl.pallas_call(functools.partial(front_kernel, modes, min(256, share)), o...  3.29 us
    pallas_call x1, Pallas kernels, output_call(): pl.pallas_call(functools.partial(output_kernel, len(arrived), lanes // RO...  3.08 us
    ppermute x2, waiting for transfers between devices, edge_to(): return lax.ppermute(value, ('section', 'tok'), pairs)  2.7 us
    pallas_call x1, Pallas kernels, lend_call(): pl.pallas_call(lend_kernel, out_shape=(jax.ShapeDtypeStruct((2, share, to...  2.17 us
  transfers between devices with their start and end apart: 7, of which 4 were waited for; matrix products, arithmetic and copies ran while one was open for 0% of the time, Pallas kernels for 20%

profile of v5, /device:TPU:1, one launch (start us, length us, event | category | flops | bytes accessed | tf_op | source)
XLA Modules:
  0.0 30.7 jit_solution(150745184787012355)
XLA Ops:
  0.0 0.0 copy-start
  0.0 0.0 copy-start.1
  0.0 0.0 copy-start.2
  0.0 0.0 copy-start.3
  0.0 2.2 %lend.1 = (bf16[2,1024,512]{2,1,0:T(8,128)(2,1)S(1)}, bf16[1024,128]{1,0:T(8,128)(2,1)S(1)}, bf16[1024,128]{1,0:T(8,128)(2,1)S(1)}) custom-call(s32[1]{0:T(128)} %bitcast.sec, s32[1]{0:T(128)} %bitcast.1.tok, bf16[1,2,2048,512]{3,2,1,0:T(8,128)(2,1)} %gate_tail.1, bf16[1,2,2048,512]{3,2,1,0:T(8,128)(2,1)} %gate_tail.1, bf16[2048,512]{1,0:T(8,128)(2,1)} %input_tail.1), custom_call_target="tpu_custom_call" | custom-call | flops 1048576 | bytes 6291456 | tf_op jit(solution)/shard_map/lend/pallas_call | solution.py:610
  2.2 0.1 collective-permute-start
  2.3 0.7 %collective-permute-start.1 = (bf16[1024,128]{1,0:T(8,128)(2,1)S(1)}, bf16[1024,128]{1,0:T(8,128)(2,1)S(1)}, u32[]{:S(2)}, u32[]{:S(2)}) collective-permute-start(bf16[1024,128]{1,0:T(8,128)(2,1)S(1)} %get-tuple-element.31), channel_id=1, source_target_pairs={{0,1},{1,2},{2,3},{3,0},{16,16},{17,17},{18,18},{19,19},{4,5},{5,6... | collective-permute-start | bytes 786440 | tf_op jit(solution)/shard_map/ppermute | solution.py:644
  3.0 4.3 %collective-permute-start.2 = (bf16[1024,128]{1,0:T(8,128)(2,1)S(1)}, bf16[1024,128]{1,0:T(8,128)(2,1)S(1)}, u32[]{:S(2)}, u32[]{:S(2)}) collective-permute-start(bf16[1024,128]{1,0:T(8,128)(2,1)S(1)} %get-tuple-element.32), channel_id=1, source_target_pairs={{0,17},{1,18},{2,19},{3,16},{16,0},{17,1},{18,2},{19,3},{4,21},{5,... | collective-permute-start | bytes 786440 | tf_op jit(solution)/shard_map/ppermute | solution.py:644
  7.2 0.0 copy-done
  7.2 0.0 copy-done.1
  7.2 0.0 copy-done.2
  7.2 0.0 copy-done.3
  7.2 4.6 %response.1 = (f32[1024,256]{1,0:T(8,128)S(1)}, f32[128,128]{1,0:T(8,128)S(1)}, f32[128,128]{1,0:T(8,128)S(1)}, bf16[64,128,256]{2,1,0:T(8,128)(2,1)S(1)}, bf16[...) custom-call(s32[1]{0:T(128)} %bitcast.sec, ...), custom_call_target="tpu_custom_call" | custom-call | flops 314572800 | bytes 6291456 | tf_op jit(solution)/shard_map/response/pallas_call | solution.py:239
  11.9 0.0 collective-permute-done.1.halo_low
  11.9 2.7 %collective-permute-done.2.halo_high = bf16[1024,128]{1,0:T(8,128)(2,1)S(1)} collective-permute-done((bf16[1024,128]{1,0:T(8,128)(2,1)S(1)}, bf16[1024,128]{1,0:T(8,128)(2,1)S(1)}, u32[]{:S(2)}, u32[]{:S(2)}) %collective-permute-start.2) | collective-permute-done | bytes 262176 | tf_op jit(solution)/shard_map/ppermute | solution.py:644
  14.6 0.0 collective-permute-done.remote_all
  14.6 3.3 %front.1 = (bf16[1024,512]{1,0:T(8,128)(2,1)S(1)}, f32[4,1024,128]{2,1,0:T(8,128)S(1)}, f32[128,128]{1,0:T(8,128)S(1)}) custom-call(s32[1]{0:T(128)} %bitcast.sec, s32[1]{0:T(128)} %bitcast.1.tok, bf16[2,1024,512]{2,1,0:T(8,128)(2,1)S(1)} %get-tuple-element.28.local_all, bf16[2,1024,512]{2,1,0:T(8,128)(2,1)S(1)} %collective-permute-done.remote_all, ...), custom_call_target="tpu_custom_call" | custom-call | flops 1048576000 | bytes 6291456 | tf_op jit(solution)/shard_map/front/pallas_call | solution.py:374
  17.9 1.8 %collective-permute-start.5 = (f32[128,128]{1,0:T(8,128)S(1)}, f32[128,128]{1,0:T(8,128)S(1)}, u32[]{:S(2)}, u32[]{:S(2)}) collective-permute-start(f32[128,128]{1,0:T(8,128)S(1)} %get-tuple-element.48), channel_id=1, source_target_pairs={{0,3},{1,0},{2,1},{3,2},{4,7},{5,4},{6,5},{7,6},{8,11},{9,8},{10,9... | collective-permute-start | bytes 196616 | tf_op jit(solution)/shard_map/ppermute | solution.py:637
  19.7 0.2 collective-permute-start.4
  19.9 1.2 %collective-permute-start.3 = (f32[128,128]{1,0:T(8,128)S(1)}, f32[128,128]{1,0:T(8,128)S(1)}, u32[]{:S(2)}, u32[]{:S(2)}) collective-permute-start(f32[128,128]{1,0:T(8,128)S(1)} %get-tuple-element.48), channel_id=1, source_target_pairs={{0,1},{1,2},{2,3},{3,0},{4,5},{5,6},{6,7},{7,4},{8,9},{9,10},{10,1... | collective-permute-start | bytes 196616 | tf_op jit(solution)/shard_map/ppermute | solution.py:637
  21.1 1.4 %within.1.within_all = f32[1024,512]{1,0:T(8,128)S(1)} custom-call(s32[1]{0:T(128)} %bitcast.sec, s32[1]{0:T(128)} %bitcast.1.tok, bf16[2,1024,512]{2,1,0:T(8,128)(2,1)S(1)} %get-tuple-element.28.local_all, bf16[2,1024,512]{2,1,0:T(8,128)(2,1)S(1)} %collective-permute-done.remote_all, bf16[1024,512]{1,0:T(8,128)(2,1)S(1)} %get-tuple-element.30.inputs_all, ...), custom_call_target="tpu_custom_call" | custom-call | flops 786432000 | bytes 6291456 | tf_op jit(solution)/shard_map/within/pallas_call | solution.py:445
  22.5 0.0 collective-permute-done.5.rest_2_
  22.5 0.3 collective-permute-done.4.rest_1_
  22.8 1.1 %collective-permute-done.3.rest_0_ = f32[128,128]{1,0:T(8,128)S(1)} collective-permute-done((f32[128,128]{1,0:T(8,128)S(1)}, f32[128,128]{1,0:T(8,128)S(1)}, u32[]{:S(2)}, u32[]{:S(2)}) %collective-permute-start.3) | collective-permute-done | bytes 65568 | tf_op jit(solution)/shard_map/ppermute | solution.py:637
  23.9 3.1 %output.1 = (bf16[1,2048,512]{2,1,0:T(8,128)(2,1)}, bf16[1024,512]{1,0:T(8,128)(2,1)S(1)}) custom-call(s32[1]{0:T(128)} %bitcast.sec, s32[1]{0:T(128)} %bitcast.1.tok, bf16[2,1024,512]{2,1,0:T(8,128)(2,1)S(1)} %get-tuple-element.28.local_all, bf16[2,1024,512]{2,1,0:T(8,128)(2,1)S(1)} %collective-permute-done.remote_all, f32[1024,512]{1,0:T(8,128)S(1)} %within.1.within_all, ...), custom_call_target="tpu_custom_call" | custom-call | flops 786432000 | bytes 6291456 | tf_op jit(solution)/shard_map/output/pallas_call | solution.py:551
  27.0 0.4 %collective-permute-start.6 = (bf16[1024,512]{1,0:T(8,128)(2,1)S(1)}, bf16[1024,512]{1,0:T(8,128)(2,1)S(1)}, u32[]{:S(2)}, u32[]{:S(2)}) collective-permute-start(bf16[1024,512]{1,0:T(8,128)(2,1)S(1)} %get-tuple-element.50), channel_id=1, source_target_pairs={{0,16},{16,0},{1,17},{17,1},{2,18},{18,2},{3,19},{19,3},{4,20},{20... | collective-permute-start | bytes 3145736 | tf_op jit(solution)/shard_map/ppermute | solution.py:637
  27.4 2.3 %collective-permute-done.6.received = bf16[1024,512]{1,0:T(8,128)(2,1)S(1)} collective-permute-done((bf16[1024,512]{1,0:T(8,128)(2,1)S(1)}, bf16[1024,512]{1,0:T(8,128)(2,1)S(1)}, u32[]{:S(2)}, u32[]{:S(2)}) %collective-permute-start.6) | collective-permute-done | bytes 1048608 | tf_op jit(solution)/shard_map/ppermute | solution.py:637
  29.7 1.0 %placing.1 = bf16[1,2048,512]{2,1,0:T(8,128)(2,1)} custom-call(s32[1]{0:T(128)} %bitcast.sec, s32[1]{0:T(128)} %bitcast.1.tok, bf16[1,2048,512]{2,1,0:T(8,128)(2,1)} %get-tuple-element.49.own, bf16[1024,512]{1,0:T(8,128)(2,1)S(1)} %collective-permute-done.6.received), custom_call_target="tpu_custom_call", output_to_operand_aliasing={{}: (2, {})} | custom-call | flops 1048576 | bytes 6291456 | tf_op jit(solution)/shard_map/placing/pallas_call | solution.py:577
Async XLA Ops:
  0.0 7.2 %copy-start = (f32[2048,16]{0,1:T(8,128)S(1)}, f32[2048,16]{0,1:T(8,128)}, u32[]{:S(2)}) copy-start(f32[2048,16]{0,1:T(8,128)} %param.22) | copy-start | bytes 393220
  0.0 7.2 %copy-start.1 = (f32[2048,16]{0,1:T(8,128)S(1)}, f32[2048,16]{0,1:T(8,128)}, u32[]{:S(2)}) copy-start(f32[2048,16]{0,1:T(8,128)} %param.21) | copy-start | bytes 393220
  0.0 7.2 %copy-start.2 = (bf16[128,256]{1,0:T(8,128)(2,1)S(1)}, bf16[128,256]{1,0:T(8,128)(2,1)}, u32[]{:S(2)}) copy-start(bf16[128,256]{1,0:T(8,128)(2,1)} %constant.35.table_l) | copy-start | bytes 196612
  0.0 7.2 %copy-start.3 = (bf16[128,256]{1,0:T(8,128)(2,1)S(1)}, bf16[128,256]{1,0:T(8,128)(2,1)}, u32[]{:S(2)}) copy-start(bf16[128,256]{1,0:T(8,128)(2,1)} %constant.32.table_h) | copy-start | bytes 196612
  2.2 12.4 %collective-permute-start = (bf16[2,1024,512]{2,1,0:T(8,128)(2,1)S(1)}, bf16[2,1024,512]{2,1,0:T(8,128)(2,1)S(1)}, u32[]{:S(2)}, u32[]{:S(2)}) collective-permute-start(bf16[2,1024,512]{2,1,0:T(8,128)(2,1)S(1)} %get-tuple-element.29), channel_id=1, source_target_pairs={{0,16},{16,0},{1,17},{17,1},{2,18},{18,2},{3,19},{19,3},{4,20},{20... | collective-permute-start | bytes 6291464 | tf_op jit(solution)/shard_map/ppermute | solution.py:637
  2.3 9.6 %collective-permute-start.1 = (bf16[1024,128]{1,0:T(8,128)(2,1)S(1)}, bf16[1024,128]{1,0:T(8,128)(2,1)S(1)}, u32[]{:S(2)}, u32[]{:S(2)}) collective-permute-start(bf16[1024,128]{1,0:T(8,128)(2,1)S(1)} %get-tuple-element.31), channel_id=1, source_target_pairs={{0,1},{1,2},{2,3},{3,0},{16,16},{17,17},{18,18},{19,19},{4,5},{5,6... | collective-permute-start | bytes 786440 | tf_op jit(solution)/shard_map/ppermute | solution.py:644
  3.0 11.6 %collective-permute-start.2 = (bf16[1024,128]{1,0:T(8,128)(2,1)S(1)}, bf16[1024,128]{1,0:T(8,128)(2,1)S(1)}, u32[]{:S(2)}, u32[]{:S(2)}) collective-permute-start(bf16[1024,128]{1,0:T(8,128)(2,1)S(1)} %get-tuple-element.32), channel_id=1, source_target_pairs={{0,17},{1,18},{2,19},{3,16},{16,0},{17,1},{18,2},{19,3},{4,21},{5,... | collective-permute-start | bytes 786440 | tf_op jit(solution)/shard_map/ppermute | solution.py:644
  17.9 4.6 %collective-permute-start.5 = (f32[128,128]{1,0:T(8,128)S(1)}, f32[128,128]{1,0:T(8,128)S(1)}, u32[]{:S(2)}, u32[]{:S(2)}) collective-permute-start(f32[128,128]{1,0:T(8,128)S(1)} %get-tuple-element.48), channel_id=1, source_target_pairs={{0,3},{1,0},{2,1},{3,2},{4,7},{5,4},{6,5},{7,6},{8,11},{9,8},{10,9... | collective-permute-start | bytes 196616 | tf_op jit(solution)/shard_map/ppermute | solution.py:637
  19.7 3.1 %collective-permute-start.4 = (f32[128,128]{1,0:T(8,128)S(1)}, f32[128,128]{1,0:T(8,128)S(1)}, u32[]{:S(2)}, u32[]{:S(2)}) collective-permute-start(f32[128,128]{1,0:T(8,128)S(1)} %get-tuple-element.48), channel_id=1, source_target_pairs={{0,2},{1,3},{2,0},{3,1},{4,6},{5,7},{6,4},{7,5},{8,10},{9,11},{10,... | collective-permute-start | bytes 196616 | tf_op jit(solution)/shard_map/ppermute | solution.py:637
  19.9 4.0 %collective-permute-start.3 = (f32[128,128]{1,0:T(8,128)S(1)}, f32[128,128]{1,0:T(8,128)S(1)}, u32[]{:S(2)}, u32[]{:S(2)}) collective-permute-start(f32[128,128]{1,0:T(8,128)S(1)} %get-tuple-element.48), channel_id=1, source_target_pairs={{0,1},{1,2},{2,3},{3,0},{4,5},{5,6},{6,7},{7,4},{8,9},{9,10},{10,1... | collective-permute-start | bytes 196616 | tf_op jit(solution)/shard_map/ppermute | solution.py:637
  27.0 2.7 %collective-permute-start.6 = (bf16[1024,512]{1,0:T(8,128)(2,1)S(1)}, bf16[1024,512]{1,0:T(8,128)(2,1)S(1)}, u32[]{:S(2)}, u32[]{:S(2)}) collective-permute-start(bf16[1024,512]{1,0:T(8,128)(2,1)S(1)} %get-tuple-element.50), channel_id=1, source_target_pairs={{0,16},{16,0},{1,17},{17,1},{2,18},{18,2},{3,19},{19,3},{4,20},{20... | collective-permute-start | bytes 3145736 | tf_op jit(solution)/shard_map/ppermute | solution.py:637

commit v6 on v5

--- a/solution.py
+++ b/solution.py
@@ -64,6 +64,7 @@
 
 PAIR = 16
 WITHIN_STEP = 512
+HALVES = 2
 COMPILER = pltpu.CompilerParams(vmem_limit_bytes=16 << 20)
 
 
@@ -254,7 +255,153 @@
     return found[:5], found[5:8], found[8:]
 
 
-def front_kernel(
+def products(members, tap_spec):
+    window = tap_spec.shape[1] // 2
+    real, packed = tap_spec[:, :window], tap_spec[:, window:]
+    lane = lax.broadcasted_iota(jnp.int32, real.shape, 1)
+    real_b = jnp.where(lane == 0, packed, real)
+    imag = jnp.where(lane == 0, 0.0, packed)
+    found = []
+    for mixed in members:
+        a, b = mixed[:, :window], mixed[:, window:]
+        found.append(
+            jnp.concatenate([a * real - b * imag, a * imag + b * real_b], axis=1).astype(
+                jnp.bfloat16
+            )
+        )
+    return found
+
+
+def doubled_spectrum(members, table):
+    rows = jnp.concatenate(members, axis=0)
+    found = dot_f32(jnp.concatenate([rows, rows], axis=1), table[...])
+    size = members[0].shape[0]
+    return [found[k * size : (k + 1) * size] for k in range(len(members))]
+
+
+def finish_medium(members, table, gates_out, gates_in, streams, targets):
+    found = dot_f32(jnp.concatenate(members, axis=0), table[...])
+    size, window = streams[0].shape
+    signals = []
+    for k in range(len(members)):
+        rows = slice(k * size, (k + 1) * size)
+        medium = found[rows, :window] + found[rows, window:]
+        gated = (gates_out[k].astype(jnp.float32) * medium).astype(jnp.bfloat16)
+        targets[k][...] = gated
+        stream = streams[k].astype(jnp.float32) + gated.astype(jnp.float32)
+        signals.append((gates_in[k].astype(jnp.float32) * stream).astype(jnp.bfloat16))
+    return signals
+
+
+def end_states(signals, powers_of_pair, pair, modes, mask):
+    rows = slice(pair * PAIR, (pair + 1) * PAIR)
+    lanes = ROWS * modes
+    left = jnp.concatenate([signal[rows] for signal in signals], axis=0)
+    found = dot_f32(left, powers_of_pair)
+    sides = []
+    for side in range(2):
+        tops = [k * PAIR + side * ROWS for k in range(len(signals))]
+        sides.append(
+            [
+                jnp.where(mask, found[top : top + ROWS, side * lanes : (side + 1) * lanes], 0.0)
+                for top in tops
+            ]
+        )
+    return sides
+
+
+def later_kernel(
+    modes,
+    step,
+    sec,
+    tok,
+    local_all,
+    remote_all,
+    inputs_all,
+    taps_all,
+    falling_all,
+    fwd_even,
+    fwd_odd,
+    inv_even,
+    inv_odd,
+    medium_all,
+    ends_all,
+    tap_spec_all,
+    edge_spec_all,
+):
+    share, tokens = inputs_all.shape
+    window = taps_all.shape[1]
+    blocks = tokens // window
+    parts = [slice(b * window, (b + 1) * window) for b in range(blocks)]
+    mask = lane_mask(modes)
+
+    def chunk(section, i):
+        first, second = (local_all, remote_all) if section == 0 else (remote_all, local_all)
+        first, second = rows_at(first, step, i, 1), rows_at(second, step, i, 1)
+        inputs = rows_at(inputs_all, step, i)
+        medium_out, ends = rows_at(medium_all, step, i), rows_at(ends_all, step, i, 1)
+        falling = rows_at(falling_all, step // PAIR, i)
+        sources = [first[1, :, part] * inputs[:, part] for part in parts]
+        tap_rows = rows_at(taps_all, step, i)[...]
+        tap_spec, *even = doubled_spectrum([tap_rows] + sources[0::2], fwd_even)
+        odd = doubled_spectrum(sources[1::2], fwd_odd)
+        in_order = [None] * blocks
+        in_order[0::2] = even
+        in_order[1::2] = odd
+        rows_at(tap_spec_all, step, i)[...] = tap_spec
+        rows_at(edge_spec_all, step, i)[...] = in_order[0]
+        mixed = products([in_order[b - 1] + in_order[b] for b in range(1, blocks)], tap_spec)
+        signals = [None] * blocks
+        for parity, table in enumerate((inv_even, inv_odd)):
+            chosen = [b for b in range(1, blocks) if b % 2 == parity]
+            if not chosen:
+                continue
+            found = finish_medium(
+                [mixed[b - 1] for b in chosen],
+                table,
+                [first[0, :, parts[b]] for b in chosen],
+                [second[1, :, parts[b]] for b in chosen],
+                [inputs[:, parts[b]] for b in chosen],
+                [medium_out.at[:, parts[b]] for b in chosen],
+            )
+            for b, signal in zip(chosen, found):
+                signals[b] = signal
+        for pair in range(step // PAIR):
+            sides = end_states(signals[1:], falling[pair], pair, modes, mask)
+            for side, found in enumerate(sides):
+                at = pair * PAIR + side * ROWS
+                for k, end in enumerate(found):
+                    ends[k + 1, at : at + ROWS, :] = end
+
+    def body(section):
+        pl.loop(0, share // step)(functools.partial(chunk, section))
+
+    by_section(sec, body)
+
+
+def later_call(place, gates, swapped, inputs, taps, falling, tables, modes):
+    share, tokens = inputs.shape
+    window = taps.shape[1]
+    lanes = ROWS * modes
+    operands = [gates, swapped, inputs, taps, falling, *tables]
+    spec = jax.ShapeDtypeStruct((share, 2 * window), jnp.float32)
+    return pl.pallas_call(
+        functools.partial(later_kernel, modes, min(256, share)),
+        out_shape=(
+            jax.ShapeDtypeStruct((share, tokens), jnp.bfloat16),
+            jax.ShapeDtypeStruct((tokens // window, share, lanes), jnp.float32),
+            spec,
+            spec,
+        ),
+        in_specs=[SMEM_SPEC] * 2 + [VMEM_SPEC] * len(operands),
+        out_specs=(VMEM_SPEC,) * 4,
+        name="later",
+        cost_estimate=cost(share, tokens, 1500),
+        compiler_params=COMPILER,
+    )(*place, *operands)
+
+
+def first_kernel(
     modes,
     step,
     sec,
@@ -264,100 +411,59 @@
     inputs_all,
     halo_low,
     halo_high,
-    taps_all,
     rates,
     falling_all,
-    fwd_even,
+    tap_spec_all,
+    edge_spec_all,
     fwd_odd,
     inv_even,
-    inv_odd,
+    medium_before,
+    ends_before,
     medium_all,
     ends_all,
     total_all,
     leaps_all,
 ):
-    share, tokens = inputs_all.shape
-    window = taps_all.shape[1]
-    blocks = tokens // window
-    forward = (fwd_even, fwd_odd)
-    inverse = (inv_even, inv_odd)
+    share = inputs_all.shape[0]
+    window = tap_spec_all.shape[1] // 2
+    part = slice(0, window)
+    mask = lane_mask(modes)
     leaps_all[...] = jnp.exp(-rates[...] * window)
 
     def chunk(section, i):
         first, second = (local_all, remote_all) if section == 0 else (remote_all, local_all)
         first, second = rows_at(first, step, i, 1), rows_at(second, step, i, 1)
         halo = rows_at(halo_low if section == 0 else halo_high, step, i)
-        inputs, taps = rows_at(inputs_all, step, i), rows_at(taps_all, step, i)
-        medium_out, ends = rows_at(medium_all, step, i), rows_at(ends_all, step, i, 1)
         leaps = rows_at(leaps_all, step // ROWS, i)
         falling = rows_at(falling_all, step // PAIR, i)
+        ends = rows_at(ends_all, step, i, 1)
+        started = jnp.where(tok[0] > 0, 1.0, 0.0).astype(jnp.bfloat16)
+        (before,) = doubled_spectrum([halo[...] * started], fwd_odd)
+        mixed = products(
+            [before + rows_at(edge_spec_all, step, i)[...]],
+            rows_at(tap_spec_all, step, i)[...],
+        )
+        signals = finish_medium(
+            mixed,
+            inv_even,
+            [first[0, :, part]],
+            [second[1, :, part]],
+            [rows_at(inputs_all, step, i)[:, part]],
+            [rows_at(medium_all, step, i).at[:, part]],
+        )
+        sums = []
+        for pair in range(step // PAIR):
+            sides = end_states(signals, falling[pair], pair, modes, mask)
+            for side, (end,) in enumerate(sides):
+                at = pair * PAIR + side * ROWS
+                leap = spread(leaps, 2 * pair + side)
+                ends[0, at : at + ROWS, :] = end
+                state = end
+                for k in range(1, ends.shape[0]):
+                    state = state * leap + ends[k, at : at + ROWS, :]
+                sums.append(jnp.sum(state, axis=0, keepdims=True))
         total = rows_at(total_all, step // ROWS, i)
-        channels = step
-        tap_rows = taps[...]
-        started = jnp.where(tok[0] > 0, 1.0, 0.0).astype(jnp.bfloat16)
-        parts = [slice(b * window, (b + 1) * window) for b in range(blocks)]
-        sources = [first[1, :, part] * inputs[:, part] for part in parts]
-        sources = [halo[...] * started] + sources
-        even = [tap_rows] + sources[1::2]
-        odd = sources[0::2]
-        spectra = []
-        for table, members in zip(forward, (even, odd)):
-            rows = jnp.concatenate(members, axis=0)
-            found = dot_f32(jnp.concatenate([rows, rows], axis=1), table[...])
-            spectra.append(
-                [found[k * channels : (k + 1) * channels] for k in range(len(members))]
-            )
-        lane = lax.broadcasted_iota(jnp.int32, (channels, window), 1)
-        real, packed = spectra[0][0][:, :window], spectra[0][0][:, window:]
-        real_b = jnp.where(lane == 0, packed, real)
-        imag = jnp.where(lane == 0, 0.0, packed)
-        in_order = [None] * (blocks + 1)
-        in_order[1::2] = spectra[0][1:]
-        in_order[0::2] = spectra[1]
-        products = []
-        for block in range(blocks):
-            mixed = in_order[block] + in_order[block + 1]
-            a, b = mixed[:, :window], mixed[:, window:]
-            products.append(
-                jnp.concatenate([a * real - b * imag, a * imag + b * real_b], axis=1).astype(
-                    jnp.bfloat16
-                )
-            )
-        signals = [None] * blocks
-        for parity in range(2):
-            members = products[parity::2]
-            found = dot_f32(jnp.concatenate(members, axis=0), inverse[parity][...])
-            for k in range(len(members)):
-                block = 2 * k + parity
-                rows = slice(k * channels, (k + 1) * channels)
-                medium = found[rows, :window] + found[rows, window:]
-                gate = first[0, :, parts[block]].astype(jnp.float32)
-                gated = (gate * medium).astype(jnp.bfloat16)
-                medium_out[:, parts[block]] = gated
-                stream = inputs[:, parts[block]].astype(jnp.float32) + gated.astype(jnp.float32)
-                signals[block] = (
-                    second[1, :, parts[block]].astype(jnp.float32) * stream
-                ).astype(jnp.bfloat16)
-        mask = lane_mask(modes)
-        lanes = ROWS * modes
-        sums = []
-        for pair in range(channels // PAIR):
-            rows = slice(pair * PAIR, (pair + 1) * PAIR)
-            left = jnp.concatenate([signal[rows] for signal in signals], axis=0)
-            found = dot_f32(left, falling[pair])
-            for side in range(2):
-                leap = spread(leaps, 2 * pair + side)
-                state = None
-                for b in range(blocks):
-                    top = b * PAIR + side * ROWS
-                    end = jnp.where(
-                        mask, found[top : top + ROWS, side * lanes : (side + 1) * lanes], 0.0
-                    )
-                    at = pair * PAIR + side * ROWS
-                    ends[b, at : at + ROWS, :] = end
-                    state = end if state is None else state * leap + end
-                sums.append(jnp.sum(state, axis=0, keepdims=True))
-        total[...] = jnp.concatenate(sums, axis=0)
+        total[...] = jnp.concatenate(sums, axis=0).astype(total.dtype)
 
     def body(section):
         pl.loop(0, share // step)(functools.partial(chunk, section))
@@ -365,24 +471,26 @@
     by_section(sec, body)
 
 
-def front_call(place, gates, swapped, inputs, halos, taps, rates, falling, tables, modes):
+def first_call(
+    place, gates, swapped, inputs, halos, rates, falling, specs, tables, medium, ends, modes
+):
     share, tokens = inputs.shape
-    window = taps.shape[1]
     lanes = ROWS * modes
     small = (share // ROWS, lanes)
-    operands = [gates, swapped, inputs, *halos, taps, rates, falling, *tables]
+    operands = [gates, swapped, inputs, *halos, rates, falling, *specs, *tables, medium, ends]
     return pl.pallas_call(
-        functools.partial(front_kernel, modes, min(256, share)),
+        functools.partial(first_kernel, modes, min(256, share)),
         out_shape=(
-            jax.ShapeDtypeStruct((share, tokens), jnp.bfloat16),
-            jax.ShapeDtypeStruct((tokens // window, share, lanes), jnp.float32),
-            jax.ShapeDtypeStruct(small, jnp.float32),
+            jax.ShapeDtypeStruct(medium.shape, medium.dtype),
+            jax.ShapeDtypeStruct(ends.shape, ends.dtype),
+            jax.ShapeDtypeStruct(small, jnp.bfloat16),
         ),
         in_specs=[SMEM_SPEC] * 2 + [VMEM_SPEC] * len(operands),
         out_specs=(VMEM_SPEC,) * 3,
         scratch_shapes=[pltpu.VMEM(small, jnp.float32)],
-        name="front",
-        cost_estimate=cost(share, tokens, 2000),
+        input_output_aliases={len(operands): 0, len(operands) + 1: 1},
+        name="first",
+        cost_estimate=cost(share, tokens, 500),
         compiler_params=COMPILER,
     )(*place, *operands)
 
@@ -458,6 +566,8 @@
     modes,
     window,
     step,
+    first,
+    share,
     sec,
     tok,
     local_all,
@@ -472,28 +582,33 @@
     *rest,
 ):
     arrived = rest[:count]
-    result, send, leaps_all, scales_all, shares_all, starts_all, mixed, done = rest[count:]
-    share, tokens = inputs_all.shape
+    (result, send, leaps_all, scales_all, shares_all, starts_all, mixed, done) = rest[-8:]
+    part_rows, tokens = send.shape
+    base = first // step
+    groups = pl.ds(first // ROWS, part_rows // ROWS)
     blocks = tokens // window
     mask = lane_mask(modes)
-    slow = rates[...]
+    slow = rates[groups, :]
     leap_all = jnp.exp(-slow * window)
-    scale_all = scale_rows[...] * jnp.exp(-slow)
+    scale_all = scale_rows[groups, :] * jnp.exp(-slow)
     leaps_all[...] = leap_all
     scales_all[...] = scale_all
     shares_all[...] = scale_all / (1.0 + leap_all)
     entering = jnp.zeros_like(slow)
     for k in range(count):
         known = jnp.where(tok[0] > k, 1.0, 0.0)
-        entering = entering + arrived[k][...] * (jnp.exp(-slow * (tokens * k)) * known)
+        entering = entering + arrived[k][groups, :].astype(jnp.float32) * (jnp.exp(-slow * (tokens * k)) * known)
     starts_all[...] = entering
 
     def chunk(section, out_all, i):
-        gate_out = rows_at((remote_all if section == 0 else local_all).at[0], step, i)
-        inputs, gated_medium = rows_at(inputs_all, step, i), rows_at(medium_all, step, i)
-        within, out = rows_at(within_all, step, i), rows_at(out_all, step, i)
-        ends = rows_at(ends_all, step, i, 1)
-        rising = rows_at(rising_all, step // PAIR, i)
+        out = rows_at(out_all, step, i)
+        at_all = base + i
+        gate_out = rows_at((remote_all if section == 0 else local_all).at[0], step, at_all)
+        inputs = rows_at(inputs_all, step, at_all)
+        gated_medium = rows_at(medium_all, step, at_all)
+        within = rows_at(within_all, step, at_all)
+        ends = rows_at(ends_all, step, at_all, 1)
+        rising = rows_at(rising_all, step // PAIR, at_all)
         small = step // ROWS
         leaps, scales = rows_at(leaps_all, small, i), rows_at(scales_all, small, i)
         shares, starts = rows_at(shares_all, small, i), rows_at(starts_all, small, i)
@@ -527,10 +642,13 @@
                 out[rows, part] = (stream + gate * long_out).astype(jnp.bfloat16)
 
     def body(section):
-        target = result.at[0, pl.ds(section * share, share), :]
-        early = pltpu.make_async_copy(medium_all, target if section == 0 else send, done.at[0])
+        target = result.at[0, pl.ds(section * share + first, part_rows), :]
+        source = medium_all.at[pl.ds(first, part_rows), :]
+        early = pltpu.make_async_copy(source, target if section == 0 else send, done.at[0])
         early.start()
-        pl.loop(0, share // step)(functools.partial(chunk, section, mixed if section else send))
+        pl.loop(0, part_rows // step)(
+            functools.partial(chunk, section, mixed if section else send)
+        )
         if section == 1:
             late = pltpu.make_async_copy(mixed, target, done.at[1])
             late.start()
@@ -541,100 +659,114 @@
 
 
 def output_call(
-    place, gates, swapped, within, inputs, medium, rates, scales, rising, ends, arrived, window
+    place, half, gates, swapped, within, inputs, medium, rates, scales, rising, ends, arrived, before
 ):
     share, tokens = medium.shape
     lanes = rates.shape[1]
-    step = min(256, share)
-    small = (share // ROWS, lanes)
+    window = rising.shape[1]
+    part_rows = share // HALVES
+    step = min(256, part_rows)
+    small = (part_rows // ROWS, lanes)
     operands = [gates, swapped, within, inputs, medium, rates, scales, rising, ends, *arrived]
+    result = jax.ShapeDtypeStruct((1, 2 * share, tokens), jnp.bfloat16)
+    chained = [] if before is None else [before]
     return pl.pallas_call(
-        functools.partial(output_kernel, len(arrived), lanes // ROWS, window, step),
-        out_shape=(
-            jax.ShapeDtypeStruct((1, 2 * share, tokens), jnp.bfloat16),
-            jax.ShapeDtypeStruct((share, tokens), jnp.bfloat16),
+        functools.partial(
+            output_kernel,
+            len(arrived),
+            lanes // ROWS,
+            window,
+            step,
+            half * part_rows,
+            share,
         ),
-        in_specs=[SMEM_SPEC] * 2 + [VMEM_SPEC] * len(operands),
+        out_shape=(result, jax.ShapeDtypeStruct((part_rows, tokens), jnp.bfloat16)),
+        in_specs=[SMEM_SPEC] * 2 + [VMEM_SPEC] * len(operands) + [ANY_SPEC] * len(chained),
         out_specs=(ANY_SPEC, VMEM_SPEC),
         scratch_shapes=[pltpu.VMEM(small, jnp.float32)] * 4
-        + [pltpu.VMEM((share, tokens), jnp.bfloat16), pltpu.SemaphoreType.DMA((2,))],
+        + [pltpu.VMEM((part_rows, tokens), jnp.bfloat16), pltpu.SemaphoreType.DMA((2,))],
+        input_output_aliases={2 + len(operands): 0} if chained else {},
         name="output",
-        cost_estimate=cost(share, tokens, 1500),
+        cost_estimate=cost(part_rows, tokens, 1500),
         compiler_params=COMPILER,
-    )(*place, *operands)
-
-
-def place_kernel(sec, tok, own, received, out, done):
-    share = received.shape[0]
-    other = pl.ds(pl.multiple_of((1 - sec[0]) * share, share), share)
+    )(*place, *operands, *chained)
+
+
+def place_kernel(first, share, sec, tok, own, received, out, done):
+    rows = received.shape[0]
+    other = pl.ds(pl.multiple_of((1 - sec[0]) * share + first, rows), rows)
     copy = pltpu.make_async_copy(received, out.at[0, other, :], done)
     copy.start()
     copy.wait()
 
 
-def place_call(place, own, received):
-    share, tokens = received.shape
+def place_call(place, half, own, received):
+    rows, tokens = received.shape
     return pl.pallas_call(
-        place_kernel,
+        functools.partial(place_kernel, half * rows, own.shape[1] // 2),
         out_shape=jax.ShapeDtypeStruct(own.shape, own.dtype),
         in_specs=[SMEM_SPEC] * 2 + [ANY_SPEC, VMEM_SPEC],
         out_specs=ANY_SPEC,
         scratch_shapes=[pltpu.SemaphoreType.DMA],
         input_output_aliases={2: 0},
         name="placing",
-        cost_estimate=cost(share, tokens, 2),
+        cost_estimate=cost(rows, tokens, 2),
         compiler_params=COMPILER,
     )(*place, own, received)
 
 
-def lend_kernel(sec, tok, gates, gate_tail, input_tail, out, low, high):
-    out[...] = gates[0]
-    share = low.shape[0]
-
-    @pl.when(pl.program_id(0) == 0)
-    def _():
-        for half, target in enumerate((low, high)):
-            rows = slice(half * share, (half + 1) * share)
-            target[...] = (
-                gate_tail[0, 0, rows, :].astype(jnp.float32)
-                * input_tail[rows, :].astype(jnp.float32)
-            ).astype(jnp.bfloat16)
+def lend_kernel(sec, tok, gates, inputs, lent, low, high, gate_tail, input_tail, arrival):
+    share, window = low.shape
+    tokens = inputs.shape[1]
+    tail = pl.ds(tokens - window, window)
+    other = pl.ds(pl.multiple_of((1 - sec[0]) * share, share), share)
+    copies = [
+        pltpu.make_async_copy(source, target, arrival.at[k])
+        for k, (source, target) in enumerate(
+            [
+                (gates.at[0, 1, :, tail], gate_tail),
+                (inputs.at[:, tail], input_tail),
+                (gates.at[0, :, other, :], lent),
+            ]
+        )
+    ]
+    for copy in copies:
+        copy.start()
+    copies[0].wait()
+    copies[1].wait()
+    low[...] = gate_tail[:share, :] * input_tail[:share, :]
+    high[...] = gate_tail[share:, :] * input_tail[share:, :]
+    copies[2].wait()
 
 
 def lend_call(place, gate_streams, inputs, window, share):
     channels, tokens = inputs.shape
-    step = min(512, share)
-    count = share // step
-    last = tokens // window - 1
     edge = jax.ShapeDtypeStruct((share, window), jnp.bfloat16)
     return pl.pallas_call(
         lend_kernel,
         out_shape=(jax.ShapeDtypeStruct((2, share, tokens), jnp.bfloat16), edge, edge),
-        grid_spec=pltpu.PrefetchScalarGridSpec(
-            num_scalar_prefetch=2,
-            grid=(count,),
-            in_specs=[
-                pl.BlockSpec(
-                    (1, 2, step, tokens), lambda i, p, t: (0, 0, (1 - p[0]) * count + i, 0)
-                ),
-                pl.BlockSpec((1, 1, channels, window), lambda i, p, t: (0, 1, 0, last)),
-                pl.BlockSpec((channels, window), lambda i, p, t: (0, last)),
-            ],
-            out_specs=(
-                pl.BlockSpec((2, step, tokens), lambda i, p, t: (0, i, 0)),
-                pl.BlockSpec((share, window), lambda i, p, t: (0, 0)),
-                pl.BlockSpec((share, window), lambda i, p, t: (0, 0)),
-            ),
-        ),
+        in_specs=[SMEM_SPEC] * 2 + [ANY_SPEC] * 2,
+        out_specs=(VMEM_SPEC,) * 3,
+        scratch_shapes=[pltpu.VMEM((channels, window), jnp.bfloat16)] * 2
+        + [pltpu.SemaphoreType.DMA((3,))],
         name="lend",
         cost_estimate=cost(share, tokens, 2),
         compiler_params=COMPILER,
-    )(*place, *parked(gate_streams, gate_streams, inputs))
+    )(*place, *parked(gate_streams, inputs))
 
 
 def ring(value, axis, by):
     peers = lax.axis_size(axis)
     return lax.ppermute(value, axis, [(i, (i + by) % peers) for i in range(peers)])
+
+
+def onward(value, by):
+    peers = lax.axis_size("tok")
+    sources, targets = range(peers - by, peers), range(by)
+    alone = [i for i in sources if i in targets]
+    spare = zip([i for i in sources if i not in alone], [i for i in targets if i not in alone])
+    pairs = [(i, i + by) for i in range(peers - by)] + [(i, i) for i in alone] + list(spare)
+    return lax.ppermute(value, "tok", pairs)
 
 
 def edge_to(value, section):
@@ -672,15 +804,46 @@
     )
     response, rates, scales, rising, falling = built
     gates, inputs, taps = own
-    medium, ends, total = front_call(
-        place, gates, swapped, inputs, halos, taps, rates, falling, tables[:4], modes
-    )
-    arrived = [ring(total, "tok", by) for by in range(1, lax.axis_size("tok"))]
+    medium, ends, *specs = later_call(
+        place, gates, swapped, inputs, taps, falling, tables[:4], modes
+    )
+    medium, ends, total = first_call(
+        place,
+        gates,
+        swapped,
+        inputs,
+        halos,
+        rates,
+        falling,
+        specs,
+        tables[1:3],
+        medium,
+        ends,
+        modes,
+    )
+    arrived = [onward(total, by) for by in range(1, lax.axis_size("tok"))]
     within = within_call(place, gates, swapped, inputs, medium, response, tables[4:])
-    keep, send = output_call(
-        place, gates, swapped, within, inputs, medium, rates, scales, rising, ends, arrived, window
-    )
-    return place_call(place, keep, ring(send, "section", 1))
+    result, received = None, []
+    for half in range(HALVES):
+        result, send = output_call(
+            place,
+            half,
+            gates,
+            swapped,
+            within,
+            inputs,
+            medium,
+            rates,
+            scales,
+            rising,
+            ends,
+            arrived,
+            result,
+        )
+        received.append(ring(send, "section", 1))
+    for half in range(HALVES):
+        result = place_call(place, half, result, received[half])
+    return result
 
 
 def solution(mesh):

time: 31.2 us -> 31.5 us (level)
  waiting for transfers between devices: 6.41 us -> 2.59 us
  Pallas kernels: 15.5 us -> 18.6 us
  starting transfers between devices: 8.68 us -> 9.77 us
    ppermute x0 -> x3, starting transfers between devices: none -> 4.61 us  [onward(): return lax.ppermute(value, 'tok', pairs)]
    ppermute x5 -> x3, starting transfers between devices: 3.74 us -> 0.21 us  [ring(): lax.ppermute(value, axis, [(i, (i + by) % peers) for i in range(peers)])]
    ppermute x2, waiting for transfers between devices: 2.7 us -> 0.01 us  [edge_to(): return lax.ppermute(value, ('section', 'tok'), pairs)]
    ppermute x5 -> x3, waiting for transfers between devices: 3.71 us -> 1.08 us  [ring(): lax.ppermute(value, axis, [(i, (i + by) % peers) for i in range(peers)])]
    pallas_call x2 -> x4, Pallas kernels: 4.27 us -> 6.85 us  [the longest x1 3.07 us: later_call(): pl.pallas_call(functools.partial(later_kernel, modes, min(256, share)), o...]
    ppermute x0 -> x3, waiting for transfers between devices: none -> 1.51 us  [onward(): return lax.ppermute(value, 'tok', pairs)]
    pallas_call x1 -> x2, Pallas kernels: 3.08 us -> 3.74 us  [output_call(): pl.pallas_call(functools.partial(output_kernel, len(arrived), lanes // RO...]
  transfers between devices with their start and end apart: 7 -> 8, of which waited for: 4 -> 3; matrix products, arithmetic and copies ran while one was open for 0% -> 0% of each run, Pallas kernels for 20% -> 38%
where the time goes in v6:
time: 31.5 us; the launch traced here: 31.2 us
  Pallas kernels  18.6 us (59%)
  starting transfers between devices  9.77 us (31%)
  waiting for transfers between devices  2.59 us (8%)
    ppermute x2, starting transfers between devices, edge_to(): return lax.ppermute(value, ('section', 'tok'), pairs)  4.94 us
    pallas_call x1, Pallas kernels, response_call(): pl.pallas_call(functools.partial(response_kernel, len(tables)), out_shape...  4.63 us
    ppermute x3, starting transfers between devices, onward(): return lax.ppermute(value, 'tok', pairs)  4.61 us
    pallas_call x2, Pallas kernels, output_call(): pl.pallas_call(functools.partial(output_kernel, len(arrived), lanes // RO...  3.74 us
    pallas_call x1, Pallas kernels, later_call(): pl.pallas_call(functools.partial(later_kernel, modes, min(256, share)), o...  3.07 us
    pallas_call x1, Pallas kernels, first_call(): pl.pallas_call(functools.partial(first_kernel, modes, min(256, share)), o...  2.17 us
    pallas_call x1, Pallas kernels, lend_call(): pl.pallas_call(lend_kernel, out_shape=(jax.ShapeDtypeStruct((2, share, to...  2.03 us
    pallas_call x2, Pallas kernels, place_call(): pl.pallas_call(functools.partial(place_kernel, half * rows, own.shape[1]...  1.61 us
  transfers between devices with their start and end apart: 8, of which 3 were waited for; matrix products, arithmetic and copies ran while one was open for 0% of the time, Pallas kernels for 38%

profile of v6, /device:TPU:1, one launch (start us, length us, event | category | flops | bytes accessed | tf_op | source)
XLA Modules:
  0.0 31.2 jit_solution(18408153041620176357)
XLA Ops:
  0.0 0.0 copy-start
  0.0 0.0 copy-start.1
  0.0 0.0 copy-start.2
  0.0 0.0 copy-start.3
  0.0 2.0 %lend.1 = (bf16[2,1024,512]{2,1,0:T(8,128)(2,1)S(1)}, bf16[1024,128]{1,0:T(8,128)(2,1)S(1)}, bf16[1024,128]{1,0:T(8,128)(2,1)S(1)}) custom-call(s32[1]{0:T(128)} %bitcast.sec, s32[1]{0:T(128)} %bitcast.1.tok, bf16[1,2,2048,512]{3,2,1,0:T(8,128)(2,1)} %gates.1, bf16[2048,512]{1,0:T(8,128)(2,1)} %inputs.1), custom_call_target="tpu_custom_call" | custom-call | flops 1048576 | bytes 6291456 | tf_op jit(solution)/shard_map/lend/pallas_call | solution.py:745
  2.1 0.1 collective-permute-start
  2.1 0.7 %collective-permute-start.1 = (bf16[1024,128]{1,0:T(8,128)(2,1)S(1)}, bf16[1024,128]{1,0:T(8,128)(2,1)S(1)}, u32[]{:S(2)}, u32[]{:S(2)}) collective-permute-start(bf16[1024,128]{1,0:T(8,128)(2,1)S(1)} %get-tuple-element.37), channel_id=1, source_target_pairs={{0,1},{1,2},{2,3},{3,0},{16,16},{17,17},{18,18},{19,19},{4,5},{5,6... | collective-permute-start | bytes 786440 | tf_op jit(solution)/shard_map/ppermute | solution.py:776
  2.8 4.3 %collective-permute-start.2 = (bf16[1024,128]{1,0:T(8,128)(2,1)S(1)}, bf16[1024,128]{1,0:T(8,128)(2,1)S(1)}, u32[]{:S(2)}, u32[]{:S(2)}) collective-permute-start(bf16[1024,128]{1,0:T(8,128)(2,1)S(1)} %get-tuple-element.38), channel_id=1, source_target_pairs={{0,17},{1,18},{2,19},{3,16},{16,0},{17,1},{18,2},{19,3},{4,21},{5,... | collective-permute-start | bytes 786440 | tf_op jit(solution)/shard_map/ppermute | solution.py:776
  7.1 0.0 copy-done
  7.1 0.0 copy-done.1
  7.1 0.0 copy-done.2
  7.1 0.0 copy-done.3
  7.1 4.6 %response.1 = (f32[1024,256]{1,0:T(8,128)S(1)}, f32[128,128]{1,0:T(8,128)S(1)}, f32[128,128]{1,0:T(8,128)S(1)}, bf16[64,128,256]{2,1,0:T(8,128)(2,1)S(1)}, bf16[...) custom-call(s32[1]{0:T(128)} %bitcast.sec, ...), custom_call_target="tpu_custom_call" | custom-call | flops 314572800 | bytes 6291456 | tf_op jit(solution)/shard_map/response/pallas_call | solution.py:240
  11.7 0.0 collective-permute-done.remote_all
  11.8 3.1 %later.1 = (bf16[1024,512]{1,0:T(8,128)(2,1)S(1)}, f32[4,1024,128]{2,1,0:T(8,128)S(1)}, f32[1024,256]{1,0:T(8,128)S(1)}, f32[1024,256]{1,0:T(8,128)S(1)}) custom-call(s32[1]{0:T(128)} %bitcast.sec, s32[1]{0:T(128)} %bitcast.1.tok, bf16[2,1024,512]{2,1,0:T(8,128)(2,1)S(1)} %get-tuple-element.34.local_all, ...), custom_call_target="tpu_custom_call" | custom-call | flops 786432000 | bytes 6291456 | tf_op jit(solution)/shard_map/later/pallas_call | solution.py:388
  14.8 0.0 collective-permute-done.1.halo_low
  14.8 0.0 collective-permute-done.2.halo_high
  14.9 2.2 %first.1 = (bf16[1024,512]{1,0:T(8,128)(2,1)S(1)}, f32[4,1024,128]{2,1,0:T(8,128)S(1)}, bf16[128,128]{1,0:T(8,128)(2,1)S(1)}) custom-call(s32[1]{0:T(128)} %bitcast.sec, s32[1]{0:T(128)} %bitcast.1.tok, bf16[2,1024,512]{2,1,0:T(8,128)(2,1)S(1)} %get-tuple-element.34.local_all, ...), custom_call_target="tpu_custom_call", output_to_operand_aliasing={{0}: (13, {}), {1}: (14, {})} | custom-call | flops 262144000 | bytes 6291456 | tf_op jit(solution)/shard_map/first/pallas_call | solution.py:481
  17.0 3.2 %collective-permute-start.5 = (bf16[128,128]{1,0:T(8,128)(2,1)S(1)}, bf16[128,128]{1,0:T(8,128)(2,1)S(1)}, u32[]{:S(2)}, u32[]{:S(2)}) collective-permute-start(bf16[128,128]{1,0:T(8,128)(2,1)S(1)} %get-tuple-element.58), channel_id=1, source_target_pairs={{0,3},{1,1},{2,2},{3,0},{4,7},{5,5},{6,6},{7,4},{8,11},{9,9},{10,1... | collective-permute-start | bytes 98312 | tf_op jit(solution)/shard_map/ppermute | solution.py:769
  20.3 0.1 collective-permute-start.4
  20.3 1.3 %collective-permute-start.3 = (bf16[128,128]{1,0:T(8,128)(2,1)S(1)}, bf16[128,128]{1,0:T(8,128)(2,1)S(1)}, u32[]{:S(2)}, u32[]{:S(2)}) collective-permute-start(bf16[128,128]{1,0:T(8,128)(2,1)S(1)} %get-tuple-element.58), channel_id=1, source_target_pairs={{0,1},{1,2},{2,3},{3,0},{4,5},{5,6},{6,7},{7,4},{8,9},{9,10},{10,1... | collective-permute-start | bytes 98312 | tf_op jit(solution)/shard_map/ppermute | solution.py:769
  21.7 1.4 %within.1.within_all = f32[1024,512]{1,0:T(8,128)S(1)} custom-call(s32[1]{0:T(128)} %bitcast.sec, s32[1]{0:T(128)} %bitcast.1.tok, bf16[2,1024,512]{2,1,0:T(8,128)(2,1)S(1)} %get-tuple-element.34.local_all, bf16[2,1024,512]{2,1,0:T(8,128)(2,1)S(1)} %collective-permute-done.remote_all, bf16[1024,512]{1,0:T(8,128)(2,1)S(1)} %get-tuple-element.36.inputs_all, ...), custom_call_target="tpu_custom_call" | custom-call | flops 786432000 | bytes 6291456 | tf_op jit(solution)/shard_map/within/pallas_call | solution.py:553
  23.0 0.0 collective-permute-done.5.rest_2_
  23.0 1.0 %collective-permute-done.4.rest_1_ = bf16[128,128]{1,0:T(8,128)(2,1)S(1)} collective-permute-done((bf16[128,128]{1,0:T(8,128)(2,1)S(1)}, bf16[128,128]{1,0:T(8,128)(2,1)S(1)}, u32[]{:S(2)}, u32[]{:S(2)}) %collective-permute-start.4) | collective-permute-done | bytes 32800 | tf_op jit(solution)/shard_map/ppermute | solution.py:769
  24.1 0.5 %collective-permute-done.3.rest_0_ = bf16[128,128]{1,0:T(8,128)(2,1)S(1)} collective-permute-done((bf16[128,128]{1,0:T(8,128)(2,1)S(1)}, bf16[128,128]{1,0:T(8,128)(2,1)S(1)}, u32[]{:S(2)}, u32[]{:S(2)}) %collective-permute-start.3) | collective-permute-done | bytes 32800 | tf_op jit(solution)/shard_map/ppermute | solution.py:769
  24.5 1.9 %output.2 = (bf16[1,2048,512]{2,1,0:T(8,128)(2,1)}, bf16[512,512]{1,0:T(8,128)(2,1)S(1)}) custom-call(s32[1]{0:T(128)} %bitcast.sec, s32[1]{0:T(128)} %bitcast.1.tok, bf16[2,1024,512]{2,1,0:T(8,128)(2,1)S(1)} %get-tuple-element.34.local_all, bf16[2,1024,512]{2,1,0:T(8,128)(2,1)S(1)} %collective-permute-done.remote_all, f32[1024,512]{1,0:T(8,128)S(1)} %within.1.within_all, ...), custom_call_target="tpu_custom_call" | custom-call | flops 393216000 | bytes 3145728 | tf_op jit(solution)/shard_map/output/pallas_call | solution.py:673
  26.4 0.1 collective-permute-start.6
  26.5 1.9 %output.3 = (bf16[1,2048,512]{2,1,0:T(8,128)(2,1)}, bf16[512,512]{1,0:T(8,128)(2,1)S(1)}) custom-call(s32[1]{0:T(128)} %bitcast.sec, s32[1]{0:T(128)} %bitcast.1.tok, bf16[2,1024,512]{2,1,0:T(8,128)(2,1)S(1)} %get-tuple-element.34.local_all, bf16[2,1024,512]{2,1,0:T(8,128)(2,1)S(1)} %collective-permute-done.remote_all, ...), custom_call_target="tpu_custom_call", output_to_operand_aliasing={{0}: (14, {})} | custom-call | flops 393216000 | bytes 3145728 | tf_op jit(solution)/shard_map/output/pallas_call | solution.py:673
  28.4 0.1 collective-permute-start.7
  28.5 0.0 collective-permute-done.6.received
  28.5 0.8 %placing.2.own = bf16[1,2048,512]{2,1,0:T(8,128)(2,1)} custom-call(s32[1]{0:T(128)} %bitcast.sec, s32[1]{0:T(128)} %bitcast.1.tok, bf16[1,2048,512]{2,1,0:T(8,128)(2,1)} %get-tuple-element.60.own, bf16[512,512]{1,0:T(8,128)(2,1)S(1)} %collective-permute-done.6.received), custom_call_target="tpu_custom_call", output_to_operand_aliasing={{}: (2, {})} | custom-call | flops 524288 | bytes 3145728 | tf_op jit(solution)/shard_map/placing/pallas_call | solution.py:705
  29.3 1.1 %collective-permute-done.7.received = bf16[512,512]{1,0:T(8,128)(2,1)S(1)} collective-permute-done((bf16[512,512]{1,0:T(8,128)(2,1)S(1)}, bf16[512,512]{1,0:T(8,128)(2,1)S(1)}, u32[]{:S(2)}, u32[]{:S(2)}) %collective-permute-start.7) | collective-permute-done | bytes 524320 | tf_op jit(solution)/shard_map/ppermute | solution.py:760
  30.4 0.8 %placing.3 = bf16[1,2048,512]{2,1,0:T(8,128)(2,1)} custom-call(s32[1]{0:T(128)} %bitcast.sec, s32[1]{0:T(128)} %bitcast.1.tok, bf16[1,2048,512]{2,1,0:T(8,128)(2,1)} %placing.2.own, bf16[512,512]{1,0:T(8,128)(2,1)S(1)} %collective-permute-done.7.received), custom_call_target="tpu_custom_call", output_to_operand_aliasing={{}: (2, {})} | custom-call | flops 524288 | bytes 3145728 | tf_op jit(solution)/shard_map/placing/pallas_call | solution.py:705
Async XLA Ops:
  0.0 7.1 %copy-start = (f32[2048,16]{0,1:T(8,128)S(1)}, f32[2048,16]{0,1:T(8,128)}, u32[]{:S(2)}) copy-start(f32[2048,16]{0,1:T(8,128)} %param.22) | copy-start | bytes 393220
  0.0 7.1 %copy-start.1 = (f32[2048,16]{0,1:T(8,128)S(1)}, f32[2048,16]{0,1:T(8,128)}, u32[]{:S(2)}) copy-start(f32[2048,16]{0,1:T(8,128)} %param.21) | copy-start | bytes 393220
  0.0 7.1 %copy-start.2 = (bf16[128,256]{1,0:T(8,128)(2,1)S(1)}, bf16[128,256]{1,0:T(8,128)(2,1)}, u32[]{:S(2)}) copy-start(bf16[128,256]{1,0:T(8,128)(2,1)} %constant.35.table_l) | copy-start | bytes 196612
  0.0 7.1 %copy-start.3 = (bf16[128,256]{1,0:T(8,128)(2,1)S(1)}, bf16[128,256]{1,0:T(8,128)(2,1)}, u32[]{:S(2)}) copy-start(bf16[128,256]{1,0:T(8,128)(2,1)} %constant.32.table_h) | copy-start | bytes 196612
  2.1 9.7 %collective-permute-start = (bf16[2,1024,512]{2,1,0:T(8,128)(2,1)S(1)}, bf16[2,1024,512]{2,1,0:T(8,128)(2,1)S(1)}, u32[]{:S(2)}, u32[]{:S(2)}) collective-permute-start(bf16[2,1024,512]{2,1,0:T(8,128)(2,1)S(1)} %get-tuple-element.35), channel_id=1, source_target_pairs={{0,16},{16,0},{1,17},{17,1},{2,18},{18,2},{3,19},{19,3},{4,20},{20... | collective-permute-start | bytes 6291464 | tf_op jit(solution)/shard_map/ppermute | solution.py:760
  2.1 12.7 %collective-permute-start.1 = (bf16[1024,128]{1,0:T(8,128)(2,1)S(1)}, bf16[1024,128]{1,0:T(8,128)(2,1)S(1)}, u32[]{:S(2)}, u32[]{:S(2)}) collective-permute-start(bf16[1024,128]{1,0:T(8,128)(2,1)S(1)} %get-tuple-element.37), channel_id=1, source_target_pairs={{0,1},{1,2},{2,3},{3,0},{16,16},{17,17},{18,18},{19,19},{4,5},{5,6... | collective-permute-start | bytes 786440 | tf_op jit(solution)/shard_map/ppermute | solution.py:776
  2.8 12.0 %collective-permute-start.2 = (bf16[1024,128]{1,0:T(8,128)(2,1)S(1)}, bf16[1024,128]{1,0:T(8,128)(2,1)S(1)}, u32[]{:S(2)}, u32[]{:S(2)}) collective-permute-start(bf16[1024,128]{1,0:T(8,128)(2,1)S(1)} %get-tuple-element.38), channel_id=1, source_target_pairs={{0,17},{1,18},{2,19},{3,16},{16,0},{17,1},{18,2},{19,3},{4,21},{5,... | collective-permute-start | bytes 786440 | tf_op jit(solution)/shard_map/ppermute | solution.py:776
  17.0 6.0 %collective-permute-start.5 = (bf16[128,128]{1,0:T(8,128)(2,1)S(1)}, bf16[128,128]{1,0:T(8,128)(2,1)S(1)}, u32[]{:S(2)}, u32[]{:S(2)}) collective-permute-start(bf16[128,128]{1,0:T(8,128)(2,1)S(1)} %get-tuple-element.58), channel_id=1, source_target_pairs={{0,3},{1,1},{2,2},{3,0},{4,7},{5,5},{6,6},{7,4},{8,11},{9,9},{10,1... | collective-permute-start | bytes 98312 | tf_op jit(solution)/shard_map/ppermute | solution.py:769
  20.3 3.8 %collective-permute-start.4 = (bf16[128,128]{1,0:T(8,128)(2,1)S(1)}, bf16[128,128]{1,0:T(8,128)(2,1)S(1)}, u32[]{:S(2)}, u32[]{:S(2)}) collective-permute-start(bf16[128,128]{1,0:T(8,128)(2,1)S(1)} %get-tuple-element.58), channel_id=1, source_target_pairs={{0,2},{1,3},{2,0},{3,1},{4,6},{5,7},{6,4},{7,5},{8,10},{9,11},{10,... | collective-permute-start | bytes 98312 | tf_op jit(solution)/shard_map/ppermute | solution.py:769
  20.3 4.2 %collective-permute-start.3 = (bf16[128,128]{1,0:T(8,128)(2,1)S(1)}, bf16[128,128]{1,0:T(8,128)(2,1)S(1)}, u32[]{:S(2)}, u32[]{:S(2)}) collective-permute-start(bf16[128,128]{1,0:T(8,128)(2,1)S(1)} %get-tuple-element.58), channel_id=1, source_target_pairs={{0,1},{1,2},{2,3},{3,0},{4,5},{5,6},{6,7},{7,4},{8,9},{9,10},{10,1... | collective-permute-start | bytes 98312 | tf_op jit(solution)/shard_map/ppermute | solution.py:769
  26.4 2.0 %collective-permute-start.6 = (bf16[512,512]{1,0:T(8,128)(2,1)S(1)}, bf16[512,512]{1,0:T(8,128)(2,1)S(1)}, u32[]{:S(2)}, u32[]{:S(2)}) collective-permute-start(bf16[512,512]{1,0:T(8,128)(2,1)S(1)} %get-tuple-element.61), channel_id=1, source_target_pairs={{0,16},{16,0},{1,17},{17,1},{2,18},{18,2},{3,19},{19,3},{4,20},{20... | collective-permute-start | bytes 1572872 | tf_op jit(solution)/shard_map/ppermute | solution.py:760
  28.4 2.0 %collective-permute-start.7 = (bf16[512,512]{1,0:T(8,128)(2,1)S(1)}, bf16[512,512]{1,0:T(8,128)(2,1)S(1)}, u32[]{:S(2)}, u32[]{:S(2)}) collective-permute-start(bf16[512,512]{1,0:T(8,128)(2,1)S(1)} %get-tuple-element.62), channel_id=1, source_target_pairs={{0,16},{16,0},{1,17},{17,1},{2,18},{18,2},{3,19},{19,3},{4,20},{20... | collective-permute-start | bytes 1572872 | tf_op jit(solution)/shard_map/ppermute | solution.py:760

commit v7 on v6

--- a/solution.py
+++ b/solution.py
@@ -311,7 +311,6 @@
 
 
 def later_kernel(
-    modes,
     step,
     sec,
     tok,
@@ -319,13 +318,12 @@
     remote_all,
     inputs_all,
     taps_all,
-    falling_all,
     fwd_even,
     fwd_odd,
     inv_even,
     inv_odd,
     medium_all,
-    ends_all,
+    signals_all,
     tap_spec_all,
     edge_spec_all,
 ):
@@ -333,14 +331,12 @@
     window = taps_all.shape[1]
     blocks = tokens // window
     parts = [slice(b * window, (b + 1) * window) for b in range(blocks)]
-    mask = lane_mask(modes)
 
     def chunk(section, i):
         first, second = (local_all, remote_all) if section == 0 else (remote_all, local_all)
         first, second = rows_at(first, step, i, 1), rows_at(second, step, i, 1)
         inputs = rows_at(inputs_all, step, i)
-        medium_out, ends = rows_at(medium_all, step, i), rows_at(ends_all, step, i, 1)
-        falling = rows_at(falling_all, step // PAIR, i)
+        medium_out, signals = rows_at(medium_all, step, i), rows_at(signals_all, step, i)
         sources = [first[1, :, part] * inputs[:, part] for part in parts]
         tap_rows = rows_at(taps_all, step, i)[...]
         tap_spec, *even = doubled_spectrum([tap_rows] + sources[0::2], fwd_even)
@@ -351,7 +347,6 @@
         rows_at(tap_spec_all, step, i)[...] = tap_spec
         rows_at(edge_spec_all, step, i)[...] = in_order[0]
         mixed = products([in_order[b - 1] + in_order[b] for b in range(1, blocks)], tap_spec)
-        signals = [None] * blocks
         for parity, table in enumerate((inv_even, inv_odd)):
             chosen = [b for b in range(1, blocks) if b % 2 == parity]
             if not chosen:
@@ -365,13 +360,7 @@
                 [medium_out.at[:, parts[b]] for b in chosen],
             )
             for b, signal in zip(chosen, found):
-                signals[b] = signal
-        for pair in range(step // PAIR):
-            sides = end_states(signals[1:], falling[pair], pair, modes, mask)
-            for side, found in enumerate(sides):
-                at = pair * PAIR + side * ROWS
-                for k, end in enumerate(found):
-                    ends[k + 1, at : at + ROWS, :] = end
+                signals[:, parts[b]] = signal
 
     def body(section):
         pl.loop(0, share // step)(functools.partial(chunk, section))
@@ -379,20 +368,15 @@
     by_section(sec, body)
 
 
-def later_call(place, gates, swapped, inputs, taps, falling, tables, modes):
+def later_call(place, gates, swapped, inputs, taps, tables):
     share, tokens = inputs.shape
     window = taps.shape[1]
-    lanes = ROWS * modes
-    operands = [gates, swapped, inputs, taps, falling, *tables]
+    operands = [gates, swapped, inputs, taps, *tables]
     spec = jax.ShapeDtypeStruct((share, 2 * window), jnp.float32)
+    wide = jax.ShapeDtypeStruct((share, tokens), jnp.bfloat16)
     return pl.pallas_call(
-        functools.partial(later_kernel, modes, min(256, share)),
-        out_shape=(
-            jax.ShapeDtypeStruct((share, tokens), jnp.bfloat16),
-            jax.ShapeDtypeStruct((tokens // window, share, lanes), jnp.float32),
-            spec,
-            spec,
-        ),
+        functools.partial(later_kernel, min(256, share)),
+        out_shape=(wide, wide, spec, spec),
         in_specs=[SMEM_SPEC] * 2 + [VMEM_SPEC] * len(operands),
         out_specs=(VMEM_SPEC,) * 4,
         name="later",
@@ -418,8 +402,9 @@
     fwd_odd,
     inv_even,
     medium_before,
-    ends_before,
+    signals_before,
     medium_all,
+    signals_all,
     ends_all,
     total_all,
     leaps_all,
@@ -443,7 +428,7 @@
             [before + rows_at(edge_spec_all, step, i)[...]],
             rows_at(tap_spec_all, step, i)[...],
         )
-        signals = finish_medium(
+        (signal,) = finish_medium(
             mixed,
             inv_even,
             [first[0, :, part]],
@@ -451,16 +436,21 @@
             [rows_at(inputs_all, step, i)[:, part]],
             [rows_at(medium_all, step, i).at[:, part]],
         )
+        signals = rows_at(signals_all, step, i)
+        signals[:, part] = signal
+        members = [signal] + [
+            signals[:, b * window : (b + 1) * window] for b in range(1, ends.shape[0])
+        ]
         sums = []
         for pair in range(step // PAIR):
-            sides = end_states(signals, falling[pair], pair, modes, mask)
-            for side, (end,) in enumerate(sides):
+            sides = end_states(members, falling[pair], pair, modes, mask)
+            for side, found in enumerate(sides):
                 at = pair * PAIR + side * ROWS
                 leap = spread(leaps, 2 * pair + side)
-                ends[0, at : at + ROWS, :] = end
-                state = end
-                for k in range(1, ends.shape[0]):
-                    state = state * leap + ends[k, at : at + ROWS, :]
+                state = None
+                for b, end in enumerate(found):
+                    ends[b, at : at + ROWS, :] = end
+                    state = end if state is None else state * leap + end
                 sums.append(jnp.sum(state, axis=0, keepdims=True))
         total = rows_at(total_all, step // ROWS, i)
         total[...] = jnp.concatenate(sums, axis=0).astype(total.dtype)
@@ -472,21 +462,23 @@
 
 
 def first_call(
-    place, gates, swapped, inputs, halos, rates, falling, specs, tables, medium, ends, modes
+    place, gates, swapped, inputs, halos, rates, falling, specs, tables, medium, signals, modes
 ):
     share, tokens = inputs.shape
+    window = halos[0].shape[1]
     lanes = ROWS * modes
     small = (share // ROWS, lanes)
-    operands = [gates, swapped, inputs, *halos, rates, falling, *specs, *tables, medium, ends]
+    operands = [gates, swapped, inputs, *halos, rates, falling, *specs, *tables, medium, signals]
     return pl.pallas_call(
         functools.partial(first_kernel, modes, min(256, share)),
         out_shape=(
             jax.ShapeDtypeStruct(medium.shape, medium.dtype),
-            jax.ShapeDtypeStruct(ends.shape, ends.dtype),
+            jax.ShapeDtypeStruct(signals.shape, signals.dtype),
+            jax.ShapeDtypeStruct((tokens // window, share, lanes), jnp.float32),
             jax.ShapeDtypeStruct(small, jnp.bfloat16),
         ),
         in_specs=[SMEM_SPEC] * 2 + [VMEM_SPEC] * len(operands),
-        out_specs=(VMEM_SPEC,) * 3,
+        out_specs=(VMEM_SPEC,) * 4,
         scratch_shapes=[pltpu.VMEM(small, jnp.float32)],
         input_output_aliases={len(operands): 0, len(operands) + 1: 1},
         name="first",
@@ -497,36 +489,24 @@
 
 def within_kernel(
     step,
-    sec,
-    tok,
-    local_all,
-    remote_all,
-    inputs_all,
-    medium_all,
+    signals_all,
     response_all,
     fwd_h,
     fwd_l,
     inverse,
     out_all,
 ):
-    share, tokens = inputs_all.shape
+    share, tokens = signals_all.shape
     size = fwd_h.shape[0]
     half = size // 2
 
-    def chunk(section, i):
-        gate_in = rows_at((remote_all if section == 0 else local_all).at[1], step, i)
-        inputs, gated_medium = rows_at(inputs_all, step, i), rows_at(medium_all, step, i)
+    def chunk(i):
+        signals = rows_at(signals_all, step, i)
         response, out = rows_at(response_all, step, i), rows_at(out_all, step, i)
         channels = step
         real, imag = response[:, :half], response[:, half:]
         parts = [slice(k * size, (k + 1) * size) for k in range(tokens // size)]
-        signals = []
-        for part in parts:
-            stream = inputs[:, part].astype(jnp.float32) + gated_medium[:, part].astype(
-                jnp.float32
-            )
-            signals.append((gate_in[:, part].astype(jnp.float32) * stream).astype(jnp.bfloat16))
-        signal = jnp.concatenate(signals, axis=0)
+        signal = jnp.concatenate([signals[:, part] for part in parts], axis=0)
         spec = dot_f32(signal, fwd_h[...]) + dot_f32(signal, fwd_l[...])
         filtered = []
         for k in range(len(parts)):
@@ -541,24 +521,21 @@
         for k, part in enumerate(parts):
             out[:, part] = found[k * channels : (k + 1) * channels]
 
-    def body(section):
-        pl.loop(0, share // step)(functools.partial(chunk, section))
-
-    by_section(sec, body)
-
-
-def within_call(place, gates, swapped, inputs, medium, response, tables):
-    share, tokens = inputs.shape
-    operands = [gates, swapped, inputs, medium, response, *tables]
+    pl.loop(0, share // step)(chunk)
+
+
+def within_call(signals, response, tables):
+    share, tokens = signals.shape
+    operands = [signals, response, *tables]
     return pl.pallas_call(
         functools.partial(within_kernel, min(WITHIN_STEP, share)),
         out_shape=jax.ShapeDtypeStruct((share, tokens), jnp.float32),
-        in_specs=[SMEM_SPEC] * 2 + [VMEM_SPEC] * len(operands),
+        in_specs=[VMEM_SPEC] * len(operands),
         out_specs=VMEM_SPEC,
         name="within",
         cost_estimate=cost(share, tokens, 1500),
         compiler_params=COMPILER,
-    )(*place, *operands)
+    )(*operands)
 
 
 def output_kernel(
@@ -582,7 +559,7 @@
     *rest,
 ):
     arrived = rest[:count]
-    (result, send, leaps_all, scales_all, shares_all, starts_all, mixed, done) = rest[-8:]
+    (result, send, keep, leaps_all, scales_all, shares_all, starts_all, done) = rest[-8:]
     part_rows, tokens = send.shape
     base = first // step
     groups = pl.ds(first // ROWS, part_rows // ROWS)
@@ -644,16 +621,12 @@
     def body(section):
         target = result.at[0, pl.ds(section * share + first, part_rows), :]
         source = medium_all.at[pl.ds(first, part_rows), :]
-        early = pltpu.make_async_copy(source, target if section == 0 else send, done.at[0])
-        early.start()
+        copy = pltpu.make_async_copy(source, send if section else target, done)
+        copy.start()
         pl.loop(0, part_rows // step)(
-            functools.partial(chunk, section, mixed if section else send)
+            functools.partial(chunk, section, keep if section else send)
         )
-        if section == 1:
-            late = pltpu.make_async_copy(mixed, target, done.at[1])
-            late.start()
-            late.wait()
-        early.wait()
+        copy.wait()
 
     by_section(sec, body)
 
@@ -680,11 +653,11 @@
             half * part_rows,
             share,
         ),
-        out_shape=(result, jax.ShapeDtypeStruct((part_rows, tokens), jnp.bfloat16)),
+        out_shape=(result,) + (jax.ShapeDtypeStruct((part_rows, tokens), jnp.bfloat16),) * 2,
         in_specs=[SMEM_SPEC] * 2 + [VMEM_SPEC] * len(operands) + [ANY_SPEC] * len(chained),
-        out_specs=(ANY_SPEC, VMEM_SPEC),
+        out_specs=(ANY_SPEC, VMEM_SPEC, VMEM_SPEC),
         scratch_shapes=[pltpu.VMEM(small, jnp.float32)] * 4
-        + [pltpu.VMEM((part_rows, tokens), jnp.bfloat16), pltpu.SemaphoreType.DMA((2,))],
+        + [pltpu.SemaphoreType.DMA],
         input_output_aliases={2 + len(operands): 0} if chained else {},
         name="output",
         cost_estimate=cost(part_rows, tokens, 1500),
@@ -692,27 +665,37 @@
     )(*place, *operands, *chained)
 
 
-def place_kernel(first, share, sec, tok, own, received, out, done):
+def place_kernel(first, share, sec, tok, before, received, keep, out, done):
     rows = received.shape[0]
-    other = pl.ds(pl.multiple_of((1 - sec[0]) * share + first, rows), rows)
-    copy = pltpu.make_async_copy(received, out.at[0, other, :], done)
-    copy.start()
-    copy.wait()
-
-
-def place_call(place, half, own, received):
+
+    def target(section):
+        return out.at[0, pl.ds(pl.multiple_of(section * share + first, rows), rows), :]
+
+    foreign = pltpu.make_async_copy(received, target(1 - sec[0]), done.at[0])
+    foreign.start()
+
+    @pl.when(sec[0] == 1)
+    def _():
+        own = pltpu.make_async_copy(keep, target(1), done.at[1])
+        own.start()
+        own.wait()
+
+    foreign.wait()
+
+
+def place_call(place, half, before, received, keep):
     rows, tokens = received.shape
     return pl.pallas_call(
-        functools.partial(place_kernel, half * rows, own.shape[1] // 2),
-        out_shape=jax.ShapeDtypeStruct(own.shape, own.dtype),
-        in_specs=[SMEM_SPEC] * 2 + [ANY_SPEC, VMEM_SPEC],
+        functools.partial(place_kernel, half * rows, before.shape[1] // 2),
+        out_shape=jax.ShapeDtypeStruct(before.shape, before.dtype),
+        in_specs=[SMEM_SPEC] * 2 + [ANY_SPEC, VMEM_SPEC, VMEM_SPEC],
         out_specs=ANY_SPEC,
-        scratch_shapes=[pltpu.SemaphoreType.DMA],
+        scratch_shapes=[pltpu.SemaphoreType.DMA((2,))],
         input_output_aliases={2: 0},
         name="placing",
         cost_estimate=cost(rows, tokens, 2),
         compiler_params=COMPILER,
-    )(*place, own, received)
+    )(*place, before, received, keep)
 
 
 def lend_kernel(sec, tok, gates, inputs, lent, low, high, gate_tail, input_tail, arrival):
@@ -804,10 +787,8 @@
     )
     response, rates, scales, rising, falling = built
     gates, inputs, taps = own
-    medium, ends, *specs = later_call(
-        place, gates, swapped, inputs, taps, falling, tables[:4], modes
-    )
-    medium, ends, total = first_call(
+    medium, signals, *specs = later_call(place, gates, swapped, inputs, taps, tables[:4])
+    medium, signals, ends, total = first_call(
         place,
         gates,
         swapped,
@@ -818,14 +799,14 @@
         specs,
         tables[1:3],
         medium,
-        ends,
+        signals,
         modes,
     )
     arrived = [onward(total, by) for by in range(1, lax.axis_size("tok"))]
-    within = within_call(place, gates, swapped, inputs, medium, response, tables[4:])
-    result, received = None, []
+    within = within_call(signals, response, tables[4:])
+    result, waiting = None, []
     for half in range(HALVES):
-        result, send = output_call(
+        result, send, keep = output_call(
             place,
             half,
             gates,
@@ -840,9 +821,9 @@
             arrived,
             result,
         )
-        received.append(ring(send, "section", 1))
-    for half in range(HALVES):
-        result = place_call(place, half, result, received[half])
+        waiting.append((ring(send, "section", 1), keep))
+    for half, (received, keep) in enumerate(waiting):
+        result = place_call(place, half, result, received, keep)
     return result
 
 

time: 31.5 us -> 29.8 us (0.946)
  Pallas kernels: 18.6 us -> 16.6 us
  starting transfers between devices: 9.77 us -> 10.2 us
    pallas_call x2, Pallas kernels: 3.74 us -> 2.15 us  [output_call(): pl.pallas_call(functools.partial(output_kernel, len(arrived), lanes // RO...]
    ppermute x3, waiting for transfers between devices: 1.08 us -> 0.55 us  [ring(): lax.ppermute(value, axis, [(i, (i + by) % peers) for i in range(peers)])]
    pallas_call x3, Pallas kernels: 4.68 us -> 4.16 us  [the longest x1 2.19 us: later_call(): pl.pallas_call(functools.partial(later_kernel, min(256, share)), out_shap...]
    ppermute x2, waiting for transfers between devices: 0.01 us -> 0.49 us  [edge_to(): return lax.ppermute(value, ('section', 'tok'), pairs)]
    ppermute x3, starting transfers between devices: 0.21 us -> 0.66 us  [ring(): lax.ppermute(value, axis, [(i, (i + by) % peers) for i in range(peers)])]
  transfers between devices with their start and end apart: 8 -> 8, of which waited for: 3 -> 6; matrix products, arithmetic and copies ran while one was open for 0% -> 0% of each run, Pallas kernels for 38% -> 35%
where the time goes in v7:
time: 29.8 us; the launch traced here: 29.4 us
  Pallas kernels  16.6 us (56%)
  starting transfers between devices  10.2 us (34%)
  waiting for transfers between devices  2.44 us (8%)
    ppermute x2, starting transfers between devices, edge_to(): return lax.ppermute(value, ('section', 'tok'), pairs)  4.94 us
    pallas_call x1, Pallas kernels, response_call(): pl.pallas_call(functools.partial(response_kernel, len(tables)), out_shape...  4.64 us
    ppermute x3, starting transfers between devices, onward(): return lax.ppermute(value, 'tok', pairs)  4.61 us
    pallas_call x1, Pallas kernels, first_call(): pl.pallas_call(functools.partial(first_kernel, modes, min(256, share)), o...  2.22 us
    pallas_call x1, Pallas kernels, later_call(): pl.pallas_call(functools.partial(later_kernel, min(256, share)), out_shap...  2.19 us
    pallas_call x2, Pallas kernels, output_call(): pl.pallas_call(functools.partial(output_kernel, len(arrived), lanes // RO...  2.15 us
    pallas_call x1, Pallas kernels, lend_call(): pl.pallas_call(lend_kernel, out_shape=(jax.ShapeDtypeStruct((2, share, to...  2.03 us
    pallas_call x2, Pallas kernels, place_call(): pl.pallas_call(functools.partial(place_kernel, half * rows, before.shape[...  1.97 us
  transfers between devices with their start and end apart: 8, of which 6 were waited for; matrix products, arithmetic and copies ran while one was open for 0% of the time, Pallas kernels for 35%

profile of v7, /device:TPU:1, one launch (start us, length us, event | category | flops | bytes accessed | tf_op | source)
XLA Modules:
  0.0 29.4 jit_solution(7873342314160511335)
XLA Ops:
  0.0 0.0 copy-start
  0.0 0.0 copy-start.1
  0.0 0.0 copy-start.2
  0.0 0.0 copy-start.3
  0.0 2.0 %lend.1 = (bf16[2,1024,512]{2,1,0:T(8,128)(2,1)S(1)}, bf16[1024,128]{1,0:T(8,128)(2,1)S(1)}, bf16[1024,128]{1,0:T(8,128)(2,1)S(1)}) custom-call(s32[1]{0:T(128)} %bitcast.sec, s32[1]{0:T(128)} %bitcast.1.tok, bf16[1,2,2048,512]{3,2,1,0:T(8,128)(2,1)} %gates.1, bf16[2048,512]{1,0:T(8,128)(2,1)} %inputs.1), custom_call_target="tpu_custom_call" | custom-call | flops 1048576 | bytes 6291456 | tf_op jit(solution)/shard_map/lend/pallas_call | solution.py:728
  2.1 0.1 collective-permute-start
  2.1 0.7 %collective-permute-start.1 = (bf16[1024,128]{1,0:T(8,128)(2,1)S(1)}, bf16[1024,128]{1,0:T(8,128)(2,1)S(1)}, u32[]{:S(2)}, u32[]{:S(2)}) collective-permute-start(bf16[1024,128]{1,0:T(8,128)(2,1)S(1)} %get-tuple-element.40), channel_id=1, source_target_pairs={{0,1},{1,2},{2,3},{3,0},{16,16},{17,17},{18,18},{19,19},{4,5},{5,6... | collective-permute-start | bytes 786440 | tf_op jit(solution)/shard_map/ppermute | solution.py:759
  2.8 4.3 %collective-permute-start.2 = (bf16[1024,128]{1,0:T(8,128)(2,1)S(1)}, bf16[1024,128]{1,0:T(8,128)(2,1)S(1)}, u32[]{:S(2)}, u32[]{:S(2)}) collective-permute-start(bf16[1024,128]{1,0:T(8,128)(2,1)S(1)} %get-tuple-element.41), channel_id=1, source_target_pairs={{0,17},{1,18},{2,19},{3,16},{16,0},{17,1},{18,2},{19,3},{4,21},{5,... | collective-permute-start | bytes 786440 | tf_op jit(solution)/shard_map/ppermute | solution.py:759
  7.1 0.0 copy-done
  7.1 0.0 copy-done.1
  7.1 0.0 copy-done.2
  7.1 0.0 copy-done.3
  7.1 4.6 %response.1 = (f32[1024,256]{1,0:T(8,128)S(1)}, f32[128,128]{1,0:T(8,128)S(1)}, f32[128,128]{1,0:T(8,128)S(1)}, bf16[64,128,256]{2,1,0:T(8,128)(2,1)S(1)}, bf16[...) custom-call(s32[1]{0:T(128)} %bitcast.sec, ...), custom_call_target="tpu_custom_call" | custom-call | flops 314572800 | bytes 6291456 | tf_op jit(solution)/shard_map/response/pallas_call | solution.py:240
  11.7 0.0 collective-permute-done.remote_all
  11.8 2.2 %later.1 = (bf16[1024,512]{1,0:T(8,128)(2,1)S(1)}, bf16[1024,512]{1,0:T(8,128)(2,1)S(1)}, f32[1024,256]{1,0:T(8,128)S(1)}, f32[1024,256]{1,0:T(8,128)S(1)}) custom-call(s32[1]{0:T(128)} %bitcast.sec, s32[1]{0:T(128)} %bitcast.1.tok, bf16[2,1024,512]{2,1,0:T(8,128)(2,1)S(1)} %get-tuple-element.37.local_all, ...), custom_call_target="tpu_custom_call" | custom-call | flops 786432000 | bytes 6291456 | tf_op jit(solution)/shard_map/later/pallas_call | solution.py:377
  14.0 0.0 collective-permute-done.1.halo_low
  14.0 0.5 %collective-permute-done.2.halo_high = bf16[1024,128]{1,0:T(8,128)(2,1)S(1)} collective-permute-done((bf16[1024,128]{1,0:T(8,128)(2,1)S(1)}, bf16[1024,128]{1,0:T(8,128)(2,1)S(1)}, u32[]{:S(2)}, u32[]{:S(2)}) %collective-permute-start.2) | collective-permute-done | bytes 262176 | tf_op jit(solution)/shard_map/ppermute | solution.py:759
  14.4 2.2 %first.1 = (bf16[1024,512]{1,0:T(8,128)(2,1)S(1)}, bf16[1024,512]{1,0:T(8,128)(2,1)S(1)}, f32[4,1024,128]{2,1,0:T(8,128)S(1)}, bf16[128,128]{1,0:T(8,128)(2,1)S(1)}) custom-call(s32[1]{0:T(128)} %bitcast.sec, s32[1]{0:T(128)} %bitcast.1.tok, bf16[2,1024,512]{2,1,0:T(8,128)(2,1)S(1)} %get-tuple-element.37.local_all, ...), custom_call_target="tpu_custom_call", output_to_operand_aliasing={{0}: (13, {}), {1}: (14, {})} | custom-call | flops 262144000 | bytes 6291456 | tf_op jit(solution)/shard_map/first/pallas_call | solution.py:472
  16.7 3.6 %collective-permute-start.5 = (bf16[128,128]{1,0:T(8,128)(2,1)S(1)}, bf16[128,128]{1,0:T(8,128)(2,1)S(1)}, u32[]{:S(2)}, u32[]{:S(2)}) collective-permute-start(bf16[128,128]{1,0:T(8,128)(2,1)S(1)} %get-tuple-element.62), channel_id=1, source_target_pairs={{0,3},{1,1},{2,2},{3,0},{4,7},{5,5},{6,6},{7,4},{8,11},{9,9},{10,1... | collective-permute-start | bytes 98312 | tf_op jit(solution)/shard_map/ppermute | solution.py:752
  20.3 0.1 collective-permute-start.4
  20.4 0.9 %collective-permute-start.3 = (bf16[128,128]{1,0:T(8,128)(2,1)S(1)}, bf16[128,128]{1,0:T(8,128)(2,1)S(1)}, u32[]{:S(2)}, u32[]{:S(2)}) collective-permute-start(bf16[128,128]{1,0:T(8,128)(2,1)S(1)} %get-tuple-element.62), channel_id=1, source_target_pairs={{0,1},{1,2},{2,3},{3,0},{4,5},{5,6},{6,7},{7,4},{8,9},{9,10},{10,1... | collective-permute-start | bytes 98312 | tf_op jit(solution)/shard_map/ppermute | solution.py:752
  21.3 1.4 %within.1.within_all = f32[1024,512]{1,0:T(8,128)S(1)} custom-call(bf16[1024,512]{1,0:T(8,128)(2,1)S(1)} %get-tuple-element.53.signals_all, f32[1024,256]{1,0:T(8,128)S(1)} %get-tuple-element.54.response_all, bf16[256,256]{1,0:T(8,128)(2,1)S(1)} %get-tuple-element.55.fwd_h, bf16[256,256]{1,0:T(8,128)(2,1)S(1)} %get-tuple-element.56.fwd_l, ...), custom_call_target="tpu_custom_call" | custom-call | flops 786432000 | bytes 6291456 | tf_op jit(solution)/shard_map/within/pallas_call | solution.py:530
  22.7 0.1 collective-permute-done.5.rest_2_
  22.8 0.9 %collective-permute-done.4.rest_1_ = bf16[128,128]{1,0:T(8,128)(2,1)S(1)} collective-permute-done((bf16[128,128]{1,0:T(8,128)(2,1)S(1)}, bf16[128,128]{1,0:T(8,128)(2,1)S(1)}, u32[]{:S(2)}, u32[]{:S(2)}) %collective-permute-start.4) | collective-permute-done | bytes 32800 | tf_op jit(solution)/shard_map/ppermute | solution.py:752
  23.7 0.4 %collective-permute-done.3.rest_0_ = bf16[128,128]{1,0:T(8,128)(2,1)S(1)} collective-permute-done((bf16[128,128]{1,0:T(8,128)(2,1)S(1)}, bf16[128,128]{1,0:T(8,128)(2,1)S(1)}, u32[]{:S(2)}, u32[]{:S(2)}) %collective-permute-start.3) | collective-permute-done | bytes 32800 | tf_op jit(solution)/shard_map/ppermute | solution.py:752
  24.1 1.1 %output.2 = (bf16[1,2048,512]{2,1,0:T(8,128)(2,1)}, bf16[512,512]{1,0:T(8,128)(2,1)S(1)}, bf16[512,512]{1,0:T(8,128)(2,1)S(1)}) custom-call(s32[1]{0:T(128)} %bitcast.sec, s32[1]{0:T(128)} %bitcast.1.tok, bf16[2,1024,512]{2,1,0:T(8,128)(2,1)S(1)} %get-tuple-element.37.local_all, bf16[2,1024,512]{2,1,0:T(8,128)(2,1)S(1)} %collective-permute-done.remote_all, ...), custom_call_target="tpu_custom_call" | custom-call | flops 393216000 | bytes 3145728 | tf_op jit(solution)/shard_map/output/pallas_call | solution.py:646
  25.2 0.1 collective-permute-start.6
  25.3 1.1 %output.3 = (bf16[1,2048,512]{2,1,0:T(8,128)(2,1)}, bf16[512,512]{1,0:T(8,128)(2,1)S(1)}, bf16[512,512]{1,0:T(8,128)(2,1)S(1)}) custom-call(s32[1]{0:T(128)} %bitcast.sec, s32[1]{0:T(128)} %bitcast.1.tok, bf16[2,1024,512]{2,1,0:T(8,128)(2,1)S(1)} %get-tuple-element.37.local_all, ...), custom_call_target="tpu_custom_call", output_to_operand_aliasing={{0}: (14, {})} | custom-call | flops 393216000 | bytes 3145728 | tf_op jit(solution)/shard_map/output/pallas_call | solution.py:646
  26.4 0.5 %collective-permute-start.7 = (bf16[512,512]{1,0:T(8,128)(2,1)S(1)}, bf16[512,512]{1,0:T(8,128)(2,1)S(1)}, u32[]{:S(2)}, u32[]{:S(2)}) collective-permute-start(bf16[512,512]{1,0:T(8,128)(2,1)S(1)} %get-tuple-element.67), channel_id=1, source_target_pairs={{0,16},{16,0},{1,17},{17,1},{2,18},{18,2},{3,19},{19,3},{4,20},{20... | collective-permute-start | bytes 1572872 | tf_op jit(solution)/shard_map/ppermute | solution.py:743
  26.9 0.3 collective-permute-done.6.received
  27.2 1.0 %placing.2.before = bf16[1,2048,512]{2,1,0:T(8,128)(2,1)} custom-call(s32[1]{0:T(128)} %bitcast.sec, s32[1]{0:T(128)} %bitcast.1.tok, bf16[1,2048,512]{2,1,0:T(8,128)(2,1)} %get-tuple-element.64.before, bf16[512,512]{1,0:T(8,128)(2,1)S(1)} %collective-permute-done.6.received, bf16[512,512]{1,0:T(8,128)(2,1)S(1)} %get-tuple-element.66.keep), custom_call_target="tpu_custom_call", output_to_operand_aliasing={{}: (2, {})} | custom-call | flops 524288 | bytes 3145728 | tf_op jit(solution)/shard_map/placing/pallas_call | solution.py:688
  28.2 0.3 collective-permute-done.7.received
  28.4 1.0 %placing.3 = bf16[1,2048,512]{2,1,0:T(8,128)(2,1)} custom-call(s32[1]{0:T(128)} %bitcast.sec, s32[1]{0:T(128)} %bitcast.1.tok, bf16[1,2048,512]{2,1,0:T(8,128)(2,1)} %placing.2.before, bf16[512,512]{1,0:T(8,128)(2,1)S(1)} %collective-permute-done.7.received, bf16[512,512]{1,0:T(8,128)(2,1)S(1)} %get-tuple-element.68.keep), custom_call_target="tpu_custom_call", output_to_operand_aliasing={{}: (2, {})} | custom-call | flops 524288 | bytes 3145728 | tf_op jit(solution)/shard_map/placing/pallas_call | solution.py:688
Async XLA Ops:
  0.0 7.1 %copy-start = (f32[2048,16]{0,1:T(8,128)S(1)}, f32[2048,16]{0,1:T(8,128)}, u32[]{:S(2)}) copy-start(f32[2048,16]{0,1:T(8,128)} %param.22) | copy-start | bytes 393220
  0.0 7.1 %copy-start.1 = (f32[2048,16]{0,1:T(8,128)S(1)}, f32[2048,16]{0,1:T(8,128)}, u32[]{:S(2)}) copy-start(f32[2048,16]{0,1:T(8,128)} %param.21) | copy-start | bytes 393220
  0.0 7.1 %copy-start.2 = (bf16[128,256]{1,0:T(8,128)(2,1)S(1)}, bf16[128,256]{1,0:T(8,128)(2,1)}, u32[]{:S(2)}) copy-start(bf16[128,256]{1,0:T(8,128)(2,1)} %constant.35.table_l) | copy-start | bytes 196612
  0.0 7.1 %copy-start.3 = (bf16[128,256]{1,0:T(8,128)(2,1)S(1)}, bf16[128,256]{1,0:T(8,128)(2,1)}, u32[]{:S(2)}) copy-start(bf16[128,256]{1,0:T(8,128)(2,1)} %constant.32.table_h) | copy-start | bytes 196612
  2.1 9.7 %collective-permute-start = (bf16[2,1024,512]{2,1,0:T(8,128)(2,1)S(1)}, bf16[2,1024,512]{2,1,0:T(8,128)(2,1)S(1)}, u32[]{:S(2)}, u32[]{:S(2)}) collective-permute-start(bf16[2,1024,512]{2,1,0:T(8,128)(2,1)S(1)} %get-tuple-element.38), channel_id=1, source_target_pairs={{0,16},{16,0},{1,17},{17,1},{2,18},{18,2},{3,19},{19,3},{4,20},{20... | collective-permute-start | bytes 6291464 | tf_op jit(solution)/shard_map/ppermute | solution.py:743
  2.1 11.8 %collective-permute-start.1 = (bf16[1024,128]{1,0:T(8,128)(2,1)S(1)}, bf16[1024,128]{1,0:T(8,128)(2,1)S(1)}, u32[]{:S(2)}, u32[]{:S(2)}) collective-permute-start(bf16[1024,128]{1,0:T(8,128)(2,1)S(1)} %get-tuple-element.40), channel_id=1, source_target_pairs={{0,1},{1,2},{2,3},{3,0},{16,16},{17,17},{18,18},{19,19},{4,5},{5,6... | collective-permute-start | bytes 786440 | tf_op jit(solution)/shard_map/ppermute | solution.py:759
  2.8 11.6 %collective-permute-start.2 = (bf16[1024,128]{1,0:T(8,128)(2,1)S(1)}, bf16[1024,128]{1,0:T(8,128)(2,1)S(1)}, u32[]{:S(2)}, u32[]{:S(2)}) collective-permute-start(bf16[1024,128]{1,0:T(8,128)(2,1)S(1)} %get-tuple-element.41), channel_id=1, source_target_pairs={{0,17},{1,18},{2,19},{3,16},{16,0},{17,1},{18,2},{19,3},{4,21},{5,... | collective-permute-start | bytes 786440 | tf_op jit(solution)/shard_map/ppermute | solution.py:759
  16.7 6.2 %collective-permute-start.5 = (bf16[128,128]{1,0:T(8,128)(2,1)S(1)}, bf16[128,128]{1,0:T(8,128)(2,1)S(1)}, u32[]{:S(2)}, u32[]{:S(2)}) collective-permute-start(bf16[128,128]{1,0:T(8,128)(2,1)S(1)} %get-tuple-element.62), channel_id=1, source_target_pairs={{0,3},{1,1},{2,2},{3,0},{4,7},{5,5},{6,6},{7,4},{8,11},{9,9},{10,1... | collective-permute-start | bytes 98312 | tf_op jit(solution)/shard_map/ppermute | solution.py:752
  20.3 3.4 %collective-permute-start.4 = (bf16[128,128]{1,0:T(8,128)(2,1)S(1)}, bf16[128,128]{1,0:T(8,128)(2,1)S(1)}, u32[]{:S(2)}, u32[]{:S(2)}) collective-permute-start(bf16[128,128]{1,0:T(8,128)(2,1)S(1)} %get-tuple-element.62), channel_id=1, source_target_pairs={{0,2},{1,3},{2,0},{3,1},{4,6},{5,7},{6,4},{7,5},{8,10},{9,11},{10,... | collective-permute-start | bytes 98312 | tf_op jit(solution)/shard_map/ppermute | solution.py:752
  20.4 3.7 %collective-permute-start.3 = (bf16[128,128]{1,0:T(8,128)(2,1)S(1)}, bf16[128,128]{1,0:T(8,128)(2,1)S(1)}, u32[]{:S(2)}, u32[]{:S(2)}) collective-permute-start(bf16[128,128]{1,0:T(8,128)(2,1)S(1)} %get-tuple-element.62), channel_id=1, source_target_pairs={{0,1},{1,2},{2,3},{3,0},{4,5},{5,6},{6,7},{7,4},{8,9},{9,10},{10,1... | collective-permute-start | bytes 98312 | tf_op jit(solution)/shard_map/ppermute | solution.py:752
  25.2 2.0 %collective-permute-start.6 = (bf16[512,512]{1,0:T(8,128)(2,1)S(1)}, bf16[512,512]{1,0:T(8,128)(2,1)S(1)}, u32[]{:S(2)}, u32[]{:S(2)}) collective-permute-start(bf16[512,512]{1,0:T(8,128)(2,1)S(1)} %get-tuple-element.65), channel_id=1, source_target_pairs={{0,16},{16,0},{1,17},{17,1},{2,18},{18,2},{3,19},{19,3},{4,20},{20... | collective-permute-start | bytes 1572872 | tf_op jit(solution)/shard_map/ppermute | solution.py:743
  26.4 2.1 %collective-permute-start.7 = (bf16[512,512]{1,0:T(8,128)(2,1)S(1)}, bf16[512,512]{1,0:T(8,128)(2,1)S(1)}, u32[]{:S(2)}, u32[]{:S(2)}) collective-permute-start(bf16[512,512]{1,0:T(8,128)(2,1)S(1)} %get-tuple-element.67), channel_id=1, source_target_pairs={{0,16},{16,0},{1,17},{17,1},{2,18},{18,2},{3,19},{19,3},{4,20},{20... | collective-permute-start | bytes 1572872 | tf_op jit(solution)/shard_map/ppermute | solution.py:743

commit v8 on v7

--- a/solution.py
+++ b/solution.py
@@ -64,6 +64,7 @@
 
 PAIR = 16
 WITHIN_STEP = 512
+STEP = 512
 HALVES = 2
 COMPILER = pltpu.CompilerParams(vmem_limit_bytes=16 << 20)
 
@@ -375,7 +376,7 @@
     spec = jax.ShapeDtypeStruct((share, 2 * window), jnp.float32)
     wide = jax.ShapeDtypeStruct((share, tokens), jnp.bfloat16)
     return pl.pallas_call(
-        functools.partial(later_kernel, min(256, share)),
+        functools.partial(later_kernel, min(STEP, share)),
         out_shape=(wide, wide, spec, spec),
         in_specs=[SMEM_SPEC] * 2 + [VMEM_SPEC] * len(operands),
         out_specs=(VMEM_SPEC,) * 4,
@@ -470,7 +471,7 @@
     small = (share // ROWS, lanes)
     operands = [gates, swapped, inputs, *halos, rates, falling, *specs, *tables, medium, signals]
     return pl.pallas_call(
-        functools.partial(first_kernel, modes, min(256, share)),
+        functools.partial(first_kernel, modes, min(STEP, share)),
         out_shape=(
             jax.ShapeDtypeStruct(medium.shape, medium.dtype),
             jax.ShapeDtypeStruct(signals.shape, signals.dtype),
@@ -573,8 +574,12 @@
     shares_all[...] = scale_all / (1.0 + leap_all)
     entering = jnp.zeros_like(slow)
     for k in range(count):
-        known = jnp.where(tok[0] > k, 1.0, 0.0)
-        entering = entering + arrived[k][groups, :].astype(jnp.float32) * (jnp.exp(-slow * (tokens * k)) * known)
+        gap = tok[0] - (tok[0] ^ (k + 1))
+        known = jnp.where(gap > 0, 1.0, 0.0)
+        distance = (tokens * jnp.maximum(gap - 1, 0)).astype(jnp.float32)
+        entering = entering + arrived[k][groups, :].astype(jnp.float32) * (
+            jnp.exp(-slow * distance) * known
+        )
     starts_all[...] = entering
 
     def chunk(section, out_all, i):
@@ -638,7 +643,7 @@
     lanes = rates.shape[1]
     window = rising.shape[1]
     part_rows = share // HALVES
-    step = min(256, part_rows)
+    step = min(STEP, part_rows)
     small = (part_rows // ROWS, lanes)
     operands = [gates, swapped, within, inputs, medium, rates, scales, rising, ends, *arrived]
     result = jax.ShapeDtypeStruct((1, 2 * share, tokens), jnp.bfloat16)
@@ -743,13 +748,9 @@
     return lax.ppermute(value, axis, [(i, (i + by) % peers) for i in range(peers)])
 
 
-def onward(value, by):
+def met(value, by):
     peers = lax.axis_size("tok")
-    sources, targets = range(peers - by, peers), range(by)
-    alone = [i for i in sources if i in targets]
-    spare = zip([i for i in sources if i not in alone], [i for i in targets if i not in alone])
-    pairs = [(i, i + by) for i in range(peers - by)] + [(i, i) for i in alone] + list(spare)
-    return lax.ppermute(value, "tok", pairs)
+    return lax.ppermute(value, "tok", [(i, i ^ by) for i in range(peers)])
 
 
 def edge_to(value, section):
@@ -802,7 +803,7 @@
         signals,
         modes,
     )
-    arrived = [onward(total, by) for by in range(1, lax.axis_size("tok"))]
+    arrived = [met(total, by) for by in range(1, lax.axis_size("tok"))]
     within = within_call(signals, response, tables[4:])
     result, waiting = None, []
     for half in range(HALVES):

time: 29.8 us -> 27.2 us (0.913)
  Pallas kernels: 16.6 us -> 15.1 us
  starting transfers between devices: 10.2 us -> 9.49 us
    ppermute x3, starting transfers between devices: 4.61 us -> 2.96 us  [met(): return lax.ppermute(value, 'tok', [(i, i ^ by) for i in range(peers)])]
    pallas_call x2, Pallas kernels: 4.41 us -> 3.18 us  [the longest x1 1.77 us: later_call(): pl.pallas_call(functools.partial(later_kernel, min(STEP, share)), out_sha...]
    ppermute x3, waiting for transfers between devices: 1.4 us -> 0.42 us  [met(): return lax.ppermute(value, 'tok', [(i, i ^ by) for i in range(peers)])]
    ppermute x3, starting transfers between devices: 0.66 us -> 1.59 us  [ring(): lax.ppermute(value, axis, [(i, (i + by) % peers) for i in range(peers)])]
    ppermute x2, waiting for transfers between devices: 0.49 us -> 0.91 us  [edge_to(): return lax.ppermute(value, ('section', 'tok'), pairs)]
    ppermute x3, waiting for transfers between devices: 0.55 us -> 0.91 us  [ring(): lax.ppermute(value, axis, [(i, (i + by) % peers) for i in range(peers)])]
  transfers between devices with their start and end apart: 8 -> 8, of which waited for: 6 -> 5; matrix products, arithmetic and copies ran while one was open for 0% -> 0% of each run, Pallas kernels for 35% -> 36%
where the time goes in v8:
time: 27.2 us; the launch traced here: 27 us
  Pallas kernels  15.1 us (56%)
  starting transfers between devices  9.49 us (35%)
  waiting for transfers between devices  2.23 us (8%)
    ppermute x2, starting transfers between devices, edge_to(): return lax.ppermute(value, ('section', 'tok'), pairs)  4.94 us
    pallas_call x1, Pallas kernels, response_call(): pl.pallas_call(functools.partial(response_kernel, len(tables)), out_shape...  4.64 us
    ppermute x3, starting transfers between devices, met(): return lax.ppermute(value, 'tok', [(i, i ^ by) for i in range(peers)])  2.96 us
    pallas_call x1, Pallas kernels, lend_call(): pl.pallas_call(lend_kernel, out_shape=(jax.ShapeDtypeStruct((2, share, to...  2.03 us
    pallas_call x2, Pallas kernels, place_call(): pl.pallas_call(functools.partial(place_kernel, half * rows, before.shape[...  1.97 us
    pallas_call x2, Pallas kernels, output_call(): pl.pallas_call(functools.partial(output_kernel, len(arrived), lanes // RO...  1.93 us
    pallas_call x1, Pallas kernels, later_call(): pl.pallas_call(functools.partial(later_kernel, min(STEP, share)), out_sha...  1.77 us
    ppermute x3, starting transfers between devices, ring(): lax.ppermute(value, axis, [(i, (i + by) % peers) for i in range(peers)])  1.59 us
  transfers between devices with their start and end apart: 8, of which 5 were waited for; matrix products, arithmetic and copies ran while one was open for 0% of the time, Pallas kernels for 36%

profile of v8, /device:TPU:1, one launch (start us, length us, event | category | flops | bytes accessed | tf_op | source)
XLA Modules:
  0.0 27.0 jit_solution(14005027755745951858)
XLA Ops:
  0.0 0.0 copy-start
  0.0 0.0 copy-start.1
  0.0 0.0 copy-start.2
  0.0 0.0 copy-start.3
  0.0 2.0 %lend.1 = (bf16[2,1024,512]{2,1,0:T(8,128)(2,1)S(1)}, bf16[1024,128]{1,0:T(8,128)(2,1)S(1)}, bf16[1024,128]{1,0:T(8,128)(2,1)S(1)}) custom-call(s32[1]{0:T(128)} %bitcast.sec, s32[1]{0:T(128)} %bitcast.1.tok, bf16[1,2,2048,512]{3,2,1,0:T(8,128)(2,1)} %gates.1, bf16[2048,512]{1,0:T(8,128)(2,1)} %inputs.1), custom_call_target="tpu_custom_call" | custom-call | flops 1048576 | bytes 6291456 | tf_op jit(solution)/shard_map/lend/pallas_call | solution.py:733
  2.1 0.1 collective-permute-start
  2.1 0.7 %collective-permute-start.1 = (bf16[1024,128]{1,0:T(8,128)(2,1)S(1)}, bf16[1024,128]{1,0:T(8,128)(2,1)S(1)}, u32[]{:S(2)}, u32[]{:S(2)}) collective-permute-start(bf16[1024,128]{1,0:T(8,128)(2,1)S(1)} %get-tuple-element.40), channel_id=1, source_target_pairs={{0,1},{1,2},{2,3},{3,0},{16,16},{17,17},{18,18},{19,19},{4,5},{5,6... | collective-permute-start | bytes 786440 | tf_op jit(solution)/shard_map/ppermute | solution.py:760
  2.8 4.3 %collective-permute-start.2 = (bf16[1024,128]{1,0:T(8,128)(2,1)S(1)}, bf16[1024,128]{1,0:T(8,128)(2,1)S(1)}, u32[]{:S(2)}, u32[]{:S(2)}) collective-permute-start(bf16[1024,128]{1,0:T(8,128)(2,1)S(1)} %get-tuple-element.41), channel_id=1, source_target_pairs={{0,17},{1,18},{2,19},{3,16},{16,0},{17,1},{18,2},{19,3},{4,21},{5,... | collective-permute-start | bytes 786440 | tf_op jit(solution)/shard_map/ppermute | solution.py:760
  7.1 0.0 copy-done
  7.1 0.0 copy-done.1
  7.1 0.0 copy-done.2
  7.1 0.0 copy-done.3
  7.1 4.6 %response.1 = (f32[1024,256]{1,0:T(8,128)S(1)}, f32[128,128]{1,0:T(8,128)S(1)}, f32[128,128]{1,0:T(8,128)S(1)}, bf16[64,128,256]{2,1,0:T(8,128)(2,1)S(1)}, bf16[...) custom-call(s32[1]{0:T(128)} %bitcast.sec, ...), custom_call_target="tpu_custom_call" | custom-call | flops 314572800 | bytes 6291456 | tf_op jit(solution)/shard_map/response/pallas_call | solution.py:241
  11.7 0.0 collective-permute-done.remote_all
  11.8 1.8 %later.1 = (bf16[1024,512]{1,0:T(8,128)(2,1)S(1)}, bf16[1024,512]{1,0:T(8,128)(2,1)S(1)}, f32[1024,256]{1,0:T(8,128)S(1)}, f32[1024,256]{1,0:T(8,128)S(1)}) custom-call(s32[1]{0:T(128)} %bitcast.sec, s32[1]{0:T(128)} %bitcast.1.tok, bf16[2,1024,512]{2,1,0:T(8,128)(2,1)S(1)} %get-tuple-element.37.local_all, ...), custom_call_target="tpu_custom_call" | custom-call | flops 786432000 | bytes 6291456 | tf_op jit(solution)/shard_map/later/pallas_call | solution.py:378
  13.5 0.0 collective-permute-done.1.halo_low
  13.5 0.9 %collective-permute-done.2.halo_high = bf16[1024,128]{1,0:T(8,128)(2,1)S(1)} collective-permute-done((bf16[1024,128]{1,0:T(8,128)(2,1)S(1)}, bf16[1024,128]{1,0:T(8,128)(2,1)S(1)}, u32[]{:S(2)}, u32[]{:S(2)}) %collective-permute-start.2) | collective-permute-done | bytes 262176 | tf_op jit(solution)/shard_map/ppermute | solution.py:760
  14.4 1.4 %first.1 = (bf16[1024,512]{1,0:T(8,128)(2,1)S(1)}, bf16[1024,512]{1,0:T(8,128)(2,1)S(1)}, f32[4,1024,128]{2,1,0:T(8,128)S(1)}, bf16[128,128]{1,0:T(8,128)(2,1)S(1)}) custom-call(s32[1]{0:T(128)} %bitcast.sec, s32[1]{0:T(128)} %bitcast.1.tok, bf16[2,1024,512]{2,1,0:T(8,128)(2,1)S(1)} %get-tuple-element.37.local_all, ...), custom_call_target="tpu_custom_call", output_to_operand_aliasing={{0}: (13, {}), {1}: (14, {})} | custom-call | flops 262144000 | bytes 6291456 | tf_op jit(solution)/shard_map/first/pallas_call | solution.py:473
  15.9 1.8 %collective-permute-start.5 = (bf16[128,128]{1,0:T(8,128)(2,1)S(1)}, bf16[128,128]{1,0:T(8,128)(2,1)S(1)}, u32[]{:S(2)}, u32[]{:S(2)}) collective-permute-start(bf16[128,128]{1,0:T(8,128)(2,1)S(1)} %get-tuple-element.62), channel_id=1, source_target_pairs={{0,3},{1,2},{2,1},{3,0},{4,7},{5,6},{6,5},{7,4},{8,11},{9,10},{10,... | collective-permute-start | bytes 98312 | tf_op jit(solution)/shard_map/ppermute | solution.py:753
  17.7 0.2 collective-permute-start.4
  17.9 0.9 %collective-permute-start.3 = (bf16[128,128]{1,0:T(8,128)(2,1)S(1)}, bf16[128,128]{1,0:T(8,128)(2,1)S(1)}, u32[]{:S(2)}, u32[]{:S(2)}) collective-permute-start(bf16[128,128]{1,0:T(8,128)(2,1)S(1)} %get-tuple-element.62), channel_id=1, source_target_pairs={{0,1},{1,0},{2,3},{3,2},{4,5},{5,4},{6,7},{7,6},{8,9},{9,8},{10,11... | collective-permute-start | bytes 98312 | tf_op jit(solution)/shard_map/ppermute | solution.py:753
  18.8 1.4 %within.1.within_all = f32[1024,512]{1,0:T(8,128)S(1)} custom-call(bf16[1024,512]{1,0:T(8,128)(2,1)S(1)} %get-tuple-element.53.signals_all, f32[1024,256]{1,0:T(8,128)S(1)} %get-tuple-element.54.response_all, bf16[256,256]{1,0:T(8,128)(2,1)S(1)} %get-tuple-element.55.fwd_h, bf16[256,256]{1,0:T(8,128)(2,1)S(1)} %get-tuple-element.56.fwd_l, ...), custom_call_target="tpu_custom_call" | custom-call | flops 786432000 | bytes 6291456 | tf_op jit(solution)/shard_map/within/pallas_call | solution.py:531
  20.2 0.0 collective-permute-done.5.rest_2_
  20.2 0.2 collective-permute-done.4.rest_1_
  20.4 0.2 collective-permute-done.3.rest_0_
  20.7 1.0 %output.2 = (bf16[1,2048,512]{2,1,0:T(8,128)(2,1)}, bf16[512,512]{1,0:T(8,128)(2,1)S(1)}, bf16[512,512]{1,0:T(8,128)(2,1)S(1)}) custom-call(s32[1]{0:T(128)} %bitcast.sec, s32[1]{0:T(128)} %bitcast.1.tok, bf16[2,1024,512]{2,1,0:T(8,128)(2,1)S(1)} %get-tuple-element.37.local_all, bf16[2,1024,512]{2,1,0:T(8,128)(2,1)S(1)} %collective-permute-done.remote_all, ...), custom_call_target="tpu_custom_call" | custom-call | flops 393216000 | bytes 3145728 | tf_op jit(solution)/shard_map/output/pallas_call | solution.py:651
  21.6 1.4 %collective-permute-start.6 = (bf16[512,512]{1,0:T(8,128)(2,1)S(1)}, bf16[512,512]{1,0:T(8,128)(2,1)S(1)}, u32[]{:S(2)}, u32[]{:S(2)}) collective-permute-start(bf16[512,512]{1,0:T(8,128)(2,1)S(1)} %get-tuple-element.65), channel_id=1, source_target_pairs={{0,16},{16,0},{1,17},{17,1},{2,18},{18,2},{3,19},{19,3},{4,20},{20... | collective-permute-start | bytes 1572872 | tf_op jit(solution)/shard_map/ppermute | solution.py:748
  23.1 1.0 %output.3 = (bf16[1,2048,512]{2,1,0:T(8,128)(2,1)}, bf16[512,512]{1,0:T(8,128)(2,1)S(1)}, bf16[512,512]{1,0:T(8,128)(2,1)S(1)}) custom-call(s32[1]{0:T(128)} %bitcast.sec, s32[1]{0:T(128)} %bitcast.1.tok, bf16[2,1024,512]{2,1,0:T(8,128)(2,1)S(1)} %get-tuple-element.37.local_all, ...), custom_call_target="tpu_custom_call", output_to_operand_aliasing={{0}: (14, {})} | custom-call | flops 393216000 | bytes 3145728 | tf_op jit(solution)/shard_map/output/pallas_call | solution.py:651
  24.1 0.1 collective-permute-start.7
  24.1 0.5 %collective-permute-done.6.received = bf16[512,512]{1,0:T(8,128)(2,1)S(1)} collective-permute-done((bf16[512,512]{1,0:T(8,128)(2,1)S(1)}, bf16[512,512]{1,0:T(8,128)(2,1)S(1)}, u32[]{:S(2)}, u32[]{:S(2)}) %collective-permute-start.6) | collective-permute-done | bytes 524320 | tf_op jit(solution)/shard_map/ppermute | solution.py:748
  24.6 1.0 %placing.2.before = bf16[1,2048,512]{2,1,0:T(8,128)(2,1)} custom-call(s32[1]{0:T(128)} %bitcast.sec, s32[1]{0:T(128)} %bitcast.1.tok, bf16[1,2048,512]{2,1,0:T(8,128)(2,1)} %get-tuple-element.64.before, bf16[512,512]{1,0:T(8,128)(2,1)S(1)} %collective-permute-done.6.received, bf16[512,512]{1,0:T(8,128)(2,1)S(1)} %get-tuple-element.66.keep), custom_call_target="tpu_custom_call", output_to_operand_aliasing={{}: (2, {})} | custom-call | flops 524288 | bytes 3145728 | tf_op jit(solution)/shard_map/placing/pallas_call | solution.py:693
  25.6 0.4 %collective-permute-done.7.received = bf16[512,512]{1,0:T(8,128)(2,1)S(1)} collective-permute-done((bf16[512,512]{1,0:T(8,128)(2,1)S(1)}, bf16[512,512]{1,0:T(8,128)(2,1)S(1)}, u32[]{:S(2)}, u32[]{:S(2)}) %collective-permute-start.7) | collective-permute-done | bytes 524320 | tf_op jit(solution)/shard_map/ppermute | solution.py:748
  26.0 1.0 %placing.3 = bf16[1,2048,512]{2,1,0:T(8,128)(2,1)} custom-call(s32[1]{0:T(128)} %bitcast.sec, s32[1]{0:T(128)} %bitcast.1.tok, bf16[1,2048,512]{2,1,0:T(8,128)(2,1)} %placing.2.before, bf16[512,512]{1,0:T(8,128)(2,1)S(1)} %collective-permute-done.7.received, bf16[512,512]{1,0:T(8,128)(2,1)S(1)} %get-tuple-element.68.keep), custom_call_target="tpu_custom_call", output_to_operand_aliasing={{}: (2, {})} | custom-call | flops 524288 | bytes 3145728 | tf_op jit(solution)/shard_map/placing/pallas_call | solution.py:693
Async XLA Ops:
  0.0 7.1 %copy-start = (f32[2048,16]{0,1:T(8,128)S(1)}, f32[2048,16]{0,1:T(8,128)}, u32[]{:S(2)}) copy-start(f32[2048,16]{0,1:T(8,128)} %param.22) | copy-start | bytes 393220
  0.0 7.1 %copy-start.1 = (f32[2048,16]{0,1:T(8,128)S(1)}, f32[2048,16]{0,1:T(8,128)}, u32[]{:S(2)}) copy-start(f32[2048,16]{0,1:T(8,128)} %param.21) | copy-start | bytes 393220
  0.0 7.1 %copy-start.2 = (bf16[128,256]{1,0:T(8,128)(2,1)S(1)}, bf16[128,256]{1,0:T(8,128)(2,1)}, u32[]{:S(2)}) copy-start(bf16[128,256]{1,0:T(8,128)(2,1)} %constant.35.table_l) | copy-start | bytes 196612
  0.0 7.1 %copy-start.3 = (bf16[128,256]{1,0:T(8,128)(2,1)S(1)}, bf16[128,256]{1,0:T(8,128)(2,1)}, u32[]{:S(2)}) copy-start(bf16[128,256]{1,0:T(8,128)(2,1)} %constant.32.table_h) | copy-start | bytes 196612
  2.1 9.7 %collective-permute-start = (bf16[2,1024,512]{2,1,0:T(8,128)(2,1)S(1)}, bf16[2,1024,512]{2,1,0:T(8,128)(2,1)S(1)}, u32[]{:S(2)}, u32[]{:S(2)}) collective-permute-start(bf16[2,1024,512]{2,1,0:T(8,128)(2,1)S(1)} %get-tuple-element.38), channel_id=1, source_target_pairs={{0,16},{16,0},{1,17},{17,1},{2,18},{18,2},{3,19},{19,3},{4,20},{20... | collective-permute-start | bytes 6291464 | tf_op jit(solution)/shard_map/ppermute | solution.py:748
  2.1 11.4 %collective-permute-start.1 = (bf16[1024,128]{1,0:T(8,128)(2,1)S(1)}, bf16[1024,128]{1,0:T(8,128)(2,1)S(1)}, u32[]{:S(2)}, u32[]{:S(2)}) collective-permute-start(bf16[1024,128]{1,0:T(8,128)(2,1)S(1)} %get-tuple-element.40), channel_id=1, source_target_pairs={{0,1},{1,2},{2,3},{3,0},{16,16},{17,17},{18,18},{19,19},{4,5},{5,6... | collective-permute-start | bytes 786440 | tf_op jit(solution)/shard_map/ppermute | solution.py:760
  2.8 11.6 %collective-permute-start.2 = (bf16[1024,128]{1,0:T(8,128)(2,1)S(1)}, bf16[1024,128]{1,0:T(8,128)(2,1)S(1)}, u32[]{:S(2)}, u32[]{:S(2)}) collective-permute-start(bf16[1024,128]{1,0:T(8,128)(2,1)S(1)} %get-tuple-element.41), channel_id=1, source_target_pairs={{0,17},{1,18},{2,19},{3,16},{16,0},{17,1},{18,2},{19,3},{4,21},{5,... | collective-permute-start | bytes 786440 | tf_op jit(solution)/shard_map/ppermute | solution.py:760
  15.9 4.4 %collective-permute-start.5 = (bf16[128,128]{1,0:T(8,128)(2,1)S(1)}, bf16[128,128]{1,0:T(8,128)(2,1)S(1)}, u32[]{:S(2)}, u32[]{:S(2)}) collective-permute-start(bf16[128,128]{1,0:T(8,128)(2,1)S(1)} %get-tuple-element.62), channel_id=1, source_target_pairs={{0,3},{1,2},{2,1},{3,0},{4,7},{5,6},{6,5},{7,4},{8,11},{9,10},{10,... | collective-permute-start | bytes 98312 | tf_op jit(solution)/shard_map/ppermute | solution.py:753
  17.7 2.8 %collective-permute-start.4 = (bf16[128,128]{1,0:T(8,128)(2,1)S(1)}, bf16[128,128]{1,0:T(8,128)(2,1)S(1)}, u32[]{:S(2)}, u32[]{:S(2)}) collective-permute-start(bf16[128,128]{1,0:T(8,128)(2,1)S(1)} %get-tuple-element.62), channel_id=1, source_target_pairs={{0,2},{1,3},{2,0},{3,1},{4,6},{5,7},{6,4},{7,5},{8,10},{9,11},{10,... | collective-permute-start | bytes 98312 | tf_op jit(solution)/shard_map/ppermute | solution.py:753
  17.9 2.8 %collective-permute-start.3 = (bf16[128,128]{1,0:T(8,128)(2,1)S(1)}, bf16[128,128]{1,0:T(8,128)(2,1)S(1)}, u32[]{:S(2)}, u32[]{:S(2)}) collective-permute-start(bf16[128,128]{1,0:T(8,128)(2,1)S(1)} %get-tuple-element.62), channel_id=1, source_target_pairs={{0,1},{1,0},{2,3},{3,2},{4,5},{5,4},{6,7},{7,6},{8,9},{9,8},{10,11... | collective-permute-start | bytes 98312 | tf_op jit(solution)/shard_map/ppermute | solution.py:753
  21.6 3.0 %collective-permute-start.6 = (bf16[512,512]{1,0:T(8,128)(2,1)S(1)}, bf16[512,512]{1,0:T(8,128)(2,1)S(1)}, u32[]{:S(2)}, u32[]{:S(2)}) collective-permute-start(bf16[512,512]{1,0:T(8,128)(2,1)S(1)} %get-tuple-element.65), channel_id=1, source_target_pairs={{0,16},{16,0},{1,17},{17,1},{2,18},{18,2},{3,19},{19,3},{4,20},{20... | collective-permute-start | bytes 1572872 | tf_op jit(solution)/shard_map/ppermute | solution.py:748
  24.1 2.0 %collective-permute-start.7 = (bf16[512,512]{1,0:T(8,128)(2,1)S(1)}, bf16[512,512]{1,0:T(8,128)(2,1)S(1)}, u32[]{:S(2)}, u32[]{:S(2)}) collective-permute-start(bf16[512,512]{1,0:T(8,128)(2,1)S(1)} %get-tuple-element.67), channel_id=1, source_target_pairs={{0,16},{16,0},{1,17},{17,1},{2,18},{18,2},{3,19},{19,3},{4,20},{20... | collective-permute-start | bytes 1572872 | tf_op jit(solution)/shard_map/ppermute | solution.py:748

commit v9 on v8

--- a/solution.py
+++ b/solution.py
@@ -63,7 +63,6 @@
 
 
 PAIR = 16
-WITHIN_STEP = 512
 STEP = 512
 HALVES = 2
 COMPILER = pltpu.CompilerParams(vmem_limit_bytes=16 << 20)
@@ -100,6 +99,11 @@
     if not isinstance(i, int):
         start = pl.multiple_of(start, step)
     return ref.at[(slice(None),) * axis + (pl.ds(start, step),)]
+
+
+def both_gates(local, remote, section, step, i):
+    mine, other = rows_at(local, step, i, 1), rows_at(remote, step, i, 1)
+    return (mine, other) if section == 0 else (other, mine)
 
 
 def by_section(sec, body):
@@ -160,7 +164,7 @@
     )
 
 
-def response_kernel(count, sec, tok, rates, residues, table_h, table_l, *rest):
+def response_kernel(count, window, sec, tok, rates, residues, *rest):
     gates, inputs, taps = rest[:3]
     tables = rest[3 : 3 + count]
     out, rate_rows, scale_rows, rising, falling = rest[3 + count : 8 + count]
@@ -168,9 +172,8 @@
     own_tables = rest[11 + count : 11 + 2 * count]
     tall, hops, scales, arrival = rest[11 + 2 * count :]
     share = out.shape[0]
+    step = tall.shape[0]
     modes = rates.shape[0]
-    window = table_h.shape[0]
-    step = tall.shape[0]
     first = pl.multiple_of(sec[0] * share, share)
     mine = pl.ds(first, share)
     pairs = [(gates.at[0, :, mine, :], own_gates)]
@@ -196,7 +199,7 @@
         hops[...] = jnp.exp(-slow * ROWS)
         scales[...] = scale / (1.0 + jnp.exp(-slow * window))
         up, down = rows_at(rising, step // PAIR, i), rows_at(falling, step // PAIR, i)
-        parts = []
+        own_out = rows_at(out, step, i)
         for pair in range(step // PAIR):
             both = two_sided(
                 jnp.where(mask, spread(scales, 2 * pair), 0.0),
@@ -208,13 +211,8 @@
             up[pair] = table
             down[pair] = both_powers(own_rates, hops, pair, window, True)
             found = dot_turned(both, table)
-            parts.append(found[:PAIR] + found[PAIR:])
-        response = jnp.concatenate(parts, axis=0)
-        high = response.astype(jnp.bfloat16)
-        low = (response - high.astype(jnp.float32)).astype(jnp.bfloat16)
-        rows_at(out, step, i)[...] = dot_f32(high, table_h[...]) + (
-            dot_f32(low, table_h[...]) + dot_f32(high, table_l[...])
-        )
+            out_rows = pl.ds(pair * PAIR, PAIR)
+            own_out[out_rows, :] = found[:PAIR] + found[PAIR:]
 
     for copy in copies:
         copy.wait()
@@ -222,14 +220,13 @@
 
 def response_call(place, rates, residues, gates, inputs, taps, tables, window, share):
     tokens = inputs.shape[1]
-    step = min(256, share)
+    step = min(STEP, share)
     modes = rates.shape[0]
     lanes = ROWS * modes
-    spectra = split_pair(turned_tables(window)[2])
     small = (step // ROWS, lanes)
     shape = lambda dims, kind=jnp.float32: jax.ShapeDtypeStruct(dims, kind)
     power_shape = shape((share // PAIR, window, 2 * lanes), jnp.bfloat16)
-    outs = [shape((share, 2 * window))] + [shape((share // ROWS, lanes))] * 2
+    outs = [shape((share, window))] + [shape((share // ROWS, lanes))] * 2
     outs += [power_shape] * 2
     outs += [
         shape((2, share, tokens), gates.dtype),
@@ -239,9 +236,9 @@
     outs += [shape(t.shape, t.dtype) for t in tables]
     staged = 3 + len(tables)
     found = pl.pallas_call(
-        functools.partial(response_kernel, len(tables)),
+        functools.partial(response_kernel, len(tables), window),
         out_shape=tuple(outs),
-        in_specs=[SMEM_SPEC] * 2 + [VMEM_SPEC] * 4 + [ANY_SPEC] * staged,
+        in_specs=[SMEM_SPEC] * 2 + [VMEM_SPEC] * 2 + [ANY_SPEC] * staged,
         out_specs=(VMEM_SPEC,) * len(outs),
         scratch_shapes=[
             pltpu.VMEM((step, modes), jnp.float32),
@@ -250,9 +247,9 @@
             pltpu.SemaphoreType.DMA((staged,)),
         ],
         name="response",
-        cost_estimate=cost(share, 4 * window, 600),
+        cost_estimate=cost(share, 4 * window, 900),
         compiler_params=COMPILER,
-    )(*place, rates, residues, *spectra, *parked(gates, inputs, taps, *tables))
+    )(*place, rates, residues, *parked(gates, inputs, taps, *tables))
     return found[:5], found[5:8], found[8:]
 
 
@@ -316,7 +313,7 @@
     sec,
     tok,
     local_all,
-    remote_all,
+    swapped,
     inputs_all,
     taps_all,
     fwd_even,
@@ -327,15 +324,26 @@
     signals_all,
     tap_spec_all,
     edge_spec_all,
+    remote_all,
+    arrival,
 ):
     share, tokens = inputs_all.shape
     window = taps_all.shape[1]
     blocks = tokens // window
     parts = [slice(b * window, (b + 1) * window) for b in range(blocks)]
 
+    def fetch(i):
+        source = pl.ds(pl.multiple_of(sec[0] * share + i * step, step), step)
+        return pltpu.make_async_copy(
+            swapped.at[:, source, :], rows_at(remote_all, step, i, 1), arrival.at[i]
+        )
+
+    for i in range(share // step):
+        fetch(i).start()
+
     def chunk(section, i):
-        first, second = (local_all, remote_all) if section == 0 else (remote_all, local_all)
-        first, second = rows_at(first, step, i, 1), rows_at(second, step, i, 1)
+        fetch(i).wait()
+        first, second = both_gates(local_all, remote_all, section, step, i)
         inputs = rows_at(inputs_all, step, i)
         medium_out, signals = rows_at(medium_all, step, i), rows_at(signals_all, step, i)
         sources = [first[1, :, part] * inputs[:, part] for part in parts]
@@ -372,14 +380,15 @@
 def later_call(place, gates, swapped, inputs, taps, tables):
     share, tokens = inputs.shape
     window = taps.shape[1]
-    operands = [gates, swapped, inputs, taps, *tables]
+    operands = [gates, *parked(swapped), inputs, taps, *tables]
     spec = jax.ShapeDtypeStruct((share, 2 * window), jnp.float32)
     wide = jax.ShapeDtypeStruct((share, tokens), jnp.bfloat16)
     return pl.pallas_call(
         functools.partial(later_kernel, min(STEP, share)),
-        out_shape=(wide, wide, spec, spec),
-        in_specs=[SMEM_SPEC] * 2 + [VMEM_SPEC] * len(operands),
-        out_specs=(VMEM_SPEC,) * 4,
+        out_shape=(wide, wide, spec, spec, jax.ShapeDtypeStruct(gates.shape, gates.dtype)),
+        in_specs=[SMEM_SPEC] * 2 + [VMEM_SPEC, ANY_SPEC] + [VMEM_SPEC] * (len(operands) - 2),
+        out_specs=(VMEM_SPEC,) * 5,
+        scratch_shapes=[pltpu.SemaphoreType.DMA((share // min(STEP, share),))],
         name="later",
         cost_estimate=cost(share, tokens, 1500),
         compiler_params=COMPILER,
@@ -417,8 +426,7 @@
     leaps_all[...] = jnp.exp(-rates[...] * window)
 
     def chunk(section, i):
-        first, second = (local_all, remote_all) if section == 0 else (remote_all, local_all)
-        first, second = rows_at(first, step, i, 1), rows_at(second, step, i, 1)
+        first, second = both_gates(local_all, remote_all, section, step, i)
         halo = rows_at(halo_low if section == 0 else halo_high, step, i)
         leaps = rows_at(leaps_all, step // ROWS, i)
         falling = rows_at(falling_all, step // PAIR, i)
@@ -471,7 +479,7 @@
     small = (share // ROWS, lanes)
     operands = [gates, swapped, inputs, *halos, rates, falling, *specs, *tables, medium, signals]
     return pl.pallas_call(
-        functools.partial(first_kernel, modes, min(STEP, share)),
+        functools.partial(first_kernel, modes, min(2 * STEP, share)),
         out_shape=(
             jax.ShapeDtypeStruct(medium.shape, medium.dtype),
             jax.ShapeDtypeStruct(signals.shape, signals.dtype),
@@ -495,6 +503,8 @@
     fwd_h,
     fwd_l,
     inverse,
+    table_h,
+    table_l,
     out_all,
 ):
     share, tokens = signals_all.shape
@@ -503,7 +513,12 @@
 
     def chunk(i):
         signals = rows_at(signals_all, step, i)
-        response, out = rows_at(response_all, step, i), rows_at(out_all, step, i)
+        taps, out = rows_at(response_all, step, i)[...], rows_at(out_all, step, i)
+        high = taps.astype(jnp.bfloat16)
+        low = (taps - high.astype(jnp.float32)).astype(jnp.bfloat16)
+        response = dot_f32(jnp.concatenate([high, low], axis=1), table_h[...]) + dot_f32(
+            high, table_l[...]
+        )
         channels = step
         real, imag = response[:, :half], response[:, half:]
         parts = [slice(k * size, (k + 1) * size) for k in range(tokens // size)]
@@ -529,7 +544,7 @@
     share, tokens = signals.shape
     operands = [signals, response, *tables]
     return pl.pallas_call(
-        functools.partial(within_kernel, min(WITHIN_STEP, share)),
+        functools.partial(within_kernel, min(2 * STEP, share)),
         out_shape=jax.ShapeDtypeStruct((share, tokens), jnp.float32),
         in_specs=[VMEM_SPEC] * len(operands),
         out_specs=VMEM_SPEC,
@@ -585,7 +600,7 @@
     def chunk(section, out_all, i):
         out = rows_at(out_all, step, i)
         at_all = base + i
-        gate_out = rows_at((remote_all if section == 0 else local_all).at[0], step, at_all)
+        gate_out = both_gates(local_all, remote_all, section, step, at_all)[1].at[0]
         inputs = rows_at(inputs_all, step, at_all)
         gated_medium = rows_at(medium_all, step, at_all)
         within = rows_at(within_all, step, at_all)
@@ -601,13 +616,13 @@
             for side in range(2):
                 group = 2 * pair + side
                 leap, scale = spread(leaps, group), spread(scales, group)
-                share = spread(shares, group)
+                portion = spread(shares, group)
                 state = jnp.where(mask, spread(starts, group), 0.0)
                 at = pair * PAIR + side * ROWS
                 lefts = []
                 for b in range(blocks):
                     end = ends[b, at : at + ROWS, :]
-                    lefts.append(state * scale + end * share)
+                    lefts.append(state * scale + end * portion)
                     state = state * leap + end
                 sides.append(lefts)
             left = jnp.concatenate(
@@ -703,44 +718,36 @@
     )(*place, before, received, keep)
 
 
-def lend_kernel(sec, tok, gates, inputs, lent, low, high, gate_tail, input_tail, arrival):
+def edge_kernel(gates, inputs, low, high, gate_tail, input_tail, arrival):
     share, window = low.shape
-    tokens = inputs.shape[1]
-    tail = pl.ds(tokens - window, window)
-    other = pl.ds(pl.multiple_of((1 - sec[0]) * share, share), share)
+    tail = pl.ds(inputs.shape[1] - window, window)
+    pairs = [(gates.at[0, 1, :, tail], gate_tail), (inputs.at[:, tail], input_tail)]
     copies = [
         pltpu.make_async_copy(source, target, arrival.at[k])
-        for k, (source, target) in enumerate(
-            [
-                (gates.at[0, 1, :, tail], gate_tail),
-                (inputs.at[:, tail], input_tail),
-                (gates.at[0, :, other, :], lent),
-            ]
-        )
+        for k, (source, target) in enumerate(pairs)
     ]
     for copy in copies:
         copy.start()
-    copies[0].wait()
-    copies[1].wait()
+    for copy in copies:
+        copy.wait()
     low[...] = gate_tail[:share, :] * input_tail[:share, :]
     high[...] = gate_tail[share:, :] * input_tail[share:, :]
-    copies[2].wait()
-
-
-def lend_call(place, gate_streams, inputs, window, share):
+
+
+def edge_call(gate_streams, inputs, window, share):
     channels, tokens = inputs.shape
     edge = jax.ShapeDtypeStruct((share, window), jnp.bfloat16)
     return pl.pallas_call(
-        lend_kernel,
-        out_shape=(jax.ShapeDtypeStruct((2, share, tokens), jnp.bfloat16), edge, edge),
-        in_specs=[SMEM_SPEC] * 2 + [ANY_SPEC] * 2,
-        out_specs=(VMEM_SPEC,) * 3,
+        edge_kernel,
+        out_shape=(edge, edge),
+        in_specs=[ANY_SPEC] * 2,
+        out_specs=(VMEM_SPEC,) * 2,
         scratch_shapes=[pltpu.VMEM((channels, window), jnp.bfloat16)] * 2
-        + [pltpu.SemaphoreType.DMA((3,))],
-        name="lend",
+        + [pltpu.SemaphoreType.DMA((2,))],
+        name="edge",
         cost_estimate=cost(share, tokens, 2),
         compiler_params=COMPILER,
-    )(*place, *parked(gate_streams, inputs))
+    )(*parked(gate_streams, inputs))
 
 
 def ring(value, axis, by):
@@ -769,12 +776,14 @@
     place = tuple(
         lax.axis_index(axis).astype(jnp.int32).reshape(1) for axis in ("section", "tok")
     )
-    lent, *edges = lend_call(place, gate_streams, inputs, window, share)
+    edges = edge_call(gate_streams, inputs, window, share)
     halos = [edge_to(edges[s], s) for s in range(2)]
-    swapped = ring(lent, "section", 1)
+    swapped = ring(gate_streams[0], "section", 1)
     forward, inverse = fourier_tables(window)
-    turned, back, _ = turned_tables(window)
+    turned, back, doubled = turned_tables(window)
     tables = [*forward, *inverse, *split_pair(turned), split_pair(back)[0]]
+    high, low = split_pair(doubled)
+    tables += [jnp.concatenate([high, high], axis=0), low]
     built, own, tables = response_call(
         place,
         decay_rates.T,
@@ -788,11 +797,13 @@
     )
     response, rates, scales, rising, falling = built
     gates, inputs, taps = own
-    medium, signals, *specs = later_call(place, gates, swapped, inputs, taps, tables[:4])
+    medium, signals, *specs, remote = later_call(
+        place, gates, swapped, inputs, taps, tables[:4]
+    )
     medium, signals, ends, total = first_call(
         place,
         gates,
-        swapped,
+        remote,
         inputs,
         halos,
         rates,
@@ -811,7 +822,7 @@
             place,
             half,
             gates,
-            swapped,
+            remote,
             within,
             inputs,
             medium,

time: 27.2 us -> 26.4 us (0.971)
  waiting for transfers between devices: 2.23 us -> 3.37 us
  starting transfers between devices: 9.49 us -> 8.53 us
  Pallas kernels: 15.1 us -> 14.3 us
    pallas_call x4, Pallas kernels: 9.48 us -> 7.35 us  [the longest x1 3.34 us: response_call(): pl.pallas_call(functools.partial(response_kernel, len(tables), window), o...]
    pallas_call x1, Pallas kernels: 1.77 us -> 3.01 us  [later_call(): pl.pallas_call(functools.partial(later_kernel, min(STEP, share)), out_sha...]
    ppermute x3, waiting for transfers between devices: 0.42 us -> 1.59 us  [met(): return lax.ppermute(value, 'tok', [(i, i ^ by) for i in range(peers)])]
    ppermute x3, starting transfers between devices: 1.59 us -> 0.62 us  [ring(): lax.ppermute(value, axis, [(i, (i + by) % peers) for i in range(peers)])]
  transfers between devices with their start and end apart: 8 -> 8, of which waited for: 5 -> 4; matrix products, arithmetic and copies ran while one was open for 0% -> 0% of each run, Pallas kernels for 36% -> 42%
where the time goes in v9:
time: 26.4 us; the launch traced here: 26.3 us
  Pallas kernels  14.3 us (54%)
  starting transfers between devices  8.53 us (32%)
  waiting for transfers between devices  3.37 us (13%)
    ppermute x2, starting transfers between devices, edge_to(): return lax.ppermute(value, ('section', 'tok'), pairs)  4.94 us
    pallas_call x1, Pallas kernels, response_call(): pl.pallas_call(functools.partial(response_kernel, len(tables), window), o...  3.34 us
    pallas_call x1, Pallas kernels, later_call(): pl.pallas_call(functools.partial(later_kernel, min(STEP, share)), out_sha...  3.01 us
    ppermute x3, starting transfers between devices, met(): return lax.ppermute(value, 'tok', [(i, i ^ by) for i in range(peers)])  2.96 us
    pallas_call x2, Pallas kernels, place_call(): pl.pallas_call(functools.partial(place_kernel, half * rows, before.shape[...  1.97 us
    pallas_call x2, Pallas kernels, output_call(): pl.pallas_call(functools.partial(output_kernel, len(arrived), lanes // RO...  1.93 us
    ppermute x3, waiting for transfers between devices, met(): return lax.ppermute(value, 'tok', [(i, i ^ by) for i in range(peers)])  1.59 us
    pallas_call x1, Pallas kernels, edge_call(): pl.pallas_call(edge_kernel, out_shape=(edge, edge), in_specs=[ANY_SPEC] *...  1.39 us
  transfers between devices with their start and end apart: 8, of which 4 were waited for; matrix products, arithmetic and copies ran while one was open for 0% of the time, Pallas kernels for 42%

profile of v9, /device:TPU:1, one launch (start us, length us, event | category | flops | bytes accessed | tf_op | source)
XLA Modules:
  0.0 26.3 jit_solution(14621542722511889825)
XLA Ops:
  0.0 0.0 copy-start
  0.0 0.0 copy-start.1
  0.0 0.0 collective-permute-start
  0.0 1.4 %edge.1 = (bf16[1024,128]{1,0:T(8,128)(2,1)S(1)}, bf16[1024,128]{1,0:T(8,128)(2,1)S(1)}) custom-call(bf16[1,2,2048,512]{3,2,1,0:T(8,128)(2,1)} %gates.1, bf16[2048,512]{1,0:T(8,128)(2,1)} %inputs.1), custom_call_target="tpu_custom_call" | custom-call | flops 1048576 | bytes 6291456 | tf_op jit(solution)/shard_map/edge/pallas_call | solution.py:740
  1.4 0.7 %collective-permute-start.1 = (bf16[1024,128]{1,0:T(8,128)(2,1)S(1)}, bf16[1024,128]{1,0:T(8,128)(2,1)S(1)}, u32[]{:S(2)}, u32[]{:S(2)}) collective-permute-start(bf16[1024,128]{1,0:T(8,128)(2,1)S(1)} %get-tuple-element.47), channel_id=1, source_target_pairs={{0,1},{1,2},{2,3},{3,0},{16,16},{17,17},{18,18},{19,19},{4,5},{5,6... | collective-permute-start | bytes 786440 | tf_op jit(solution)/shard_map/ppermute | solution.py:767
  2.1 4.3 %collective-permute-start.2 = (bf16[1024,128]{1,0:T(8,128)(2,1)S(1)}, bf16[1024,128]{1,0:T(8,128)(2,1)S(1)}, u32[]{:S(2)}, u32[]{:S(2)}) collective-permute-start(bf16[1024,128]{1,0:T(8,128)(2,1)S(1)} %get-tuple-element.48), channel_id=1, source_target_pairs={{0,17},{1,18},{2,19},{3,16},{16,0},{17,1},{18,2},{19,3},{4,21},{5,... | collective-permute-start | bytes 786440 | tf_op jit(solution)/shard_map/ppermute | solution.py:767
  6.4 0.0 copy-done
  6.4 0.0 copy-done.1
  6.4 3.3 %response.1 = (f32[1024,128]{1,0:T(8,128)S(1)}, f32[128,128]{1,0:T(8,128)S(1)}, f32[128,128]{1,0:T(8,128)S(1)}, bf16[64,128,256]{2,1,0:T(8,128)(2,1)S(1)}, bf16[...) custom-call(s32[1]{0:T(128)} %bitcast.sec, ...), custom_call_target="tpu_custom_call" | custom-call | flops 471859200 | bytes 6291456 | tf_op jit(solution)/shard_map/response/pallas_call | solution.py:238
  9.7 0.0 collective-permute-done.swapped
  9.7 3.0 %later.1 = (bf16[1024,512]{1,0:T(8,128)(2,1)S(1)}, bf16[1024,512]{1,0:T(8,128)(2,1)S(1)}, f32[1024,256]{1,0:T(8,128)S(1)}, f32[1024,256]{1,0:T(8,128)S(1)}, bf16[2,1024,512]{2,1,0:T(8,128)(2,1)S(1)}) custom-call(s32[1]{0:T(128)} %bitcast.sec, s32[1]{0:T(128)} %bitcast.1.tok, bf16[2,1024,512]{2,1,0:T(8,128)(2,1)S(1)} %get-tuple-element.39.local_all, ...), custom_call_target="tpu_custom_call" | custom-call | flops 786432000 | bytes 6291456 | tf_op jit(solution)/shard_map/later/pallas_call | solution.py:386
  12.7 0.0 collective-permute-done.1.halo_low
  12.8 1.0 %collective-permute-done.2.halo_high = bf16[1024,128]{1,0:T(8,128)(2,1)S(1)} collective-permute-done((bf16[1024,128]{1,0:T(8,128)(2,1)S(1)}, bf16[1024,128]{1,0:T(8,128)(2,1)S(1)}, u32[]{:S(2)}, u32[]{:S(2)}) %collective-permute-start.2) | collective-permute-done | bytes 262176 | tf_op jit(solution)/shard_map/ppermute | solution.py:767
  13.7 1.3 %first.1 = (bf16[1024,512]{1,0:T(8,128)(2,1)S(1)}, bf16[1024,512]{1,0:T(8,128)(2,1)S(1)}, f32[4,1024,128]{2,1,0:T(8,128)S(1)}, bf16[128,128]{1,0:T(8,128)(2,1)S(1)}) custom-call(s32[1]{0:T(128)} %bitcast.sec, s32[1]{0:T(128)} %bitcast.1.tok, bf16[2,1024,512]{2,1,0:T(8,128)(2,1)S(1)} %get-tuple-element.39.local_all, ...), custom_call_target="tpu_custom_call", output_to_operand_aliasing={{0}: (13, {}), {1}: (14, {})} | custom-call | flops 262144000 | bytes 6291456 | tf_op jit(solution)/shard_map/first/pallas_call | solution.py:481
  15.0 0.8 %collective-permute-start.3 = (bf16[128,128]{1,0:T(8,128)(2,1)S(1)}, bf16[128,128]{1,0:T(8,128)(2,1)S(1)}, u32[]{:S(2)}, u32[]{:S(2)}) collective-permute-start(bf16[128,128]{1,0:T(8,128)(2,1)S(1)} %get-tuple-element.66), channel_id=1, source_target_pairs={{0,1},{1,0},{2,3},{3,2},{4,5},{5,4},{6,7},{7,6},{8,9},{9,8},{10,11... | collective-permute-start | bytes 98312 | tf_op jit(solution)/shard_map/ppermute | solution.py:760
  15.8 1.2 %collective-permute-start.4 = (bf16[128,128]{1,0:T(8,128)(2,1)S(1)}, bf16[128,128]{1,0:T(8,128)(2,1)S(1)}, u32[]{:S(2)}, u32[]{:S(2)}) collective-permute-start(bf16[128,128]{1,0:T(8,128)(2,1)S(1)} %get-tuple-element.66), channel_id=1, source_target_pairs={{0,2},{1,3},{2,0},{3,1},{4,6},{5,7},{6,4},{7,5},{8,10},{9,11},{10,... | collective-permute-start | bytes 98312 | tf_op jit(solution)/shard_map/ppermute | solution.py:760
  17.1 0.9 %collective-permute-start.5 = (bf16[128,128]{1,0:T(8,128)(2,1)S(1)}, bf16[128,128]{1,0:T(8,128)(2,1)S(1)}, u32[]{:S(2)}, u32[]{:S(2)}) collective-permute-start(bf16[128,128]{1,0:T(8,128)(2,1)S(1)} %get-tuple-element.66), channel_id=1, source_target_pairs={{0,3},{1,2},{2,1},{3,0},{4,7},{5,6},{6,5},{7,4},{8,11},{9,10},{10,... | collective-permute-start | bytes 98312 | tf_op jit(solution)/shard_map/ppermute | solution.py:760
  18.0 1.4 %within.1.within_all = f32[1024,512]{1,0:T(8,128)S(1)} custom-call(bf16[1024,512]{1,0:T(8,128)(2,1)S(1)} %get-tuple-element.55.signals_all, f32[1024,128]{1,0:T(8,128)S(1)} %get-tuple-element.56.response_all, bf16[256,256]{1,0:T(8,128)(2,1)S(1)} %get-tuple-element.57.fwd_h, bf16[256,256]{1,0:T(8,128)(2,1)S(1)} %get-tuple-element.58.fwd_l, ...), custom_call_target="tpu_custom_call" | custom-call | flops 786432000 | bytes 6291456 | tf_op jit(solution)/shard_map/within/pallas_call | solution.py:546
  19.3 0.0 collective-permute-done.3.rest_0_
  19.3 0.0 collective-permute-done.4.rest_1_
  19.3 1.6 %collective-permute-done.5.rest_2_ = bf16[128,128]{1,0:T(8,128)(2,1)S(1)} collective-permute-done((bf16[128,128]{1,0:T(8,128)(2,1)S(1)}, bf16[128,128]{1,0:T(8,128)(2,1)S(1)}, u32[]{:S(2)}, u32[]{:S(2)}) %collective-permute-start.5) | collective-permute-done | bytes 32800 | tf_op jit(solution)/shard_map/ppermute | solution.py:760
  20.9 1.0 %output.2 = (bf16[1,2048,512]{2,1,0:T(8,128)(2,1)}, bf16[512,512]{1,0:T(8,128)(2,1)S(1)}, bf16[512,512]{1,0:T(8,128)(2,1)S(1)}) custom-call(s32[1]{0:T(128)} %bitcast.sec, s32[1]{0:T(128)} %bitcast.1.tok, bf16[2,1024,512]{2,1,0:T(8,128)(2,1)S(1)} %get-tuple-element.39.local_all, bf16[2,1024,512]{2,1,0:T(8,128)(2,1)S(1)} %get-tuple-element.46.remote_all, ...), custom_call_target="tpu_custom_call" | custom-call | flops 393216000 | bytes 3145728 | tf_op jit(solution)/shard_map/output/pallas_call | solution.py:666
  21.9 0.4 %collective-permute-start.6 = (bf16[512,512]{1,0:T(8,128)(2,1)S(1)}, bf16[512,512]{1,0:T(8,128)(2,1)S(1)}, u32[]{:S(2)}, u32[]{:S(2)}) collective-permute-start(bf16[512,512]{1,0:T(8,128)(2,1)S(1)} %get-tuple-element.69), channel_id=1, source_target_pairs={{0,16},{16,0},{1,17},{17,1},{2,18},{18,2},{3,19},{19,3},{4,20},{20... | collective-permute-start | bytes 1572872 | tf_op jit(solution)/shard_map/ppermute | solution.py:755
  22.3 1.0 %output.3 = (bf16[1,2048,512]{2,1,0:T(8,128)(2,1)}, bf16[512,512]{1,0:T(8,128)(2,1)S(1)}, bf16[512,512]{1,0:T(8,128)(2,1)S(1)}) custom-call(s32[1]{0:T(128)} %bitcast.sec, s32[1]{0:T(128)} %bitcast.1.tok, bf16[2,1024,512]{2,1,0:T(8,128)(2,1)S(1)} %get-tuple-element.39.local_all, ...), custom_call_target="tpu_custom_call", output_to_operand_aliasing={{0}: (14, {})} | custom-call | flops 393216000 | bytes 3145728 | tf_op jit(solution)/shard_map/output/pallas_call | solution.py:666
  23.3 0.2 collective-permute-start.7
  23.5 0.4 %collective-permute-done.6.received = bf16[512,512]{1,0:T(8,128)(2,1)S(1)} collective-permute-done((bf16[512,512]{1,0:T(8,128)(2,1)S(1)}, bf16[512,512]{1,0:T(8,128)(2,1)S(1)}, u32[]{:S(2)}, u32[]{:S(2)}) %collective-permute-start.6) | collective-permute-done | bytes 524320 | tf_op jit(solution)/shard_map/ppermute | solution.py:755
  23.9 1.0 %placing.2.before = bf16[1,2048,512]{2,1,0:T(8,128)(2,1)} custom-call(s32[1]{0:T(128)} %bitcast.sec, s32[1]{0:T(128)} %bitcast.1.tok, bf16[1,2048,512]{2,1,0:T(8,128)(2,1)} %get-tuple-element.68.before, bf16[512,512]{1,0:T(8,128)(2,1)S(1)} %collective-permute-done.6.received, bf16[512,512]{1,0:T(8,128)(2,1)S(1)} %get-tuple-element.70.keep), custom_call_target="tpu_custom_call", output_to_operand_aliasing={{}: (2, {})} | custom-call | flops 524288 | bytes 3145728 | tf_op jit(solution)/shard_map/placing/pallas_call | solution.py:708
  24.9 0.4 %collective-permute-done.7.received = bf16[512,512]{1,0:T(8,128)(2,1)S(1)} collective-permute-done((bf16[512,512]{1,0:T(8,128)(2,1)S(1)}, bf16[512,512]{1,0:T(8,128)(2,1)S(1)}, u32[]{:S(2)}, u32[]{:S(2)}) %collective-permute-start.7) | collective-permute-done | bytes 524320 | tf_op jit(solution)/shard_map/ppermute | solution.py:755
  25.3 1.0 %placing.3 = bf16[1,2048,512]{2,1,0:T(8,128)(2,1)} custom-call(s32[1]{0:T(128)} %bitcast.sec, s32[1]{0:T(128)} %bitcast.1.tok, bf16[1,2048,512]{2,1,0:T(8,128)(2,1)} %placing.2.before, bf16[512,512]{1,0:T(8,128)(2,1)S(1)} %collective-permute-done.7.received, bf16[512,512]{1,0:T(8,128)(2,1)S(1)} %get-tuple-element.72.keep), custom_call_target="tpu_custom_call", output_to_operand_aliasing={{}: (2, {})} | custom-call | flops 524288 | bytes 3145728 | tf_op jit(solution)/shard_map/placing/pallas_call | solution.py:708
Async XLA Ops:
  0.0 6.4 %copy-start = (f32[2048,16]{0,1:T(8,128)S(1)}, f32[2048,16]{0,1:T(8,128)}, u32[]{:S(2)}) copy-start(f32[2048,16]{0,1:T(8,128)} %param.22) | copy-start | bytes 393220
  0.0 6.4 %copy-start.1 = (f32[2048,16]{0,1:T(8,128)S(1)}, f32[2048,16]{0,1:T(8,128)}, u32[]{:S(2)}) copy-start(f32[2048,16]{0,1:T(8,128)} %param.21) | copy-start | bytes 393220
  0.0 9.7 %collective-permute-start = (bf16[2,2048,512]{2,1,0:T(8,128)(2,1)}, bf16[2,2048,512]{2,1,0:T(8,128)(2,1)}, u32[]{:S(2)}, u32[]{:S(2)}) collective-permute-start(bf16[2,2048,512]{2,1,0:T(8,128)(2,1)} %bitcast.7), channel_id=1, source_target_pairs={{0,16},{16,0},{1,17},{17,1},{2,18},{18,2},{3,19},{19,3},{4,20},{20... | collective-permute-start | bytes 12582920 | tf_op jit(solution)/shard_map/ppermute | solution.py:755
  1.4 11.3 %collective-permute-start.1 = (bf16[1024,128]{1,0:T(8,128)(2,1)S(1)}, bf16[1024,128]{1,0:T(8,128)(2,1)S(1)}, u32[]{:S(2)}, u32[]{:S(2)}) collective-permute-start(bf16[1024,128]{1,0:T(8,128)(2,1)S(1)} %get-tuple-element.47), channel_id=1, source_target_pairs={{0,1},{1,2},{2,3},{3,0},{16,16},{17,17},{18,18},{19,19},{4,5},{5,6... | collective-permute-start | bytes 786440 | tf_op jit(solution)/shard_map/ppermute | solution.py:767
  2.1 11.6 %collective-permute-start.2 = (bf16[1024,128]{1,0:T(8,128)(2,1)S(1)}, bf16[1024,128]{1,0:T(8,128)(2,1)S(1)}, u32[]{:S(2)}, u32[]{:S(2)}) collective-permute-start(bf16[1024,128]{1,0:T(8,128)(2,1)S(1)} %get-tuple-element.48), channel_id=1, source_target_pairs={{0,17},{1,18},{2,19},{3,16},{16,0},{17,1},{18,2},{19,3},{4,21},{5,... | collective-permute-start | bytes 786440 | tf_op jit(solution)/shard_map/ppermute | solution.py:767
  15.0 4.3 %collective-permute-start.3 = (bf16[128,128]{1,0:T(8,128)(2,1)S(1)}, bf16[128,128]{1,0:T(8,128)(2,1)S(1)}, u32[]{:S(2)}, u32[]{:S(2)}) collective-permute-start(bf16[128,128]{1,0:T(8,128)(2,1)S(1)} %get-tuple-element.66), channel_id=1, source_target_pairs={{0,1},{1,0},{2,3},{3,2},{4,5},{5,4},{6,7},{7,6},{8,9},{9,8},{10,11... | collective-permute-start | bytes 98312 | tf_op jit(solution)/shard_map/ppermute | solution.py:760
  15.8 3.5 %collective-permute-start.4 = (bf16[128,128]{1,0:T(8,128)(2,1)S(1)}, bf16[128,128]{1,0:T(8,128)(2,1)S(1)}, u32[]{:S(2)}, u32[]{:S(2)}) collective-permute-start(bf16[128,128]{1,0:T(8,128)(2,1)S(1)} %get-tuple-element.66), channel_id=1, source_target_pairs={{0,2},{1,3},{2,0},{3,1},{4,6},{5,7},{6,4},{7,5},{8,10},{9,11},{10,... | collective-permute-start | bytes 98312 | tf_op jit(solution)/shard_map/ppermute | solution.py:760
  17.1 3.9 %collective-permute-start.5 = (bf16[128,128]{1,0:T(8,128)(2,1)S(1)}, bf16[128,128]{1,0:T(8,128)(2,1)S(1)}, u32[]{:S(2)}, u32[]{:S(2)}) collective-permute-start(bf16[128,128]{1,0:T(8,128)(2,1)S(1)} %get-tuple-element.66), channel_id=1, source_target_pairs={{0,3},{1,2},{2,1},{3,0},{4,7},{5,6},{6,5},{7,4},{8,11},{9,10},{10,... | collective-permute-start | bytes 98312 | tf_op jit(solution)/shard_map/ppermute | solution.py:760
  21.9 2.0 %collective-permute-start.6 = (bf16[512,512]{1,0:T(8,128)(2,1)S(1)}, bf16[512,512]{1,0:T(8,128)(2,1)S(1)}, u32[]{:S(2)}, u32[]{:S(2)}) collective-permute-start(bf16[512,512]{1,0:T(8,128)(2,1)S(1)} %get-tuple-element.69), channel_id=1, source_target_pairs={{0,16},{16,0},{1,17},{17,1},{2,18},{18,2},{3,19},{19,3},{4,20},{20... | collective-permute-start | bytes 1572872 | tf_op jit(solution)/shard_map/ppermute | solution.py:755
  23.3 2.0 %collective-permute-start.7 = (bf16[512,512]{1,0:T(8,128)(2,1)S(1)}, bf16[512,512]{1,0:T(8,128)(2,1)S(1)}, u32[]{:S(2)}, u32[]{:S(2)}) collective-permute-start(bf16[512,512]{1,0:T(8,128)(2,1)S(1)} %get-tuple-element.71), channel_id=1, source_target_pairs={{0,16},{16,0},{1,17},{17,1},{2,18},{18,2},{3,19},{19,3},{4,20},{20... | collective-permute-start | bytes 1572872 | tf_op jit(solution)/shard_map/ppermute | solution.py:755

commit v10 on v9

--- a/solution.py
+++ b/solution.py
@@ -7,6 +7,7 @@
 from jax.experimental import pallas as pl
 from jax.experimental.pallas import tpu as pltpu
 from jax.sharding import PartitionSpec as P
+
 
 ROWS = 8
 
@@ -156,7 +157,7 @@
 
 
 def in_rows(ref, tall):
-    modes, channels = ref.shape
+    _, channels = ref.shape
     tall[...] = ref[...].T
     count = channels // ROWS
     return jnp.concatenate(
@@ -768,11 +769,10 @@
 
 
 def on_device(gate_streams, inputs, medium_taps, residues, decay_rates):
-    channels, tokens = inputs.shape
+    channels, _ = inputs.shape
     share = channels // 2
     window = medium_taps.shape[1]
     modes = decay_rates.shape[1]
-    section = lax.axis_index("section")
     place = tuple(
         lax.axis_index(axis).astype(jnp.int32).reshape(1) for axis in ("section", "tok")
     )
@@ -814,7 +814,9 @@
         signals,
         modes,
     )
-    arrived = [met(total, by) for by in range(1, lax.axis_size("tok"))]
+    arrived = []
+    for by in range(1, lax.axis_size("tok")):
+        arrived.append(met(total, by))
     within = within_call(signals, response, tables[4:])
     result, waiting = None, []
     for half in range(HALVES):

time: 26.4 us -> 26.4 us (level)
  no operation moved by 1% of the time
where the time goes in v10:
time: 26.4 us; the launch traced here: 26.3 us
  Pallas kernels  14.3 us (54%)
  starting transfers between devices  8.53 us (32%)
  waiting for transfers between devices  3.37 us (13%)
    ppermute x2, starting transfers between devices, edge_to(): return lax.ppermute(value, ('section', 'tok'), pairs)  4.94 us
    pallas_call x1, Pallas kernels, response_call(): pl.pallas_call(functools.partial(response_kernel, len(tables), window), o...  3.34 us
    pallas_call x1, Pallas kernels, later_call(): pl.pallas_call(functools.partial(later_kernel, min(STEP, share)), out_sha...  3.01 us
    ppermute x3, starting transfers between devices, met(): return lax.ppermute(value, 'tok', [(i, i ^ by) for i in range(peers)])  2.96 us
    pallas_call x2, Pallas kernels, place_call(): pl.pallas_call(functools.partial(place_kernel, half * rows, before.shape[...  1.97 us
    pallas_call x2, Pallas kernels, output_call(): pl.pallas_call(functools.partial(output_kernel, len(arrived), lanes // RO...  1.93 us
    ppermute x3, waiting for transfers between devices, met(): return lax.ppermute(value, 'tok', [(i, i ^ by) for i in range(peers)])  1.59 us
    pallas_call x1, Pallas kernels, edge_call(): pl.pallas_call(edge_kernel, out_shape=(edge, edge), in_specs=[ANY_SPEC] *...  1.39 us
  transfers between devices with their start and end apart: 8, of which 4 were waited for; matrix products, arithmetic and copies ran while one was open for 0% of the time, Pallas kernels for 42%

profile of v10, /device:TPU:1, one launch (start us, length us, event | category | flops | bytes accessed | tf_op | source)
XLA Modules:
  0.0 26.3 jit_solution(14621542722511889825)
XLA Ops:
  0.0 0.0 copy-start
  0.0 0.0 copy-start.1
  0.0 0.0 collective-permute-start
  0.0 1.4 %edge.1 = (bf16[1024,128]{1,0:T(8,128)(2,1)S(1)}, bf16[1024,128]{1,0:T(8,128)(2,1)S(1)}) custom-call(bf16[1,2,2048,512]{3,2,1,0:T(8,128)(2,1)} %gates.1, bf16[2048,512]{1,0:T(8,128)(2,1)} %inputs.1), custom_call_target="tpu_custom_call" | custom-call | flops 1048576 | bytes 6291456 | tf_op jit(solution)/shard_map/edge/pallas_call | solution.py:741
  1.4 0.7 %collective-permute-start.1 = (bf16[1024,128]{1,0:T(8,128)(2,1)S(1)}, bf16[1024,128]{1,0:T(8,128)(2,1)S(1)}, u32[]{:S(2)}, u32[]{:S(2)}) collective-permute-start(bf16[1024,128]{1,0:T(8,128)(2,1)S(1)} %get-tuple-element.47), channel_id=1, source_target_pairs={{0,1},{1,2},{2,3},{3,0},{16,16},{17,17},{18,18},{19,19},{4,5},{5,6... | collective-permute-start | bytes 786440 | tf_op jit(solution)/shard_map/ppermute | solution.py:768
  2.1 4.3 %collective-permute-start.2 = (bf16[1024,128]{1,0:T(8,128)(2,1)S(1)}, bf16[1024,128]{1,0:T(8,128)(2,1)S(1)}, u32[]{:S(2)}, u32[]{:S(2)}) collective-permute-start(bf16[1024,128]{1,0:T(8,128)(2,1)S(1)} %get-tuple-element.48), channel_id=1, source_target_pairs={{0,17},{1,18},{2,19},{3,16},{16,0},{17,1},{18,2},{19,3},{4,21},{5,... | collective-permute-start | bytes 786440 | tf_op jit(solution)/shard_map/ppermute | solution.py:768
  6.4 0.0 copy-done
  6.4 0.0 copy-done.1
  6.4 3.3 %response.1 = (f32[1024,128]{1,0:T(8,128)S(1)}, f32[128,128]{1,0:T(8,128)S(1)}, f32[128,128]{1,0:T(8,128)S(1)}, bf16[64,128,256]{2,1,0:T(8,128)(2,1)S(1)}, bf16[...) custom-call(s32[1]{0:T(128)} %bitcast.sec, ...), custom_call_target="tpu_custom_call" | custom-call | flops 471859200 | bytes 6291456 | tf_op jit(solution)/shard_map/response/pallas_call | solution.py:239
  9.7 0.0 collective-permute-done.swapped
  9.7 3.0 %later.1 = (bf16[1024,512]{1,0:T(8,128)(2,1)S(1)}, bf16[1024,512]{1,0:T(8,128)(2,1)S(1)}, f32[1024,256]{1,0:T(8,128)S(1)}, f32[1024,256]{1,0:T(8,128)S(1)}, bf16[2,1024,512]{2,1,0:T(8,128)(2,1)S(1)}) custom-call(s32[1]{0:T(128)} %bitcast.sec, s32[1]{0:T(128)} %bitcast.1.tok, bf16[2,1024,512]{2,1,0:T(8,128)(2,1)S(1)} %get-tuple-element.39.local_all, ...), custom_call_target="tpu_custom_call" | custom-call | flops 786432000 | bytes 6291456 | tf_op jit(solution)/shard_map/later/pallas_call | solution.py:387
  12.7 0.0 collective-permute-done.1.halo_low
  12.8 1.0 %collective-permute-done.2.halo_high = bf16[1024,128]{1,0:T(8,128)(2,1)S(1)} collective-permute-done((bf16[1024,128]{1,0:T(8,128)(2,1)S(1)}, bf16[1024,128]{1,0:T(8,128)(2,1)S(1)}, u32[]{:S(2)}, u32[]{:S(2)}) %collective-permute-start.2) | collective-permute-done | bytes 262176 | tf_op jit(solution)/shard_map/ppermute | solution.py:768
  13.7 1.3 %first.1 = (bf16[1024,512]{1,0:T(8,128)(2,1)S(1)}, bf16[1024,512]{1,0:T(8,128)(2,1)S(1)}, f32[4,1024,128]{2,1,0:T(8,128)S(1)}, bf16[128,128]{1,0:T(8,128)(2,1)S(1)}) custom-call(s32[1]{0:T(128)} %bitcast.sec, s32[1]{0:T(128)} %bitcast.1.tok, bf16[2,1024,512]{2,1,0:T(8,128)(2,1)S(1)} %get-tuple-element.39.local_all, ...), custom_call_target="tpu_custom_call", output_to_operand_aliasing={{0}: (13, {}), {1}: (14, {})} | custom-call | flops 262144000 | bytes 6291456 | tf_op jit(solution)/shard_map/first/pallas_call | solution.py:482
  15.0 0.8 %collective-permute-start.3 = (bf16[128,128]{1,0:T(8,128)(2,1)S(1)}, bf16[128,128]{1,0:T(8,128)(2,1)S(1)}, u32[]{:S(2)}, u32[]{:S(2)}) collective-permute-start(bf16[128,128]{1,0:T(8,128)(2,1)S(1)} %get-tuple-element.66), channel_id=1, source_target_pairs={{0,1},{1,0},{2,3},{3,2},{4,5},{5,4},{6,7},{7,6},{8,9},{9,8},{10,11... | collective-permute-start | bytes 98312 | tf_op jit(solution)/shard_map/ppermute | solution.py:761
  15.8 1.2 %collective-permute-start.4 = (bf16[128,128]{1,0:T(8,128)(2,1)S(1)}, bf16[128,128]{1,0:T(8,128)(2,1)S(1)}, u32[]{:S(2)}, u32[]{:S(2)}) collective-permute-start(bf16[128,128]{1,0:T(8,128)(2,1)S(1)} %get-tuple-element.66), channel_id=1, source_target_pairs={{0,2},{1,3},{2,0},{3,1},{4,6},{5,7},{6,4},{7,5},{8,10},{9,11},{10,... | collective-permute-start | bytes 98312 | tf_op jit(solution)/shard_map/ppermute | solution.py:761
  17.1 0.9 %collective-permute-start.5 = (bf16[128,128]{1,0:T(8,128)(2,1)S(1)}, bf16[128,128]{1,0:T(8,128)(2,1)S(1)}, u32[]{:S(2)}, u32[]{:S(2)}) collective-permute-start(bf16[128,128]{1,0:T(8,128)(2,1)S(1)} %get-tuple-element.66), channel_id=1, source_target_pairs={{0,3},{1,2},{2,1},{3,0},{4,7},{5,6},{6,5},{7,4},{8,11},{9,10},{10,... | collective-permute-start | bytes 98312 | tf_op jit(solution)/shard_map/ppermute | solution.py:761
  18.0 1.4 %within.1.within_all = f32[1024,512]{1,0:T(8,128)S(1)} custom-call(bf16[1024,512]{1,0:T(8,128)(2,1)S(1)} %get-tuple-element.55.signals_all, f32[1024,128]{1,0:T(8,128)S(1)} %get-tuple-element.56.response_all, bf16[256,256]{1,0:T(8,128)(2,1)S(1)} %get-tuple-element.57.fwd_h, bf16[256,256]{1,0:T(8,128)(2,1)S(1)} %get-tuple-element.58.fwd_l, ...), custom_call_target="tpu_custom_call" | custom-call | flops 786432000 | bytes 6291456 | tf_op jit(solution)/shard_map/within/pallas_call | solution.py:547
  19.3 0.0 collective-permute-done.3.rest_0_
  19.3 0.0 collective-permute-done.4.rest_1_
  19.3 1.6 %collective-permute-done.5.rest_2_ = bf16[128,128]{1,0:T(8,128)(2,1)S(1)} collective-permute-done((bf16[128,128]{1,0:T(8,128)(2,1)S(1)}, bf16[128,128]{1,0:T(8,128)(2,1)S(1)}, u32[]{:S(2)}, u32[]{:S(2)}) %collective-permute-start.5) | collective-permute-done | bytes 32800 | tf_op jit(solution)/shard_map/ppermute | solution.py:761
  20.9 1.0 %output.2 = (bf16[1,2048,512]{2,1,0:T(8,128)(2,1)}, bf16[512,512]{1,0:T(8,128)(2,1)S(1)}, bf16[512,512]{1,0:T(8,128)(2,1)S(1)}) custom-call(s32[1]{0:T(128)} %bitcast.sec, s32[1]{0:T(128)} %bitcast.1.tok, bf16[2,1024,512]{2,1,0:T(8,128)(2,1)S(1)} %get-tuple-element.39.local_all, bf16[2,1024,512]{2,1,0:T(8,128)(2,1)S(1)} %get-tuple-element.46.remote_all, ...), custom_call_target="tpu_custom_call" | custom-call | flops 393216000 | bytes 3145728 | tf_op jit(solution)/shard_map/output/pallas_call | solution.py:667
  21.9 0.4 %collective-permute-start.6 = (bf16[512,512]{1,0:T(8,128)(2,1)S(1)}, bf16[512,512]{1,0:T(8,128)(2,1)S(1)}, u32[]{:S(2)}, u32[]{:S(2)}) collective-permute-start(bf16[512,512]{1,0:T(8,128)(2,1)S(1)} %get-tuple-element.69), channel_id=1, source_target_pairs={{0,16},{16,0},{1,17},{17,1},{2,18},{18,2},{3,19},{19,3},{4,20},{20... | collective-permute-start | bytes 1572872 | tf_op jit(solution)/shard_map/ppermute | solution.py:756
  22.3 1.0 %output.3 = (bf16[1,2048,512]{2,1,0:T(8,128)(2,1)}, bf16[512,512]{1,0:T(8,128)(2,1)S(1)}, bf16[512,512]{1,0:T(8,128)(2,1)S(1)}) custom-call(s32[1]{0:T(128)} %bitcast.sec, s32[1]{0:T(128)} %bitcast.1.tok, bf16[2,1024,512]{2,1,0:T(8,128)(2,1)S(1)} %get-tuple-element.39.local_all, ...), custom_call_target="tpu_custom_call", output_to_operand_aliasing={{0}: (14, {})} | custom-call | flops 393216000 | bytes 3145728 | tf_op jit(solution)/shard_map/output/pallas_call | solution.py:667
  23.3 0.2 collective-permute-start.7
  23.5 0.4 %collective-permute-done.6.received = bf16[512,512]{1,0:T(8,128)(2,1)S(1)} collective-permute-done((bf16[512,512]{1,0:T(8,128)(2,1)S(1)}, bf16[512,512]{1,0:T(8,128)(2,1)S(1)}, u32[]{:S(2)}, u32[]{:S(2)}) %collective-permute-start.6) | collective-permute-done | bytes 524320 | tf_op jit(solution)/shard_map/ppermute | solution.py:756
  23.9 1.0 %placing.2.before = bf16[1,2048,512]{2,1,0:T(8,128)(2,1)} custom-call(s32[1]{0:T(128)} %bitcast.sec, s32[1]{0:T(128)} %bitcast.1.tok, bf16[1,2048,512]{2,1,0:T(8,128)(2,1)} %get-tuple-element.68.before, bf16[512,512]{1,0:T(8,128)(2,1)S(1)} %collective-permute-done.6.received, bf16[512,512]{1,0:T(8,128)(2,1)S(1)} %get-tuple-element.70.keep), custom_call_target="tpu_custom_call", output_to_operand_aliasing={{}: (2, {})} | custom-call | flops 524288 | bytes 3145728 | tf_op jit(solution)/shard_map/placing/pallas_call | solution.py:709
  24.9 0.4 %collective-permute-done.7.received = bf16[512,512]{1,0:T(8,128)(2,1)S(1)} collective-permute-done((bf16[512,512]{1,0:T(8,128)(2,1)S(1)}, bf16[512,512]{1,0:T(8,128)(2,1)S(1)}, u32[]{:S(2)}, u32[]{:S(2)}) %collective-permute-start.7) | collective-permute-done | bytes 524320 | tf_op jit(solution)/shard_map/ppermute | solution.py:756
  25.3 1.0 %placing.3 = bf16[1,2048,512]{2,1,0:T(8,128)(2,1)} custom-call(s32[1]{0:T(128)} %bitcast.sec, s32[1]{0:T(128)} %bitcast.1.tok, bf16[1,2048,512]{2,1,0:T(8,128)(2,1)} %placing.2.before, bf16[512,512]{1,0:T(8,128)(2,1)S(1)} %collective-permute-done.7.received, bf16[512,512]{1,0:T(8,128)(2,1)S(1)} %get-tuple-element.72.keep), custom_call_target="tpu_custom_call", output_to_operand_aliasing={{}: (2, {})} | custom-call | flops 524288 | bytes 3145728 | tf_op jit(solution)/shard_map/placing/pallas_call | solution.py:709
Async XLA Ops:
  0.0 6.4 %copy-start = (f32[2048,16]{0,1:T(8,128)S(1)}, f32[2048,16]{0,1:T(8,128)}, u32[]{:S(2)}) copy-start(f32[2048,16]{0,1:T(8,128)} %param.22) | copy-start | bytes 393220
  0.0 6.4 %copy-start.1 = (f32[2048,16]{0,1:T(8,128)S(1)}, f32[2048,16]{0,1:T(8,128)}, u32[]{:S(2)}) copy-start(f32[2048,16]{0,1:T(8,128)} %param.21) | copy-start | bytes 393220
  0.0 9.7 %collective-permute-start = (bf16[2,2048,512]{2,1,0:T(8,128)(2,1)}, bf16[2,2048,512]{2,1,0:T(8,128)(2,1)}, u32[]{:S(2)}, u32[]{:S(2)}) collective-permute-start(bf16[2,2048,512]{2,1,0:T(8,128)(2,1)} %bitcast.7), channel_id=1, source_target_pairs={{0,16},{16,0},{1,17},{17,1},{2,18},{18,2},{3,19},{19,3},{4,20},{20... | collective-permute-start | bytes 12582920 | tf_op jit(solution)/shard_map/ppermute | solution.py:756
  1.4 11.3 %collective-permute-start.1 = (bf16[1024,128]{1,0:T(8,128)(2,1)S(1)}, bf16[1024,128]{1,0:T(8,128)(2,1)S(1)}, u32[]{:S(2)}, u32[]{:S(2)}) collective-permute-start(bf16[1024,128]{1,0:T(8,128)(2,1)S(1)} %get-tuple-element.47), channel_id=1, source_target_pairs={{0,1},{1,2},{2,3},{3,0},{16,16},{17,17},{18,18},{19,19},{4,5},{5,6... | collective-permute-start | bytes 786440 | tf_op jit(solution)/shard_map/ppermute | solution.py:768
  2.1 11.6 %collective-permute-start.2 = (bf16[1024,128]{1,0:T(8,128)(2,1)S(1)}, bf16[1024,128]{1,0:T(8,128)(2,1)S(1)}, u32[]{:S(2)}, u32[]{:S(2)}) collective-permute-start(bf16[1024,128]{1,0:T(8,128)(2,1)S(1)} %get-tuple-element.48), channel_id=1, source_target_pairs={{0,17},{1,18},{2,19},{3,16},{16,0},{17,1},{18,2},{19,3},{4,21},{5,... | collective-permute-start | bytes 786440 | tf_op jit(solution)/shard_map/ppermute | solution.py:768
  15.0 4.3 %collective-permute-start.3 = (bf16[128,128]{1,0:T(8,128)(2,1)S(1)}, bf16[128,128]{1,0:T(8,128)(2,1)S(1)}, u32[]{:S(2)}, u32[]{:S(2)}) collective-permute-start(bf16[128,128]{1,0:T(8,128)(2,1)S(1)} %get-tuple-element.66), channel_id=1, source_target_pairs={{0,1},{1,0},{2,3},{3,2},{4,5},{5,4},{6,7},{7,6},{8,9},{9,8},{10,11... | collective-permute-start | bytes 98312 | tf_op jit(solution)/shard_map/ppermute | solution.py:761
  15.8 3.5 %collective-permute-start.4 = (bf16[128,128]{1,0:T(8,128)(2,1)S(1)}, bf16[128,128]{1,0:T(8,128)(2,1)S(1)}, u32[]{:S(2)}, u32[]{:S(2)}) collective-permute-start(bf16[128,128]{1,0:T(8,128)(2,1)S(1)} %get-tuple-element.66), channel_id=1, source_target_pairs={{0,2},{1,3},{2,0},{3,1},{4,6},{5,7},{6,4},{7,5},{8,10},{9,11},{10,... | collective-permute-start | bytes 98312 | tf_op jit(solution)/shard_map/ppermute | solution.py:761
  17.1 3.9 %collective-permute-start.5 = (bf16[128,128]{1,0:T(8,128)(2,1)S(1)}, bf16[128,128]{1,0:T(8,128)(2,1)S(1)}, u32[]{:S(2)}, u32[]{:S(2)}) collective-permute-start(bf16[128,128]{1,0:T(8,128)(2,1)S(1)} %get-tuple-element.66), channel_id=1, source_target_pairs={{0,3},{1,2},{2,1},{3,0},{4,7},{5,6},{6,5},{7,4},{8,11},{9,10},{10,... | collective-permute-start | bytes 98312 | tf_op jit(solution)/shard_map/ppermute | solution.py:761
  21.9 2.0 %collective-permute-start.6 = (bf16[512,512]{1,0:T(8,128)(2,1)S(1)}, bf16[512,512]{1,0:T(8,128)(2,1)S(1)}, u32[]{:S(2)}, u32[]{:S(2)}) collective-permute-start(bf16[512,512]{1,0:T(8,128)(2,1)S(1)} %get-tuple-element.69), channel_id=1, source_target_pairs={{0,16},{16,0},{1,17},{17,1},{2,18},{18,2},{3,19},{19,3},{4,20},{20... | collective-permute-start | bytes 1572872 | tf_op jit(solution)/shard_map/ppermute | solution.py:756
  23.3 2.0 %collective-permute-start.7 = (bf16[512,512]{1,0:T(8,128)(2,1)S(1)}, bf16[512,512]{1,0:T(8,128)(2,1)S(1)}, u32[]{:S(2)}, u32[]{:S(2)}) collective-permute-start(bf16[512,512]{1,0:T(8,128)(2,1)S(1)} %get-tuple-element.71), channel_id=1, source_target_pairs={{0,16},{16,0},{1,17},{17,1},{2,18},{18,2},{3,19},{19,3},{4,20},{20... | collective-permute-start | bytes 1572872 | tf_op jit(solution)/shard_map/ppermute | solution.py:756

commit v11 on v10

--- a/solution.py
+++ b/solution.py
@@ -343,7 +343,8 @@
         fetch(i).start()
 
     def chunk(section, i):
-        fetch(i).wait()
+        if section == 1:
+            fetch(i).wait()
         first, second = both_gates(local_all, remote_all, section, step, i)
         inputs = rows_at(inputs_all, step, i)
         medium_out, signals = rows_at(medium_all, step, i), rows_at(signals_all, step, i)
@@ -357,6 +358,8 @@
         rows_at(tap_spec_all, step, i)[...] = tap_spec
         rows_at(edge_spec_all, step, i)[...] = in_order[0]
         mixed = products([in_order[b - 1] + in_order[b] for b in range(1, blocks)], tap_spec)
+        if section == 0:
+            fetch(i).wait()
         for parity, table in enumerate((inv_even, inv_odd)):
             chosen = [b for b in range(1, blocks) if b % 2 == parity]
             if not chosen:
@@ -686,43 +689,50 @@
     )(*place, *operands, *chained)
 
 
-def place_kernel(first, share, sec, tok, before, received, keep, out, done):
+def place_kernel(first, share, sec, before, received, *rest):
+    kept, (out, done) = rest[:-2], rest[-2:]
     rows = received.shape[0]
 
-    def target(section):
-        return out.at[0, pl.ds(pl.multiple_of(section * share + first, rows), rows), :]
-
-    foreign = pltpu.make_async_copy(received, target(1 - sec[0]), done.at[0])
+    def target(section, start):
+        return out.at[0, pl.ds(pl.multiple_of(section * share + start, rows), rows), :]
+
+    foreign = pltpu.make_async_copy(received, target(1 - sec[0], first), done.at[0])
     foreign.start()
 
     @pl.when(sec[0] == 1)
     def _():
-        own = pltpu.make_async_copy(keep, target(1), done.at[1])
-        own.start()
-        own.wait()
+        copies = [
+            pltpu.make_async_copy(keep, target(1, k * rows), done.at[k + 1])
+            for k, keep in enumerate(kept)
+        ]
+        for copy in copies:
+            copy.start()
+        for copy in copies:
+            copy.wait()
 
     foreign.wait()
 
 
-def place_call(place, half, before, received, keep):
+def place_call(place, half, before, received, kept):
     rows, tokens = received.shape
     return pl.pallas_call(
         functools.partial(place_kernel, half * rows, before.shape[1] // 2),
         out_shape=jax.ShapeDtypeStruct(before.shape, before.dtype),
-        in_specs=[SMEM_SPEC] * 2 + [ANY_SPEC, VMEM_SPEC, VMEM_SPEC],
+        in_specs=[SMEM_SPEC, ANY_SPEC] + [VMEM_SPEC] * (1 + len(kept)),
         out_specs=ANY_SPEC,
-        scratch_shapes=[pltpu.SemaphoreType.DMA((2,))],
-        input_output_aliases={2: 0},
+        scratch_shapes=[pltpu.SemaphoreType.DMA((1 + len(kept),))],
+        input_output_aliases={1: 0},
         name="placing",
         cost_estimate=cost(rows, tokens, 2),
         compiler_params=COMPILER,
-    )(*place, before, received, keep)
-
-
-def edge_kernel(gates, inputs, low, high, gate_tail, input_tail, arrival):
-    share, window = low.shape
+    )(place[0], before, received, *kept)
+
+
+def edge_kernel(first, gates, inputs, edge, gate_tail, input_tail, arrival):
+    share, window = edge.shape
+    rows = pl.ds(first, share)
     tail = pl.ds(inputs.shape[1] - window, window)
-    pairs = [(gates.at[0, 1, :, tail], gate_tail), (inputs.at[:, tail], input_tail)]
+    pairs = [(gates.at[0, 1, rows, tail], gate_tail), (inputs.at[rows, tail], input_tail)]
     copies = [
         pltpu.make_async_copy(source, target, arrival.at[k])
         for k, (source, target) in enumerate(pairs)
@@ -731,22 +741,19 @@
         copy.start()
     for copy in copies:
         copy.wait()
-    low[...] = gate_tail[:share, :] * input_tail[:share, :]
-    high[...] = gate_tail[share:, :] * input_tail[share:, :]
-
-
-def edge_call(gate_streams, inputs, window, share):
-    channels, tokens = inputs.shape
-    edge = jax.ShapeDtypeStruct((share, window), jnp.bfloat16)
+    edge[...] = gate_tail[...] * input_tail[...]
+
+
+def edge_call(gate_streams, inputs, window, share, half):
     return pl.pallas_call(
-        edge_kernel,
-        out_shape=(edge, edge),
+        functools.partial(edge_kernel, half * share),
+        out_shape=jax.ShapeDtypeStruct((share, window), jnp.bfloat16),
         in_specs=[ANY_SPEC] * 2,
-        out_specs=(VMEM_SPEC,) * 2,
-        scratch_shapes=[pltpu.VMEM((channels, window), jnp.bfloat16)] * 2
+        out_specs=VMEM_SPEC,
+        scratch_shapes=[pltpu.VMEM((share, window), jnp.bfloat16)] * 2
         + [pltpu.SemaphoreType.DMA((2,))],
         name="edge",
-        cost_estimate=cost(share, tokens, 2),
+        cost_estimate=cost(share, window, 2),
         compiler_params=COMPILER,
     )(*parked(gate_streams, inputs))
 
@@ -776,8 +783,10 @@
     place = tuple(
         lax.axis_index(axis).astype(jnp.int32).reshape(1) for axis in ("section", "tok")
     )
-    edges = edge_call(gate_streams, inputs, window, share)
-    halos = [edge_to(edges[s], s) for s in range(2)]
+    halos = []
+    for half in range(2):
+        edge = edge_call(gate_streams, inputs, window, share, half)
+        halos.append(edge_to(edge, half))
     swapped = ring(gate_streams[0], "section", 1)
     forward, inverse = fourier_tables(window)
     turned, back, doubled = turned_tables(window)
@@ -836,8 +845,9 @@
             result,
         )
         waiting.append((ring(send, "section", 1), keep))
-    for half, (received, keep) in enumerate(waiting):
-        result = place_call(place, half, result, received, keep)
+    kept = [keep for _, keep in waiting]
+    for half, (received, _) in enumerate(waiting):
+        result = place_call(place, half, result, received, [] if half else kept)
     return result
 
 

time: 26.4 us -> 26.7 us (1.011)
  Pallas kernels: 14.3 us -> 15.1 us
  waiting for transfers between devices: 3.37 us -> 2.66 us
    ppermute x2, waiting for transfers between devices: 0.97 us -> 0.01 us  [edge_to(): return lax.ppermute(value, ('section', 'tok'), pairs)]
    pallas_call x1 -> x2, Pallas kernels: 1.39 us -> 2.23 us  [edge_call(): pl.pallas_call(functools.partial(edge_kernel, half * share), out_shape=ja...]
    ppermute x3, waiting for transfers between devices: 1.59 us -> 1.92 us  [met(): return lax.ppermute(value, 'tok', [(i, i ^ by) for i in range(peers)])]
  transfers between devices with their start and end apart: 8 -> 8, of which waited for: 4 -> 3; matrix products, arithmetic and copies ran while one was open for 0% -> 0% of each run, Pallas kernels for 42% -> 46%
where the time goes in v11:
time: 26.7 us; the launch traced here: 26.4 us
  Pallas kernels  15.1 us (57%)
  starting transfers between devices  8.49 us (32%)
  waiting for transfers between devices  2.66 us (10%)
    ppermute x2, starting transfers between devices, edge_to(): return lax.ppermute(value, ('section', 'tok'), pairs)  5.06 us
    pallas_call x1, Pallas kernels, response_call(): pl.pallas_call(functools.partial(response_kernel, len(tables), window), o...  3.34 us
    pallas_call x1, Pallas kernels, later_call(): pl.pallas_call(functools.partial(later_kernel, min(STEP, share)), out_sha...  3.01 us
    ppermute x3, starting transfers between devices, met(): return lax.ppermute(value, 'tok', [(i, i ^ by) for i in range(peers)])  2.78 us
    pallas_call x2, Pallas kernels, edge_call(): pl.pallas_call(functools.partial(edge_kernel, half * share), out_shape=ja...  2.23 us
    pallas_call x2, Pallas kernels, place_call(): pl.pallas_call(functools.partial(place_kernel, half * rows, before.shape[...  1.96 us
    pallas_call x2, Pallas kernels, output_call(): pl.pallas_call(functools.partial(output_kernel, len(arrived), lanes // RO...  1.93 us
    ppermute x3, waiting for transfers between devices, met(): return lax.ppermute(value, 'tok', [(i, i ^ by) for i in range(peers)])  1.92 us
  transfers between devices with their start and end apart: 8, of which 3 were waited for; matrix products, arithmetic and copies ran while one was open for 0% of the time, Pallas kernels for 46%

profile of v11, /device:TPU:1, one launch (start us, length us, event | category | flops | bytes accessed | tf_op | source)
XLA Modules:
  0.0 26.4 jit_solution(2523906701509448866)
XLA Ops:
  0.0 0.0 collective-permute-start
  0.0 1.1 %edge.2 = bf16[1024,128]{1,0:T(8,128)(2,1)S(1)} custom-call(bf16[1,2,2048,512]{3,2,1,0:T(8,128)(2,1)} %gates.3, bf16[2048,512]{1,0:T(8,128)(2,1)} %inputs.3), custom_call_target="tpu_custom_call" | custom-call | flops 262144 | bytes 1572864 | tf_op jit(solution)/shard_map/edge/pallas_call | solution.py:748
  1.1 0.0 copy-start
  1.1 0.0 copy-start.1
  1.2 0.8 %collective-permute-start.1 = (bf16[1024,128]{1,0:T(8,128)(2,1)S(1)}, bf16[1024,128]{1,0:T(8,128)(2,1)S(1)}, u32[]{:S(2)}, u32[]{:S(2)}) collective-permute-start(bf16[1024,128]{1,0:T(8,128)(2,1)S(1)} %edge.2), channel_id=1, source_target_pairs={{0,1},{1,2},{2,3},{3,0},{16,16},{17,17},{18,18},{19,19},{4,5},{5,6... | collective-permute-start | bytes 786440 | tf_op jit(solution)/shard_map/ppermute | solution.py:775
  2.0 1.1 %edge.3 = bf16[1024,128]{1,0:T(8,128)(2,1)S(1)} custom-call(bf16[1,2,2048,512]{3,2,1,0:T(8,128)(2,1)} %gates.3, bf16[2048,512]{1,0:T(8,128)(2,1)} %inputs.3), custom_call_target="tpu_custom_call" | custom-call | flops 262144 | bytes 1572864 | tf_op jit(solution)/shard_map/edge/pallas_call | solution.py:748
  3.1 4.3 %collective-permute-start.2 = (bf16[1024,128]{1,0:T(8,128)(2,1)S(1)}, bf16[1024,128]{1,0:T(8,128)(2,1)S(1)}, u32[]{:S(2)}, u32[]{:S(2)}) collective-permute-start(bf16[1024,128]{1,0:T(8,128)(2,1)S(1)} %edge.3), channel_id=1, source_target_pairs={{0,17},{1,18},{2,19},{3,16},{16,0},{17,1},{18,2},{19,3},{4,21},{5,... | collective-permute-start | bytes 786440 | tf_op jit(solution)/shard_map/ppermute | solution.py:775
  7.4 0.0 copy-done
  7.4 0.0 copy-done.1
  7.4 3.3 %response.1 = (f32[1024,128]{1,0:T(8,128)S(1)}, f32[128,128]{1,0:T(8,128)S(1)}, f32[128,128]{1,0:T(8,128)S(1)}, bf16[64,128,256]{2,1,0:T(8,128)(2,1)S(1)}, bf16[...) custom-call(s32[1]{0:T(128)} %bitcast.sec, ...), custom_call_target="tpu_custom_call" | custom-call | flops 471859200 | bytes 6291456 | tf_op jit(solution)/shard_map/response/pallas_call | solution.py:239
  10.7 0.0 collective-permute-done.swapped
  10.7 3.0 %later.1 = (bf16[1024,512]{1,0:T(8,128)(2,1)S(1)}, bf16[1024,512]{1,0:T(8,128)(2,1)S(1)}, f32[1024,256]{1,0:T(8,128)S(1)}, f32[1024,256]{1,0:T(8,128)S(1)}, bf16[2,1024,512]{2,1,0:T(8,128)(2,1)S(1)}) custom-call(s32[1]{0:T(128)} %bitcast.sec, s32[1]{0:T(128)} %bitcast.1.tok, bf16[2,1024,512]{2,1,0:T(8,128)(2,1)S(1)} %get-tuple-element.37.local_all, ...), custom_call_target="tpu_custom_call" | custom-call | flops 786432000 | bytes 6291456 | tf_op jit(solution)/shard_map/later/pallas_call | solution.py:390
  13.7 0.0 collective-permute-done.1.halo_low
  13.7 0.0 collective-permute-done.2.halo_high
  13.8 1.3 %first.1 = (bf16[1024,512]{1,0:T(8,128)(2,1)S(1)}, bf16[1024,512]{1,0:T(8,128)(2,1)S(1)}, f32[4,1024,128]{2,1,0:T(8,128)S(1)}, bf16[128,128]{1,0:T(8,128)(2,1)S(1)}) custom-call(s32[1]{0:T(128)} %bitcast.sec, s32[1]{0:T(128)} %bitcast.1.tok, bf16[2,1024,512]{2,1,0:T(8,128)(2,1)S(1)} %get-tuple-element.37.local_all, ...), custom_call_target="tpu_custom_call", output_to_operand_aliasing={{0}: (13, {}), {1}: (14, {})} | custom-call | flops 262144000 | bytes 6291456 | tf_op jit(solution)/shard_map/first/pallas_call | solution.py:485
  15.0 1.3 %collective-permute-start.3 = (bf16[128,128]{1,0:T(8,128)(2,1)S(1)}, bf16[128,128]{1,0:T(8,128)(2,1)S(1)}, u32[]{:S(2)}, u32[]{:S(2)}) collective-permute-start(bf16[128,128]{1,0:T(8,128)(2,1)S(1)} %get-tuple-element.62), channel_id=1, source_target_pairs={{0,1},{1,0},{2,3},{3,2},{4,5},{5,4},{6,7},{7,6},{8,9},{9,8},{10,11... | collective-permute-start | bytes 98312 | tf_op jit(solution)/shard_map/ppermute | solution.py:768
  16.3 0.6 %collective-permute-start.4 = (bf16[128,128]{1,0:T(8,128)(2,1)S(1)}, bf16[128,128]{1,0:T(8,128)(2,1)S(1)}, u32[]{:S(2)}, u32[]{:S(2)}) collective-permute-start(bf16[128,128]{1,0:T(8,128)(2,1)S(1)} %get-tuple-element.62), channel_id=1, source_target_pairs={{0,2},{1,3},{2,0},{3,1},{4,6},{5,7},{6,4},{7,5},{8,10},{9,11},{10,... | collective-permute-start | bytes 98312 | tf_op jit(solution)/shard_map/ppermute | solution.py:768
  16.9 0.9 %collective-permute-start.5 = (bf16[128,128]{1,0:T(8,128)(2,1)S(1)}, bf16[128,128]{1,0:T(8,128)(2,1)S(1)}, u32[]{:S(2)}, u32[]{:S(2)}) collective-permute-start(bf16[128,128]{1,0:T(8,128)(2,1)S(1)} %get-tuple-element.62), channel_id=1, source_target_pairs={{0,3},{1,2},{2,1},{3,0},{4,7},{5,6},{6,5},{7,4},{8,11},{9,10},{10,... | collective-permute-start | bytes 98312 | tf_op jit(solution)/shard_map/ppermute | solution.py:768
  17.8 1.4 %within.1.within_all = f32[1024,512]{1,0:T(8,128)S(1)} custom-call(bf16[1024,512]{1,0:T(8,128)(2,1)S(1)} %get-tuple-element.51.signals_all, f32[1024,128]{1,0:T(8,128)S(1)} %get-tuple-element.52.response_all, bf16[256,256]{1,0:T(8,128)(2,1)S(1)} %get-tuple-element.53.fwd_h, bf16[256,256]{1,0:T(8,128)(2,1)S(1)} %get-tuple-element.54.fwd_l, ...), custom_call_target="tpu_custom_call" | custom-call | flops 786432000 | bytes 6291456 | tf_op jit(solution)/shard_map/within/pallas_call | solution.py:550
  19.2 0.0 collective-permute-done.3.rest_0_
  19.2 0.0 collective-permute-done.4.rest_1_
  19.2 1.9 %collective-permute-done.5.rest_2_ = bf16[128,128]{1,0:T(8,128)(2,1)S(1)} collective-permute-done((bf16[128,128]{1,0:T(8,128)(2,1)S(1)}, bf16[128,128]{1,0:T(8,128)(2,1)S(1)}, u32[]{:S(2)}, u32[]{:S(2)}) %collective-permute-start.5) | collective-permute-done | bytes 32800 | tf_op jit(solution)/shard_map/ppermute | solution.py:768
  21.1 1.0 %output.2 = (bf16[1,2048,512]{2,1,0:T(8,128)(2,1)}, bf16[512,512]{1,0:T(8,128)(2,1)S(1)}, bf16[512,512]{1,0:T(8,128)(2,1)S(1)}) custom-call(s32[1]{0:T(128)} %bitcast.sec, s32[1]{0:T(128)} %bitcast.1.tok, bf16[2,1024,512]{2,1,0:T(8,128)(2,1)S(1)} %get-tuple-element.37.local_all, bf16[2,1024,512]{2,1,0:T(8,128)(2,1)S(1)} %get-tuple-element.44.remote_all, ...), custom_call_target="tpu_custom_call" | custom-call | flops 393216000 | bytes 3145728 | tf_op jit(solution)/shard_map/output/pallas_call | solution.py:670
  22.1 0.6 %collective-permute-start.6 = (bf16[512,512]{1,0:T(8,128)(2,1)S(1)}, bf16[512,512]{1,0:T(8,128)(2,1)S(1)}, u32[]{:S(2)}, u32[]{:S(2)}) collective-permute-start(bf16[512,512]{1,0:T(8,128)(2,1)S(1)} %get-tuple-element.65), channel_id=1, source_target_pairs={{0,16},{16,0},{1,17},{17,1},{2,18},{18,2},{3,19},{19,3},{4,20},{20... | collective-permute-start | bytes 1572872 | tf_op jit(solution)/shard_map/ppermute | solution.py:763
  22.7 1.0 %output.3 = (bf16[1,2048,512]{2,1,0:T(8,128)(2,1)}, bf16[512,512]{1,0:T(8,128)(2,1)S(1)}, bf16[512,512]{1,0:T(8,128)(2,1)S(1)}) custom-call(s32[1]{0:T(128)} %bitcast.sec, s32[1]{0:T(128)} %bitcast.1.tok, bf16[2,1024,512]{2,1,0:T(8,128)(2,1)S(1)} %get-tuple-element.37.local_all, ...), custom_call_target="tpu_custom_call", output_to_operand_aliasing={{0}: (14, {})} | custom-call | flops 393216000 | bytes 3145728 | tf_op jit(solution)/shard_map/output/pallas_call | solution.py:670
  23.6 0.1 collective-permute-start.7
  23.7 0.5 %collective-permute-done.6.received = bf16[512,512]{1,0:T(8,128)(2,1)S(1)} collective-permute-done((bf16[512,512]{1,0:T(8,128)(2,1)S(1)}, bf16[512,512]{1,0:T(8,128)(2,1)S(1)}, u32[]{:S(2)}, u32[]{:S(2)}) %collective-permute-start.6) | collective-permute-done | bytes 524320 | tf_op jit(solution)/shard_map/ppermute | solution.py:763
  24.2 1.2 %placing.2.before = bf16[1,2048,512]{2,1,0:T(8,128)(2,1)} custom-call(s32[1]{0:T(128)} %bitcast.sec, bf16[1,2048,512]{2,1,0:T(8,128)(2,1)} %get-tuple-element.64.before, bf16[512,512]{1,0:T(8,128)(2,1)S(1)} %collective-permute-done.6.received, bf16[512,512]{1,0:T(8,128)(2,1)S(1)} %get-tuple-element.66.rest_0_, ...), custom_call_target="tpu_custom_call", output_to_operand_aliasing={{}: (1, {})} | custom-call | flops 524288 | bytes 3145728 | tf_op jit(solution)/shard_map/placing/pallas_call | solution.py:718
  25.4 0.2 collective-permute-done.7.received
  25.6 0.8 %placing.3 = bf16[1,2048,512]{2,1,0:T(8,128)(2,1)} custom-call(s32[1]{0:T(128)} %bitcast.sec, bf16[1,2048,512]{2,1,0:T(8,128)(2,1)} %placing.2.before, bf16[512,512]{1,0:T(8,128)(2,1)S(1)} %collective-permute-done.7.received), custom_call_target="tpu_custom_call", output_to_operand_aliasing={{}: (1, {})} | custom-call | flops 524288 | bytes 3145728 | tf_op jit(solution)/shard_map/placing/pallas_call | solution.py:718
Async XLA Ops:
  0.0 10.7 %collective-permute-start = (bf16[2,2048,512]{2,1,0:T(8,128)(2,1)}, bf16[2,2048,512]{2,1,0:T(8,128)(2,1)}, u32[]{:S(2)}, u32[]{:S(2)}) collective-permute-start(bf16[2,2048,512]{2,1,0:T(8,128)(2,1)} %bitcast.7), channel_id=1, source_target_pairs={{0,16},{16,0},{1,17},{17,1},{2,18},{18,2},{3,19},{19,3},{4,20},{20... | collective-permute-start | bytes 12582920 | tf_op jit(solution)/shard_map/ppermute | solution.py:763
  1.1 6.2 %copy-start = (f32[2048,16]{0,1:T(8,128)S(1)}, f32[2048,16]{0,1:T(8,128)}, u32[]{:S(2)}) copy-start(f32[2048,16]{0,1:T(8,128)} %param.22) | copy-start | bytes 393220
  1.1 6.2 %copy-start.1 = (f32[2048,16]{0,1:T(8,128)S(1)}, f32[2048,16]{0,1:T(8,128)}, u32[]{:S(2)}) copy-start(f32[2048,16]{0,1:T(8,128)} %param.21) | copy-start | bytes 393220
  1.2 12.6 %collective-permute-start.1 = (bf16[1024,128]{1,0:T(8,128)(2,1)S(1)}, bf16[1024,128]{1,0:T(8,128)(2,1)S(1)}, u32[]{:S(2)}, u32[]{:S(2)}) collective-permute-start(bf16[1024,128]{1,0:T(8,128)(2,1)S(1)} %edge.2), channel_id=1, source_target_pairs={{0,1},{1,2},{2,3},{3,0},{16,16},{17,17},{18,18},{19,19},{4,5},{5,6... | collective-permute-start | bytes 786440 | tf_op jit(solution)/shard_map/ppermute | solution.py:775
  3.1 10.6 %collective-permute-start.2 = (bf16[1024,128]{1,0:T(8,128)(2,1)S(1)}, bf16[1024,128]{1,0:T(8,128)(2,1)S(1)}, u32[]{:S(2)}, u32[]{:S(2)}) collective-permute-start(bf16[1024,128]{1,0:T(8,128)(2,1)S(1)} %edge.3), channel_id=1, source_target_pairs={{0,17},{1,18},{2,19},{3,16},{16,0},{17,1},{18,2},{19,3},{4,21},{5,... | collective-permute-start | bytes 786440 | tf_op jit(solution)/shard_map/ppermute | solution.py:775
  15.0 4.2 %collective-permute-start.3 = (bf16[128,128]{1,0:T(8,128)(2,1)S(1)}, bf16[128,128]{1,0:T(8,128)(2,1)S(1)}, u32[]{:S(2)}, u32[]{:S(2)}) collective-permute-start(bf16[128,128]{1,0:T(8,128)(2,1)S(1)} %get-tuple-element.62), channel_id=1, source_target_pairs={{0,1},{1,0},{2,3},{3,2},{4,5},{5,4},{6,7},{7,6},{8,9},{9,8},{10,11... | collective-permute-start | bytes 98312 | tf_op jit(solution)/shard_map/ppermute | solution.py:768
  16.3 2.9 %collective-permute-start.4 = (bf16[128,128]{1,0:T(8,128)(2,1)S(1)}, bf16[128,128]{1,0:T(8,128)(2,1)S(1)}, u32[]{:S(2)}, u32[]{:S(2)}) collective-permute-start(bf16[128,128]{1,0:T(8,128)(2,1)S(1)} %get-tuple-element.62), channel_id=1, source_target_pairs={{0,2},{1,3},{2,0},{3,1},{4,6},{5,7},{6,4},{7,5},{8,10},{9,11},{10,... | collective-permute-start | bytes 98312 | tf_op jit(solution)/shard_map/ppermute | solution.py:768
  16.9 4.2 %collective-permute-start.5 = (bf16[128,128]{1,0:T(8,128)(2,1)S(1)}, bf16[128,128]{1,0:T(8,128)(2,1)S(1)}, u32[]{:S(2)}, u32[]{:S(2)}) collective-permute-start(bf16[128,128]{1,0:T(8,128)(2,1)S(1)} %get-tuple-element.62), channel_id=1, source_target_pairs={{0,3},{1,2},{2,1},{3,0},{4,7},{5,6},{6,5},{7,4},{8,11},{9,10},{10,... | collective-permute-start | bytes 98312 | tf_op jit(solution)/shard_map/ppermute | solution.py:768
  22.1 2.1 %collective-permute-start.6 = (bf16[512,512]{1,0:T(8,128)(2,1)S(1)}, bf16[512,512]{1,0:T(8,128)(2,1)S(1)}, u32[]{:S(2)}, u32[]{:S(2)}) collective-permute-start(bf16[512,512]{1,0:T(8,128)(2,1)S(1)} %get-tuple-element.65), channel_id=1, source_target_pairs={{0,16},{16,0},{1,17},{17,1},{2,18},{18,2},{3,19},{19,3},{4,20},{20... | collective-permute-start | bytes 1572872 | tf_op jit(solution)/shard_map/ppermute | solution.py:763
  23.6 2.0 %collective-permute-start.7 = (bf16[512,512]{1,0:T(8,128)(2,1)S(1)}, bf16[512,512]{1,0:T(8,128)(2,1)S(1)}, u32[]{:S(2)}, u32[]{:S(2)}) collective-permute-start(bf16[512,512]{1,0:T(8,128)(2,1)S(1)} %get-tuple-element.68), channel_id=1, source_target_pairs={{0,16},{16,0},{1,17},{17,1},{2,18},{18,2},{3,19},{19,3},{4,20},{20... | collective-permute-start | bytes 1572872 | tf_op jit(solution)/shard_map/ppermute | solution.py:763

commit v12 on v11

--- a/solution.py
+++ b/solution.py
@@ -314,7 +314,7 @@
     sec,
     tok,
     local_all,
-    swapped,
+    remote_all,
     inputs_all,
     taps_all,
     fwd_even,
@@ -325,26 +325,13 @@
     signals_all,
     tap_spec_all,
     edge_spec_all,
-    remote_all,
-    arrival,
 ):
     share, tokens = inputs_all.shape
     window = taps_all.shape[1]
     blocks = tokens // window
     parts = [slice(b * window, (b + 1) * window) for b in range(blocks)]
 
-    def fetch(i):
-        source = pl.ds(pl.multiple_of(sec[0] * share + i * step, step), step)
-        return pltpu.make_async_copy(
-            swapped.at[:, source, :], rows_at(remote_all, step, i, 1), arrival.at[i]
-        )
-
-    for i in range(share // step):
-        fetch(i).start()
-
     def chunk(section, i):
-        if section == 1:
-            fetch(i).wait()
         first, second = both_gates(local_all, remote_all, section, step, i)
         inputs = rows_at(inputs_all, step, i)
         medium_out, signals = rows_at(medium_all, step, i), rows_at(signals_all, step, i)
@@ -358,8 +345,6 @@
         rows_at(tap_spec_all, step, i)[...] = tap_spec
         rows_at(edge_spec_all, step, i)[...] = in_order[0]
         mixed = products([in_order[b - 1] + in_order[b] for b in range(1, blocks)], tap_spec)
-        if section == 0:
-            fetch(i).wait()
         for parity, table in enumerate((inv_even, inv_odd)):
             chosen = [b for b in range(1, blocks) if b % 2 == parity]
             if not chosen:
@@ -381,18 +366,17 @@
     by_section(sec, body)
 
 
-def later_call(place, gates, swapped, inputs, taps, tables):
+def later_call(place, gates, remote, inputs, taps, tables):
     share, tokens = inputs.shape
     window = taps.shape[1]
-    operands = [gates, *parked(swapped), inputs, taps, *tables]
+    operands = [gates, remote, inputs, taps, *tables]
     spec = jax.ShapeDtypeStruct((share, 2 * window), jnp.float32)
     wide = jax.ShapeDtypeStruct((share, tokens), jnp.bfloat16)
     return pl.pallas_call(
         functools.partial(later_kernel, min(STEP, share)),
-        out_shape=(wide, wide, spec, spec, jax.ShapeDtypeStruct(gates.shape, gates.dtype)),
-        in_specs=[SMEM_SPEC] * 2 + [VMEM_SPEC, ANY_SPEC] + [VMEM_SPEC] * (len(operands) - 2),
-        out_specs=(VMEM_SPEC,) * 5,
-        scratch_shapes=[pltpu.SemaphoreType.DMA((share // min(STEP, share),))],
+        out_shape=(wide, wide, spec, spec),
+        in_specs=[SMEM_SPEC] * 2 + [VMEM_SPEC] * len(operands),
+        out_specs=(VMEM_SPEC,) * 4,
         name="later",
         cost_estimate=cost(share, tokens, 1500),
         compiler_params=COMPILER,
@@ -728,34 +712,44 @@
     )(place[0], before, received, *kept)
 
 
-def edge_kernel(first, gates, inputs, edge, gate_tail, input_tail, arrival):
-    share, window = edge.shape
-    rows = pl.ds(first, share)
-    tail = pl.ds(inputs.shape[1] - window, window)
-    pairs = [(gates.at[0, 1, rows, tail], gate_tail), (inputs.at[rows, tail], input_tail)]
+def lend_kernel(sec, tok, gates, inputs, lent, low, high, gate_tail, input_tail, arrival):
+    share, window = low.shape
+    tokens = inputs.shape[1]
+    tail = pl.ds(tokens - window, window)
+    other = pl.ds(pl.multiple_of((1 - sec[0]) * share, share), share)
     copies = [
         pltpu.make_async_copy(source, target, arrival.at[k])
-        for k, (source, target) in enumerate(pairs)
+        for k, (source, target) in enumerate(
+            [
+                (gates.at[0, 1, :, tail], gate_tail),
+                (inputs.at[:, tail], input_tail),
+                (gates.at[0, :, other, :], lent),
+            ]
+        )
     ]
     for copy in copies:
         copy.start()
-    for copy in copies:
-        copy.wait()
-    edge[...] = gate_tail[...] * input_tail[...]
-
-
-def edge_call(gate_streams, inputs, window, share, half):
+    copies[0].wait()
+    copies[1].wait()
+    low[...] = gate_tail[:share, :] * input_tail[:share, :]
+    high[...] = gate_tail[share:, :] * input_tail[share:, :]
+    copies[2].wait()
+
+
+def lend_call(place, gate_streams, inputs, window, share):
+    channels, tokens = inputs.shape
+    edge = jax.ShapeDtypeStruct((share, window), jnp.bfloat16)
     return pl.pallas_call(
-        functools.partial(edge_kernel, half * share),
-        out_shape=jax.ShapeDtypeStruct((share, window), jnp.bfloat16),
-        in_specs=[ANY_SPEC] * 2,
-        out_specs=VMEM_SPEC,
-        scratch_shapes=[pltpu.VMEM((share, window), jnp.bfloat16)] * 2
-        + [pltpu.SemaphoreType.DMA((2,))],
-        name="edge",
-        cost_estimate=cost(share, window, 2),
+        lend_kernel,
+        out_shape=(jax.ShapeDtypeStruct((2, share, tokens), jnp.bfloat16), edge, edge),
+        in_specs=[SMEM_SPEC] * 2 + [ANY_SPEC] * 2,
+        out_specs=(VMEM_SPEC,) * 3,
+        scratch_shapes=[pltpu.VMEM((channels, window), jnp.bfloat16)] * 2
+        + [pltpu.SemaphoreType.DMA((3,))],
+        name="lend",
+        cost_estimate=cost(share, tokens, 2),
         compiler_params=COMPILER,
-    )(*parked(gate_streams, inputs))
+    )(*place, *parked(gate_streams, inputs))
 
 
 def ring(value, axis, by):
@@ -783,11 +777,11 @@
     place = tuple(
         lax.axis_index(axis).astype(jnp.int32).reshape(1) for axis in ("section", "tok")
     )
+    lent, *edges = lend_call(place, gate_streams, inputs, window, share)
     halos = []
     for half in range(2):
-        edge = edge_call(gate_streams, inputs, window, share, half)
-        halos.append(edge_to(edge, half))
-    swapped = ring(gate_streams[0], "section", 1)
+        halos.append(edge_to(edges[half], half))
+    remote = ring(lent, "section", 1)
     forward, inverse = fourier_tables(window)
     turned, back, doubled = turned_tables(window)
     tables = [*forward, *inverse, *split_pair(turned), split_pair(back)[0]]
@@ -806,9 +800,7 @@
     )
     response, rates, scales, rising, falling = built
     gates, inputs, taps = own
-    medium, signals, *specs, remote = later_call(
-        place, gates, swapped, inputs, taps, tables[:4]
-    )
+    medium, signals, *specs = later_call(place, gates, remote, inputs, taps, tables[:4])
     medium, signals, ends, total = first_call(
         place,
         gates,

time: 26.7 us -> 26.9 us (level)
  Pallas kernels: 15.1 us -> 13.6 us
  starting transfers between devices: 8.49 us -> 9.49 us
  waiting for transfers between devices: 2.66 us -> 3.4 us
    ppermute x2, waiting for transfers between devices: 0.01 us -> 2.21 us  [edge_to(): return lax.ppermute(value, ('section', 'tok'), pairs)]
    ppermute x3, waiting for transfers between devices: 1.92 us -> 0.46 us  [met(): return lax.ppermute(value, 'tok', [(i, i ^ by) for i in range(peers)])]
    pallas_call x1, Pallas kernels: 3.01 us -> 1.77 us  [later_call(): pl.pallas_call(functools.partial(later_kernel, min(STEP, share)), out_sha...]
    ppermute x3, starting transfers between devices: 0.64 us -> 1.6 us  [ring(): lax.ppermute(value, axis, [(i, (i + by) % peers) for i in range(peers)])]
    pallas_call x2 -> x1, Pallas kernels: 2.23 us -> 2.02 us  [lend_call(): pl.pallas_call(lend_kernel, out_shape=(jax.ShapeDtypeStruct((2, share, to...]
  transfers between devices with their start and end apart: 8 -> 8, of which waited for: 3 -> 5; matrix products, arithmetic and copies ran while one was open for 0% -> 0% of each run, Pallas kernels for 46% -> 32%
where the time goes in v12:
time: 26.9 us; the launch traced here: 26.6 us
  Pallas kernels  13.6 us (51%)
  starting transfers between devices  9.49 us (35%)
  waiting for transfers between devices  3.4 us (13%)
    ppermute x2, starting transfers between devices, edge_to(): return lax.ppermute(value, ('section', 'tok'), pairs)  4.94 us
    pallas_call x1, Pallas kernels, response_call(): pl.pallas_call(functools.partial(response_kernel, len(tables), window), o...  3.34 us
    ppermute x3, starting transfers between devices, met(): return lax.ppermute(value, 'tok', [(i, i ^ by) for i in range(peers)])  2.95 us
    ppermute x2, waiting for transfers between devices, edge_to(): return lax.ppermute(value, ('section', 'tok'), pairs)  2.21 us
    pallas_call x1, Pallas kernels, lend_call(): pl.pallas_call(lend_kernel, out_shape=(jax.ShapeDtypeStruct((2, share, to...  2.02 us
    pallas_call x2, Pallas kernels, place_call(): pl.pallas_call(functools.partial(place_kernel, half * rows, before.shape[...  1.96 us
    pallas_call x2, Pallas kernels, output_call(): pl.pallas_call(functools.partial(output_kernel, len(arrived), lanes // RO...  1.93 us
    pallas_call x1, Pallas kernels, later_call(): pl.pallas_call(functools.partial(later_kernel, min(STEP, share)), out_sha...  1.77 us
  transfers between devices with their start and end apart: 8, of which 5 were waited for; matrix products, arithmetic and copies ran while one was open for 0% of the time, Pallas kernels for 32%

profile of v12, /device:TPU:1, one launch (start us, length us, event | category | flops | bytes accessed | tf_op | source)
XLA Modules:
  0.0 26.6 jit_solution(13277666155368990333)
XLA Ops:
  0.0 0.0 copy-start
  0.0 0.0 copy-start.1
  0.0 2.0 %lend.1 = (bf16[2,1024,512]{2,1,0:T(8,128)(2,1)S(1)}, bf16[1024,128]{1,0:T(8,128)(2,1)S(1)}, bf16[1024,128]{1,0:T(8,128)(2,1)S(1)}) custom-call(s32[1]{0:T(128)} %bitcast.sec, s32[1]{0:T(128)} %bitcast.1.tok, bf16[1,2,2048,512]{3,2,1,0:T(8,128)(2,1)} %gates.1, bf16[2048,512]{1,0:T(8,128)(2,1)} %inputs.1), custom_call_target="tpu_custom_call" | custom-call | flops 1048576 | bytes 6291456 | tf_op jit(solution)/shard_map/lend/pallas_call | solution.py:742
  2.0 0.1 collective-permute-start
  2.1 0.7 %collective-permute-start.1 = (bf16[1024,128]{1,0:T(8,128)(2,1)S(1)}, bf16[1024,128]{1,0:T(8,128)(2,1)S(1)}, u32[]{:S(2)}, u32[]{:S(2)}) collective-permute-start(bf16[1024,128]{1,0:T(8,128)(2,1)S(1)} %get-tuple-element.42), channel_id=1, source_target_pairs={{0,1},{1,2},{2,3},{3,0},{16,16},{17,17},{18,18},{19,19},{4,5},{5,6... | collective-permute-start | bytes 786440 | tf_op jit(solution)/shard_map/ppermute | solution.py:769
  2.8 4.3 %collective-permute-start.2 = (bf16[1024,128]{1,0:T(8,128)(2,1)S(1)}, bf16[1024,128]{1,0:T(8,128)(2,1)S(1)}, u32[]{:S(2)}, u32[]{:S(2)}) collective-permute-start(bf16[1024,128]{1,0:T(8,128)(2,1)S(1)} %get-tuple-element.43), channel_id=1, source_target_pairs={{0,17},{1,18},{2,19},{3,16},{16,0},{17,1},{18,2},{19,3},{4,21},{5,... | collective-permute-start | bytes 786440 | tf_op jit(solution)/shard_map/ppermute | solution.py:769
  7.1 0.0 copy-done
  7.1 0.0 copy-done.1
  7.1 3.3 %response.1 = (f32[1024,128]{1,0:T(8,128)S(1)}, f32[128,128]{1,0:T(8,128)S(1)}, f32[128,128]{1,0:T(8,128)S(1)}, bf16[64,128,256]{2,1,0:T(8,128)(2,1)S(1)}, bf16[...) custom-call(s32[1]{0:T(128)} %bitcast.sec, ...), custom_call_target="tpu_custom_call" | custom-call | flops 471859200 | bytes 6291456 | tf_op jit(solution)/shard_map/response/pallas_call | solution.py:239
  10.4 0.0 collective-permute-done.remote_all
  10.4 1.8 %later.1 = (bf16[1024,512]{1,0:T(8,128)(2,1)S(1)}, bf16[1024,512]{1,0:T(8,128)(2,1)S(1)}, f32[1024,256]{1,0:T(8,128)S(1)}, f32[1024,256]{1,0:T(8,128)S(1)}) custom-call(s32[1]{0:T(128)} %bitcast.sec, s32[1]{0:T(128)} %bitcast.1.tok, bf16[2,1024,512]{2,1,0:T(8,128)(2,1)S(1)} %get-tuple-element.39.local_all, ...), custom_call_target="tpu_custom_call" | custom-call | flops 786432000 | bytes 6291456 | tf_op jit(solution)/shard_map/later/pallas_call | solution.py:375
  12.2 0.0 collective-permute-done.1.halo_low
  12.2 2.2 %collective-permute-done.2.halo_high = bf16[1024,128]{1,0:T(8,128)(2,1)S(1)} collective-permute-done((bf16[1024,128]{1,0:T(8,128)(2,1)S(1)}, bf16[1024,128]{1,0:T(8,128)(2,1)S(1)}, u32[]{:S(2)}, u32[]{:S(2)}) %collective-permute-start.2) | collective-permute-done | bytes 262176 | tf_op jit(solution)/shard_map/ppermute | solution.py:769
  14.4 1.3 %first.1 = (bf16[1024,512]{1,0:T(8,128)(2,1)S(1)}, bf16[1024,512]{1,0:T(8,128)(2,1)S(1)}, f32[4,1024,128]{2,1,0:T(8,128)S(1)}, bf16[128,128]{1,0:T(8,128)(2,1)S(1)}) custom-call(s32[1]{0:T(128)} %bitcast.sec, s32[1]{0:T(128)} %bitcast.1.tok, bf16[2,1024,512]{2,1,0:T(8,128)(2,1)S(1)} %get-tuple-element.39.local_all, ...), custom_call_target="tpu_custom_call", output_to_operand_aliasing={{0}: (13, {}), {1}: (14, {})} | custom-call | flops 262144000 | bytes 6291456 | tf_op jit(solution)/shard_map/first/pallas_call | solution.py:469
  15.7 1.8 %collective-permute-start.5 = (bf16[128,128]{1,0:T(8,128)(2,1)S(1)}, bf16[128,128]{1,0:T(8,128)(2,1)S(1)}, u32[]{:S(2)}, u32[]{:S(2)}) collective-permute-start(bf16[128,128]{1,0:T(8,128)(2,1)S(1)} %get-tuple-element.66), channel_id=1, source_target_pairs={{0,3},{1,2},{2,1},{3,0},{4,7},{5,6},{6,5},{7,4},{8,11},{9,10},{10,... | collective-permute-start | bytes 98312 | tf_op jit(solution)/shard_map/ppermute | solution.py:762
  17.5 0.2 collective-permute-start.4
  17.7 0.9 %collective-permute-start.3 = (bf16[128,128]{1,0:T(8,128)(2,1)S(1)}, bf16[128,128]{1,0:T(8,128)(2,1)S(1)}, u32[]{:S(2)}, u32[]{:S(2)}) collective-permute-start(bf16[128,128]{1,0:T(8,128)(2,1)S(1)} %get-tuple-element.66), channel_id=1, source_target_pairs={{0,1},{1,0},{2,3},{3,2},{4,5},{5,4},{6,7},{7,6},{8,9},{9,8},{10,11... | collective-permute-start | bytes 98312 | tf_op jit(solution)/shard_map/ppermute | solution.py:762
  18.6 1.4 %within.1.within_all = f32[1024,512]{1,0:T(8,128)S(1)} custom-call(bf16[1024,512]{1,0:T(8,128)(2,1)S(1)} %get-tuple-element.55.signals_all, f32[1024,128]{1,0:T(8,128)S(1)} %get-tuple-element.56.response_all, bf16[256,256]{1,0:T(8,128)(2,1)S(1)} %get-tuple-element.57.fwd_h, bf16[256,256]{1,0:T(8,128)(2,1)S(1)} %get-tuple-element.58.fwd_l, ...), custom_call_target="tpu_custom_call" | custom-call | flops 786432000 | bytes 6291456 | tf_op jit(solution)/shard_map/within/pallas_call | solution.py:534
  20.0 0.0 collective-permute-done.5.rest_2_
  20.0 0.2 collective-permute-done.4.rest_1_
  20.2 0.2 collective-permute-done.3.rest_0_
  20.5 1.0 %output.2 = (bf16[1,2048,512]{2,1,0:T(8,128)(2,1)}, bf16[512,512]{1,0:T(8,128)(2,1)S(1)}, bf16[512,512]{1,0:T(8,128)(2,1)S(1)}) custom-call(s32[1]{0:T(128)} %bitcast.sec, s32[1]{0:T(128)} %bitcast.1.tok, bf16[2,1024,512]{2,1,0:T(8,128)(2,1)S(1)} %get-tuple-element.39.local_all, bf16[2,1024,512]{2,1,0:T(8,128)(2,1)S(1)} %collective-permute-done.remote_all, ...), custom_call_target="tpu_custom_call" | custom-call | flops 393216000 | bytes 3145728 | tf_op jit(solution)/shard_map/output/pallas_call | solution.py:654
  21.4 1.4 %collective-permute-start.6 = (bf16[512,512]{1,0:T(8,128)(2,1)S(1)}, bf16[512,512]{1,0:T(8,128)(2,1)S(1)}, u32[]{:S(2)}, u32[]{:S(2)}) collective-permute-start(bf16[512,512]{1,0:T(8,128)(2,1)S(1)} %get-tuple-element.69), channel_id=1, source_target_pairs={{0,16},{16,0},{1,17},{17,1},{2,18},{18,2},{3,19},{19,3},{4,20},{20... | collective-permute-start | bytes 1572872 | tf_op jit(solution)/shard_map/ppermute | solution.py:757
  22.9 1.0 %output.3 = (bf16[1,2048,512]{2,1,0:T(8,128)(2,1)}, bf16[512,512]{1,0:T(8,128)(2,1)S(1)}, bf16[512,512]{1,0:T(8,128)(2,1)S(1)}) custom-call(s32[1]{0:T(128)} %bitcast.sec, s32[1]{0:T(128)} %bitcast.1.tok, bf16[2,1024,512]{2,1,0:T(8,128)(2,1)S(1)} %get-tuple-element.39.local_all, ...), custom_call_target="tpu_custom_call", output_to_operand_aliasing={{0}: (14, {})} | custom-call | flops 393216000 | bytes 3145728 | tf_op jit(solution)/shard_map/output/pallas_call | solution.py:654
  23.9 0.1 collective-permute-start.7
  23.9 0.5 %collective-permute-done.6.received = bf16[512,512]{1,0:T(8,128)(2,1)S(1)} collective-permute-done((bf16[512,512]{1,0:T(8,128)(2,1)S(1)}, bf16[512,512]{1,0:T(8,128)(2,1)S(1)}, u32[]{:S(2)}, u32[]{:S(2)}) %collective-permute-start.6) | collective-permute-done | bytes 524320 | tf_op jit(solution)/shard_map/ppermute | solution.py:757
  24.4 1.2 %placing.2.before = bf16[1,2048,512]{2,1,0:T(8,128)(2,1)} custom-call(s32[1]{0:T(128)} %bitcast.sec, bf16[1,2048,512]{2,1,0:T(8,128)(2,1)} %get-tuple-element.68.before, bf16[512,512]{1,0:T(8,128)(2,1)S(1)} %collective-permute-done.6.received, bf16[512,512]{1,0:T(8,128)(2,1)S(1)} %get-tuple-element.70.rest_0_, ...), custom_call_target="tpu_custom_call", output_to_operand_aliasing={{}: (1, {})} | custom-call | flops 524288 | bytes 3145728 | tf_op jit(solution)/shard_map/placing/pallas_call | solution.py:702
  25.6 0.2 collective-permute-done.7.received
  25.8 0.8 %placing.3 = bf16[1,2048,512]{2,1,0:T(8,128)(2,1)} custom-call(s32[1]{0:T(128)} %bitcast.sec, bf16[1,2048,512]{2,1,0:T(8,128)(2,1)} %placing.2.before, bf16[512,512]{1,0:T(8,128)(2,1)S(1)} %collective-permute-done.7.received), custom_call_target="tpu_custom_call", output_to_operand_aliasing={{}: (1, {})} | custom-call | flops 524288 | bytes 3145728 | tf_op jit(solution)/shard_map/placing/pallas_call | solution.py:702
Async XLA Ops:
  0.0 7.1 %copy-start = (f32[2048,16]{0,1:T(8,128)S(1)}, f32[2048,16]{0,1:T(8,128)}, u32[]{:S(2)}) copy-start(f32[2048,16]{0,1:T(8,128)} %param.22) | copy-start | bytes 393220
  0.0 7.1 %copy-start.1 = (f32[2048,16]{0,1:T(8,128)S(1)}, f32[2048,16]{0,1:T(8,128)}, u32[]{:S(2)}) copy-start(f32[2048,16]{0,1:T(8,128)} %param.21) | copy-start | bytes 393220
  2.0 8.4 %collective-permute-start = (bf16[2,1024,512]{2,1,0:T(8,128)(2,1)S(1)}, bf16[2,1024,512]{2,1,0:T(8,128)(2,1)S(1)}, u32[]{:S(2)}, u32[]{:S(2)}) collective-permute-start(bf16[2,1024,512]{2,1,0:T(8,128)(2,1)S(1)} %get-tuple-element.40), channel_id=1, source_target_pairs={{0,16},{16,0},{1,17},{17,1},{2,18},{18,2},{3,19},{19,3},{4,20},{20... | collective-permute-start | bytes 6291464 | tf_op jit(solution)/shard_map/ppermute | solution.py:757
  2.1 10.1 %collective-permute-start.1 = (bf16[1024,128]{1,0:T(8,128)(2,1)S(1)}, bf16[1024,128]{1,0:T(8,128)(2,1)S(1)}, u32[]{:S(2)}, u32[]{:S(2)}) collective-permute-start(bf16[1024,128]{1,0:T(8,128)(2,1)S(1)} %get-tuple-element.42), channel_id=1, source_target_pairs={{0,1},{1,2},{2,3},{3,0},{16,16},{17,17},{18,18},{19,19},{4,5},{5,6... | collective-permute-start | bytes 786440 | tf_op jit(solution)/shard_map/ppermute | solution.py:769
  2.8 11.6 %collective-permute-start.2 = (bf16[1024,128]{1,0:T(8,128)(2,1)S(1)}, bf16[1024,128]{1,0:T(8,128)(2,1)S(1)}, u32[]{:S(2)}, u32[]{:S(2)}) collective-permute-start(bf16[1024,128]{1,0:T(8,128)(2,1)S(1)} %get-tuple-element.43), channel_id=1, source_target_pairs={{0,17},{1,18},{2,19},{3,16},{16,0},{17,1},{18,2},{19,3},{4,21},{5,... | collective-permute-start | bytes 786440 | tf_op jit(solution)/shard_map/ppermute | solution.py:769
  15.7 4.3 %collective-permute-start.5 = (bf16[128,128]{1,0:T(8,128)(2,1)S(1)}, bf16[128,128]{1,0:T(8,128)(2,1)S(1)}, u32[]{:S(2)}, u32[]{:S(2)}) collective-permute-start(bf16[128,128]{1,0:T(8,128)(2,1)S(1)} %get-tuple-element.66), channel_id=1, source_target_pairs={{0,3},{1,2},{2,1},{3,0},{4,7},{5,6},{6,5},{7,4},{8,11},{9,10},{10,... | collective-permute-start | bytes 98312 | tf_op jit(solution)/shard_map/ppermute | solution.py:762
  17.5 2.8 %collective-permute-start.4 = (bf16[128,128]{1,0:T(8,128)(2,1)S(1)}, bf16[128,128]{1,0:T(8,128)(2,1)S(1)}, u32[]{:S(2)}, u32[]{:S(2)}) collective-permute-start(bf16[128,128]{1,0:T(8,128)(2,1)S(1)} %get-tuple-element.66), channel_id=1, source_target_pairs={{0,2},{1,3},{2,0},{3,1},{4,6},{5,7},{6,4},{7,5},{8,10},{9,11},{10,... | collective-permute-start | bytes 98312 | tf_op jit(solution)/shard_map/ppermute | solution.py:762
  17.7 2.8 %collective-permute-start.3 = (bf16[128,128]{1,0:T(8,128)(2,1)S(1)}, bf16[128,128]{1,0:T(8,128)(2,1)S(1)}, u32[]{:S(2)}, u32[]{:S(2)}) collective-permute-start(bf16[128,128]{1,0:T(8,128)(2,1)S(1)} %get-tuple-element.66), channel_id=1, source_target_pairs={{0,1},{1,0},{2,3},{3,2},{4,5},{5,4},{6,7},{7,6},{8,9},{9,8},{10,11... | collective-permute-start | bytes 98312 | tf_op jit(solution)/shard_map/ppermute | solution.py:762
  21.4 3.0 %collective-permute-start.6 = (bf16[512,512]{1,0:T(8,128)(2,1)S(1)}, bf16[512,512]{1,0:T(8,128)(2,1)S(1)}, u32[]{:S(2)}, u32[]{:S(2)}) collective-permute-start(bf16[512,512]{1,0:T(8,128)(2,1)S(1)} %get-tuple-element.69), channel_id=1, source_target_pairs={{0,16},{16,0},{1,17},{17,1},{2,18},{18,2},{3,19},{19,3},{4,20},{20... | collective-permute-start | bytes 1572872 | tf_op jit(solution)/shard_map/ppermute | solution.py:757
  23.9 2.0 %collective-permute-start.7 = (bf16[512,512]{1,0:T(8,128)(2,1)S(1)}, bf16[512,512]{1,0:T(8,128)(2,1)S(1)}, u32[]{:S(2)}, u32[]{:S(2)}) collective-permute-start(bf16[512,512]{1,0:T(8,128)(2,1)S(1)} %get-tuple-element.72), channel_id=1, source_target_pairs={{0,16},{16,0},{1,17},{17,1},{2,18},{18,2},{3,19},{19,3},{4,20},{20... | collective-permute-start | bytes 1572872 | tf_op jit(solution)/shard_map/ppermute | solution.py:757

commit v13 on v11

--- a/solution.py
+++ b/solution.py
@@ -333,18 +333,17 @@
     blocks = tokens // window
     parts = [slice(b * window, (b + 1) * window) for b in range(blocks)]
 
-    def fetch(i):
+    def fetch(kind, i):
         source = pl.ds(pl.multiple_of(sec[0] * share + i * step, step), step)
         return pltpu.make_async_copy(
-            swapped.at[:, source, :], rows_at(remote_all, step, i, 1), arrival.at[i]
+            swapped.at[kind, source, :],
+            rows_at(remote_all.at[kind], step, i),
+            arrival.at[kind, i],
         )
-
-    for i in range(share // step):
-        fetch(i).start()
 
     def chunk(section, i):
         if section == 1:
-            fetch(i).wait()
+            fetch(1, i).wait()
         first, second = both_gates(local_all, remote_all, section, step, i)
         inputs = rows_at(inputs_all, step, i)
         medium_out, signals = rows_at(medium_all, step, i), rows_at(signals_all, step, i)
@@ -359,7 +358,10 @@
         rows_at(edge_spec_all, step, i)[...] = in_order[0]
         mixed = products([in_order[b - 1] + in_order[b] for b in range(1, blocks)], tap_spec)
         if section == 0:
-            fetch(i).wait()
+            fetch(1, i).wait()
+            fetch(0, i).start()
+        else:
+            fetch(0, i).wait()
         for parity, table in enumerate((inv_even, inv_odd)):
             chosen = [b for b in range(1, blocks) if b % 2 == parity]
             if not chosen:
@@ -376,7 +378,14 @@
                 signals[:, parts[b]] = signal
 
     def body(section):
+        for i in range(share // step):
+            fetch(1, i).start()
+            if section == 1:
+                fetch(0, i).start()
         pl.loop(0, share // step)(functools.partial(chunk, section))
+        if section == 0:
+            for i in range(share // step):
+                fetch(0, i).wait()
 
     by_section(sec, body)
 
@@ -392,7 +401,7 @@
         out_shape=(wide, wide, spec, spec, jax.ShapeDtypeStruct(gates.shape, gates.dtype)),
         in_specs=[SMEM_SPEC] * 2 + [VMEM_SPEC, ANY_SPEC] + [VMEM_SPEC] * (len(operands) - 2),
         out_specs=(VMEM_SPEC,) * 5,
-        scratch_shapes=[pltpu.SemaphoreType.DMA((share // min(STEP, share),))],
+        scratch_shapes=[pltpu.SemaphoreType.DMA((2, share // min(STEP, share)))],
         name="later",
         cost_estimate=cost(share, tokens, 1500),
         compiler_params=COMPILER,
@@ -728,11 +737,10 @@
     )(place[0], before, received, *kept)
 
 
-def edge_kernel(first, gates, inputs, edge, gate_tail, input_tail, arrival):
-    share, window = edge.shape
-    rows = pl.ds(first, share)
+def edge_kernel(gates, inputs, low, high, gate_tail, input_tail, arrival):
+    share, window = low.shape
     tail = pl.ds(inputs.shape[1] - window, window)
-    pairs = [(gates.at[0, 1, rows, tail], gate_tail), (inputs.at[rows, tail], input_tail)]
+    pairs = [(gates.at[0, 1, :, tail], gate_tail), (inputs.at[:, tail], input_tail)]
     copies = [
         pltpu.make_async_copy(source, target, arrival.at[k])
         for k, (source, target) in enumerate(pairs)
@@ -741,19 +749,22 @@
         copy.start()
     for copy in copies:
         copy.wait()
-    edge[...] = gate_tail[...] * input_tail[...]
-
-
-def edge_call(gate_streams, inputs, window, share, half):
+    low[...] = gate_tail[:share, :] * input_tail[:share, :]
+    high[...] = gate_tail[share:, :] * input_tail[share:, :]
+
+
+def edge_call(gate_streams, inputs, window, share):
+    channels, tokens = inputs.shape
+    edge = jax.ShapeDtypeStruct((share, window), jnp.bfloat16)
     return pl.pallas_call(
-        functools.partial(edge_kernel, half * share),
-        out_shape=jax.ShapeDtypeStruct((share, window), jnp.bfloat16),
+        edge_kernel,
+        out_shape=(edge, edge),
         in_specs=[ANY_SPEC] * 2,
-        out_specs=VMEM_SPEC,
-        scratch_shapes=[pltpu.VMEM((share, window), jnp.bfloat16)] * 2
+        out_specs=(VMEM_SPEC,) * 2,
+        scratch_shapes=[pltpu.VMEM((channels, window), jnp.bfloat16)] * 2
         + [pltpu.SemaphoreType.DMA((2,))],
         name="edge",
-        cost_estimate=cost(share, window, 2),
+        cost_estimate=cost(share, tokens, 2),
         compiler_params=COMPILER,
     )(*parked(gate_streams, inputs))
 
@@ -783,10 +794,8 @@
     place = tuple(
         lax.axis_index(axis).astype(jnp.int32).reshape(1) for axis in ("section", "tok")
     )
-    halos = []
-    for half in range(2):
-        edge = edge_call(gate_streams, inputs, window, share, half)
-        halos.append(edge_to(edge, half))
+    edges = edge_call(gate_streams, inputs, window, share)
+    halos = [edge_to(edges[s], s) for s in range(2)]
     swapped = ring(gate_streams[0], "section", 1)
     forward, inverse = fourier_tables(window)
     turned, back, doubled = turned_tables(window)

time: 26.7 us -> 26.9 us (level)
  waiting for transfers between devices: 2.66 us -> 3.31 us
  Pallas kernels: 15.1 us -> 14.6 us
    pallas_call x2 -> x1, Pallas kernels: 2.23 us -> 1.39 us  [edge_call(): pl.pallas_call(edge_kernel, out_shape=(edge, edge), in_specs=[ANY_SPEC] *...]
    ppermute x2, waiting for transfers between devices: 0.01 us -> 0.64 us  [edge_to(): return lax.ppermute(value, ('section', 'tok'), pairs)]
    pallas_call x1, Pallas kernels: 3.01 us -> 3.34 us  [later_call(): pl.pallas_call(functools.partial(later_kernel, min(STEP, share)), out_sha...]
  transfers between devices with their start and end apart: 8 -> 8, of which waited for: 3 -> 4; matrix products, arithmetic and copies ran while one was open for 0% -> 0% of each run, Pallas kernels for 46% -> 44%
where the time goes in v13:
time: 26.9 us; the launch traced here: 26.5 us
  Pallas kernels  14.6 us (54%)
  starting transfers between devices  8.53 us (32%)
  waiting for transfers between devices  3.31 us (12%)
    ppermute x2, starting transfers between devices, edge_to(): return lax.ppermute(value, ('section', 'tok'), pairs)  4.94 us
    pallas_call x1, Pallas kernels, later_call(): pl.pallas_call(functools.partial(later_kernel, min(STEP, share)), out_sha...  3.34 us
    pallas_call x1, Pallas kernels, response_call(): pl.pallas_call(functools.partial(response_kernel, len(tables), window), o...  3.34 us
    ppermute x3, starting transfers between devices, met(): return lax.ppermute(value, 'tok', [(i, i ^ by) for i in range(peers)])  2.96 us
    ppermute x3, waiting for transfers between devices, met(): return lax.ppermute(value, 'tok', [(i, i ^ by) for i in range(peers)])  2.03 us
    pallas_call x2, Pallas kernels, place_call(): pl.pallas_call(functools.partial(place_kernel, half * rows, before.shape[...  1.96 us
    pallas_call x2, Pallas kernels, output_call(): pl.pallas_call(functools.partial(output_kernel, len(arrived), lanes // RO...  1.92 us
    pallas_call x1, Pallas kernels, edge_call(): pl.pallas_call(edge_kernel, out_shape=(edge, edge), in_specs=[ANY_SPEC] *...  1.39 us
  transfers between devices with their start and end apart: 8, of which 4 were waited for; matrix products, arithmetic and copies ran while one was open for 0% of the time, Pallas kernels for 44%

profile of v13, /device:TPU:1, one launch (start us, length us, event | category | flops | bytes accessed | tf_op | source)
XLA Modules:
  0.0 26.5 jit_solution(9568253149854819295)
XLA Ops:
  0.0 0.0 copy-start
  0.0 0.0 copy-start.1
  0.0 0.0 collective-permute-start
  0.0 1.4 %edge.1 = (bf16[1024,128]{1,0:T(8,128)(2,1)S(1)}, bf16[1024,128]{1,0:T(8,128)(2,1)S(1)}) custom-call(bf16[1,2,2048,512]{3,2,1,0:T(8,128)(2,1)} %gates.1, bf16[2048,512]{1,0:T(8,128)(2,1)} %inputs.1), custom_call_target="tpu_custom_call" | custom-call | flops 1048576 | bytes 6291456 | tf_op jit(solution)/shard_map/edge/pallas_call | solution.py:759
  1.4 0.7 %collective-permute-start.1 = (bf16[1024,128]{1,0:T(8,128)(2,1)S(1)}, bf16[1024,128]{1,0:T(8,128)(2,1)S(1)}, u32[]{:S(2)}, u32[]{:S(2)}) collective-permute-start(bf16[1024,128]{1,0:T(8,128)(2,1)S(1)} %get-tuple-element.47), channel_id=1, source_target_pairs={{0,1},{1,2},{2,3},{3,0},{16,16},{17,17},{18,18},{19,19},{4,5},{5,6... | collective-permute-start | bytes 786440 | tf_op jit(solution)/shard_map/ppermute | solution.py:786
  2.1 4.3 %collective-permute-start.2 = (bf16[1024,128]{1,0:T(8,128)(2,1)S(1)}, bf16[1024,128]{1,0:T(8,128)(2,1)S(1)}, u32[]{:S(2)}, u32[]{:S(2)}) collective-permute-start(bf16[1024,128]{1,0:T(8,128)(2,1)S(1)} %get-tuple-element.48), channel_id=1, source_target_pairs={{0,17},{1,18},{2,19},{3,16},{16,0},{17,1},{18,2},{19,3},{4,21},{5,... | collective-permute-start | bytes 786440 | tf_op jit(solution)/shard_map/ppermute | solution.py:786
  6.4 0.0 copy-done
  6.4 0.0 copy-done.1
  6.4 3.3 %response.1 = (f32[1024,128]{1,0:T(8,128)S(1)}, f32[128,128]{1,0:T(8,128)S(1)}, f32[128,128]{1,0:T(8,128)S(1)}, bf16[64,128,256]{2,1,0:T(8,128)(2,1)S(1)}, bf16[...) custom-call(s32[1]{0:T(128)} %bitcast.sec, ...), custom_call_target="tpu_custom_call" | custom-call | flops 471859200 | bytes 6291456 | tf_op jit(solution)/shard_map/response/pallas_call | solution.py:239
  9.7 0.0 collective-permute-done.swapped
  9.7 3.3 %later.1 = (bf16[1024,512]{1,0:T(8,128)(2,1)S(1)}, bf16[1024,512]{1,0:T(8,128)(2,1)S(1)}, f32[1024,256]{1,0:T(8,128)S(1)}, f32[1024,256]{1,0:T(8,128)S(1)}, bf16[2,1024,512]{2,1,0:T(8,128)(2,1)S(1)}) custom-call(s32[1]{0:T(128)} %bitcast.sec, s32[1]{0:T(128)} %bitcast.1.tok, bf16[2,1024,512]{2,1,0:T(8,128)(2,1)S(1)} %get-tuple-element.39.local_all, ...), custom_call_target="tpu_custom_call" | custom-call | flops 786432000 | bytes 6291456 | tf_op jit(solution)/shard_map/later/pallas_call | solution.py:399
  13.1 0.0 collective-permute-done.1.halo_low
  13.1 0.6 %collective-permute-done.2.halo_high = bf16[1024,128]{1,0:T(8,128)(2,1)S(1)} collective-permute-done((bf16[1024,128]{1,0:T(8,128)(2,1)S(1)}, bf16[1024,128]{1,0:T(8,128)(2,1)S(1)}, u32[]{:S(2)}, u32[]{:S(2)}) %collective-permute-start.2) | collective-permute-done | bytes 262176 | tf_op jit(solution)/shard_map/ppermute | solution.py:786
  13.7 1.3 %first.1 = (bf16[1024,512]{1,0:T(8,128)(2,1)S(1)}, bf16[1024,512]{1,0:T(8,128)(2,1)S(1)}, f32[4,1024,128]{2,1,0:T(8,128)S(1)}, bf16[128,128]{1,0:T(8,128)(2,1)S(1)}) custom-call(s32[1]{0:T(128)} %bitcast.sec, s32[1]{0:T(128)} %bitcast.1.tok, bf16[2,1024,512]{2,1,0:T(8,128)(2,1)S(1)} %get-tuple-element.39.local_all, ...), custom_call_target="tpu_custom_call", output_to_operand_aliasing={{0}: (13, {}), {1}: (14, {})} | custom-call | flops 262144000 | bytes 6291456 | tf_op jit(solution)/shard_map/first/pallas_call | solution.py:494
  15.0 0.8 %collective-permute-start.3 = (bf16[128,128]{1,0:T(8,128)(2,1)S(1)}, bf16[128,128]{1,0:T(8,128)(2,1)S(1)}, u32[]{:S(2)}, u32[]{:S(2)}) collective-permute-start(bf16[128,128]{1,0:T(8,128)(2,1)S(1)} %get-tuple-element.66), channel_id=1, source_target_pairs={{0,1},{1,0},{2,3},{3,2},{4,5},{5,4},{6,7},{7,6},{8,9},{9,8},{10,11... | collective-permute-start | bytes 98312 | tf_op jit(solution)/shard_map/ppermute | solution.py:779
  15.8 1.2 %collective-permute-start.4 = (bf16[128,128]{1,0:T(8,128)(2,1)S(1)}, bf16[128,128]{1,0:T(8,128)(2,1)S(1)}, u32[]{:S(2)}, u32[]{:S(2)}) collective-permute-start(bf16[128,128]{1,0:T(8,128)(2,1)S(1)} %get-tuple-element.66), channel_id=1, source_target_pairs={{0,2},{1,3},{2,0},{3,1},{4,6},{5,7},{6,4},{7,5},{8,10},{9,11},{10,... | collective-permute-start | bytes 98312 | tf_op jit(solution)/shard_map/ppermute | solution.py:779
  17.1 0.9 %collective-permute-start.5 = (bf16[128,128]{1,0:T(8,128)(2,1)S(1)}, bf16[128,128]{1,0:T(8,128)(2,1)S(1)}, u32[]{:S(2)}, u32[]{:S(2)}) collective-permute-start(bf16[128,128]{1,0:T(8,128)(2,1)S(1)} %get-tuple-element.66), channel_id=1, source_target_pairs={{0,3},{1,2},{2,1},{3,0},{4,7},{5,6},{6,5},{7,4},{8,11},{9,10},{10,... | collective-permute-start | bytes 98312 | tf_op jit(solution)/shard_map/ppermute | solution.py:779
  18.0 1.4 %within.1.within_all = f32[1024,512]{1,0:T(8,128)S(1)} custom-call(bf16[1024,512]{1,0:T(8,128)(2,1)S(1)} %get-tuple-element.55.signals_all, f32[1024,128]{1,0:T(8,128)S(1)} %get-tuple-element.56.response_all, bf16[256,256]{1,0:T(8,128)(2,1)S(1)} %get-tuple-element.57.fwd_h, bf16[256,256]{1,0:T(8,128)(2,1)S(1)} %get-tuple-element.58.fwd_l, ...), custom_call_target="tpu_custom_call" | custom-call | flops 786432000 | bytes 6291456 | tf_op jit(solution)/shard_map/within/pallas_call | solution.py:559
  19.3 0.0 collective-permute-done.3.rest_0_
  19.3 0.0 collective-permute-done.4.rest_1_
  19.3 2.0 %collective-permute-done.5.rest_2_ = bf16[128,128]{1,0:T(8,128)(2,1)S(1)} collective-permute-done((bf16[128,128]{1,0:T(8,128)(2,1)S(1)}, bf16[128,128]{1,0:T(8,128)(2,1)S(1)}, u32[]{:S(2)}, u32[]{:S(2)}) %collective-permute-start.5) | collective-permute-done | bytes 32800 | tf_op jit(solution)/shard_map/ppermute | solution.py:779
  21.4 1.0 %output.2 = (bf16[1,2048,512]{2,1,0:T(8,128)(2,1)}, bf16[512,512]{1,0:T(8,128)(2,1)S(1)}, bf16[512,512]{1,0:T(8,128)(2,1)S(1)}) custom-call(s32[1]{0:T(128)} %bitcast.sec, s32[1]{0:T(128)} %bitcast.1.tok, bf16[2,1024,512]{2,1,0:T(8,128)(2,1)S(1)} %get-tuple-element.39.local_all, bf16[2,1024,512]{2,1,0:T(8,128)(2,1)S(1)} %get-tuple-element.46.remote_all, ...), custom_call_target="tpu_custom_call" | custom-call | flops 393216000 | bytes 3145728 | tf_op jit(solution)/shard_map/output/pallas_call | solution.py:679
  22.3 0.4 %collective-permute-start.6 = (bf16[512,512]{1,0:T(8,128)(2,1)S(1)}, bf16[512,512]{1,0:T(8,128)(2,1)S(1)}, u32[]{:S(2)}, u32[]{:S(2)}) collective-permute-start(bf16[512,512]{1,0:T(8,128)(2,1)S(1)} %get-tuple-element.69), channel_id=1, source_target_pairs={{0,16},{16,0},{1,17},{17,1},{2,18},{18,2},{3,19},{19,3},{4,20},{20... | collective-permute-start | bytes 1572872 | tf_op jit(solution)/shard_map/ppermute | solution.py:774
  22.8 1.0 %output.3 = (bf16[1,2048,512]{2,1,0:T(8,128)(2,1)}, bf16[512,512]{1,0:T(8,128)(2,1)S(1)}, bf16[512,512]{1,0:T(8,128)(2,1)S(1)}) custom-call(s32[1]{0:T(128)} %bitcast.sec, s32[1]{0:T(128)} %bitcast.1.tok, bf16[2,1024,512]{2,1,0:T(8,128)(2,1)S(1)} %get-tuple-element.39.local_all, ...), custom_call_target="tpu_custom_call", output_to_operand_aliasing={{0}: (14, {})} | custom-call | flops 393216000 | bytes 3145728 | tf_op jit(solution)/shard_map/output/pallas_call | solution.py:679
  23.8 0.2 collective-permute-start.7
  23.9 0.4 %collective-permute-done.6.received = bf16[512,512]{1,0:T(8,128)(2,1)S(1)} collective-permute-done((bf16[512,512]{1,0:T(8,128)(2,1)S(1)}, bf16[512,512]{1,0:T(8,128)(2,1)S(1)}, u32[]{:S(2)}, u32[]{:S(2)}) %collective-permute-start.6) | collective-permute-done | bytes 524320 | tf_op jit(solution)/shard_map/ppermute | solution.py:774
  24.3 1.2 %placing.2.before = bf16[1,2048,512]{2,1,0:T(8,128)(2,1)} custom-call(s32[1]{0:T(128)} %bitcast.sec, bf16[1,2048,512]{2,1,0:T(8,128)(2,1)} %get-tuple-element.68.before, bf16[512,512]{1,0:T(8,128)(2,1)S(1)} %collective-permute-done.6.received, bf16[512,512]{1,0:T(8,128)(2,1)S(1)} %get-tuple-element.70.rest_0_, ...), custom_call_target="tpu_custom_call", output_to_operand_aliasing={{}: (1, {})} | custom-call | flops 524288 | bytes 3145728 | tf_op jit(solution)/shard_map/placing/pallas_call | solution.py:727
  25.5 0.2 collective-permute-done.7.received
  25.7 0.8 %placing.3 = bf16[1,2048,512]{2,1,0:T(8,128)(2,1)} custom-call(s32[1]{0:T(128)} %bitcast.sec, bf16[1,2048,512]{2,1,0:T(8,128)(2,1)} %placing.2.before, bf16[512,512]{1,0:T(8,128)(2,1)S(1)} %collective-permute-done.7.received), custom_call_target="tpu_custom_call", output_to_operand_aliasing={{}: (1, {})} | custom-call | flops 524288 | bytes 3145728 | tf_op jit(solution)/shard_map/placing/pallas_call | solution.py:727
Async XLA Ops:
  0.0 6.4 %copy-start = (f32[2048,16]{0,1:T(8,128)S(1)}, f32[2048,16]{0,1:T(8,128)}, u32[]{:S(2)}) copy-start(f32[2048,16]{0,1:T(8,128)} %param.22) | copy-start | bytes 393220
  0.0 6.4 %copy-start.1 = (f32[2048,16]{0,1:T(8,128)S(1)}, f32[2048,16]{0,1:T(8,128)}, u32[]{:S(2)}) copy-start(f32[2048,16]{0,1:T(8,128)} %param.21) | copy-start | bytes 393220
  0.0 9.7 %collective-permute-start = (bf16[2,2048,512]{2,1,0:T(8,128)(2,1)}, bf16[2,2048,512]{2,1,0:T(8,128)(2,1)}, u32[]{:S(2)}, u32[]{:S(2)}) collective-permute-start(bf16[2,2048,512]{2,1,0:T(8,128)(2,1)} %bitcast.7), channel_id=1, source_target_pairs={{0,16},{16,0},{1,17},{17,1},{2,18},{18,2},{3,19},{19,3},{4,20},{20... | collective-permute-start | bytes 12582920 | tf_op jit(solution)/shard_map/ppermute | solution.py:774
  1.4 11.7 %collective-permute-start.1 = (bf16[1024,128]{1,0:T(8,128)(2,1)S(1)}, bf16[1024,128]{1,0:T(8,128)(2,1)S(1)}, u32[]{:S(2)}, u32[]{:S(2)}) collective-permute-start(bf16[1024,128]{1,0:T(8,128)(2,1)S(1)} %get-tuple-element.47), channel_id=1, source_target_pairs={{0,1},{1,2},{2,3},{3,0},{16,16},{17,17},{18,18},{19,19},{4,5},{5,6... | collective-permute-start | bytes 786440 | tf_op jit(solution)/shard_map/ppermute | solution.py:786
  2.1 11.6 %collective-permute-start.2 = (bf16[1024,128]{1,0:T(8,128)(2,1)S(1)}, bf16[1024,128]{1,0:T(8,128)(2,1)S(1)}, u32[]{:S(2)}, u32[]{:S(2)}) collective-permute-start(bf16[1024,128]{1,0:T(8,128)(2,1)S(1)} %get-tuple-element.48), channel_id=1, source_target_pairs={{0,17},{1,18},{2,19},{3,16},{16,0},{17,1},{18,2},{19,3},{4,21},{5,... | collective-permute-start | bytes 786440 | tf_op jit(solution)/shard_map/ppermute | solution.py:786
  15.0 4.3 %collective-permute-start.3 = (bf16[128,128]{1,0:T(8,128)(2,1)S(1)}, bf16[128,128]{1,0:T(8,128)(2,1)S(1)}, u32[]{:S(2)}, u32[]{:S(2)}) collective-permute-start(bf16[128,128]{1,0:T(8,128)(2,1)S(1)} %get-tuple-element.66), channel_id=1, source_target_pairs={{0,1},{1,0},{2,3},{3,2},{4,5},{5,4},{6,7},{7,6},{8,9},{9,8},{10,11... | collective-permute-start | bytes 98312 | tf_op jit(solution)/shard_map/ppermute | solution.py:779
  15.8 3.5 %collective-permute-start.4 = (bf16[128,128]{1,0:T(8,128)(2,1)S(1)}, bf16[128,128]{1,0:T(8,128)(2,1)S(1)}, u32[]{:S(2)}, u32[]{:S(2)}) collective-permute-start(bf16[128,128]{1,0:T(8,128)(2,1)S(1)} %get-tuple-element.66), channel_id=1, source_target_pairs={{0,2},{1,3},{2,0},{3,1},{4,6},{5,7},{6,4},{7,5},{8,10},{9,11},{10,... | collective-permute-start | bytes 98312 | tf_op jit(solution)/shard_map/ppermute | solution.py:779
  17.1 4.3 %collective-permute-start.5 = (bf16[128,128]{1,0:T(8,128)(2,1)S(1)}, bf16[128,128]{1,0:T(8,128)(2,1)S(1)}, u32[]{:S(2)}, u32[]{:S(2)}) collective-permute-start(bf16[128,128]{1,0:T(8,128)(2,1)S(1)} %get-tuple-element.66), channel_id=1, source_target_pairs={{0,3},{1,2},{2,1},{3,0},{4,7},{5,6},{6,5},{7,4},{8,11},{9,10},{10,... | collective-permute-start | bytes 98312 | tf_op jit(solution)/shard_map/ppermute | solution.py:779
  22.3 2.0 %collective-permute-start.6 = (bf16[512,512]{1,0:T(8,128)(2,1)S(1)}, bf16[512,512]{1,0:T(8,128)(2,1)S(1)}, u32[]{:S(2)}, u32[]{:S(2)}) collective-permute-start(bf16[512,512]{1,0:T(8,128)(2,1)S(1)} %get-tuple-element.69), channel_id=1, source_target_pairs={{0,16},{16,0},{1,17},{17,1},{2,18},{18,2},{3,19},{19,3},{4,20},{20... | collective-permute-start | bytes 1572872 | tf_op jit(solution)/shard_map/ppermute | solution.py:774
  23.8 2.0 %collective-permute-start.7 = (bf16[512,512]{1,0:T(8,128)(2,1)S(1)}, bf16[512,512]{1,0:T(8,128)(2,1)S(1)}, u32[]{:S(2)}, u32[]{:S(2)}) collective-permute-start(bf16[512,512]{1,0:T(8,128)(2,1)S(1)} %get-tuple-element.72), channel_id=1, source_target_pairs={{0,16},{16,0},{1,17},{17,1},{2,18},{18,2},{3,19},{19,3},{4,20},{20... | collective-permute-start | bytes 1572872 | tf_op jit(solution)/shard_map/ppermute | solution.py:774

commit v14 on v13

--- a/solution.py
+++ b/solution.py
@@ -333,17 +333,17 @@
     blocks = tokens // window
     parts = [slice(b * window, (b + 1) * window) for b in range(blocks)]
 
-    def fetch(kind, i):
+    def fetch(i):
         source = pl.ds(pl.multiple_of(sec[0] * share + i * step, step), step)
         return pltpu.make_async_copy(
-            swapped.at[kind, source, :],
-            rows_at(remote_all.at[kind], step, i),
-            arrival.at[kind, i],
+            swapped.at[:, source, :], rows_at(remote_all, step, i, 1), arrival.at[i]
         )
 
+    for i in range(share // step):
+        fetch(i).start()
+
     def chunk(section, i):
-        if section == 1:
-            fetch(1, i).wait()
+        fetch(i).wait()
         first, second = both_gates(local_all, remote_all, section, step, i)
         inputs = rows_at(inputs_all, step, i)
         medium_out, signals = rows_at(medium_all, step, i), rows_at(signals_all, step, i)
@@ -357,11 +357,6 @@
         rows_at(tap_spec_all, step, i)[...] = tap_spec
         rows_at(edge_spec_all, step, i)[...] = in_order[0]
         mixed = products([in_order[b - 1] + in_order[b] for b in range(1, blocks)], tap_spec)
-        if section == 0:
-            fetch(1, i).wait()
-            fetch(0, i).start()
-        else:
-            fetch(0, i).wait()
         for parity, table in enumerate((inv_even, inv_odd)):
             chosen = [b for b in range(1, blocks) if b % 2 == parity]
             if not chosen:
@@ -378,14 +373,7 @@
                 signals[:, parts[b]] = signal
 
     def body(section):
-        for i in range(share // step):
-            fetch(1, i).start()
-            if section == 1:
-                fetch(0, i).start()
         pl.loop(0, share // step)(functools.partial(chunk, section))
-        if section == 0:
-            for i in range(share // step):
-                fetch(0, i).wait()
 
     by_section(sec, body)
 
@@ -401,7 +389,7 @@
         out_shape=(wide, wide, spec, spec, jax.ShapeDtypeStruct(gates.shape, gates.dtype)),
         in_specs=[SMEM_SPEC] * 2 + [VMEM_SPEC, ANY_SPEC] + [VMEM_SPEC] * (len(operands) - 2),
         out_specs=(VMEM_SPEC,) * 5,
-        scratch_shapes=[pltpu.SemaphoreType.DMA((2, share // min(STEP, share)))],
+        scratch_shapes=[pltpu.SemaphoreType.DMA((share // min(STEP, share),))],
         name="later",
         cost_estimate=cost(share, tokens, 1500),
         compiler_params=COMPILER,

time: 26.9 us -> 26.4 us (0.981)
  Pallas kernels: 14.6 us -> 14.3 us
    ppermute x3, waiting for transfers between devices: 2.03 us -> 1.59 us  [met(): return lax.ppermute(value, 'tok', [(i, i ^ by) for i in range(peers)])]
    pallas_call x1, Pallas kernels: 3.34 us -> 3.01 us  [later_call(): pl.pallas_call(functools.partial(later_kernel, min(STEP, share)), out_sha...]
    ppermute x2, waiting for transfers between devices: 0.64 us -> 0.97 us  [edge_to(): return lax.ppermute(value, ('section', 'tok'), pairs)]
  transfers between devices with their start and end apart: 8 -> 8, of which waited for: 4 -> 4; matrix products, arithmetic and copies ran while one was open for 0% -> 0% of each run, Pallas kernels for 44% -> 43%
where the time goes in v14:
time: 26.4 us; the launch traced here: 26.1 us
  Pallas kernels  14.3 us (54%)
  starting transfers between devices  8.53 us (32%)
  waiting for transfers between devices  3.19 us (12%)
    ppermute x2, starting transfers between devices, edge_to(): return lax.ppermute(value, ('section', 'tok'), pairs)  4.94 us
    pallas_call x1, Pallas kernels, response_call(): pl.pallas_call(functools.partial(response_kernel, len(tables), window), o...  3.34 us
    pallas_call x1, Pallas kernels, later_call(): pl.pallas_call(functools.partial(later_kernel, min(STEP, share)), out_sha...  3.01 us
    ppermute x3, starting transfers between devices, met(): return lax.ppermute(value, 'tok', [(i, i ^ by) for i in range(peers)])  2.96 us
    pallas_call x2, Pallas kernels, place_call(): pl.pallas_call(functools.partial(place_kernel, half * rows, before.shape[...  1.96 us
    pallas_call x2, Pallas kernels, output_call(): pl.pallas_call(functools.partial(output_kernel, len(arrived), lanes // RO...  1.93 us
    ppermute x3, waiting for transfers between devices, met(): return lax.ppermute(value, 'tok', [(i, i ^ by) for i in range(peers)])  1.59 us
    pallas_call x1, Pallas kernels, edge_call(): pl.pallas_call(edge_kernel, out_shape=(edge, edge), in_specs=[ANY_SPEC] *...  1.39 us
  transfers between devices with their start and end apart: 8, of which 4 were waited for; matrix products, arithmetic and copies ran while one was open for 0% of the time, Pallas kernels for 43%

profile of v14, /device:TPU:1, one launch (start us, length us, event | category | flops | bytes accessed | tf_op | source)
XLA Modules:
  0.0 26.1 jit_solution(3090092316989012244)
XLA Ops:
  0.0 0.0 copy-start
  0.0 0.0 copy-start.1
  0.0 0.0 collective-permute-start
  0.0 1.4 %edge.1 = (bf16[1024,128]{1,0:T(8,128)(2,1)S(1)}, bf16[1024,128]{1,0:T(8,128)(2,1)S(1)}) custom-call(bf16[1,2,2048,512]{3,2,1,0:T(8,128)(2,1)} %gates.1, bf16[2048,512]{1,0:T(8,128)(2,1)} %inputs.1), custom_call_target="tpu_custom_call" | custom-call | flops 1048576 | bytes 6291456 | tf_op jit(solution)/shard_map/edge/pallas_call | solution.py:747
  1.4 0.7 %collective-permute-start.1 = (bf16[1024,128]{1,0:T(8,128)(2,1)S(1)}, bf16[1024,128]{1,0:T(8,128)(2,1)S(1)}, u32[]{:S(2)}, u32[]{:S(2)}) collective-permute-start(bf16[1024,128]{1,0:T(8,128)(2,1)S(1)} %get-tuple-element.47), channel_id=1, source_target_pairs={{0,1},{1,2},{2,3},{3,0},{16,16},{17,17},{18,18},{19,19},{4,5},{5,6... | collective-permute-start | bytes 786440 | tf_op jit(solution)/shard_map/ppermute | solution.py:774
  2.1 4.3 %collective-permute-start.2 = (bf16[1024,128]{1,0:T(8,128)(2,1)S(1)}, bf16[1024,128]{1,0:T(8,128)(2,1)S(1)}, u32[]{:S(2)}, u32[]{:S(2)}) collective-permute-start(bf16[1024,128]{1,0:T(8,128)(2,1)S(1)} %get-tuple-element.48), channel_id=1, source_target_pairs={{0,17},{1,18},{2,19},{3,16},{16,0},{17,1},{18,2},{19,3},{4,21},{5,... | collective-permute-start | bytes 786440 | tf_op jit(solution)/shard_map/ppermute | solution.py:774
  6.4 0.0 copy-done
  6.4 0.0 copy-done.1
  6.4 3.3 %response.1 = (f32[1024,128]{1,0:T(8,128)S(1)}, f32[128,128]{1,0:T(8,128)S(1)}, f32[128,128]{1,0:T(8,128)S(1)}, bf16[64,128,256]{2,1,0:T(8,128)(2,1)S(1)}, bf16[...) custom-call(s32[1]{0:T(128)} %bitcast.sec, ...), custom_call_target="tpu_custom_call" | custom-call | flops 471859200 | bytes 6291456 | tf_op jit(solution)/shard_map/response/pallas_call | solution.py:239
  9.7 0.0 collective-permute-done.swapped
  9.7 3.0 %later.1 = (bf16[1024,512]{1,0:T(8,128)(2,1)S(1)}, bf16[1024,512]{1,0:T(8,128)(2,1)S(1)}, f32[1024,256]{1,0:T(8,128)S(1)}, f32[1024,256]{1,0:T(8,128)S(1)}, bf16[2,1024,512]{2,1,0:T(8,128)(2,1)S(1)}) custom-call(s32[1]{0:T(128)} %bitcast.sec, s32[1]{0:T(128)} %bitcast.1.tok, bf16[2,1024,512]{2,1,0:T(8,128)(2,1)S(1)} %get-tuple-element.39.local_all, ...), custom_call_target="tpu_custom_call" | custom-call | flops 786432000 | bytes 6291456 | tf_op jit(solution)/shard_map/later/pallas_call | solution.py:387
  12.7 0.0 collective-permute-done.1.halo_low
  12.8 1.0 %collective-permute-done.2.halo_high = bf16[1024,128]{1,0:T(8,128)(2,1)S(1)} collective-permute-done((bf16[1024,128]{1,0:T(8,128)(2,1)S(1)}, bf16[1024,128]{1,0:T(8,128)(2,1)S(1)}, u32[]{:S(2)}, u32[]{:S(2)}) %collective-permute-start.2) | collective-permute-done | bytes 262176 | tf_op jit(solution)/shard_map/ppermute | solution.py:774
  13.7 1.3 %first.1 = (bf16[1024,512]{1,0:T(8,128)(2,1)S(1)}, bf16[1024,512]{1,0:T(8,128)(2,1)S(1)}, f32[4,1024,128]{2,1,0:T(8,128)S(1)}, bf16[128,128]{1,0:T(8,128)(2,1)S(1)}) custom-call(s32[1]{0:T(128)} %bitcast.sec, s32[1]{0:T(128)} %bitcast.1.tok, bf16[2,1024,512]{2,1,0:T(8,128)(2,1)S(1)} %get-tuple-element.39.local_all, ...), custom_call_target="tpu_custom_call", output_to_operand_aliasing={{0}: (13, {}), {1}: (14, {})} | custom-call | flops 262144000 | bytes 6291456 | tf_op jit(solution)/shard_map/first/pallas_call | solution.py:482
  15.0 0.8 %collective-permute-start.3 = (bf16[128,128]{1,0:T(8,128)(2,1)S(1)}, bf16[128,128]{1,0:T(8,128)(2,1)S(1)}, u32[]{:S(2)}, u32[]{:S(2)}) collective-permute-start(bf16[128,128]{1,0:T(8,128)(2,1)S(1)} %get-tuple-element.66), channel_id=1, source_target_pairs={{0,1},{1,0},{2,3},{3,2},{4,5},{5,4},{6,7},{7,6},{8,9},{9,8},{10,11... | collective-permute-start | bytes 98312 | tf_op jit(solution)/shard_map/ppermute | solution.py:767
  15.8 1.2 %collective-permute-start.4 = (bf16[128,128]{1,0:T(8,128)(2,1)S(1)}, bf16[128,128]{1,0:T(8,128)(2,1)S(1)}, u32[]{:S(2)}, u32[]{:S(2)}) collective-permute-start(bf16[128,128]{1,0:T(8,128)(2,1)S(1)} %get-tuple-element.66), channel_id=1, source_target_pairs={{0,2},{1,3},{2,0},{3,1},{4,6},{5,7},{6,4},{7,5},{8,10},{9,11},{10,... | collective-permute-start | bytes 98312 | tf_op jit(solution)/shard_map/ppermute | solution.py:767
  17.1 0.9 %collective-permute-start.5 = (bf16[128,128]{1,0:T(8,128)(2,1)S(1)}, bf16[128,128]{1,0:T(8,128)(2,1)S(1)}, u32[]{:S(2)}, u32[]{:S(2)}) collective-permute-start(bf16[128,128]{1,0:T(8,128)(2,1)S(1)} %get-tuple-element.66), channel_id=1, source_target_pairs={{0,3},{1,2},{2,1},{3,0},{4,7},{5,6},{6,5},{7,4},{8,11},{9,10},{10,... | collective-permute-start | bytes 98312 | tf_op jit(solution)/shard_map/ppermute | solution.py:767
  18.0 1.4 %within.1.within_all = f32[1024,512]{1,0:T(8,128)S(1)} custom-call(bf16[1024,512]{1,0:T(8,128)(2,1)S(1)} %get-tuple-element.55.signals_all, f32[1024,128]{1,0:T(8,128)S(1)} %get-tuple-element.56.response_all, bf16[256,256]{1,0:T(8,128)(2,1)S(1)} %get-tuple-element.57.fwd_h, bf16[256,256]{1,0:T(8,128)(2,1)S(1)} %get-tuple-element.58.fwd_l, ...), custom_call_target="tpu_custom_call" | custom-call | flops 786432000 | bytes 6291456 | tf_op jit(solution)/shard_map/within/pallas_call | solution.py:547
  19.3 0.0 collective-permute-done.3.rest_0_
  19.3 0.0 collective-permute-done.4.rest_1_
  19.3 1.6 %collective-permute-done.5.rest_2_ = bf16[128,128]{1,0:T(8,128)(2,1)S(1)} collective-permute-done((bf16[128,128]{1,0:T(8,128)(2,1)S(1)}, bf16[128,128]{1,0:T(8,128)(2,1)S(1)}, u32[]{:S(2)}, u32[]{:S(2)}) %collective-permute-start.5) | collective-permute-done | bytes 32800 | tf_op jit(solution)/shard_map/ppermute | solution.py:767
  20.9 1.0 %output.2 = (bf16[1,2048,512]{2,1,0:T(8,128)(2,1)}, bf16[512,512]{1,0:T(8,128)(2,1)S(1)}, bf16[512,512]{1,0:T(8,128)(2,1)S(1)}) custom-call(s32[1]{0:T(128)} %bitcast.sec, s32[1]{0:T(128)} %bitcast.1.tok, bf16[2,1024,512]{2,1,0:T(8,128)(2,1)S(1)} %get-tuple-element.39.local_all, bf16[2,1024,512]{2,1,0:T(8,128)(2,1)S(1)} %get-tuple-element.46.remote_all, ...), custom_call_target="tpu_custom_call" | custom-call | flops 393216000 | bytes 3145728 | tf_op jit(solution)/shard_map/output/pallas_call | solution.py:667
  21.9 0.4 %collective-permute-start.6 = (bf16[512,512]{1,0:T(8,128)(2,1)S(1)}, bf16[512,512]{1,0:T(8,128)(2,1)S(1)}, u32[]{:S(2)}, u32[]{:S(2)}) collective-permute-start(bf16[512,512]{1,0:T(8,128)(2,1)S(1)} %get-tuple-element.69), channel_id=1, source_target_pairs={{0,16},{16,0},{1,17},{17,1},{2,18},{18,2},{3,19},{19,3},{4,20},{20... | collective-permute-start | bytes 1572872 | tf_op jit(solution)/shard_map/ppermute | solution.py:762
  22.3 1.0 %output.3 = (bf16[1,2048,512]{2,1,0:T(8,128)(2,1)}, bf16[512,512]{1,0:T(8,128)(2,1)S(1)}, bf16[512,512]{1,0:T(8,128)(2,1)S(1)}) custom-call(s32[1]{0:T(128)} %bitcast.sec, s32[1]{0:T(128)} %bitcast.1.tok, bf16[2,1024,512]{2,1,0:T(8,128)(2,1)S(1)} %get-tuple-element.39.local_all, ...), custom_call_target="tpu_custom_call", output_to_operand_aliasing={{0}: (14, {})} | custom-call | flops 393216000 | bytes 3145728 | tf_op jit(solution)/shard_map/output/pallas_call | solution.py:667
  23.3 0.2 collective-permute-start.7
  23.5 0.4 %collective-permute-done.6.received = bf16[512,512]{1,0:T(8,128)(2,1)S(1)} collective-permute-done((bf16[512,512]{1,0:T(8,128)(2,1)S(1)}, bf16[512,512]{1,0:T(8,128)(2,1)S(1)}, u32[]{:S(2)}, u32[]{:S(2)}) %collective-permute-start.6) | collective-permute-done | bytes 524320 | tf_op jit(solution)/shard_map/ppermute | solution.py:762
  23.9 1.2 %placing.2.before = bf16[1,2048,512]{2,1,0:T(8,128)(2,1)} custom-call(s32[1]{0:T(128)} %bitcast.sec, bf16[1,2048,512]{2,1,0:T(8,128)(2,1)} %get-tuple-element.68.before, bf16[512,512]{1,0:T(8,128)(2,1)S(1)} %collective-permute-done.6.received, bf16[512,512]{1,0:T(8,128)(2,1)S(1)} %get-tuple-element.70.rest_0_, ...), custom_call_target="tpu_custom_call", output_to_operand_aliasing={{}: (1, {})} | custom-call | flops 524288 | bytes 3145728 | tf_op jit(solution)/shard_map/placing/pallas_call | solution.py:715
  25.1 0.2 collective-permute-done.7.received
  25.3 0.8 %placing.3 = bf16[1,2048,512]{2,1,0:T(8,128)(2,1)} custom-call(s32[1]{0:T(128)} %bitcast.sec, bf16[1,2048,512]{2,1,0:T(8,128)(2,1)} %placing.2.before, bf16[512,512]{1,0:T(8,128)(2,1)S(1)} %collective-permute-done.7.received), custom_call_target="tpu_custom_call", output_to_operand_aliasing={{}: (1, {})} | custom-call | flops 524288 | bytes 3145728 | tf_op jit(solution)/shard_map/placing/pallas_call | solution.py:715
Async XLA Ops:
  0.0 6.4 %copy-start = (f32[2048,16]{0,1:T(8,128)S(1)}, f32[2048,16]{0,1:T(8,128)}, u32[]{:S(2)}) copy-start(f32[2048,16]{0,1:T(8,128)} %param.22) | copy-start | bytes 393220
  0.0 6.4 %copy-start.1 = (f32[2048,16]{0,1:T(8,128)S(1)}, f32[2048,16]{0,1:T(8,128)}, u32[]{:S(2)}) copy-start(f32[2048,16]{0,1:T(8,128)} %param.21) | copy-start | bytes 393220
  0.0 9.7 %collective-permute-start = (bf16[2,2048,512]{2,1,0:T(8,128)(2,1)}, bf16[2,2048,512]{2,1,0:T(8,128)(2,1)}, u32[]{:S(2)}, u32[]{:S(2)}) collective-permute-start(bf16[2,2048,512]{2,1,0:T(8,128)(2,1)} %bitcast.7), channel_id=1, source_target_pairs={{0,16},{16,0},{1,17},{17,1},{2,18},{18,2},{3,19},{19,3},{4,20},{20... | collective-permute-start | bytes 12582920 | tf_op jit(solution)/shard_map/ppermute | solution.py:762
  1.4 11.3 %collective-permute-start.1 = (bf16[1024,128]{1,0:T(8,128)(2,1)S(1)}, bf16[1024,128]{1,0:T(8,128)(2,1)S(1)}, u32[]{:S(2)}, u32[]{:S(2)}) collective-permute-start(bf16[1024,128]{1,0:T(8,128)(2,1)S(1)} %get-tuple-element.47), channel_id=1, source_target_pairs={{0,1},{1,2},{2,3},{3,0},{16,16},{17,17},{18,18},{19,19},{4,5},{5,6... | collective-permute-start | bytes 786440 | tf_op jit(solution)/shard_map/ppermute | solution.py:774
  2.1 11.6 %collective-permute-start.2 = (bf16[1024,128]{1,0:T(8,128)(2,1)S(1)}, bf16[1024,128]{1,0:T(8,128)(2,1)S(1)}, u32[]{:S(2)}, u32[]{:S(2)}) collective-permute-start(bf16[1024,128]{1,0:T(8,128)(2,1)S(1)} %get-tuple-element.48), channel_id=1, source_target_pairs={{0,17},{1,18},{2,19},{3,16},{16,0},{17,1},{18,2},{19,3},{4,21},{5,... | collective-permute-start | bytes 786440 | tf_op jit(solution)/shard_map/ppermute | solution.py:774
  15.0 4.3 %collective-permute-start.3 = (bf16[128,128]{1,0:T(8,128)(2,1)S(1)}, bf16[128,128]{1,0:T(8,128)(2,1)S(1)}, u32[]{:S(2)}, u32[]{:S(2)}) collective-permute-start(bf16[128,128]{1,0:T(8,128)(2,1)S(1)} %get-tuple-element.66), channel_id=1, source_target_pairs={{0,1},{1,0},{2,3},{3,2},{4,5},{5,4},{6,7},{7,6},{8,9},{9,8},{10,11... | collective-permute-start | bytes 98312 | tf_op jit(solution)/shard_map/ppermute | solution.py:767
  15.8 3.5 %collective-permute-start.4 = (bf16[128,128]{1,0:T(8,128)(2,1)S(1)}, bf16[128,128]{1,0:T(8,128)(2,1)S(1)}, u32[]{:S(2)}, u32[]{:S(2)}) collective-permute-start(bf16[128,128]{1,0:T(8,128)(2,1)S(1)} %get-tuple-element.66), channel_id=1, source_target_pairs={{0,2},{1,3},{2,0},{3,1},{4,6},{5,7},{6,4},{7,5},{8,10},{9,11},{10,... | collective-permute-start | bytes 98312 | tf_op jit(solution)/shard_map/ppermute | solution.py:767
  17.1 3.9 %collective-permute-start.5 = (bf16[128,128]{1,0:T(8,128)(2,1)S(1)}, bf16[128,128]{1,0:T(8,128)(2,1)S(1)}, u32[]{:S(2)}, u32[]{:S(2)}) collective-permute-start(bf16[128,128]{1,0:T(8,128)(2,1)S(1)} %get-tuple-element.66), channel_id=1, source_target_pairs={{0,3},{1,2},{2,1},{3,0},{4,7},{5,6},{6,5},{7,4},{8,11},{9,10},{10,... | collective-permute-start | bytes 98312 | tf_op jit(solution)/shard_map/ppermute | solution.py:767
  21.9 2.0 %collective-permute-start.6 = (bf16[512,512]{1,0:T(8,128)(2,1)S(1)}, bf16[512,512]{1,0:T(8,128)(2,1)S(1)}, u32[]{:S(2)}, u32[]{:S(2)}) collective-permute-start(bf16[512,512]{1,0:T(8,128)(2,1)S(1)} %get-tuple-element.69), channel_id=1, source_target_pairs={{0,16},{16,0},{1,17},{17,1},{2,18},{18,2},{3,19},{19,3},{4,20},{20... | collective-permute-start | bytes 1572872 | tf_op jit(solution)/shard_map/ppermute | solution.py:762
  23.3 2.0 %collective-permute-start.7 = (bf16[512,512]{1,0:T(8,128)(2,1)S(1)}, bf16[512,512]{1,0:T(8,128)(2,1)S(1)}, u32[]{:S(2)}, u32[]{:S(2)}) collective-permute-start(bf16[512,512]{1,0:T(8,128)(2,1)S(1)} %get-tuple-element.72), channel_id=1, source_target_pairs={{0,16},{16,0},{1,17},{17,1},{2,18},{18,2},{3,19},{19,3},{4,20},{20... | collective-permute-start | bytes 1572872 | tf_op jit(solution)/shard_map/ppermute | solution.py:762

commit v15 on v10

--- a/solution.py
+++ b/solution.py
@@ -722,17 +722,20 @@
 def edge_kernel(gates, inputs, low, high, gate_tail, input_tail, arrival):
     share, window = low.shape
     tail = pl.ds(inputs.shape[1] - window, window)
-    pairs = [(gates.at[0, 1, :, tail], gate_tail), (inputs.at[:, tail], input_tail)]
-    copies = [
-        pltpu.make_async_copy(source, target, arrival.at[k])
-        for k, (source, target) in enumerate(pairs)
-    ]
+    halves = [pl.ds(k * share, share) for k in range(2)]
+    copies = []
+    for k, rows in enumerate(halves):
+        pairs = [(gates.at[0, 1, rows, tail], gate_tail), (inputs.at[rows, tail], input_tail)]
+        for m, (source, target) in enumerate(pairs):
+            copies.append(
+                pltpu.make_async_copy(source, target.at[rows, :], arrival.at[2 * k + m])
+            )
     for copy in copies:
         copy.start()
-    for copy in copies:
-        copy.wait()
-    low[...] = gate_tail[:share, :] * input_tail[:share, :]
-    high[...] = gate_tail[share:, :] * input_tail[share:, :]
+    for k, (rows, edge) in enumerate(zip(halves, (low, high))):
+        copies[2 * k].wait()
+        copies[2 * k + 1].wait()
+        edge[...] = gate_tail[rows, :] * input_tail[rows, :]
 
 
 def edge_call(gate_streams, inputs, window, share):
@@ -744,7 +747,7 @@
         in_specs=[ANY_SPEC] * 2,
         out_specs=(VMEM_SPEC,) * 2,
         scratch_shapes=[pltpu.VMEM((channels, window), jnp.bfloat16)] * 2
-        + [pltpu.SemaphoreType.DMA((2,))],
+        + [pltpu.SemaphoreType.DMA((4,))],
         name="edge",
         cost_estimate=cost(share, tokens, 2),
         compiler_params=COMPILER,

time: 26.4 us -> 26.5 us (level)
  no operation moved by 1% of the time
where the time goes in v15:
time: 26.5 us; the launch traced here: 26.3 us
  Pallas kernels  14.2 us (54%)
  starting transfers between devices  8.53 us (32%)
  waiting for transfers between devices  3.46 us (13%)
    ppermute x2, starting transfers between devices, edge_to(): return lax.ppermute(value, ('section', 'tok'), pairs)  4.94 us
    pallas_call x1, Pallas kernels, response_call(): pl.pallas_call(functools.partial(response_kernel, len(tables), window), o...  3.34 us
    pallas_call x1, Pallas kernels, later_call(): pl.pallas_call(functools.partial(later_kernel, min(STEP, share)), out_sha...  3.01 us
    ppermute x3, starting transfers between devices, met(): return lax.ppermute(value, 'tok', [(i, i ^ by) for i in range(peers)])  2.96 us
    pallas_call x2, Pallas kernels, place_call(): pl.pallas_call(functools.partial(place_kernel, half * rows, before.shape[...  1.97 us
    pallas_call x2, Pallas kernels, output_call(): pl.pallas_call(functools.partial(output_kernel, len(arrived), lanes // RO...  1.93 us
    ppermute x3, waiting for transfers between devices, met(): return lax.ppermute(value, 'tok', [(i, i ^ by) for i in range(peers)])  1.68 us
    pallas_call x1, Pallas kernels, within_call(): pl.pallas_call(functools.partial(within_kernel, min(2 * STEP, share)), ou...  1.37 us
  transfers between devices with their start and end apart: 8, of which 4 were waited for; matrix products, arithmetic and copies ran while one was open for 0% of the time, Pallas kernels for 42%

profile of v15, /device:TPU:1, one launch (start us, length us, event | category | flops | bytes accessed | tf_op | source)
XLA Modules:
  0.0 26.3 jit_solution(6452872977089498202)
XLA Ops:
  0.0 0.0 copy-start
  0.0 0.0 copy-start.1
  0.0 0.0 collective-permute-start
  0.0 1.3 %edge.1 = (bf16[1024,128]{1,0:T(8,128)(2,1)S(1)}, bf16[1024,128]{1,0:T(8,128)(2,1)S(1)}) custom-call(bf16[1,2,2048,512]{3,2,1,0:T(8,128)(2,1)} %gates.1, bf16[2048,512]{1,0:T(8,128)(2,1)} %inputs.1), custom_call_target="tpu_custom_call" | custom-call | flops 1048576 | bytes 6291456 | tf_op jit(solution)/shard_map/edge/pallas_call | solution.py:744
  1.4 0.7 %collective-permute-start.1 = (bf16[1024,128]{1,0:T(8,128)(2,1)S(1)}, bf16[1024,128]{1,0:T(8,128)(2,1)S(1)}, u32[]{:S(2)}, u32[]{:S(2)}) collective-permute-start(bf16[1024,128]{1,0:T(8,128)(2,1)S(1)} %get-tuple-element.47), channel_id=1, source_target_pairs={{0,1},{1,2},{2,3},{3,0},{16,16},{17,17},{18,18},{19,19},{4,5},{5,6... | collective-permute-start | bytes 786440 | tf_op jit(solution)/shard_map/ppermute | solution.py:771
  2.1 4.3 %collective-permute-start.2 = (bf16[1024,128]{1,0:T(8,128)(2,1)S(1)}, bf16[1024,128]{1,0:T(8,128)(2,1)S(1)}, u32[]{:S(2)}, u32[]{:S(2)}) collective-permute-start(bf16[1024,128]{1,0:T(8,128)(2,1)S(1)} %get-tuple-element.48), channel_id=1, source_target_pairs={{0,17},{1,18},{2,19},{3,16},{16,0},{17,1},{18,2},{19,3},{4,21},{5,... | collective-permute-start | bytes 786440 | tf_op jit(solution)/shard_map/ppermute | solution.py:771
  6.3 0.0 copy-done
  6.3 0.0 copy-done.1
  6.3 3.3 %response.1 = (f32[1024,128]{1,0:T(8,128)S(1)}, f32[128,128]{1,0:T(8,128)S(1)}, f32[128,128]{1,0:T(8,128)S(1)}, bf16[64,128,256]{2,1,0:T(8,128)(2,1)S(1)}, bf16[...) custom-call(s32[1]{0:T(128)} %bitcast.sec, ...), custom_call_target="tpu_custom_call" | custom-call | flops 471859200 | bytes 6291456 | tf_op jit(solution)/shard_map/response/pallas_call | solution.py:239
  9.7 0.0 collective-permute-done.swapped
  9.7 3.0 %later.1 = (bf16[1024,512]{1,0:T(8,128)(2,1)S(1)}, bf16[1024,512]{1,0:T(8,128)(2,1)S(1)}, f32[1024,256]{1,0:T(8,128)S(1)}, f32[1024,256]{1,0:T(8,128)S(1)}, bf16[2,1024,512]{2,1,0:T(8,128)(2,1)S(1)}) custom-call(s32[1]{0:T(128)} %bitcast.sec, s32[1]{0:T(128)} %bitcast.1.tok, bf16[2,1024,512]{2,1,0:T(8,128)(2,1)S(1)} %get-tuple-element.39.local_all, ...), custom_call_target="tpu_custom_call" | custom-call | flops 786432000 | bytes 6291456 | tf_op jit(solution)/shard_map/later/pallas_call | solution.py:387
  12.7 0.0 collective-permute-done.1.halo_low
  12.7 1.0 %collective-permute-done.2.halo_high = bf16[1024,128]{1,0:T(8,128)(2,1)S(1)} collective-permute-done((bf16[1024,128]{1,0:T(8,128)(2,1)S(1)}, bf16[1024,128]{1,0:T(8,128)(2,1)S(1)}, u32[]{:S(2)}, u32[]{:S(2)}) %collective-permute-start.2) | collective-permute-done | bytes 262176 | tf_op jit(solution)/shard_map/ppermute | solution.py:771
  13.7 1.3 %first.1 = (bf16[1024,512]{1,0:T(8,128)(2,1)S(1)}, bf16[1024,512]{1,0:T(8,128)(2,1)S(1)}, f32[4,1024,128]{2,1,0:T(8,128)S(1)}, bf16[128,128]{1,0:T(8,128)(2,1)S(1)}) custom-call(s32[1]{0:T(128)} %bitcast.sec, s32[1]{0:T(128)} %bitcast.1.tok, bf16[2,1024,512]{2,1,0:T(8,128)(2,1)S(1)} %get-tuple-element.39.local_all, ...), custom_call_target="tpu_custom_call", output_to_operand_aliasing={{0}: (13, {}), {1}: (14, {})} | custom-call | flops 262144000 | bytes 6291456 | tf_op jit(solution)/shard_map/first/pallas_call | solution.py:482
  15.0 0.8 %collective-permute-start.3 = (bf16[128,128]{1,0:T(8,128)(2,1)S(1)}, bf16[128,128]{1,0:T(8,128)(2,1)S(1)}, u32[]{:S(2)}, u32[]{:S(2)}) collective-permute-start(bf16[128,128]{1,0:T(8,128)(2,1)S(1)} %get-tuple-element.66), channel_id=1, source_target_pairs={{0,1},{1,0},{2,3},{3,2},{4,5},{5,4},{6,7},{7,6},{8,9},{9,8},{10,11... | collective-permute-start | bytes 98312 | tf_op jit(solution)/shard_map/ppermute | solution.py:764
  15.8 1.2 %collective-permute-start.4 = (bf16[128,128]{1,0:T(8,128)(2,1)S(1)}, bf16[128,128]{1,0:T(8,128)(2,1)S(1)}, u32[]{:S(2)}, u32[]{:S(2)}) collective-permute-start(bf16[128,128]{1,0:T(8,128)(2,1)S(1)} %get-tuple-element.66), channel_id=1, source_target_pairs={{0,2},{1,3},{2,0},{3,1},{4,6},{5,7},{6,4},{7,5},{8,10},{9,11},{10,... | collective-permute-start | bytes 98312 | tf_op jit(solution)/shard_map/ppermute | solution.py:764
  17.0 0.9 %collective-permute-start.5 = (bf16[128,128]{1,0:T(8,128)(2,1)S(1)}, bf16[128,128]{1,0:T(8,128)(2,1)S(1)}, u32[]{:S(2)}, u32[]{:S(2)}) collective-permute-start(bf16[128,128]{1,0:T(8,128)(2,1)S(1)} %get-tuple-element.66), channel_id=1, source_target_pairs={{0,3},{1,2},{2,1},{3,0},{4,7},{5,6},{6,5},{7,4},{8,11},{9,10},{10,... | collective-permute-start | bytes 98312 | tf_op jit(solution)/shard_map/ppermute | solution.py:764
  17.9 1.4 %within.1.within_all = f32[1024,512]{1,0:T(8,128)S(1)} custom-call(bf16[1024,512]{1,0:T(8,128)(2,1)S(1)} %get-tuple-element.55.signals_all, f32[1024,128]{1,0:T(8,128)S(1)} %get-tuple-element.56.response_all, bf16[256,256]{1,0:T(8,128)(2,1)S(1)} %get-tuple-element.57.fwd_h, bf16[256,256]{1,0:T(8,128)(2,1)S(1)} %get-tuple-element.58.fwd_l, ...), custom_call_target="tpu_custom_call" | custom-call | flops 786432000 | bytes 6291456 | tf_op jit(solution)/shard_map/within/pallas_call | solution.py:547
  19.3 0.0 collective-permute-done.3.rest_0_
  19.3 0.0 collective-permute-done.4.rest_1_
  19.3 1.7 %collective-permute-done.5.rest_2_ = bf16[128,128]{1,0:T(8,128)(2,1)S(1)} collective-permute-done((bf16[128,128]{1,0:T(8,128)(2,1)S(1)}, bf16[128,128]{1,0:T(8,128)(2,1)S(1)}, u32[]{:S(2)}, u32[]{:S(2)}) %collective-permute-start.5) | collective-permute-done | bytes 32800 | tf_op jit(solution)/shard_map/ppermute | solution.py:764
  21.0 1.0 %output.2 = (bf16[1,2048,512]{2,1,0:T(8,128)(2,1)}, bf16[512,512]{1,0:T(8,128)(2,1)S(1)}, bf16[512,512]{1,0:T(8,128)(2,1)S(1)}) custom-call(s32[1]{0:T(128)} %bitcast.sec, s32[1]{0:T(128)} %bitcast.1.tok, bf16[2,1024,512]{2,1,0:T(8,128)(2,1)S(1)} %get-tuple-element.39.local_all, bf16[2,1024,512]{2,1,0:T(8,128)(2,1)S(1)} %get-tuple-element.46.remote_all, ...), custom_call_target="tpu_custom_call" | custom-call | flops 393216000 | bytes 3145728 | tf_op jit(solution)/shard_map/output/pallas_call | solution.py:667
  21.9 0.4 %collective-permute-start.6 = (bf16[512,512]{1,0:T(8,128)(2,1)S(1)}, bf16[512,512]{1,0:T(8,128)(2,1)S(1)}, u32[]{:S(2)}, u32[]{:S(2)}) collective-permute-start(bf16[512,512]{1,0:T(8,128)(2,1)S(1)} %get-tuple-element.69), channel_id=1, source_target_pairs={{0,16},{16,0},{1,17},{17,1},{2,18},{18,2},{3,19},{19,3},{4,20},{20... | collective-permute-start | bytes 1572872 | tf_op jit(solution)/shard_map/ppermute | solution.py:759
  22.4 1.0 %output.3 = (bf16[1,2048,512]{2,1,0:T(8,128)(2,1)}, bf16[512,512]{1,0:T(8,128)(2,1)S(1)}, bf16[512,512]{1,0:T(8,128)(2,1)S(1)}) custom-call(s32[1]{0:T(128)} %bitcast.sec, s32[1]{0:T(128)} %bitcast.1.tok, bf16[2,1024,512]{2,1,0:T(8,128)(2,1)S(1)} %get-tuple-element.39.local_all, ...), custom_call_target="tpu_custom_call", output_to_operand_aliasing={{0}: (14, {})} | custom-call | flops 393216000 | bytes 3145728 | tf_op jit(solution)/shard_map/output/pallas_call | solution.py:667
  23.3 0.2 collective-permute-start.7
  23.5 0.4 %collective-permute-done.6.received = bf16[512,512]{1,0:T(8,128)(2,1)S(1)} collective-permute-done((bf16[512,512]{1,0:T(8,128)(2,1)S(1)}, bf16[512,512]{1,0:T(8,128)(2,1)S(1)}, u32[]{:S(2)}, u32[]{:S(2)}) %collective-permute-start.6) | collective-permute-done | bytes 524320 | tf_op jit(solution)/shard_map/ppermute | solution.py:759
  23.9 1.0 %placing.2.before = bf16[1,2048,512]{2,1,0:T(8,128)(2,1)} custom-call(s32[1]{0:T(128)} %bitcast.sec, s32[1]{0:T(128)} %bitcast.1.tok, bf16[1,2048,512]{2,1,0:T(8,128)(2,1)} %get-tuple-element.68.before, bf16[512,512]{1,0:T(8,128)(2,1)S(1)} %collective-permute-done.6.received, bf16[512,512]{1,0:T(8,128)(2,1)S(1)} %get-tuple-element.70.keep), custom_call_target="tpu_custom_call", output_to_operand_aliasing={{}: (2, {})} | custom-call | flops 524288 | bytes 3145728 | tf_op jit(solution)/shard_map/placing/pallas_call | solution.py:709
  24.9 0.4 %collective-permute-done.7.received = bf16[512,512]{1,0:T(8,128)(2,1)S(1)} collective-permute-done((bf16[512,512]{1,0:T(8,128)(2,1)S(1)}, bf16[512,512]{1,0:T(8,128)(2,1)S(1)}, u32[]{:S(2)}, u32[]{:S(2)}) %collective-permute-start.7) | collective-permute-done | bytes 524320 | tf_op jit(solution)/shard_map/ppermute | solution.py:759
  25.3 1.0 %placing.3 = bf16[1,2048,512]{2,1,0:T(8,128)(2,1)} custom-call(s32[1]{0:T(128)} %bitcast.sec, s32[1]{0:T(128)} %bitcast.1.tok, bf16[1,2048,512]{2,1,0:T(8,128)(2,1)} %placing.2.before, bf16[512,512]{1,0:T(8,128)(2,1)S(1)} %collective-permute-done.7.received, bf16[512,512]{1,0:T(8,128)(2,1)S(1)} %get-tuple-element.72.keep), custom_call_target="tpu_custom_call", output_to_operand_aliasing={{}: (2, {})} | custom-call | flops 524288 | bytes 3145728 | tf_op jit(solution)/shard_map/placing/pallas_call | solution.py:709
Async XLA Ops:
  0.0 6.3 %copy-start = (f32[2048,16]{0,1:T(8,128)S(1)}, f32[2048,16]{0,1:T(8,128)}, u32[]{:S(2)}) copy-start(f32[2048,16]{0,1:T(8,128)} %param.22) | copy-start | bytes 393220
  0.0 6.3 %copy-start.1 = (f32[2048,16]{0,1:T(8,128)S(1)}, f32[2048,16]{0,1:T(8,128)}, u32[]{:S(2)}) copy-start(f32[2048,16]{0,1:T(8,128)} %param.21) | copy-start | bytes 393220
  0.0 9.7 %collective-permute-start = (bf16[2,2048,512]{2,1,0:T(8,128)(2,1)}, bf16[2,2048,512]{2,1,0:T(8,128)(2,1)}, u32[]{:S(2)}, u32[]{:S(2)}) collective-permute-start(bf16[2,2048,512]{2,1,0:T(8,128)(2,1)} %bitcast.7), channel_id=1, source_target_pairs={{0,16},{16,0},{1,17},{17,1},{2,18},{18,2},{3,19},{19,3},{4,20},{20... | collective-permute-start | bytes 12582920 | tf_op jit(solution)/shard_map/ppermute | solution.py:759
  1.4 11.3 %collective-permute-start.1 = (bf16[1024,128]{1,0:T(8,128)(2,1)S(1)}, bf16[1024,128]{1,0:T(8,128)(2,1)S(1)}, u32[]{:S(2)}, u32[]{:S(2)}) collective-permute-start(bf16[1024,128]{1,0:T(8,128)(2,1)S(1)} %get-tuple-element.47), channel_id=1, source_target_pairs={{0,1},{1,2},{2,3},{3,0},{16,16},{17,17},{18,18},{19,19},{4,5},{5,6... | collective-permute-start | bytes 786440 | tf_op jit(solution)/shard_map/ppermute | solution.py:771
  2.1 11.6 %collective-permute-start.2 = (bf16[1024,128]{1,0:T(8,128)(2,1)S(1)}, bf16[1024,128]{1,0:T(8,128)(2,1)S(1)}, u32[]{:S(2)}, u32[]{:S(2)}) collective-permute-start(bf16[1024,128]{1,0:T(8,128)(2,1)S(1)} %get-tuple-element.48), channel_id=1, source_target_pairs={{0,17},{1,18},{2,19},{3,16},{16,0},{17,1},{18,2},{19,3},{4,21},{5,... | collective-permute-start | bytes 786440 | tf_op jit(solution)/shard_map/ppermute | solution.py:771
  15.0 4.3 %collective-permute-start.3 = (bf16[128,128]{1,0:T(8,128)(2,1)S(1)}, bf16[128,128]{1,0:T(8,128)(2,1)S(1)}, u32[]{:S(2)}, u32[]{:S(2)}) collective-permute-start(bf16[128,128]{1,0:T(8,128)(2,1)S(1)} %get-tuple-element.66), channel_id=1, source_target_pairs={{0,1},{1,0},{2,3},{3,2},{4,5},{5,4},{6,7},{7,6},{8,9},{9,8},{10,11... | collective-permute-start | bytes 98312 | tf_op jit(solution)/shard_map/ppermute | solution.py:764
  15.8 3.5 %collective-permute-start.4 = (bf16[128,128]{1,0:T(8,128)(2,1)S(1)}, bf16[128,128]{1,0:T(8,128)(2,1)S(1)}, u32[]{:S(2)}, u32[]{:S(2)}) collective-permute-start(bf16[128,128]{1,0:T(8,128)(2,1)S(1)} %get-tuple-element.66), channel_id=1, source_target_pairs={{0,2},{1,3},{2,0},{3,1},{4,6},{5,7},{6,4},{7,5},{8,10},{9,11},{10,... | collective-permute-start | bytes 98312 | tf_op jit(solution)/shard_map/ppermute | solution.py:764
  17.0 3.9 %collective-permute-start.5 = (bf16[128,128]{1,0:T(8,128)(2,1)S(1)}, bf16[128,128]{1,0:T(8,128)(2,1)S(1)}, u32[]{:S(2)}, u32[]{:S(2)}) collective-permute-start(bf16[128,128]{1,0:T(8,128)(2,1)S(1)} %get-tuple-element.66), channel_id=1, source_target_pairs={{0,3},{1,2},{2,1},{3,0},{4,7},{5,6},{6,5},{7,4},{8,11},{9,10},{10,... | collective-permute-start | bytes 98312 | tf_op jit(solution)/shard_map/ppermute | solution.py:764
  21.9 2.0 %collective-permute-start.6 = (bf16[512,512]{1,0:T(8,128)(2,1)S(1)}, bf16[512,512]{1,0:T(8,128)(2,1)S(1)}, u32[]{:S(2)}, u32[]{:S(2)}) collective-permute-start(bf16[512,512]{1,0:T(8,128)(2,1)S(1)} %get-tuple-element.69), channel_id=1, source_target_pairs={{0,16},{16,0},{1,17},{17,1},{2,18},{18,2},{3,19},{19,3},{4,20},{20... | collective-permute-start | bytes 1572872 | tf_op jit(solution)/shard_map/ppermute | solution.py:759
  23.3 2.0 %collective-permute-start.7 = (bf16[512,512]{1,0:T(8,128)(2,1)S(1)}, bf16[512,512]{1,0:T(8,128)(2,1)S(1)}, u32[]{:S(2)}, u32[]{:S(2)}) collective-permute-start(bf16[512,512]{1,0:T(8,128)(2,1)S(1)} %get-tuple-element.71), channel_id=1, source_target_pairs={{0,16},{16,0},{1,17},{17,1},{2,18},{18,2},{3,19},{19,3},{4,20},{20... | collective-permute-start | bytes 1572872 | tf_op jit(solution)/shard_map/ppermute | solution.py:759
